TPU v7x, 32 devices: a whole 2x2x4 slice. The times are simulated.
32 devices in a mesh: row: 8 (over y, x, core), col: 4 (over z).
Axes of the slice: x: 2, y: 2, z: 4, core: 2. Of those that a mesh axis runs over, the one named last changes fastest.
Arguments:
- potential: float32 [3, 128, 64, 256], P(None, 'row', 'col'), may hold values from -6 to 6
- source: float32 [3, 128, 64, 256], P(None, 'row', 'col'), may hold values from -3.2 to 3.2
- labels: int32 [128, 64, 256], P('row', 'col'), may hold values from 0 to 7
- coil_mask: int32 [128, 64, 256], P('row', 'col'), may hold values 0 or 1
- floor_table: float32 [8], replicated, may hold values from 0.3 to 3
- rise_table: float32 [8], replicated, may hold values from 0.5 to 5
Outputs:
- field: float32 [3, 128, 64, 256], P(None, 'row', 'col')
- reluct: float32 [128, 64, 256], P('row', 'col')
- coarse_target: float32 [3, 16, 8, 32], P(None, None, 'col')
Inputs may be any that keep to these rules, and one draw needn't show every extreme that they name: `labels`: each cell's material.
All inputs are finite; a program needn't handle non-finite values. No bound on the sum of `coil_mask` on one device may be relied on, other than what follows from the above.
Results may differ from a plain program's by a relative error of at most 0.00019.
Values sent between devices are 32-bit elements; how exact they have to be, the bound alone decides.
No kernel may reach another device: no remote copies, remote signals or barrier semaphores. Data moves between devices by JAX's collectives and lax.ppermute only.
A program may use at most 128 MiB of HBM per device.

v0:
```python
import jax
import jax.numpy as jnp
from jax import lax
from jax.sharding import PartitionSpec as P

ITERS = 3
SWEEPS = 2
COARSE_SWEEPS = 16
COARSEN = 8


relax = 0.8


def with_halo(block, sides, width):
    for axis, dim in sides:
        count = lax.axis_size(axis)
        forward = [(i, i + 1) for i in range(count - 1)]
        backward = [(target, source) for source, target in forward]
        low = lax.ppermute(
            lax.slice_in_dim(block, block.shape[dim] - width, None, axis=dim), axis, forward
        )
        high = lax.ppermute(lax.slice_in_dim(block, 0, width, axis=dim), axis, backward)
        block = jnp.concatenate([low, block, high], axis=dim)
    return block


def pad_depth(values):
    widths = [(0, 0)] * (values.ndim - 1) + [(1, 1)]
    return jnp.pad(values, widths)


def pad_plane(values, reach):
    widths = [(0, 0)] * (values.ndim - 3) + [(reach, reach), (reach, reach), (0, 0)]
    return jnp.pad(values, widths)


def field_square(field):

    def along_x(comp):
        return 0.5 * (field[comp, 2:, 1:-1] - field[comp, :-2, 1:-1])

    def along_y(comp):
        return 0.5 * (field[comp, 1:-1, 2:] - field[comp, 1:-1, :-2])

    def along_z(comp):
        padded = pad_depth(field[comp, 1:-1, 1:-1])
        return 0.5 * (padded[..., 2:] - padded[..., :-2])

    first = along_y(2) - along_z(1)
    second = along_z(0) - along_x(2)
    third = along_x(1) - along_y(0)
    return first * first + second * second + third * third


def reluctivity(square, labels, floor_table, rise_table):
    floor_cell = jnp.zeros(labels.shape, jnp.float32)
    rise_cell = jnp.zeros(labels.shape, jnp.float32)
    for label in range(floor_table.shape[0]):
        chosen = labels == label
        floor_cell = jnp.where(chosen, floor_table[label], floor_cell)
        rise_cell = jnp.where(chosen, rise_table[label], rise_cell)
    return floor_cell + rise_cell * (square / (1.0 + square))


def operator(field, reluct):
    centre = reluct[1:-1, 1:-1]
    depth_reluct = pad_depth(centre)
    coeffs = [
        0.5 * (centre + reluct[2:, 1:-1]),
        0.5 * (centre + reluct[:-2, 1:-1]),
        0.5 * (centre + reluct[1:-1, 2:]),
        0.5 * (centre + reluct[1:-1, :-2]),
        0.5 * (centre + depth_reluct[..., 2:]),
        0.5 * (centre + depth_reluct[..., :-2]),
    ]
    centre_cells = field[:, 1:-1, 1:-1]
    depth_field = pad_depth(centre_cells)
    neighbours = [
        field[:, 2:, 1:-1],
        field[:, :-2, 1:-1],
        field[:, 1:-1, 2:],
        field[:, 1:-1, :-2],
        depth_field[..., 2:],
        depth_field[..., :-2],
    ]
    diagonal = coeffs[0]
    offdiag = coeffs[0] * neighbours[0]
    for number in range(1, 6):
        diagonal = diagonal + coeffs[number]
        offdiag = offdiag + coeffs[number] * neighbours[number]
    applied = diagonal * centre_cells - offdiag
    return (diagonal, applied, centre_cells)


def relax_step(field, reluct, driving):
    diagonal, applied, centre = operator(field, reluct)
    return centre + relax * (driving - applied) / diagonal


def restrict(resid, reluct):
    block = COARSEN
    comps, size_x, size_y, size_z = resid.shape
    coarse_resid = resid.reshape(
        comps, size_x // block, block, size_y // block, block, size_z // block, block
    ).sum(axis=(2, 4, 6))
    coarse_reluct = reluct.reshape(
        size_x // block, block, size_y // block, block, size_z // block, block
    ).mean(axis=(1, 3, 5))
    return (coarse_resid, coarse_reluct)


def coarse_solve(coarse_resid, coarse_reluct):
    face_area = float(COARSEN * COARSEN)
    padded_reluct = pad_plane(coarse_reluct, 1)
    target = coarse_resid / face_area

    def sweep_once(count, correction):
        diagonal, applied, centre = operator(pad_plane(correction, 1), padded_reluct)
        return centre + relax * (target - applied) / diagonal

    correction = lax.fori_loop(0, COARSE_SWEEPS, sweep_once, jnp.zeros_like(coarse_resid))
    diagonal, applied, centre = operator(pad_plane(correction, 1), padded_reluct)
    leftover = jnp.sum(target - applied, axis=(1, 2, 3))
    total_diag = jnp.sum(diagonal)
    return correction + (leftover / total_diag)[:, None, None, None]


def spread(correction):
    block = COARSEN
    comps, size_x, size_y, size_z = correction.shape
    wide = jnp.broadcast_to(
        correction[:, :, None, :, None, :, None],
        (comps, size_x, block, size_y, block, size_z, block),
    )
    return wide.reshape(comps, size_x * block, size_y * block, size_z * block)


def potential_edges(field):
    return with_halo(field, (("row", 1), ("col", 2)), 1)


def shards(potential, source, labels, coil_mask, floor_table, rise_table):
    comps, size_x, size_y, size_z = potential.shape
    row_count = lax.axis_size("row")
    row_index = lax.axis_index("row")
    driving = source * coil_mask.astype(jnp.float32)
    field = potential
    reluct = jnp.zeros(labels.shape, jnp.float32)
    coarse_x = size_x // COARSEN
    coarse_target = jnp.zeros(
        (comps, row_count * coarse_x, size_y // COARSEN, size_z // COARSEN), jnp.float32
    )
    for iteration in range(ITERS):
        for section in range(SWEEPS + 1):
            field_pad = potential_edges(field)
            if section == 0:
                reluct = reluctivity(field_square(field_pad), labels, floor_table, rise_table)
                reluct_pad = with_halo(reluct, (("row", 0), ("col", 1)), 1)
            if section < SWEEPS:
                field = relax_step(field_pad, reluct_pad, driving)
            else:
                diagonal, applied, centre = operator(field_pad, reluct_pad)
                resid = driving - applied
        coarse_resid, coarse_reluct = restrict(resid, reluct)
        placed_resid = jnp.zeros(
            (comps, row_count * coarse_x) + coarse_resid.shape[2:], jnp.float32
        )
        placed_resid = lax.dynamic_update_slice_in_dim(
            placed_resid, coarse_resid, row_index * coarse_x, 1
        )
        placed_reluct = jnp.zeros((row_count * coarse_x,) + coarse_reluct.shape[1:], jnp.float32)
        placed_reluct = lax.dynamic_update_slice_in_dim(
            placed_reluct, coarse_reluct, row_index * coarse_x, 0
        )
        stripe_resid, stripe_reluct = lax.psum((placed_resid, placed_reluct), "row")
        coarse_target = stripe_resid / float(COARSEN * COARSEN)
        stripe_correction = coarse_solve(stripe_resid, stripe_reluct)
        correction = lax.dynamic_slice_in_dim(stripe_correction, row_index * coarse_x, coarse_x, 1)
        field = field + spread(correction)
    return (field, reluct, coarse_target)


def solution(mesh):
    in_specs = (
        P(None, "row", "col", None),
        P(None, "row", "col", None),
        P("row", "col", None),
        P("row", "col", None),
        P(),
        P(),
    )
    out_specs = (P(None, "row", "col", None), P("row", "col", None), P(None, None, "col", None))
    return jax.shard_map(shards, mesh=mesh, in_specs=in_specs, out_specs=out_specs, check_vma=False)
```

profile of v0, /device:TPU:0, one launch (start us, length us, event | category | flops | bytes accessed | tf_op | source)
XLA Modules:
  0.0 438.0 jit_solution(5791420597537645787)
XLA Ops:
  1.5 2.3 collective-permute-start
  7.5 1.6 fusion.339
  9.1 1.4 constant_dynamic-update-slice_fusion.4
  10.7 4.4 %collective-permute-start.3 = (f32[3,18,1,256]{3,2,1,0:T(1,128)S(1)}, f32[3,18,1,256]{3,2,1,0:T(1,128)S(1)}, u32[]{:S(2)}, u32[]{:S(2)}) collective-permute-start(f32[3,18,1,256]{3,2,1,0:T(1,128)S(1)} %get-tuple-element.449), channel_id=1, source_target_pairs={{0,1},{1,2},{2,3},{4,5},{5,6},{6,7},{8,9},{9,10},{10,11},{12,13},{... | collective-permute-start | bytes 165896 | tf_op jit(solution)/shard_map/ppermute | solution.py:20
  17.2 4.1 collective-permute-done.2
  21.2 11.5 %fusion.158 = (f32[16,16,256]{2,1,0:T(8,128)S(1)}, f32[16,16,256]{2,1,0:T(8,128)}, f32[16,16,256]{2,1,0:T(8,128)}) fusion(f32[16,16,256]{2,1,0:T(8,128)S(1)} %get-tuple-element.471, f32[16,16,256]{2,1,0:T(8,128)S(1)} %get-tuple-element.470, f32[3,18,16,256]{3,2,1,0:T(8,128)S(1)} %get-tuple-element.498, f32[3,18,1,256]{3,2,1,0:T(1,128)S(1)} %collective-permute-done.3, ...), kind=kLoop, calls=%fused_computation.304 | loop fusion | flops 2883584 | bytes 3878976 | tf_op jit(solution)/shard_map/add | solution.py:63
  34.0 3.5 collective-permute-start.5
  39.7 4.5 %collective-permute-start.7 = (f32[18,1,256]{2,1,0:T(1,128)S(1)}, f32[18,1,256]{2,1,0:T(1,128)S(1)}, u32[]{:S(2)}, u32[]{:S(2)}) collective-permute-start(f32[18,1,256]{2,1,0:T(1,128)S(1)} %get-tuple-element.481), channel_id=1, source_target_pairs={{0,1},{1,2},{2,3},{4,5},{5,6},{6,7},{8,9},{9,10},{10,11},{12,13},{... | collective-permute-start | bytes 55304 | tf_op jit(solution)/shard_map/ppermute | solution.py:20
  48.3 4.6 %collective-permute-start.9 = (f32[3,1,16,256]{3,2,1,0:T(8,128)S(1)}, f32[3,1,16,256]{3,2,1,0:T(8,128)S(1)}, u32[]{:S(2)}, u32[]{:S(2)}) collective-permute-start(f32[3,1,16,256]{3,2,1,0:T(8,128)S(1)} %get-tuple-element.468), channel_id=1, source_target_pairs={{0,4},{4,8},{8,12},{12,16},{16,20},{20,24},{24,28},{1,5},{5,9},{9,... | collective-permute-start | bytes 147464 | tf_op jit(solution)/shard_map/ppermute | solution.py:20
  53.9 3.9 collective-permute-start.11
  59.6 4.3 collective-permute-done.10
  66.7 5.1 %collective-permute-start.13 = (f32[3,1,16,256]{3,2,1,0:T(8,128)}, f32[3,1,16,256]{3,2,1,0:T(8,128)S(1)}, u32[]{:S(2)}, u32[]{:S(2)}) collective-permute-start(f32[3,1,16,256]{3,2,1,0:T(8,128)} %get-tuple-element.466), channel_id=1, source_target_pairs={{0,4},{4,8},{8,12},{12,16},{16,20},{20,24},{24,28},{1,5},{5,9},{9,... | collective-permute-start | bytes 147464 | tf_op jit(solution)/shard_map/ppermute | solution.py:20
  71.8 3.7 reshape.151
  75.5 3.3 reduce_sum.108
  78.8 3.5 collective-permute-start.15
  85.5 2.9 collective-permute-done.14
  88.4 2.5 fusion.46
  90.9 9.7 %reshape.152 = f32[3,2,8,2,8,32,8]{6,5,4,3,2,1,0:T(8,128)} reshape(f32[3,16,16,256]{3,2,1,0:T(8,128)} %fusion.46) | data formatting | bytes 1572864 | tf_op jit(solution)/shard_map/reshape | solution.py:104
  100.6 5.8 %reduce_sum.109 = f32[3,2,2,32]{3,2,1,0:T(2,128)S(1)} reduce(f32[3,2,8,2,8,32,8]{6,5,4,3,2,1,0:T(8,128)} %reshape.152, f32[]{:T(128)} %constant.115.clone.1), dimensions={2,4,6}, to_apply=%region_2.3 | reduce | flops 196224 | bytes 787972 | tf_op jit(solution)/shard_map/reduce_sum | solution.py:106
  106.4 26.8 %all-reduce.41 = (f32[16,2,32]{2,1,0:T(2,128)S(1)}, f32[3,16,2,32]{3,2,1,0:T(2,128)S(1)}) all-reduce(f32[16,2,32]{2,1,0:T(2,128)} %constant_dynamic-update-slice_fusion.12, f32[3,16,2,32]{3,2,1,0:T(2,128)S(1)} %constant_dynamic-update-slice_fusion.11), channel_id=1, replica_groups=mesh['row'=8,'col'=4] {'row'}, use_global_device_ids=true, to_apply=%region_1.2 | all-reduce | flops 4096 | bytes 32768 | tf_op jit(solution)/shard_map/psum | solution.py:176
  134.0 6.1 %while.39 = (s32[]{:T(128)}, f32[3,16,2,32]{3,2,1,0:T(2,128)S(1)}, f32[16,2,32]{2,1,0:T(2,128)S(1)}, f32[16,2,32]{2,1,0:T(2,128)S(1)}, f32[16,2,32]{2,1,0:T(2,12...) while((s32[]{:T(128)}, f32[3,16,2,32]{3,2,1,0:T(2,128)S(1)}, ...), condition=%wide.region_5.6_spmd.clone, body=%wide.region_4.5_spmd.clone.sunk | while | flops 68611 | bytes 147575 | solution.py:122
  141.2 6.3 %broadcast_in_dim.119 = f32[3,2,8,2,8,32,8]{6,5,4,3,2,1,0:T(8,128)} broadcast(f32[3,2,2,32]{3,2,1,0:T(2,128)S(1)} %dynamic-slice_add_fusion.2), dimensions={0,1,3,5} | broadcast | bytes 787968 | tf_op jit(solution)/shard_map/broadcast_in_dim | solution.py:132
  147.4 9.8 %reshape.153 = f32[3,16,16,256]{3,2,1,0:T(8,128)S(1)} reshape(f32[3,2,8,2,8,32,8]{6,5,4,3,2,1,0:T(8,128)} %broadcast_in_dim.119) | data formatting | bytes 1572864 | tf_op jit(solution)/shard_map/reshape | solution.py:136
  158.7 3.0 collective-permute-start.16
  162.7 3.5 collective-permute-start.19
  168.0 4.5 %collective-permute-done.18 = f32[3,18,1,256]{3,2,1,0:T(1,128)S(1)} collective-permute-done((f32[3,18,1,256]{3,2,1,0:T(1,128)S(1)}, f32[3,18,1,256]{3,2,1,0:T(1,128)S(1)}, u32[]{:S(2)}, u32[]{:S(2)}) %collective-permute-start.18) | collective-permute-done | bytes 55328 | tf_op jit(solution)/shard_map/ppermute | solution.py:23
  174.3 3.0 collective-permute-start.21
  179.5 4.5 %collective-permute-start.23 = (f32[18,1,256]{2,1,0:T(1,128)S(1)}, f32[18,1,256]{2,1,0:T(1,128)S(1)}, u32[]{:S(2)}, u32[]{:S(2)}) collective-permute-start(f32[18,1,256]{2,1,0:T(1,128)S(1)} %get-tuple-element.479), channel_id=1, source_target_pairs={{0,1},{1,2},{2,3},{4,5},{5,6},{6,7},{8,9},{9,10},{10,11},{12,13},{... | collective-permute-start | bytes 55304 | tf_op jit(solution)/shard_map/ppermute | solution.py:20
  184.0 1.4 collective-permute-done.23
  187.9 5.0 %collective-permute-start.25 = (f32[3,1,16,256]{3,2,1,0:T(8,128)S(1)}, f32[3,1,16,256]{3,2,1,0:T(8,128)S(1)}, u32[]{:S(2)}, u32[]{:S(2)}) collective-permute-start(f32[3,1,16,256]{3,2,1,0:T(8,128)S(1)} %get-tuple-element.460), channel_id=1, source_target_pairs={{0,4},{4,8},{8,12},{12,16},{16,20},{20,24},{24,28},{1,5},{5,9},{9,... | collective-permute-start | bytes 147464 | tf_op jit(solution)/shard_map/ppermute | solution.py:20
  193.9 3.9 collective-permute-start.27
  199.6 4.3 collective-permute-done.26
  206.7 5.1 %collective-permute-start.29 = (f32[3,1,16,256]{3,2,1,0:T(8,128)}, f32[3,1,16,256]{3,2,1,0:T(8,128)S(1)}, u32[]{:S(2)}, u32[]{:S(2)}) collective-permute-start(f32[3,1,16,256]{3,2,1,0:T(8,128)} %get-tuple-element.458), channel_id=1, source_target_pairs={{0,4},{4,8},{8,12},{12,16},{16,20},{20,24},{24,28},{1,5},{5,9},{9,... | collective-permute-start | bytes 147464 | tf_op jit(solution)/shard_map/ppermute | solution.py:20
  211.8 3.7 reshape.154
  215.5 3.3 reduce_sum.112
  218.9 2.5 collective-permute-start.31
  224.6 2.9 collective-permute-done.30
  227.5 2.5 fusion.70
  230.0 9.7 %reshape.155 = f32[3,2,8,2,8,32,8]{6,5,4,3,2,1,0:T(8,128)} reshape(f32[3,16,16,256]{3,2,1,0:T(8,128)} %fusion.70) | data formatting | bytes 1572864 | tf_op jit(solution)/shard_map/reshape | solution.py:104
  239.7 5.8 %reduce_sum.113 = f32[3,2,2,32]{3,2,1,0:T(2,128)S(1)} reduce(f32[3,2,8,2,8,32,8]{6,5,4,3,2,1,0:T(8,128)} %reshape.155, f32[]{:T(128)} %constant.115.clone.1), dimensions={2,4,6}, to_apply=%region_10.11 | reduce | flops 196224 | bytes 787972 | tf_op jit(solution)/shard_map/reduce_sum | solution.py:106
  245.5 28.2 %all-reduce.40 = (f32[16,2,32]{2,1,0:T(2,128)S(1)}, f32[3,16,2,32]{3,2,1,0:T(2,128)S(1)}) all-reduce(f32[16,2,32]{2,1,0:T(2,128)} %constant_dynamic-update-slice_fusion.10, f32[3,16,2,32]{3,2,1,0:T(2,128)S(1)} %constant_dynamic-update-slice_fusion.9), channel_id=1, replica_groups=mesh['row'=8,'col'=4] {'row'}, use_global_device_ids=true, to_apply=%region_9.10 | all-reduce | flops 4096 | bytes 32768 | tf_op jit(solution)/shard_map/psum | solution.py:176
  274.5 6.1 %while.40 = (s32[]{:T(128)}, f32[3,16,2,32]{3,2,1,0:T(2,128)S(1)}, f32[16,2,32]{2,1,0:T(2,128)S(1)}, f32[16,2,32]{2,1,0:T(2,128)S(1)}, f32[16,2,32]{2,1,0:T(2,12...) while((s32[]{:T(128)}, f32[3,16,2,32]{3,2,1,0:T(2,128)S(1)}, ...), condition=%wide.region_13.14_spmd.clone, body=%wide.region_12.13_spmd.clone.sunk | while | flops 68611 | bytes 147575 | solution.py:122
  281.6 6.3 %broadcast_in_dim.120 = f32[3,2,8,2,8,32,8]{6,5,4,3,2,1,0:T(8,128)} broadcast(f32[3,2,2,32]{3,2,1,0:T(2,128)S(1)} %dynamic-slice_add_fusion.1), dimensions={0,1,3,5} | broadcast | bytes 787968 | tf_op jit(solution)/shard_map/broadcast_in_dim | solution.py:132
  287.9 9.8 %reshape.156 = f32[3,16,16,256]{3,2,1,0:T(8,128)S(1)} reshape(f32[3,2,8,2,8,32,8]{6,5,4,3,2,1,0:T(8,128)} %broadcast_in_dim.120) | data formatting | bytes 1572864 | tf_op jit(solution)/shard_map/reshape | solution.py:136
  299.2 3.0 collective-permute-start.32
  303.2 2.5 collective-permute-start.35
  307.5 4.5 %collective-permute-done.34 = f32[3,18,1,256]{3,2,1,0:T(1,128)S(1)} collective-permute-done((f32[3,18,1,256]{3,2,1,0:T(1,128)S(1)}, f32[3,18,1,256]{3,2,1,0:T(1,128)S(1)}, u32[]{:S(2)}, u32[]{:S(2)}) %collective-permute-start.34) | collective-permute-done | bytes 55328 | tf_op jit(solution)/shard_map/ppermute | solution.py:23
  313.8 3.0 collective-permute-start.37
  319.0 4.5 %collective-permute-start.39 = (f32[18,1,256]{2,1,0:T(1,128)S(1)}, f32[18,1,256]{2,1,0:T(1,128)S(1)}, u32[]{:S(2)}, u32[]{:S(2)}) collective-permute-start(f32[18,1,256]{2,1,0:T(1,128)S(1)} %get-tuple-element.477), channel_id=1, source_target_pairs={{0,1},{1,2},{2,3},{4,5},{5,6},{6,7},{8,9},{9,10},{10,11},{12,13},{... | collective-permute-start | bytes 55304 | tf_op jit(solution)/shard_map/ppermute | solution.py:20
  327.5 5.0 %collective-permute-start.41 = (f32[3,1,16,256]{3,2,1,0:T(8,128)S(1)}, f32[3,1,16,256]{3,2,1,0:T(8,128)S(1)}, u32[]{:S(2)}, u32[]{:S(2)}) collective-permute-start(f32[3,1,16,256]{3,2,1,0:T(8,128)S(1)} %get-tuple-element.452), channel_id=1, source_target_pairs={{0,4},{4,8},{8,12},{12,16},{16,20},{20,24},{24,28},{1,5},{5,9},{9,... | collective-permute-start | bytes 147464 | tf_op jit(solution)/shard_map/ppermute | solution.py:20
  333.5 3.9 collective-permute-start.43
  339.2 4.3 collective-permute-done.42
  346.2 5.1 %collective-permute-start.45 = (f32[3,1,16,256]{3,2,1,0:T(8,128)}, f32[3,1,16,256]{3,2,1,0:T(8,128)S(1)}, u32[]{:S(2)}, u32[]{:S(2)}) collective-permute-start(f32[3,1,16,256]{3,2,1,0:T(8,128)} %get-tuple-element.450), channel_id=1, source_target_pairs={{0,4},{4,8},{8,12},{12,16},{16,20},{20,24},{24,28},{1,5},{5,9},{9,... | collective-permute-start | bytes 147464 | tf_op jit(solution)/shard_map/ppermute | solution.py:20
  351.4 3.7 reshape.157
  355.0 3.3 reduce_sum.116
  358.4 2.2 collective-permute-start.47
  363.8 2.9 collective-permute-done.46
  366.7 2.5 fusion.94
  369.2 9.7 %reshape.158 = f32[3,2,8,2,8,32,8]{6,5,4,3,2,1,0:T(8,128)} reshape(f32[3,16,16,256]{3,2,1,0:T(8,128)} %fusion.94) | data formatting | bytes 1572864 | tf_op jit(solution)/shard_map/reshape | solution.py:104
  378.9 5.8 %reduce_sum.117 = f32[3,2,2,32]{3,2,1,0:T(2,128)S(1)} reduce(f32[3,2,8,2,8,32,8]{6,5,4,3,2,1,0:T(8,128)} %reshape.158, f32[]{:T(128)} %constant.115.clone.1), dimensions={2,4,6}, to_apply=%region_18.19 | reduce | flops 196224 | bytes 787972 | tf_op jit(solution)/shard_map/reduce_sum | solution.py:106
  384.7 28.2 %all-reduce.39 = (f32[16,2,32]{2,1,0:T(2,128)S(1)}, f32[3,16,2,32]{3,2,1,0:T(2,128)S(1)}) all-reduce(f32[16,2,32]{2,1,0:T(2,128)} %constant_dynamic-update-slice_fusion.8, f32[3,16,2,32]{3,2,1,0:T(2,128)S(1)} %constant_dynamic-update-slice_fusion.7), channel_id=1, replica_groups=mesh['row'=8,'col'=4] {'row'}, use_global_device_ids=true, to_apply=%region_17.18 | all-reduce | flops 4096 | bytes 32768 | tf_op jit(solution)/shard_map/psum | solution.py:176
  413.7 6.1 %while.41 = (s32[]{:T(128)}, f32[3,16,2,32]{3,2,1,0:T(2,128)S(1)}, f32[16,2,32]{2,1,0:T(2,128)S(1)}, f32[16,2,32]{2,1,0:T(2,128)S(1)}, f32[16,2,32]{2,1,0:T(2,12...) while((s32[]{:T(128)}, f32[3,16,2,32]{3,2,1,0:T(2,128)S(1)}, ...), condition=%wide.region_21.22_spmd.clone, body=%wide.region_20.21_spmd.clone.sunk | while | flops 68611 | bytes 147575 | solution.py:122
  420.9 6.3 %broadcast_in_dim.121 = f32[3,2,8,2,8,32,8]{6,5,4,3,2,1,0:T(8,128)} broadcast(f32[3,2,2,32]{3,2,1,0:T(2,128)S(1)} %dynamic-slice_add_fusion), dimensions={0,1,3,5} | broadcast | bytes 787968 | tf_op jit(solution)/shard_map/broadcast_in_dim | solution.py:132
  427.1 9.8 %reshape.159 = f32[3,16,16,256]{3,2,1,0:T(8,128)S(1)} reshape(f32[3,2,8,2,8,32,8]{6,5,4,3,2,1,0:T(8,128)} %broadcast_in_dim.121) | data formatting | bytes 1572864 | tf_op jit(solution)/shard_map/reshape | solution.py:136
  (381 shorter events, 85.4 us)
Async XLA Ops:
  0.6 15.8 %copy-start.18 = (f32[8]{0:T(128)S(1)}, f32[8]{0:T(128)}, u32[]{:S(2)}) copy-start(f32[8]{0:T(128)} %param.16) | copy-start | bytes 100
  1.5 7.6 %collective-permute-start = (f32[3,1,16,256]{3,2,1,0:T(8,128)S(1)}, f32[3,1,16,256]{3,2,1,0:T(8,128)S(1)}, u32[]{:S(2)}, u32[]{:S(2)}) collective-permute-start(f32[3,1,16,256]{3,2,1,0:T(8,128)S(1)} %get-tuple-element.476), channel_id=1, source_target_pairs={{0,4},{4,8},{8,12},{12,16},{16,20},{20,24},{24,28},{1,5},{5,9},{9,... | collective-permute-start | bytes 147464 | tf_op jit(solution)/shard_map/ppermute | solution.py:20
  3.8 6.8 %collective-permute-start.1 = (f32[3,1,16,256]{3,2,1,0:T(8,128)S(1)}, f32[3,1,16,256]{3,2,1,0:T(8,128)S(1)}, u32[]{:S(2)}, u32[]{:S(2)}) collective-permute-start(f32[3,1,16,256]{3,2,1,0:T(8,128)S(1)} %get-tuple-element.475), channel_id=1, source_target_pairs={{4,0},{8,4},{12,8},{16,12},{20,16},{24,20},{28,24},{5,1},{9,5},{13... | collective-permute-start | bytes 147464 | tf_op jit(solution)/shard_map/ppermute | solution.py:23
  7.5 36.8 %copy-start.17 = (s32[16,16,256]{2,1,0:T(8,128)S(1)}, s32[16,16,256]{2,1,0:T(8,128)}, u32[]{:S(2)}) copy-start(s32[16,16,256]{2,1,0:T(8,128)} %param.15) | copy-start | bytes 786436
  10.6 35.4 %copy-start = (f32[3,16,16,256]{3,2,1,0:T(8,128)S(1)}, f32[3,16,16,256]{3,2,1,0:T(8,128)}, u32[]{:S(2)}) copy-start(f32[3,16,16,256]{3,2,1,0:T(8,128)} %param.13) | copy-start | bytes 2359300
  10.6 35.4 %copy-start.1 = (f32[3,16,16,256]{3,2,1,0:T(8,128)S(1)}, f32[3,16,16,256]{3,2,1,0:T(8,128)}, u32[]{:S(2)}) copy-start(f32[3,16,16,256]{3,2,1,0:T(8,128)} %param.12) | copy-start | bytes 2359300
  10.7 6.4 %collective-permute-start.3 = (f32[3,18,1,256]{3,2,1,0:T(1,128)S(1)}, f32[3,18,1,256]{3,2,1,0:T(1,128)S(1)}, u32[]{:S(2)}, u32[]{:S(2)}) collective-permute-start(f32[3,18,1,256]{3,2,1,0:T(1,128)S(1)} %get-tuple-element.449), channel_id=1, source_target_pairs={{0,1},{1,2},{2,3},{4,5},{5,6},{6,7},{8,9},{9,10},{10,11},{12,13},{... | collective-permute-start | bytes 165896 | tf_op jit(solution)/shard_map/ppermute | solution.py:20
  15.2 6.0 %collective-permute-start.2 = (f32[3,18,1,256]{3,2,1,0:T(1,128)S(1)}, f32[3,18,1,256]{3,2,1,0:T(1,128)S(1)}, u32[]{:S(2)}, u32[]{:S(2)}) collective-permute-start(f32[3,18,1,256]{3,2,1,0:T(1,128)S(1)} %get-tuple-element.448), channel_id=1, source_target_pairs={{1,0},{2,1},{3,2},{5,4},{6,5},{7,6},{9,8},{10,9},{11,10},{13,12},{... | collective-permute-start | bytes 165896 | tf_op jit(solution)/shard_map/ppermute | solution.py:23
  32.7 4.8 %collective-permute-start.4 = (f32[1,16,256]{2,1,0:T(8,128)S(1)}, f32[1,16,256]{2,1,0:T(8,128)S(1)}, u32[]{:S(2)}, u32[]{:S(2)}) collective-permute-start(f32[1,16,256]{2,1,0:T(8,128)S(1)} %get-tuple-element.488), channel_id=1, source_target_pairs={{4,0},{8,4},{12,8},{16,12},{20,16},{24,20},{28,24},{5,1},{9,5},{13... | collective-permute-start | bytes 49160 | tf_op jit(solution)/shard_map/ppermute | solution.py:23
  34.0 4.3 collective-permute-start.5
  38.4 5.9 %collective-permute-start.6 = (f32[18,1,256]{2,1,0:T(1,128)S(1)}, f32[18,1,256]{2,1,0:T(1,128)S(1)}, u32[]{:S(2)}, u32[]{:S(2)}) collective-permute-start(f32[18,1,256]{2,1,0:T(1,128)S(1)} %get-tuple-element.482), channel_id=1, source_target_pairs={{1,0},{2,1},{3,2},{5,4},{6,5},{7,6},{9,8},{10,9},{11,10},{13,12},{... | collective-permute-start | bytes 55304 | tf_op jit(solution)/shard_map/ppermute | solution.py:23
  39.7 6.0 %collective-permute-start.7 = (f32[18,1,256]{2,1,0:T(1,128)S(1)}, f32[18,1,256]{2,1,0:T(1,128)S(1)}, u32[]{:S(2)}, u32[]{:S(2)}) collective-permute-start(f32[18,1,256]{2,1,0:T(1,128)S(1)} %get-tuple-element.481), channel_id=1, source_target_pairs={{0,1},{1,2},{2,3},{4,5},{5,6},{6,7},{8,9},{9,10},{10,11},{12,13},{... | collective-permute-start | bytes 55304 | tf_op jit(solution)/shard_map/ppermute | solution.py:20
  45.9 18.8 %copy-start.3 = (f32[16,16,256]{2,1,0:T(8,128)}, f32[16,16,256]{2,1,0:T(8,128)S(1)}, u32[]{:S(2)}) copy-start(f32[16,16,256]{2,1,0:T(8,128)S(1)} %get-tuple-element.415) | copy-start | bytes 786436
  45.9 18.8 %copy-start.5 = (f32[16,16,256]{2,1,0:T(8,128)}, f32[16,16,256]{2,1,0:T(8,128)S(1)}, u32[]{:S(2)}) copy-start(f32[16,16,256]{2,1,0:T(8,128)S(1)} %get-tuple-element.416) | copy-start | bytes 786436
  47.0 5.9 %collective-permute-start.8 = (f32[3,1,16,256]{3,2,1,0:T(8,128)S(1)}, f32[3,1,16,256]{3,2,1,0:T(8,128)S(1)}, u32[]{:S(2)}, u32[]{:S(2)}) collective-permute-start(f32[3,1,16,256]{3,2,1,0:T(8,128)S(1)} %get-tuple-element.469), channel_id=1, source_target_pairs={{4,0},{8,4},{12,8},{16,12},{20,16},{24,20},{28,24},{5,1},{9,5},{13... | collective-permute-start | bytes 147464 | tf_op jit(solution)/shard_map/ppermute | solution.py:23
  48.3 5.5 %collective-permute-start.9 = (f32[3,1,16,256]{3,2,1,0:T(8,128)S(1)}, f32[3,1,16,256]{3,2,1,0:T(8,128)S(1)}, u32[]{:S(2)}, u32[]{:S(2)}) collective-permute-start(f32[3,1,16,256]{3,2,1,0:T(8,128)S(1)} %get-tuple-element.468), channel_id=1, source_target_pairs={{0,4},{4,8},{8,12},{12,16},{16,20},{20,24},{24,28},{1,5},{5,9},{9,... | collective-permute-start | bytes 147464 | tf_op jit(solution)/shard_map/ppermute | solution.py:20
  53.9 5.7 %collective-permute-start.11 = (f32[3,18,1,256]{3,2,1,0:T(1,128)S(1)}, f32[3,18,1,256]{3,2,1,0:T(1,128)S(1)}, u32[]{:S(2)}, u32[]{:S(2)}) collective-permute-start(f32[3,18,1,256]{3,2,1,0:T(1,128)S(1)} %get-tuple-element.447), channel_id=1, source_target_pairs={{0,1},{1,2},{2,3},{4,5},{5,6},{6,7},{8,9},{9,10},{10,11},{12,13},{... | collective-permute-start | bytes 165896 | tf_op jit(solution)/shard_map/ppermute | solution.py:20
  57.8 6.0 %collective-permute-start.10 = (f32[3,18,1,256]{3,2,1,0:T(1,128)S(1)}, f32[3,18,1,256]{3,2,1,0:T(1,128)S(1)}, u32[]{:S(2)}, u32[]{:S(2)}) collective-permute-start(f32[3,18,1,256]{3,2,1,0:T(1,128)S(1)} %get-tuple-element.446), channel_id=1, source_target_pairs={{1,0},{2,1},{3,2},{5,4},{6,5},{7,6},{9,8},{10,9},{11,10},{13,12},{... | collective-permute-start | bytes 165896 | tf_op jit(solution)/shard_map/ppermute | solution.py:23
  65.4 13.4 %collective-permute-start.12 = (f32[3,1,16,256]{3,2,1,0:T(8,128)}, f32[3,1,16,256]{3,2,1,0:T(8,128)S(1)}, u32[]{:S(2)}, u32[]{:S(2)}) collective-permute-start(f32[3,1,16,256]{3,2,1,0:T(8,128)} %get-tuple-element.467), channel_id=1, source_target_pairs={{4,0},{8,4},{12,8},{16,12},{20,16},{24,20},{28,24},{5,1},{9,5},{13... | collective-permute-start | bytes 147464 | tf_op jit(solution)/shard_map/ppermute | solution.py:23
  66.7 12.1 %collective-permute-start.13 = (f32[3,1,16,256]{3,2,1,0:T(8,128)}, f32[3,1,16,256]{3,2,1,0:T(8,128)S(1)}, u32[]{:S(2)}, u32[]{:S(2)}) collective-permute-start(f32[3,1,16,256]{3,2,1,0:T(8,128)} %get-tuple-element.466), channel_id=1, source_target_pairs={{0,4},{4,8},{8,12},{12,16},{16,20},{20,24},{24,28},{1,5},{5,9},{9,... | collective-permute-start | bytes 147464 | tf_op jit(solution)/shard_map/ppermute | solution.py:20
  75.5 12.9 %copy-start.4 = (f32[16,16,256]{2,1,0:T(8,128)S(1)}, f32[16,16,256]{2,1,0:T(8,128)}, u32[]{:S(2)}) copy-start(f32[16,16,256]{2,1,0:T(8,128)} %copy-done.3) | copy-start | bytes 786436
  78.8 6.7 %collective-permute-start.15 = (f32[3,18,1,256]{3,2,1,0:T(1,128)S(1)}, f32[3,18,1,256]{3,2,1,0:T(1,128)S(1)}, u32[]{:S(2)}, u32[]{:S(2)}) collective-permute-start(f32[3,18,1,256]{3,2,1,0:T(1,128)S(1)} %get-tuple-element.445), channel_id=1, source_target_pairs={{0,1},{1,2},{2,3},{4,5},{5,6},{6,7},{8,9},{9,10},{10,11},{12,13},{... | collective-permute-start | bytes 165896 | tf_op jit(solution)/shard_map/ppermute | solution.py:20
  82.3 6.0 %collective-permute-start.14 = (f32[3,18,1,256]{3,2,1,0:T(1,128)S(1)}, f32[3,18,1,256]{3,2,1,0:T(1,128)S(1)}, u32[]{:S(2)}, u32[]{:S(2)}) collective-permute-start(f32[3,18,1,256]{3,2,1,0:T(1,128)S(1)} %get-tuple-element.444), channel_id=1, source_target_pairs={{1,0},{2,1},{3,2},{5,4},{6,5},{7,6},{9,8},{10,9},{11,10},{13,12},{... | collective-permute-start | bytes 165896 | tf_op jit(solution)/shard_map/ppermute | solution.py:23
  157.2 15.3 %copy-start.12 = (f32[16,16,256]{2,1,0:T(8,128)S(1)}, f32[16,16,256]{2,1,0:T(8,128)}, u32[]{:S(2)}) copy-start(f32[16,16,256]{2,1,0:T(8,128)} %get-tuple-element.418) | copy-start | bytes 786436
  157.2 15.3 %copy-start.14 = (f32[16,16,256]{2,1,0:T(8,128)S(1)}, f32[16,16,256]{2,1,0:T(8,128)}, u32[]{:S(2)}) copy-start(f32[16,16,256]{2,1,0:T(8,128)} %get-tuple-element.419) | copy-start | bytes 786436
  157.4 4.3 collective-permute-start.17
  158.7 3.9 collective-permute-start.16
  162.7 5.3 %collective-permute-start.19 = (f32[3,18,1,256]{3,2,1,0:T(1,128)S(1)}, f32[3,18,1,256]{3,2,1,0:T(1,128)S(1)}, u32[]{:S(2)}, u32[]{:S(2)}) collective-permute-start(f32[3,18,1,256]{3,2,1,0:T(1,128)S(1)} %get-tuple-element.443), channel_id=1, source_target_pairs={{0,1},{1,2},{2,3},{4,5},{5,6},{6,7},{8,9},{9,10},{10,11},{12,13},{... | collective-permute-start | bytes 165896 | tf_op jit(solution)/shard_map/ppermute | solution.py:20
  166.2 6.3 %collective-permute-start.18 = (f32[3,18,1,256]{3,2,1,0:T(1,128)S(1)}, f32[3,18,1,256]{3,2,1,0:T(1,128)S(1)}, u32[]{:S(2)}, u32[]{:S(2)}) collective-permute-start(f32[3,18,1,256]{3,2,1,0:T(1,128)S(1)} %get-tuple-element.442), channel_id=1, source_target_pairs={{1,0},{2,1},{3,2},{5,4},{6,5},{7,6},{9,8},{10,9},{11,10},{13,12},{... | collective-permute-start | bytes 165896 | tf_op jit(solution)/shard_map/ppermute | solution.py:23
  173.0 4.3 collective-permute-start.20
  174.3 3.9 collective-permute-start.21
  178.2 5.9 %collective-permute-start.22 = (f32[18,1,256]{2,1,0:T(1,128)S(1)}, f32[18,1,256]{2,1,0:T(1,128)S(1)}, u32[]{:S(2)}, u32[]{:S(2)}) collective-permute-start(f32[18,1,256]{2,1,0:T(1,128)S(1)} %get-tuple-element.480), channel_id=1, source_target_pairs={{1,0},{2,1},{3,2},{5,4},{6,5},{7,6},{9,8},{10,9},{11,10},{13,12},{... | collective-permute-start | bytes 55304 | tf_op jit(solution)/shard_map/ppermute | solution.py:23
  179.5 6.0 %collective-permute-start.23 = (f32[18,1,256]{2,1,0:T(1,128)S(1)}, f32[18,1,256]{2,1,0:T(1,128)S(1)}, u32[]{:S(2)}, u32[]{:S(2)}) collective-permute-start(f32[18,1,256]{2,1,0:T(1,128)S(1)} %get-tuple-element.479), channel_id=1, source_target_pairs={{0,1},{1,2},{2,3},{4,5},{5,6},{6,7},{8,9},{9,10},{10,11},{12,13},{... | collective-permute-start | bytes 55304 | tf_op jit(solution)/shard_map/ppermute | solution.py:20
  185.7 19.0 %copy-start.6 = (f32[16,16,256]{2,1,0:T(8,128)}, f32[16,16,256]{2,1,0:T(8,128)S(1)}, u32[]{:S(2)}) copy-start(f32[16,16,256]{2,1,0:T(8,128)S(1)} %get-tuple-element.400) | copy-start | bytes 786436
  185.7 19.0 %copy-start.8 = (f32[16,16,256]{2,1,0:T(8,128)}, f32[16,16,256]{2,1,0:T(8,128)S(1)}, u32[]{:S(2)}) copy-start(f32[16,16,256]{2,1,0:T(8,128)S(1)} %get-tuple-element.401) | copy-start | bytes 786436
  186.6 6.3 %collective-permute-start.24 = (f32[3,1,16,256]{3,2,1,0:T(8,128)S(1)}, f32[3,1,16,256]{3,2,1,0:T(8,128)S(1)}, u32[]{:S(2)}, u32[]{:S(2)}) collective-permute-start(f32[3,1,16,256]{3,2,1,0:T(8,128)S(1)} %get-tuple-element.461), channel_id=1, source_target_pairs={{4,0},{8,4},{12,8},{16,12},{20,16},{24,20},{28,24},{5,1},{9,5},{13... | collective-permute-start | bytes 147464 | tf_op jit(solution)/shard_map/ppermute | solution.py:23
  187.9 5.9 %collective-permute-start.25 = (f32[3,1,16,256]{3,2,1,0:T(8,128)S(1)}, f32[3,1,16,256]{3,2,1,0:T(8,128)S(1)}, u32[]{:S(2)}, u32[]{:S(2)}) collective-permute-start(f32[3,1,16,256]{3,2,1,0:T(8,128)S(1)} %get-tuple-element.460), channel_id=1, source_target_pairs={{0,4},{4,8},{8,12},{12,16},{16,20},{20,24},{24,28},{1,5},{5,9},{9,... | collective-permute-start | bytes 147464 | tf_op jit(solution)/shard_map/ppermute | solution.py:20
  193.9 5.7 %collective-permute-start.27 = (f32[3,18,1,256]{3,2,1,0:T(1,128)S(1)}, f32[3,18,1,256]{3,2,1,0:T(1,128)S(1)}, u32[]{:S(2)}, u32[]{:S(2)}) collective-permute-start(f32[3,18,1,256]{3,2,1,0:T(1,128)S(1)} %get-tuple-element.441), channel_id=1, source_target_pairs={{0,1},{1,2},{2,3},{4,5},{5,6},{6,7},{8,9},{9,10},{10,11},{12,13},{... | collective-permute-start | bytes 165896 | tf_op jit(solution)/shard_map/ppermute | solution.py:20
  197.8 6.0 %collective-permute-start.26 = (f32[3,18,1,256]{3,2,1,0:T(1,128)S(1)}, f32[3,18,1,256]{3,2,1,0:T(1,128)S(1)}, u32[]{:S(2)}, u32[]{:S(2)}) collective-permute-start(f32[3,18,1,256]{3,2,1,0:T(1,128)S(1)} %get-tuple-element.440), channel_id=1, source_target_pairs={{1,0},{2,1},{3,2},{5,4},{6,5},{7,6},{9,8},{10,9},{11,10},{13,12},{... | collective-permute-start | bytes 165896 | tf_op jit(solution)/shard_map/ppermute | solution.py:23
  205.4 13.4 %collective-permute-start.28 = (f32[3,1,16,256]{3,2,1,0:T(8,128)}, f32[3,1,16,256]{3,2,1,0:T(8,128)S(1)}, u32[]{:S(2)}, u32[]{:S(2)}) collective-permute-start(f32[3,1,16,256]{3,2,1,0:T(8,128)} %get-tuple-element.459), channel_id=1, source_target_pairs={{4,0},{8,4},{12,8},{16,12},{20,16},{24,20},{28,24},{5,1},{9,5},{13... | collective-permute-start | bytes 147464 | tf_op jit(solution)/shard_map/ppermute | solution.py:23
  206.7 12.1 %collective-permute-start.29 = (f32[3,1,16,256]{3,2,1,0:T(8,128)}, f32[3,1,16,256]{3,2,1,0:T(8,128)S(1)}, u32[]{:S(2)}, u32[]{:S(2)}) collective-permute-start(f32[3,1,16,256]{3,2,1,0:T(8,128)} %get-tuple-element.458), channel_id=1, source_target_pairs={{0,4},{4,8},{8,12},{12,16},{16,20},{20,24},{24,28},{1,5},{5,9},{9,... | collective-permute-start | bytes 147464 | tf_op jit(solution)/shard_map/ppermute | solution.py:20
  218.9 5.7 %collective-permute-start.31 = (f32[3,18,1,256]{3,2,1,0:T(1,128)S(1)}, f32[3,18,1,256]{3,2,1,0:T(1,128)S(1)}, u32[]{:S(2)}, u32[]{:S(2)}) collective-permute-start(f32[3,18,1,256]{3,2,1,0:T(1,128)S(1)} %get-tuple-element.439), channel_id=1, source_target_pairs={{0,1},{1,2},{2,3},{4,5},{5,6},{6,7},{8,9},{9,10},{10,11},{12,13},{... | collective-permute-start | bytes 165896 | tf_op jit(solution)/shard_map/ppermute | solution.py:20
  221.4 6.0 %collective-permute-start.30 = (f32[3,18,1,256]{3,2,1,0:T(1,128)S(1)}, f32[3,18,1,256]{3,2,1,0:T(1,128)S(1)}, u32[]{:S(2)}, u32[]{:S(2)}) collective-permute-start(f32[3,18,1,256]{3,2,1,0:T(1,128)S(1)} %get-tuple-element.438), channel_id=1, source_target_pairs={{1,0},{2,1},{3,2},{5,4},{6,5},{7,6},{9,8},{10,9},{11,10},{13,12},{... | collective-permute-start | bytes 165896 | tf_op jit(solution)/shard_map/ppermute | solution.py:23
  297.7 14.4 %copy-start.13 = (f32[16,16,256]{2,1,0:T(8,128)S(1)}, f32[16,16,256]{2,1,0:T(8,128)}, u32[]{:S(2)}) copy-start(f32[16,16,256]{2,1,0:T(8,128)} %get-tuple-element.418) | copy-start | bytes 786436
  297.7 14.3 %copy-start.15 = (f32[16,16,256]{2,1,0:T(8,128)S(1)}, f32[16,16,256]{2,1,0:T(8,128)}, u32[]{:S(2)}) copy-start(f32[16,16,256]{2,1,0:T(8,128)} %get-tuple-element.419) | copy-start | bytes 786436
  297.9 4.3 collective-permute-start.33
  299.2 3.9 collective-permute-start.32
  303.2 4.3 collective-permute-start.35
  305.7 6.3 %collective-permute-start.34 = (f32[3,18,1,256]{3,2,1,0:T(1,128)S(1)}, f32[3,18,1,256]{3,2,1,0:T(1,128)S(1)}, u32[]{:S(2)}, u32[]{:S(2)}) collective-permute-start(f32[3,18,1,256]{3,2,1,0:T(1,128)S(1)} %get-tuple-element.436), channel_id=1, source_target_pairs={{1,0},{2,1},{3,2},{5,4},{6,5},{7,6},{9,8},{10,9},{11,10},{13,12},{... | collective-permute-start | bytes 165896 | tf_op jit(solution)/shard_map/ppermute | solution.py:23
  312.5 38.9 %copy-start.2 = (f32[16,16,256]{2,1,0:T(8,128)}, f32[16,16,256]{2,1,0:T(8,128)S(1)}, u32[]{:S(2)}) copy-start(f32[16,16,256]{2,1,0:T(8,128)S(1)} %fusion.162) | copy-start | bytes 786436
  312.5 4.3 collective-permute-start.36
  313.8 3.9 collective-permute-start.37
  317.7 5.9 %collective-permute-start.38 = (f32[18,1,256]{2,1,0:T(1,128)S(1)}, f32[18,1,256]{2,1,0:T(1,128)S(1)}, u32[]{:S(2)}, u32[]{:S(2)}) collective-permute-start(f32[18,1,256]{2,1,0:T(1,128)S(1)} %get-tuple-element.478), channel_id=1, source_target_pairs={{1,0},{2,1},{3,2},{5,4},{6,5},{7,6},{9,8},{10,9},{11,10},{13,12},{... | collective-permute-start | bytes 55304 | tf_op jit(solution)/shard_map/ppermute | solution.py:23
  319.0 6.0 %collective-permute-start.39 = (f32[18,1,256]{2,1,0:T(1,128)S(1)}, f32[18,1,256]{2,1,0:T(1,128)S(1)}, u32[]{:S(2)}, u32[]{:S(2)}) collective-permute-start(f32[18,1,256]{2,1,0:T(1,128)S(1)} %get-tuple-element.477), channel_id=1, source_target_pairs={{0,1},{1,2},{2,3},{4,5},{5,6},{6,7},{8,9},{9,10},{10,11},{12,13},{... | collective-permute-start | bytes 55304 | tf_op jit(solution)/shard_map/ppermute | solution.py:20
  325.3 19.0 %copy-start.9 = (f32[16,16,256]{2,1,0:T(8,128)}, f32[16,16,256]{2,1,0:T(8,128)S(1)}, u32[]{:S(2)}) copy-start(f32[16,16,256]{2,1,0:T(8,128)S(1)} %get-tuple-element.385) | copy-start | bytes 786436
  325.3 19.0 %copy-start.11 = (f32[16,16,256]{2,1,0:T(8,128)}, f32[16,16,256]{2,1,0:T(8,128)S(1)}, u32[]{:S(2)}) copy-start(f32[16,16,256]{2,1,0:T(8,128)S(1)} %get-tuple-element.386) | copy-start | bytes 786436
  326.2 6.3 %collective-permute-start.40 = (f32[3,1,16,256]{3,2,1,0:T(8,128)S(1)}, f32[3,1,16,256]{3,2,1,0:T(8,128)S(1)}, u32[]{:S(2)}, u32[]{:S(2)}) collective-permute-start(f32[3,1,16,256]{3,2,1,0:T(8,128)S(1)} %get-tuple-element.453), channel_id=1, source_target_pairs={{4,0},{8,4},{12,8},{16,12},{20,16},{24,20},{28,24},{5,1},{9,5},{13... | collective-permute-start | bytes 147464 | tf_op jit(solution)/shard_map/ppermute | solution.py:23
  327.5 5.9 %collective-permute-start.41 = (f32[3,1,16,256]{3,2,1,0:T(8,128)S(1)}, f32[3,1,16,256]{3,2,1,0:T(8,128)S(1)}, u32[]{:S(2)}, u32[]{:S(2)}) collective-permute-start(f32[3,1,16,256]{3,2,1,0:T(8,128)S(1)} %get-tuple-element.452), channel_id=1, source_target_pairs={{0,4},{4,8},{8,12},{12,16},{16,20},{20,24},{24,28},{1,5},{5,9},{9,... | collective-permute-start | bytes 147464 | tf_op jit(solution)/shard_map/ppermute | solution.py:20
  333.5 5.7 %collective-permute-start.43 = (f32[3,18,1,256]{3,2,1,0:T(1,128)S(1)}, f32[3,18,1,256]{3,2,1,0:T(1,128)S(1)}, u32[]{:S(2)}, u32[]{:S(2)}) collective-permute-start(f32[3,18,1,256]{3,2,1,0:T(1,128)S(1)} %get-tuple-element.435), channel_id=1, source_target_pairs={{0,1},{1,2},{2,3},{4,5},{5,6},{6,7},{8,9},{9,10},{10,11},{12,13},{... | collective-permute-start | bytes 165896 | tf_op jit(solution)/shard_map/ppermute | solution.py:20
  337.4 6.0 %collective-permute-start.42 = (f32[3,18,1,256]{3,2,1,0:T(1,128)S(1)}, f32[3,18,1,256]{3,2,1,0:T(1,128)S(1)}, u32[]{:S(2)}, u32[]{:S(2)}) collective-permute-start(f32[3,18,1,256]{3,2,1,0:T(1,128)S(1)} %get-tuple-element.434), channel_id=1, source_target_pairs={{1,0},{2,1},{3,2},{5,4},{6,5},{7,6},{9,8},{10,9},{11,10},{13,12},{... | collective-permute-start | bytes 165896 | tf_op jit(solution)/shard_map/ppermute | solution.py:23
  345.0 13.4 %collective-permute-start.44 = (f32[3,1,16,256]{3,2,1,0:T(8,128)}, f32[3,1,16,256]{3,2,1,0:T(8,128)S(1)}, u32[]{:S(2)}, u32[]{:S(2)}) collective-permute-start(f32[3,1,16,256]{3,2,1,0:T(8,128)} %get-tuple-element.451), channel_id=1, source_target_pairs={{4,0},{8,4},{12,8},{16,12},{20,16},{24,20},{28,24},{5,1},{9,5},{13... | collective-permute-start | bytes 147464 | tf_op jit(solution)/shard_map/ppermute | solution.py:23
  346.2 12.1 %collective-permute-start.45 = (f32[3,1,16,256]{3,2,1,0:T(8,128)}, f32[3,1,16,256]{3,2,1,0:T(8,128)S(1)}, u32[]{:S(2)}, u32[]{:S(2)}) collective-permute-start(f32[3,1,16,256]{3,2,1,0:T(8,128)} %get-tuple-element.450), channel_id=1, source_target_pairs={{0,4},{4,8},{8,12},{12,16},{16,20},{20,24},{24,28},{1,5},{5,9},{9,... | collective-permute-start | bytes 147464 | tf_op jit(solution)/shard_map/ppermute | solution.py:20
  358.4 5.4 %collective-permute-start.47 = (f32[3,18,1,256]{3,2,1,0:T(1,128)S(1)}, f32[3,18,1,256]{3,2,1,0:T(1,128)S(1)}, u32[]{:S(2)}, u32[]{:S(2)}) collective-permute-start(f32[3,18,1,256]{3,2,1,0:T(1,128)S(1)} %get-tuple-element.433), channel_id=1, source_target_pairs={{0,1},{1,2},{2,3},{4,5},{5,6},{6,7},{8,9},{9,10},{10,11},{12,13},{... | collective-permute-start | bytes 165896 | tf_op jit(solution)/shard_map/ppermute | solution.py:20
  360.6 6.0 %collective-permute-start.46 = (f32[3,18,1,256]{3,2,1,0:T(1,128)S(1)}, f32[3,18,1,256]{3,2,1,0:T(1,128)S(1)}, u32[]{:S(2)}, u32[]{:S(2)}) collective-permute-start(f32[3,18,1,256]{3,2,1,0:T(1,128)S(1)} %get-tuple-element.432), channel_id=1, source_target_pairs={{1,0},{2,1},{3,2},{5,4},{6,5},{7,6},{9,8},{10,9},{11,10},{13,12},{... | collective-permute-start | bytes 165896 | tf_op jit(solution)/shard_map/ppermute | solution.py:23
  (3 other events, 31.0 us)
where the time goes:
time: 441 us; the launch traced here: 438 us
  starting transfers between devices  123 us (28%)
  local copies, waits for them, and re-layouts  98.6 us (22%)
  blocking collectives  83.2 us (19%)
  other arithmetic  81.4 us (18%)
  waiting for transfers between devices  47.9 us (11%)
    ppermute x24, starting transfers between devices, with_halo(): lax.ppermute(lax.slice_in_dim(block, block.shape[dim] - width, None, axis...  92.1 us
    psum x3, blocking collectives, shards(): stripe_resid, stripe_reluct = lax.psum((placed_resid, placed_reluct), 'row')  83.2 us
    ppermute x24, waiting for transfers between devices, with_halo(): lax.ppermute(lax.slice_in_dim(block, 0, width, axis=dim), axis, backward)  34.6 us
    ppermute x24, starting transfers between devices, with_halo(): lax.ppermute(lax.slice_in_dim(block, 0, width, axis=dim), axis, backward)  31 us
    reshape x3, local copies, waits for them, and re-layouts, spread(): return wide.reshape(comps, size_x * block, size_y * block, size_z * block)  29.4 us
    reshape x3, local copies, waits for them, and re-layouts, restrict(): resid.reshape(comps, size_x // block, block, size_y // block, block, size...  29 us
    broadcast_in_dim x3, local copies, waits for them, and re-layouts, spread(): jnp.broadcast_to(correction[:, :, None, :, None, :, None], (comps, size_x...  18.8 us
    reduce_sum x3, other arithmetic, restrict(): coarse_resid = resid.reshape(comps, size_x // block, block, size_y // blo...  17.3 us
  transfers between devices with their start and end apart: 48, of which 25 were waited for; matrix products, arithmetic and copies ran while one was open for 7% of the time, Pallas kernels for 0%

commit v1 on v0

v1 whole, which is shorter than its diff:
```python
import functools
import jax
import jax.numpy as jnp
from jax import lax
from jax.experimental import pallas as pl
from jax.experimental.pallas import tpu as pltpu
from jax.sharding import PartitionSpec as P

ITERS = 3
SWEEPS = 2
COARSE_SWEEPS = 16
COARSEN = 8
RELAX = 0.8

HALO = 4
BLOCK = 16
EXT = BLOCK + 2 * HALO
LANES = 128
TOP = 8
CORE = TOP + HALO
ROWS = 40
HIGH = lax.Precision.HIGHEST
X_PAGES = 21
Y_PAGES = 124

VMEM = pl.BlockSpec(memory_space=pltpu.VMEM)
SMEM = pl.BlockSpec(memory_space=pltpu.SMEM)
PARAMS = pltpu.CompilerParams(vmem_limit_bytes=44 * 1024 * 1024)


def f32(*shape):
    return jax.ShapeDtypeStruct(shape, jnp.float32)


def place():
    return (
        lax.axis_index("row"), lax.axis_size("row"), lax.axis_index("col"), lax.axis_size("col"),
    )


def pack_x_kernel(pot_lo, pot_hi, src_lo, src_hi, mask_lo, mask_hi, lab_lo, lab_hi, out_lo, out_hi):
    for pot, src, mask, lab, out, drive, first in (
        (pot_lo, src_lo, mask_lo, lab_lo, out_lo, 0, 0), (pot_hi, src_hi, mask_hi, lab_hi, out_hi, 2, 1),
    ):
        for comp in range(3):
            out[comp * 4 : comp * 4 + 4] = pot[comp]
            for cell in range(2):
                out[12 + comp * 2 + cell] = (
                    2.0 * src[comp, drive + cell] * mask[drive + cell].astype(jnp.float32)
                )
        out[18:21] = lab[first : first + 3].astype(jnp.float32)


def pack_x(potential, source, labels, coil_mask):
    last = BLOCK // HALO - 1
    depth = potential.shape[-1]
    wide = [
        pl.BlockSpec((3, HALO, BLOCK, depth), functools.partial(lambda side, step: (0, side, 0, 0), side))
        for side in (0, last)
    ]
    thin = [
        pl.BlockSpec((HALO, BLOCK, depth), functools.partial(lambda side, step: (side, 0, 0), side))
        for side in (0, last)
    ]
    out = pl.BlockSpec((X_PAGES, BLOCK, depth), lambda step: (0, 0, 0))
    return pl.pallas_call(
        pack_x_kernel,
        grid=(1,),
        in_specs=wide + wide + thin + thin,
        out_specs=[out, out],
        out_shape=[f32(X_PAGES, BLOCK, depth)] * 2,
        compiler_params=PARAMS,
        name="pack_x",
    )(potential, potential, source, source, coil_mask, coil_mask, labels, labels)


def pack_y_kernel(
    pot_lo, pot_hi, src_lo, src_hi, mask_lo, mask_hi, lab_lo, lab_hi, low, high, out_lo, out_hi
):
    for pot, src, mask, lab, out, row, cell in (
        (pot_lo, src_lo, mask_lo, lab_lo, out_lo, 0, 0),
        (pot_hi, src_hi, mask_hi, lab_hi, out_hi, 4, BLOCK - HALO),
    ):
        wide = slice(cell, cell + 4)
        drive = 0 if cell == 0 else 2
        for comp in range(3):
            base = comp * EXT
            out[base : base + 4] = low[comp * 4 : comp * 4 + 4, wide]
            out[base + 4 : base + 20] = pot[comp, :, row : row + 4]
            out[base + 20 : base + 24] = high[comp * 4 : comp * 4 + 4, wide]
            base = 72 + comp * 10
            for x in range(20):
                if x < 2:
                    part = low[12 + comp * 2 + x, cell + drive : cell + drive + 2]
                elif x < 18:
                    rows = slice(row + drive, row + drive + 2)
                    part = 2.0 * src[comp, x - 2, rows] * mask[x - 2, rows].astype(jnp.float32)
                else:
                    part = high[12 + comp * 2 + x - 18, cell + drive : cell + drive + 2]
                out[base + x // 2, (x % 2) * 2 : (x % 2) * 2 + 2] = part
        out[102:105] = low[18:21, wide]
        out[105:121] = lab[:, row : row + 4].astype(jnp.float32)
        out[121:124] = high[18:21, wide]


def pack_y(potential, source, labels, coil_mask, low, high):
    depth = potential.shape[-1]
    wide = [
        pl.BlockSpec((3, BLOCK, 8, depth), functools.partial(lambda side, step: (0, 0, side, 0), side))
        for side in (0, BLOCK // 8 - 1)
    ]
    thin = [
        pl.BlockSpec((BLOCK, 8, depth), functools.partial(lambda side, step: (0, side, 0), side))
        for side in (0, BLOCK // 8 - 1)
    ]
    msg = pl.BlockSpec((X_PAGES, BLOCK, depth), lambda step: (0, 0, 0))
    out = pl.BlockSpec((Y_PAGES, HALO, depth), lambda step: (0, 0, 0))
    return pl.pallas_call(
        pack_y_kernel,
        grid=(1,),
        in_specs=wide + wide + thin + thin + [msg, msg],
        out_specs=[out, out],
        out_shape=[f32(Y_PAGES, HALO, depth)] * 2,
        compiler_params=PARAMS,
        name="pack_y",
    )(
        potential, potential, source, source, coil_mask, coil_mask, labels, labels, low, high
    )


def pack_edge_kernel(field, low, high, out_lo, out_hi):
    for out, cell in ((out_lo, 0), (out_hi, BLOCK - HALO)):
        wide = slice(cell, cell + 4)
        for comp in range(3):
            base = comp * EXT
            out[base : base + 4] = low[comp * 4 : comp * 4 + 4, wide]
            out[base + 4 : base + 20] = field[comp, :, wide]
            out[base + 20 : base + 24] = high[comp * 4 : comp * 4 + 4, wide]


def pack_edge(field, low, high):
    depth = field.shape[-1]
    return pl.pallas_call(
        pack_edge_kernel,
        in_specs=[VMEM] * 3,
        out_specs=[VMEM] * 2,
        out_shape=[f32(3 * EXT, HALO, depth)] * 2,
        compiler_params=PARAMS,
        name="pack_edge",
    )(field, low, high)


def coarse_solve(targets, relucts):
    shape = relucts[0].shape
    count = shape[0]
    lane = lax.broadcasted_iota(jnp.int32, shape, 1)
    row = lax.broadcasted_iota(jnp.int32, shape, 0)
    z = lane % 32
    first_y = (lane // 32) % 2 == 0
    first_x = lane // 64 == 0
    up_ok, down_ok = z < 31, z > 0
    far_ok = jnp.logical_not(
        jnp.logical_or(
            jnp.logical_and(first_x, row == 0),
            jnp.logical_and(jnp.logical_not(first_x), row == count - 1),
        )
    )

    def up(v):
        return pltpu.roll(v, LANES - 1, 1)

    def down(v):
        return pltpu.roll(v, 1, 1)

    def side(v):
        return jnp.where(first_y, pltpu.roll(v, LANES - 32, 1), pltpu.roll(v, 32, 1))

    def near(v):
        return pltpu.roll(v, 64, 1)

    def far(swapped):
        return jnp.where(first_x, pltpu.roll(swapped, 1, 0), pltpu.roll(swapped, count - 1, 0))

    sets = []
    for r in relucts:
        swapped = near(r)
        c_up = r + jnp.where(up_ok, up(r), 0.0)
        c_down = r + jnp.where(down_ok, down(r), 0.0)
        c_side = r + side(r)
        c_near = r + swapped
        c_far = r + jnp.where(far_ok, far(swapped), 0.0)
        diag = ((c_up + c_down) + (c_side + r)) + (c_near + c_far)
        c_up = jnp.where(up_ok, c_up, 0.0)
        c_down = jnp.where(down_ok, c_down, 0.0)
        c_far = jnp.where(far_ok, c_far, 0.0)
        sets.append((c_up, c_down, c_side, c_near, c_far, diag, RELAX / diag))

    def neighbours(coeffs, v):
        c_up, c_down, c_side, c_near, c_far = coeffs[:5]
        swapped = near(v)
        return (
            (c_up * up(v) + c_down * down(v)) + (c_side * side(v) + c_near * swapped)
        ) + c_far * far(swapped)

    doubled = [[2.0 * t for t in stripe] for stripe in targets]
    start = [
        [coeffs[6] * t for t in stripe] for coeffs, stripe in zip(sets, doubled)
    ]

    def sweep(step, values):
        return [
            [
                (1.0 - RELAX) * v + coeffs[6] * (t + neighbours(coeffs, v))
                for v, t in zip(stripe, stripe_t)
            ]
            for coeffs, stripe, stripe_t in zip(sets, values, doubled)
        ]

    values = lax.fori_loop(0, COARSE_SWEEPS - 1, sweep, start)
    out = []
    for coeffs, stripe, stripe_t in zip(sets, values, doubled):
        total = jnp.sum(jnp.sum(coeffs[5], axis=1, keepdims=True), axis=0, keepdims=True)
        done = []
        for v, t in zip(stripe, stripe_t):
            left = t - (coeffs[5] * v - neighbours(coeffs, v))
            left = jnp.sum(jnp.sum(left, axis=1, keepdims=True), axis=0, keepdims=True)
            done.append(v + left / total)
        out.append(done)
    return out


def pick_row(values, index):
    row = lax.broadcasted_iota(jnp.int32, values.shape, 0)
    return jnp.sum(jnp.where(row == index, values, 0.0), axis=0, keepdims=True)


def spread_matrix(group):
    lane = lax.broadcasted_iota(jnp.int32, (LANES, 2 * LANES), 0)
    cell = lax.broadcasted_iota(jnp.int32, (LANES, 2 * LANES), 1)
    return jnp.where(lane == group * 32 + cell // COARSEN, 1.0, 0.0)


def gather_matrix(group):
    cell = lax.broadcasted_iota(jnp.int32, (2 * LANES, LANES), 0)
    lane = lax.broadcasted_iota(jnp.int32, (2 * LANES, LANES), 1)
    return jnp.where(lane == group * 32 + cell // COARSEN, 1.0, 0.0)


def load_stripe(table, gathered, count, pick):
    for row in range(count):
        for comp in range(4):
            table[comp, row : row + 1, :] = pick(row)[comp : comp + 1, :]
    scale = 1.0 / float(COARSEN * COARSEN)
    return [table[comp] * scale for comp in range(3)], table[3]


def put_field(field, core, low, high, back, front, row, rows, col, cols):
    has_low, has_high = row > 0, row < rows - 1
    has_back, has_front = col > 0, col < cols - 1
    both = jnp.logical_and
    for comp in range(3):
        for half in range(2):
            z = slice(half * LANES, half * LANES + LANES)
            own = slice(CORE, CORE + BLOCK)
            field[comp, half, 4:20, own, :] = core[comp, :, :, z]
            pages = slice(comp * 4, comp * 4 + 4)
            field[comp, half, 0:4, own, :] = jnp.where(has_low, low[pages, :, z], 0.0)
            field[comp, half, 20:24, own, :] = jnp.where(has_high, high[pages, :, z], 0.0)
            base = comp * EXT
            for message, there, top in ((back, has_back, TOP), (front, has_front, CORE + BLOCK)):
                for first, last, inside in (
                    (0, 4, both(there, has_low)), (4, 20, there), (20, 24, both(there, has_high)),
                ):
                    field[comp, half, first:last, top : top + HALO, :] = jnp.where(
                        inside, message[base + first : base + last, :, z], 0.0
                    )


def put_material(
    drive, floor, rise, source, coil_mask, labels, low, high, back, front, floor_table, rise_table,
    row, rows, col, cols,
):
    has_low, has_high = row > 0, row < rows - 1
    has_back, has_front = col > 0, col < cols - 1
    both = jnp.logical_and
    for half in range(2):
        z = slice(half * LANES, half * LANES + LANES)
        own = slice(HALO, HALO + BLOCK)
        coil = 2.0 * coil_mask[:, :, z].astype(jnp.float32)
        for comp in range(3):
            drive[comp, half, 4:20, own, :] = source[comp, :, :, z] * coil
            pages = slice(12 + comp * 2, 14 + comp * 2)
            drive[comp, half, 2:4, own, :] = low[pages, :, z]
            drive[comp, half, 20:22, own, :] = high[pages, :, z]
            for x in range(20):
                page, part = 72 + comp * 10 + x // 2, (x % 2) * 2
                drive[comp, half, 2 + x, 2:4, :] = back[page, part : part + 2, z]
                drive[comp, half, 2 + x, 20:22, :] = front[page, part : part + 2, z]
        floor[half, 4:20, own, :] = labels[:, :, z].astype(jnp.float32)
        floor[half, 1:4, own, :] = jnp.where(has_low, low[18:21, :, z], -1.0)
        floor[half, 20:23, own, :] = jnp.where(has_high, high[18:21, :, z], -1.0)
        for message, there, top in ((back, has_back, 0), (front, has_front, HALO + BLOCK)):
            for first, last, inside in (
                (1, 4, both(there, has_low)), (4, 20, there), (20, 23, both(there, has_high)),
            ):
                floor[half, first:last, top : top + HALO, :] = jnp.where(
                    inside, message[101 + first : 101 + last, :, z], -1.0
                )

    def look_up(x, carry):
        for half in range(2):
            label = floor[half, x]
            floor_cell = jnp.zeros_like(label)
            rise_cell = jnp.zeros_like(label)
            for number in range(floor_table.shape[0]):
                chosen = label == float(number)
                floor_cell = jnp.where(chosen, floor_table[number], floor_cell)
                rise_cell = jnp.where(chosen, rise_table[number], rise_cell)
            floor[half, x] = floor_cell
            rise[half, x] = rise_cell
        return carry

    lax.fori_loop(1, EXT - 1, look_up, 0)


def right_of(low, high, last):
    a, b = pltpu.roll(low, LANES - 1, 1), pltpu.roll(high, LANES - 1, 1)
    return jnp.where(last, b, a), b


def left_of(low, high, first):
    a, b = pltpu.roll(low, 1, 1), pltpu.roll(high, 1, 1)
    return a, jnp.where(first, a, b)


def fine_iteration(
    field, other, reluct, c_x, c_y, c_up, c_down, weight, diag, sums, drive, floor, rise,
):
    mid = slice(TOP, TOP + EXT)
    plus = slice(TOP + 1, TOP + EXT + 1)
    minus = slice(TOP - 1, TOP + EXT - 1)
    lane = lax.broadcasted_iota(jnp.int32, (EXT, LANES), 1)
    first, last = lane == 0, lane == LANES - 1

    def reluct_plane(x, carry):
        along_z = []
        for comp in range(2):
            low, high = field[comp, 0, x, mid], field[comp, 1, x, mid]
            r0, r1 = right_of(low, high, last)
            l0, l1 = left_of(low, high, first)
            along_z.append((r0 - jnp.where(first, 0.0, l0), jnp.where(last, 0.0, r1) - l1))
        for half in range(2):
            def along_y(comp):
                return field[comp, half, x, plus] - field[comp, half, x, minus]

            def along_x(comp):
                return field[comp, half, x + 1, mid] - field[comp, half, x - 1, mid]

            b0 = along_y(2) - along_z[1][half]
            b1 = along_z[0][half] - along_x(2)
            b2 = along_x(1) - along_y(0)
            square = 0.25 * (b0 * b0 + b1 * b1 + b2 * b2)
            reluct[half, x, mid] = floor[half, x] + rise[half, x] * (square / (1.0 + square))
        return carry

    lax.fori_loop(1, EXT - 1, reluct_plane, 0)

    for half in range(2):
        c_x[half, 1, mid] = reluct[half, 1, mid] + reluct[half, 2, mid]

    def coeff_plane(x, carry):
        low, high = reluct[0, x, mid], reluct[1, x, mid]
        r0, r1 = right_of(low, high, last)
        l0, l1 = left_of(low, high, first)
        ups = (low + r0, high + jnp.where(last, 0.0, r1))
        downs = (low + jnp.where(first, 0.0, l0), high + l1)
        for half in range(2):
            here = (low, high)[half]
            x_plus = here + reluct[half, x + 1, mid]
            x_minus = here + reluct[half, x - 1, mid]
            y_plus = here + reluct[half, x, plus]
            y_minus = here + reluct[half, x, minus]
            total = ((x_plus + x_minus) + (y_plus + y_minus)) + (ups[half] + downs[half])
            c_x[half, x, mid] = x_plus
            c_y[half, x, mid] = y_plus
            c_up[half, x, mid] = ups[half] if half == 0 else jnp.where(last, 0.0, ups[half])
            c_down[half, x, mid] = jnp.where(first, 0.0, downs[half]) if half == 0 else downs[half]
            diag[half, x, mid] = total
            weight[half, x, mid] = jnp.where(floor[half, x] > 0.0, RELAX / total, 0.0)
        return carry

    lax.fori_loop(2, EXT - 2, coeff_plane, 0)

    def off_diagonal(src, comp, x, rows, first_lane, last_lane):
        rows_plus = slice(rows.start + 1, rows.stop + 1)
        rows_minus = slice(rows.start - 1, rows.stop - 1)
        low, high = src[comp, 0, x, rows], src[comp, 1, x, rows]
        rights = right_of(low, high, last_lane)
        lefts = left_of(low, high, first_lane)
        out = []
        for half in range(2):
            out.append(
                (
                    c_x[half, x, rows] * src[comp, half, x + 1, rows]
                    + c_x[half, x - 1, rows] * src[comp, half, x - 1, rows]
                )
                + (
                    c_y[half, x, rows] * src[comp, half, x, rows_plus]
                    + c_y[half, x, rows_minus] * src[comp, half, x, rows_minus]
                )
                + (c_up[half, x, rows] * rights[half] + c_down[half, x, rows] * lefts[half])
            )
        return (low, high), out

    def sweep(src, dst, begin, end):
        def plane(x, carry):
            for comp in range(3):
                here, off = off_diagonal(src, comp, x, mid, first, last)
                for half in range(2):
                    dst[comp, half, x, mid] = (1.0 - RELAX) * here[half] + weight[half, x, mid] * (
                        drive[comp, half, x] + off[half]
                    )
            return carry

        lax.fori_loop(begin, end, plane, 0)

    sweep(field, other, 2, EXT - 2)
    sweep(other, field, 3, EXT - 3)

    own = slice(CORE, CORE + BLOCK)
    lane = lax.broadcasted_iota(jnp.int32, (BLOCK, LANES), 1)
    first_own, last_own = lane == 0, lane == LANES - 1
    zero = jnp.zeros((BLOCK, LANES), jnp.float32)
    result = jnp.zeros((8, LANES), jnp.float32)
    sums[...] = jnp.zeros(sums.shape, jnp.float32)
    for coarse in range(BLOCK // COARSEN):
        def plane(step, totals):
            x = HALO + coarse * COARSEN + step
            out = []
            for comp in range(3):
                here, off = off_diagonal(field, comp, x, own, first_own, last_own)
                for half in range(2):
                    out.append(
                        totals[comp * 2 + half]
                        + (
                            drive[comp, half, x, HALO : HALO + BLOCK]
                            - (diag[half, x, own] * here[half] - off[half])
                        )
                    )
            for half in range(2):
                out.append(totals[6 + half] + reluct[half, x, own])
            return tuple(out)

        totals = lax.fori_loop(0, COARSEN, plane, (zero,) * 8)
        for part in range(BLOCK // COARSEN):
            group = coarse * 2 + part
            for comp in range(4):
                scale = 0.5 if comp < 3 else 1.0 / float(COARSEN ** 3)
                for half in range(2):
                    block = totals[comp * 2 + half][part * COARSEN : (part + 1) * COARSEN]
                    sums[group, comp : comp + 1, half * LANES : (half + 1) * LANES] = scale * jnp.sum(
                        block, axis=0, keepdims=True
                    )
            result = result + jnp.dot(
                sums[group], gather_matrix(group), precision=HIGH, preferred_element_type=jnp.float32
            )
    return result[0:4]


SCRATCH = (
    [pltpu.VMEM((3, 2, EXT, ROWS, LANES), jnp.float32)] * 2
    + [pltpu.VMEM((2, EXT, ROWS, LANES), jnp.float32)] * 7
    + [pltpu.VMEM((4, 8, 2 * LANES), jnp.float32)]
)


def emit(field, coarse, field_out, low_out, high_out, coarse_out):
    own = slice(CORE, CORE + BLOCK)
    for comp in range(3):
        for half in range(2):
            z = slice(half * LANES, half * LANES + LANES)
            field_out[comp, :, :, z] = field[comp, half, 4:20, own, :]
            if low_out is not None:
                low_out[comp * 4 : comp * 4 + 4, :, z] = field[comp, half, 4:8, own, :]
                high_out[comp * 4 : comp * 4 + 4, :, z] = field[comp, half, 16:20, own, :]
    coarse_out[...] = jnp.broadcast_to(coarse[None], coarse_out.shape)


def first_kernel(
    potential, source, coil_mask, labels, low, high, back, front, floor_table, rise_table,
    field_out, low_out, high_out, coarse_out, drive, floor, rise, *scratch,
):
    row, rows, col, cols = place()
    field = scratch[0]
    put_field(field, potential, low, high, back, front, row, rows, col, cols)
    put_material(
        drive, floor, rise, source, coil_mask, labels, low, high, back, front, floor_table,
        rise_table, row, rows, col, cols,
    )
    coarse = fine_iteration(*scratch, drive, floor, rise)
    emit(field, coarse, field_out, low_out, high_out, coarse_out)


def first_iteration(potential, source, coil_mask, labels, low, high, back, front, tables, devices):
    depth = potential.shape[-1]
    return pl.pallas_call(
        first_kernel,
        in_specs=[VMEM] * 8 + [SMEM] * 2,
        out_specs=[VMEM] * 7,
        out_shape=[
            f32(*potential.shape),
            f32(3 * HALO, BLOCK, depth),
            f32(3 * HALO, BLOCK, depth),
            f32(devices, 4, LANES),
            f32(3, 2, EXT, EXT, LANES),
            f32(2, EXT, EXT, LANES),
            f32(2, EXT, EXT, LANES),
        ],
        scratch_shapes=SCRATCH,
        compiler_params=PARAMS,
        name="first_iteration",
    )(potential, source, coil_mask, labels, low, high, back, front, *tables)


def next_kernel(
    final, gathered, core, low, high, back, front, drive, floor, rise, *refs
):
    if final:
        field_out, coarse_out, reluct_out, *scratch = refs
        low_out = high_out = None
    else:
        field_out, low_out, high_out, coarse_out, *scratch = refs
    table, picked = scratch[-2:]
    scratch = scratch[:-2]
    row, rows, col, cols = place()
    field = scratch[0]
    targets, relucts = [], []
    for stripe in range(3):
        index = jnp.clip(col + stripe - 1, 0, cols - 1)
        target, reluct = load_stripe(
            table.at[stripe], gathered, gathered.shape[0] , lambda r: gathered[r, index]
        )
        targets.append(target)
        relucts.append(reluct)
    corrections = coarse_solve(targets, relucts)
    put_field(field, core, low, high, back, front, row, rows, col, cols)
    picked[...] = jnp.zeros(picked.shape, jnp.float32)
    for stripe in range(3):
        there = (col > 0, True, col < cols - 1)[stripe]
        for comp in range(3):
            for shift in range(3):
                line = pick_row(corrections[stripe][comp], row + shift - 1)
                spot = (stripe * 3 + comp) * 3 + shift
                picked[spot : spot + 1, :] = jnp.where(there, line, 0.0)
    wide = [
        jnp.dot(picked[...], spread_matrix(group), precision=HIGH, preferred_element_type=jnp.float32)
        for group in range(4)
    ]
    mid = slice(TOP, TOP + EXT)
    cell = lax.broadcasted_iota(jnp.int32, (EXT, LANES), 0)
    for begin, end, shift, x in ((0, 4, 0, 1), (4, 12, 1, 0), (12, 20, 1, 1), (20, 24, 2, 0)):
        for comp in range(3):
            for half in range(2):
                def line(stripe, y):
                    spot = (stripe * 3 + comp) * 3 + shift
                    return wide[x * 2 + y][spot : spot + 1, half * LANES : (half + 1) * LANES]

                tile = jnp.where(
                    cell < 12,
                    jnp.where(cell < 4, line(0, 1), line(1, 0)),
                    jnp.where(cell < 20, line(1, 1), line(2, 0)),
                )
                for plane in range(begin, end):
                    field[comp, half, plane, mid] = field[comp, half, plane, mid] + tile
    coarse = fine_iteration(*scratch, drive, floor, rise)
    emit(field, coarse, field_out, low_out, high_out, coarse_out)
    if final:
        reluct = scratch[2]
        for half in range(2):
            reluct_out[:, :, half * LANES : (half + 1) * LANES] = reluct[
                half, 4:20, CORE : CORE + BLOCK, :
            ]


def next_iteration(final, gathered, core, low, high, back, front, material, devices):
    depth = core.shape[-1]
    edge = f32(3 * HALO, BLOCK, depth)
    coarse = f32(devices, 4, LANES)
    if final:
        outs = [f32(*core.shape), coarse, f32(*core.shape[1:])]
    else:
        outs = [f32(*core.shape), edge, edge, coarse]
    return pl.pallas_call(
        functools.partial(next_kernel, final),
        in_specs=[VMEM] * 9,
        out_specs=[VMEM] * len(outs),
        out_shape=outs,
        scratch_shapes=SCRATCH
        + [
            pltpu.VMEM((3, 4, gathered.shape[0], LANES), jnp.float32),
            pltpu.VMEM((32, LANES), jnp.float32),
        ],
        compiler_params=PARAMS,
        name="last_iteration" if final else "next_iteration",
    )(gathered, core, low, high, back, front, *material)


def correct_kernel(gathered, core, field_out, target_out, table, picked):
    row, rows, col, cols = place()
    target, reluct = load_stripe(table, gathered, gathered.shape[0], lambda r: gathered[r])
    correction, = coarse_solve([target], [reluct])
    picked[...] = jnp.zeros(picked.shape, jnp.float32)
    for comp in range(3):
        picked[comp : comp + 1, :] = pick_row(correction[comp], row)
    wide = [
        jnp.dot(picked[...], spread_matrix(group), precision=HIGH, preferred_element_type=jnp.float32)
        for group in range(4)
    ]
    cell = lax.broadcasted_iota(jnp.int32, (BLOCK, 2 * LANES), 0)
    for x in range(2):
        for comp in range(3):
            tile = jnp.where(
                cell < COARSEN, wide[x * 2][comp : comp + 1, :], wide[x * 2 + 1][comp : comp + 1, :]
            )
            for plane in range(x * COARSEN, (x + 1) * COARSEN):
                field_out[comp, plane] = core[comp, plane] + tile
    for comp in range(3):
        for x in range(2):
            for y in range(2):
                group = x * 2 + y
                moved = target[comp] if group == 0 else pltpu.roll(target[comp], LANES - 32 * group, 1)
                for r in range(gathered.shape[0]):
                    target_out[comp, 2 * r + x, y : y + 1, :] = moved[r : r + 1, 0:32]


def correct(gathered, core):
    rows = gathered.shape[0]
    return pl.pallas_call(
        correct_kernel,
        in_specs=[VMEM] * 2,
        out_specs=[VMEM] * 2,
        out_shape=[f32(*core.shape), f32(3, 2 * rows, 2, 32)],
        scratch_shapes=[
            pltpu.VMEM((4, rows, LANES), jnp.float32),
            pltpu.VMEM((8, LANES), jnp.float32),
        ],
        compiler_params=PARAMS,
        name="correct",
    )(gathered, core)


def swap(axis, to_low, to_high):
    count = lax.axis_size(axis)
    forward = [(i, (i + 1) % count) for i in range(count)]
    backward = [(target, source) for source, target in forward]
    return lax.ppermute(to_high, axis, forward), lax.ppermute(to_low, axis, backward)


def shards(potential, source, labels, coil_mask, floor_table, rise_table):
    rows, cols = lax.axis_size("row"), lax.axis_size("col")
    low, high = swap("row", *pack_x(potential, source, labels, coil_mask))
    back, front = swap("col", *pack_y(potential, source, labels, coil_mask, low, high))
    field, to_low, to_high, coarse, *material = first_iteration(
        potential, source, coil_mask, labels, low, high, back, front, (floor_table, rise_table),
        rows * cols,
    )
    for iteration in range(1, ITERS):
        final = iteration == ITERS - 1
        gathered = lax.all_to_all(coarse, ("row", "col"), 0, 0)
        gathered = gathered.reshape(rows, cols, 4, LANES)
        low, high = swap("row", to_low, to_high)
        back, front = swap("col", *pack_edge(field, low, high))
        outs = next_iteration(
            final, gathered, field, low, high, back, front, material, rows if final else rows * cols
        )
        if final:
            field, coarse, reluct = outs
        else:
            field, to_low, to_high, coarse = outs
    gathered = lax.all_to_all(coarse, "row", 0, 0)
    field, coarse_target = correct(gathered, field)
    return (field, reluct, coarse_target)


def solution(mesh):
    in_specs = (
        P(None, "row", "col", None),
        P(None, "row", "col", None),
        P("row", "col", None),
        P("row", "col", None),
        P(),
        P(),
    )
    out_specs = (P(None, "row", "col", None), P("row", "col", None), P(None, None, "col", None))
    return jax.shard_map(shards, mesh=mesh, in_specs=in_specs, out_specs=out_specs, check_vma=False)
```

time: 441 us -> 147 us (0.33)
  starting transfers between devices: 123 us -> 20.5 us
  local copies, waits for them, and re-layouts: 98.6 us -> 4.17 us
  other arithmetic: 81.4 us -> 0 us
  blocking collectives: 83.2 us -> 38.8 us
  Pallas kernels: 0 us -> 43.7 us
  waiting for transfers between devices: 47.9 us -> 38.5 us
    ppermute x48 -> x12, starting transfers between devices: 123 us -> 20.5 us  [the longest x6 16.4 us: swap(): lax.ppermute(to_low, axis, backward)]
    psum x3 -> x0, blocking collectives: 83.2 us -> none  [shards(): stripe_resid, stripe_reluct = lax.psum((placed_resid, placed_reluct), 'row')]
    reshape x9 -> x0, local copies, waits for them, and re-layouts: 69.4 us -> none  [the longest x3 29.4 us: spread(): return wide.reshape(comps, size_x * block, size_y * block, size_z * block)]
    pallas_call x0 -> x8, Pallas kernels: none -> 43.7 us  [the longest x2 27.8 us: next_iteration(): pl.pallas_call(functools.partial(next_kernel, final), in_specs=[VMEM] * 9...]
    all_to_all x0 -> x3, blocking collectives: none -> 38.8 us  [the longest x2 31 us: shards(): gathered = lax.all_to_all(coarse, ('row', 'col'), 0, 0)]
    add x114 -> x0, other arithmetic: 34.5 us -> none  [the longest x3 12.4 us: reluctivity(): return floor_cell + rise_cell * (square / (1.0 + square))]
    reduce_sum x12 -> x0, other arithmetic: 30.2 us -> none  [the longest x3 17.3 us: restrict(): coarse_resid = resid.reshape(comps, size_x // block, block, size_y // blo...]
    broadcast_in_dim x3 -> x0, local copies, waits for them, and re-layouts: 18.8 us -> none  [spread(): jnp.broadcast_to(correction[:, :, None, :, None, :, None], (comps, size_x...]
  transfers between devices with their start and end apart: 48 -> 12, of which waited for: 25 -> 6; matrix products, arithmetic and copies ran while one was open for 7% -> 0% of each run, Pallas kernels for 0% -> 0%
where the time goes in v1:
time: 147 us; the launch traced here: 146 us
  Pallas kernels  43.7 us (30%)
  blocking collectives  38.8 us (26%)
  waiting for transfers between devices  38.5 us (26%)
  starting transfers between devices  20.5 us (14%)
  local copies, waits for them, and re-layouts  4.17 us (3%)
    all_to_all x2, blocking collectives, shards(): gathered = lax.all_to_all(coarse, ('row', 'col'), 0, 0)  31 us
    pallas_call x2, Pallas kernels, next_iteration(): pl.pallas_call(functools.partial(next_kernel, final), in_specs=[VMEM] * 9...  27.8 us
    ppermute x6, waiting for transfers between devices, swap(): lax.ppermute(to_high, axis, forward)  25.9 us
    ppermute x6, starting transfers between devices, swap(): lax.ppermute(to_low, axis, backward)  16.4 us
    ppermute x6, waiting for transfers between devices, swap(): lax.ppermute(to_low, axis, backward)  12.6 us
    pallas_call x1, Pallas kernels, first_iteration(): pl.pallas_call(first_kernel, in_specs=[VMEM] * 8 + [SMEM] * 2, out_specs=...  12.5 us
    all_to_all x1, blocking collectives, shards(): gathered = lax.all_to_all(coarse, 'row', 0, 0)  7.82 us
    unnamed x12, local copies, waits for them, and re-layouts  4.17 us
  transfers between devices with their start and end apart: 12, of which 6 were waited for; matrix products, arithmetic and copies ran while one was open for 0% of the time, Pallas kernels for 0%

profile of v1, /device:TPU:0, one launch (start us, length us, event | category | flops | bytes accessed | tf_op | source)
XLA Modules:
  0.0 146.4 jit_solution(7763025828291605111)
XLA Ops:
  0.6 0.0 copy-start
  0.6 1.1 copy-done
  1.8 0.0 copy-start.1
  1.8 1.1 copy-done.1
  2.9 0.0 copy-start.2
  2.9 0.9 copy-done.2
  3.8 0.0 copy-start.3
  3.9 0.9 copy-done.3
  4.9 0.5 collective-permute-start
  5.4 0.0 copy-start.4
  5.4 0.0 copy-start.5
  5.4 3.0 %collective-permute-start.1 = (f32[21,16,256]{2,1,0:T(8,128)S(1)}, f32[21,16,256]{2,1,0:T(8,128)S(1)}, u32[]{:S(2)}, u32[]{:S(2)}) collective-permute-start(f32[21,16,256]{2,1,0:T(8,128)S(1)} %get-tuple-element.28), channel_id=1, source_target_pairs={{4,0},{8,4},{12,8},{16,12},{20,16},{24,20},{28,24},{0,28},{5,1},{9... | collective-permute-start | bytes 1032200 | tf_op jit(solution)/shard_map/ppermute | solution.py:656
  8.3 5.9 %collective-permute-done.low = f32[21,16,256]{2,1,0:T(8,128)S(1)} collective-permute-done((f32[21,16,256]{2,1,0:T(8,128)S(1)}, f32[21,16,256]{2,1,0:T(8,128)S(1)}, u32[]{:S(2)}, u32[]{:S(2)}) %collective-permute-start) | collective-permute-done | bytes 344096 | tf_op jit(solution)/shard_map/ppermute | solution.py:656
  14.2 1.5 %collective-permute-done.1.high = f32[21,16,256]{2,1,0:T(8,128)S(1)} collective-permute-done((f32[21,16,256]{2,1,0:T(8,128)S(1)}, f32[21,16,256]{2,1,0:T(8,128)S(1)}, u32[]{:S(2)}, u32[]{:S(2)}) %collective-permute-start.1) | collective-permute-done | bytes 344096 | tf_op jit(solution)/shard_map/ppermute | solution.py:656
  15.7 0.3 pack_y.1
  16.0 1.6 %collective-permute-start.2 = (f32[124,4,256]{2,1,0:T(4,128)S(1)}, f32[124,4,256]{2,1,0:T(4,128)S(1)}, u32[]{:S(2)}, u32[]{:S(2)}) collective-permute-start(f32[124,4,256]{2,1,0:T(4,128)S(1)} %get-tuple-element.29), channel_id=1, source_target_pairs={{0,1},{1,2},{2,3},{3,0},{4,5},{5,6},{6,7},{7,4},{8,9},{9,10},{10,1... | collective-permute-start | bytes 1523720 | tf_op jit(solution)/shard_map/ppermute | solution.py:656
  17.7 2.2 %collective-permute-start.3 = (f32[124,4,256]{2,1,0:T(4,128)S(1)}, f32[124,4,256]{2,1,0:T(4,128)S(1)}, u32[]{:S(2)}, u32[]{:S(2)}) collective-permute-start(f32[124,4,256]{2,1,0:T(4,128)S(1)} %get-tuple-element.30), channel_id=1, source_target_pairs={{1,0},{2,1},{3,2},{0,3},{5,4},{6,5},{7,6},{4,7},{9,8},{10,9},{11,1... | collective-permute-start | bytes 1523720 | tf_op jit(solution)/shard_map/ppermute | solution.py:656
  19.9 11.7 %collective-permute-done.2.back = f32[124,4,256]{2,1,0:T(4,128)S(1)} collective-permute-done((f32[124,4,256]{2,1,0:T(4,128)S(1)}, f32[124,4,256]{2,1,0:T(4,128)S(1)}, u32[]{:S(2)}, u32[]{:S(2)}) %collective-permute-start.2) | collective-permute-done | bytes 507936 | tf_op jit(solution)/shard_map/ppermute | solution.py:656
  31.6 11.0 %collective-permute-done.3.front = f32[124,4,256]{2,1,0:T(4,128)S(1)} collective-permute-done((f32[124,4,256]{2,1,0:T(4,128)S(1)}, f32[124,4,256]{2,1,0:T(4,128)S(1)}, u32[]{:S(2)}, u32[]{:S(2)}) %collective-permute-start.3) | collective-permute-done | bytes 507936 | tf_op jit(solution)/shard_map/ppermute | solution.py:656
  42.7 0.0 copy-done.4
  42.7 0.0 copy-done.5
  42.7 12.5 %first_iteration.1 = (f32[3,16,16,256]{3,2,1,0:T(8,128)S(1)}, f32[12,16,256]{2,1,0:T(8,128)S(1)}, f32[12,16,256]{2,1,0:T(8,128)S(1)}, f32[32,4,128]{2,1,0:T(4,12...) custom-call(f32[3,16,16,256]{3,2,1,0:T(8,128)S(1)} %copy-done, ...), custom_call_target="tpu_custom_call" | custom-call | tf_op jit(solution)/shard_map/first_iteration/pallas_call | solution.py:506
  55.2 0.2 collective-permute-start.4
  55.4 2.5 %collective-permute-start.5 = (f32[12,16,256]{2,1,0:T(8,128)S(1)}, f32[12,16,256]{2,1,0:T(8,128)S(1)}, u32[]{:S(2)}, u32[]{:S(2)}) collective-permute-start(f32[12,16,256]{2,1,0:T(8,128)S(1)} %get-tuple-element.34), channel_id=1, source_target_pairs={{4,0},{8,4},{12,8},{16,12},{20,16},{24,20},{28,24},{0,28},{5,1},{9... | collective-permute-start | bytes 589832 | tf_op jit(solution)/shard_map/ppermute | solution.py:656
  57.9 4.4 %collective-permute-done.4.low = f32[12,16,256]{2,1,0:T(8,128)S(1)} collective-permute-done((f32[12,16,256]{2,1,0:T(8,128)S(1)}, f32[12,16,256]{2,1,0:T(8,128)S(1)}, u32[]{:S(2)}, u32[]{:S(2)}) %collective-permute-start.4) | collective-permute-done | bytes 196640 | tf_op jit(solution)/shard_map/ppermute | solution.py:656
  62.3 0.0 collective-permute-done.5.high
  62.4 1.1 collective-permute-start.6
  63.5 2.8 %collective-permute-start.7 = (f32[72,4,256]{2,1,0:T(4,128)S(1)}, f32[72,4,256]{2,1,0:T(4,128)S(1)}, u32[]{:S(2)}, u32[]{:S(2)}) collective-permute-start(f32[72,4,256]{2,1,0:T(4,128)S(1)} %get-tuple-element.36), channel_id=1, source_target_pairs={{1,0},{2,1},{3,2},{0,3},{5,4},{6,5},{7,6},{4,7},{9,8},{10,9},{11,1... | collective-permute-start | bytes 884744 | tf_op jit(solution)/shard_map/ppermute | solution.py:656
  66.3 15.4 %all_to_all.15 = f32[32,4,128]{2,1,0:T(4,128)S(1)} all-to-all(f32[32,4,128]{2,1,0:T(4,128)S(1)} %get-tuple-element.31), channel_id=1, replica_groups=mesh['row'=8,'col'=4] {'row','col'}, dimensions={0} | all-to-all | bytes 131072 | tf_op jit(solution)/shard_map/all_to_all | solution.py:669
  81.7 0.0 collective-permute-done.6.back
  81.7 0.0 collective-permute-done.7.front
  81.7 13.6 %next_iteration.1 = (f32[3,16,16,256]{3,2,1,0:T(8,128)S(1)}, f32[12,16,256]{2,1,0:T(8,128)S(1)}, f32[12,16,256]{2,1,0:T(8,128)S(1)}, f32[32,4,128]{2,1,0:T(4,128)S(1)}) custom-call(f32[8,4,4,128]{3,2,1,0:T(4,128)S(1)} %bitcast.3, f32[3,16,16,256]{3,2,1,0:T(8,128)S(1)} %get-tuple-element.32.field.core, f32[12,16,256]{2,1,0:T(8,128)S(1)} %collective-permute-done.4.low, ...), custom_call_target="tpu_custom_call" | custom-call | tf_op jit(solution)/shard_map/next_iteration/pallas_call | solution.py:593
  95.3 0.2 collective-permute-start.8
  95.5 2.5 %collective-permute-start.9 = (f32[12,16,256]{2,1,0:T(8,128)S(1)}, f32[12,16,256]{2,1,0:T(8,128)S(1)}, u32[]{:S(2)}, u32[]{:S(2)}) collective-permute-start(f32[12,16,256]{2,1,0:T(8,128)S(1)} %get-tuple-element.43), channel_id=1, source_target_pairs={{4,0},{8,4},{12,8},{16,12},{20,16},{24,20},{28,24},{0,28},{5,1},{9... | collective-permute-start | bytes 589832 | tf_op jit(solution)/shard_map/ppermute | solution.py:656
  98.0 3.9 %collective-permute-done.8.low = f32[12,16,256]{2,1,0:T(8,128)S(1)} collective-permute-done((f32[12,16,256]{2,1,0:T(8,128)S(1)}, f32[12,16,256]{2,1,0:T(8,128)S(1)}, u32[]{:S(2)}, u32[]{:S(2)}) %collective-permute-start.8) | collective-permute-done | bytes 196640 | tf_op jit(solution)/shard_map/ppermute | solution.py:656
  101.9 0.0 collective-permute-done.9.high
  102.0 0.5 collective-permute-start.10
  102.5 3.3 %collective-permute-start.11 = (f32[72,4,256]{2,1,0:T(4,128)S(1)}, f32[72,4,256]{2,1,0:T(4,128)S(1)}, u32[]{:S(2)}, u32[]{:S(2)}) collective-permute-start(f32[72,4,256]{2,1,0:T(4,128)S(1)} %get-tuple-element.45), channel_id=1, source_target_pairs={{1,0},{2,1},{3,2},{0,3},{5,4},{6,5},{7,6},{4,7},{9,8},{10,9},{11,1... | collective-permute-start | bytes 884744 | tf_op jit(solution)/shard_map/ppermute | solution.py:656
  105.9 15.6 %all_to_all.16 = f32[32,4,128]{2,1,0:T(4,128)S(1)} all-to-all(f32[32,4,128]{2,1,0:T(4,128)S(1)} %get-tuple-element.40), channel_id=1, replica_groups=mesh['row'=8,'col'=4] {'row','col'}, dimensions={0} | all-to-all | bytes 131072 | tf_op jit(solution)/shard_map/all_to_all | solution.py:669
  121.4 0.0 collective-permute-done.10.back
  121.4 0.0 collective-permute-done.11.front
  121.4 14.2 %last_iteration.1 = (f32[3,16,16,256]{3,2,1,0:T(8,128)S(1)}, f32[8,4,128]{2,1,0:T(4,128)S(1)}, f32[16,16,256]{2,1,0:T(8,128)}) custom-call(f32[8,4,4,128]{3,2,1,0:T(4,128)S(1)} %bitcast.2, f32[3,16,16,256]{3,2,1,0:T(8,128)S(1)} %get-tuple-element.41.field.core, f32[12,16,256]{2,1,0:T(8,128)S(1)} %collective-permute-done.8.low, ...), custom_call_target="tpu_custom_call" | custom-call | tf_op jit(solution)/shard_map/last_iteration/pallas_call | solution.py:593
  135.7 7.8 %all_to_all.17.gathered = f32[8,4,128]{2,1,0:T(4,128)S(1)} all-to-all(f32[8,4,128]{2,1,0:T(4,128)S(1)} %get-tuple-element.46), channel_id=1, replica_groups=mesh['row'=8,'col'=4] {'row'}, dimensions={0} | all-to-all | bytes 32768 | tf_op jit(solution)/shard_map/all_to_all | solution.py:680
  143.5 2.9 %correct.1 = (f32[3,16,16,256]{3,2,1,0:T(8,128)}, f32[3,16,2,32]{3,2,1,0:T(2,128)}) custom-call(f32[8,4,128]{2,1,0:T(4,128)S(1)} %all_to_all.17.gathered, f32[3,16,16,256]{3,2,1,0:T(8,128)S(1)} %get-tuple-element.47.core), custom_call_target="tpu_custom_call" | custom-call | tf_op jit(solution)/shard_map/correct/pallas_call | solution.py:638
  (3 shorter events, 0.1 us)
Async XLA Ops:
  0.6 1.1 copy-start
  1.8 1.1 copy-start.1
  2.9 0.9 copy-start.2
  3.8 0.9 copy-start.3
  4.9 9.3 %collective-permute-start = (f32[21,16,256]{2,1,0:T(8,128)S(1)}, f32[21,16,256]{2,1,0:T(8,128)S(1)}, u32[]{:S(2)}, u32[]{:S(2)}) collective-permute-start(f32[21,16,256]{2,1,0:T(8,128)S(1)} %get-tuple-element.27), channel_id=1, source_target_pairs={{0,4},{4,8},{8,12},{12,16},{16,20},{20,24},{24,28},{28,0},{1,5},{5... | collective-permute-start | bytes 1032200 | tf_op jit(solution)/shard_map/ppermute | solution.py:656
  5.4 37.3 %copy-start.4 = (f32[8]{0:T(128)S(1)}, f32[8]{0:T(128)}, u32[]{:S(2)}) copy-start(f32[8]{0:T(128)} %floor_table.1) | copy-start | bytes 100
  5.4 37.3 %copy-start.5 = (f32[8]{0:T(128)S(1)}, f32[8]{0:T(128)}, u32[]{:S(2)}) copy-start(f32[8]{0:T(128)} %rise_table.1) | copy-start | bytes 100
  5.4 10.4 %collective-permute-start.1 = (f32[21,16,256]{2,1,0:T(8,128)S(1)}, f32[21,16,256]{2,1,0:T(8,128)S(1)}, u32[]{:S(2)}, u32[]{:S(2)}) collective-permute-start(f32[21,16,256]{2,1,0:T(8,128)S(1)} %get-tuple-element.28), channel_id=1, source_target_pairs={{4,0},{8,4},{12,8},{16,12},{20,16},{24,20},{28,24},{0,28},{5,1},{9... | collective-permute-start | bytes 1032200 | tf_op jit(solution)/shard_map/ppermute | solution.py:656
  16.0 15.6 %collective-permute-start.2 = (f32[124,4,256]{2,1,0:T(4,128)S(1)}, f32[124,4,256]{2,1,0:T(4,128)S(1)}, u32[]{:S(2)}, u32[]{:S(2)}) collective-permute-start(f32[124,4,256]{2,1,0:T(4,128)S(1)} %get-tuple-element.29), channel_id=1, source_target_pairs={{0,1},{1,2},{2,3},{3,0},{4,5},{5,6},{6,7},{7,4},{8,9},{9,10},{10,1... | collective-permute-start | bytes 1523720 | tf_op jit(solution)/shard_map/ppermute | solution.py:656
  17.7 25.0 %collective-permute-start.3 = (f32[124,4,256]{2,1,0:T(4,128)S(1)}, f32[124,4,256]{2,1,0:T(4,128)S(1)}, u32[]{:S(2)}, u32[]{:S(2)}) collective-permute-start(f32[124,4,256]{2,1,0:T(4,128)S(1)} %get-tuple-element.30), channel_id=1, source_target_pairs={{1,0},{2,1},{3,2},{0,3},{5,4},{6,5},{7,6},{4,7},{9,8},{10,9},{11,1... | collective-permute-start | bytes 1523720 | tf_op jit(solution)/shard_map/ppermute | solution.py:656
  55.2 7.1 %collective-permute-start.4 = (f32[12,16,256]{2,1,0:T(8,128)S(1)}, f32[12,16,256]{2,1,0:T(8,128)S(1)}, u32[]{:S(2)}, u32[]{:S(2)}) collective-permute-start(f32[12,16,256]{2,1,0:T(8,128)S(1)} %get-tuple-element.33), channel_id=1, source_target_pairs={{0,4},{4,8},{8,12},{12,16},{16,20},{20,24},{24,28},{28,0},{1,5},{5... | collective-permute-start | bytes 589832 | tf_op jit(solution)/shard_map/ppermute | solution.py:656
  55.4 6.9 %collective-permute-start.5 = (f32[12,16,256]{2,1,0:T(8,128)S(1)}, f32[12,16,256]{2,1,0:T(8,128)S(1)}, u32[]{:S(2)}, u32[]{:S(2)}) collective-permute-start(f32[12,16,256]{2,1,0:T(8,128)S(1)} %get-tuple-element.34), channel_id=1, source_target_pairs={{4,0},{8,4},{12,8},{16,12},{20,16},{24,20},{28,24},{0,28},{5,1},{9... | collective-permute-start | bytes 589832 | tf_op jit(solution)/shard_map/ppermute | solution.py:656
  62.4 19.3 %collective-permute-start.6 = (f32[72,4,256]{2,1,0:T(4,128)S(1)}, f32[72,4,256]{2,1,0:T(4,128)S(1)}, u32[]{:S(2)}, u32[]{:S(2)}) collective-permute-start(f32[72,4,256]{2,1,0:T(4,128)S(1)} %get-tuple-element.35), channel_id=1, source_target_pairs={{0,1},{1,2},{2,3},{3,0},{4,5},{5,6},{6,7},{7,4},{8,9},{9,10},{10,1... | collective-permute-start | bytes 884744 | tf_op jit(solution)/shard_map/ppermute | solution.py:656
  63.5 18.2 %collective-permute-start.7 = (f32[72,4,256]{2,1,0:T(4,128)S(1)}, f32[72,4,256]{2,1,0:T(4,128)S(1)}, u32[]{:S(2)}, u32[]{:S(2)}) collective-permute-start(f32[72,4,256]{2,1,0:T(4,128)S(1)} %get-tuple-element.36), channel_id=1, source_target_pairs={{1,0},{2,1},{3,2},{0,3},{5,4},{6,5},{7,6},{4,7},{9,8},{10,9},{11,1... | collective-permute-start | bytes 884744 | tf_op jit(solution)/shard_map/ppermute | solution.py:656
  95.3 6.6 %collective-permute-start.8 = (f32[12,16,256]{2,1,0:T(8,128)S(1)}, f32[12,16,256]{2,1,0:T(8,128)S(1)}, u32[]{:S(2)}, u32[]{:S(2)}) collective-permute-start(f32[12,16,256]{2,1,0:T(8,128)S(1)} %get-tuple-element.42), channel_id=1, source_target_pairs={{0,4},{4,8},{8,12},{12,16},{16,20},{20,24},{24,28},{28,0},{1,5},{5... | collective-permute-start | bytes 589832 | tf_op jit(solution)/shard_map/ppermute | solution.py:656
  95.5 6.5 %collective-permute-start.9 = (f32[12,16,256]{2,1,0:T(8,128)S(1)}, f32[12,16,256]{2,1,0:T(8,128)S(1)}, u32[]{:S(2)}, u32[]{:S(2)}) collective-permute-start(f32[12,16,256]{2,1,0:T(8,128)S(1)} %get-tuple-element.43), channel_id=1, source_target_pairs={{4,0},{8,4},{12,8},{16,12},{20,16},{24,20},{28,24},{0,28},{5,1},{9... | collective-permute-start | bytes 589832 | tf_op jit(solution)/shard_map/ppermute | solution.py:656
  102.0 19.5 %collective-permute-start.10 = (f32[72,4,256]{2,1,0:T(4,128)S(1)}, f32[72,4,256]{2,1,0:T(4,128)S(1)}, u32[]{:S(2)}, u32[]{:S(2)}) collective-permute-start(f32[72,4,256]{2,1,0:T(4,128)S(1)} %get-tuple-element.44), channel_id=1, source_target_pairs={{0,1},{1,2},{2,3},{3,0},{4,5},{5,6},{6,7},{7,4},{8,9},{9,10},{10,1... | collective-permute-start | bytes 884744 | tf_op jit(solution)/shard_map/ppermute | solution.py:656
  102.5 18.9 %collective-permute-start.11 = (f32[72,4,256]{2,1,0:T(4,128)S(1)}, f32[72,4,256]{2,1,0:T(4,128)S(1)}, u32[]{:S(2)}, u32[]{:S(2)}) collective-permute-start(f32[72,4,256]{2,1,0:T(4,128)S(1)} %get-tuple-element.45), channel_id=1, source_target_pairs={{1,0},{2,1},{3,2},{0,3},{5,4},{6,5},{7,6},{4,7},{9,8},{10,9},{11,1... | collective-permute-start | bytes 884744 | tf_op jit(solution)/shard_map/ppermute | solution.py:656

commit v2 on v1

v2 whole, which is shorter than its diff:
```python
import functools
import jax
import jax.numpy as jnp
from jax import lax
from jax.experimental import pallas as pl
from jax.experimental.pallas import tpu as pltpu
from jax.sharding import PartitionSpec as P

ITERS = 3
SWEEPS = 2
COARSE_SWEEPS = 16
COARSEN = 8
RELAX = 0.8

HALO = 4
BLOCK = 16
EXT = BLOCK + 2 * HALO
LANES = 128
TOP = 8
CORE = TOP + HALO
ROWS = 40
HIGH = lax.Precision.HIGHEST
X_PAGES = 21
Y_PAGES = 88

VMEM = pl.BlockSpec(memory_space=pltpu.VMEM)
SMEM = pl.BlockSpec(memory_space=pltpu.SMEM)
PARAMS = pltpu.CompilerParams(vmem_limit_bytes=44 * 1024 * 1024)


def f32(*shape):
    return jax.ShapeDtypeStruct(shape, jnp.float32)


def turns(even, low_edge, high_edge):
    return jnp.where(even, high_edge, low_edge), jnp.where(even, low_edge, high_edge)


def corner_parts(reach):
    first = 0
    parts = []
    for distance in range(1, reach):
        parts.append((distance, first, reach - distance))
        first += reach - distance
    return parts, first


CORNER_FIELD, FIELD_ROWS = corner_parts(4)
CORNER_LABEL, LABEL_ROWS = corner_parts(3)
CORNER_DRIVE = 6 * FIELD_ROWS
CORNER_TABLE = CORNER_DRIVE + 6
CORNER_ALL = CORNER_TABLE + 2 * LABEL_ROWS
CORNER_LATER = 40


def pack_first_kernel(
    potential, source, coil_mask, labels, x_lo, x_hi, y_a, y_b,
    pot_x, src_x, mask_x, lab_x, pot_y, src_y, mask_y, lab_y, sems,
):
    even = lax.axis_index("col") % 2 == 0
    copies = []

    def fetch(ref, scratch):
        copy = pltpu.make_async_copy(ref, scratch, sems.at[len(copies)])
        copy.start()
        copies.append(copy)

    for side, (cells, pair, rows) in enumerate((
        (slice(0, 4), slice(0, 2), slice(0, 8)),
        (slice(BLOCK - 4, BLOCK), slice(BLOCK - 2, BLOCK), slice(BLOCK - 8, BLOCK)),
    )):
        fetch(potential.at[:, cells], pot_x.at[side])
        fetch(source.at[:, pair], src_x.at[side])
        fetch(coil_mask.at[pair], mask_x.at[side])
        fetch(labels.at[cells], lab_x.at[side])
        fetch(potential.at[:, :, rows], pot_y.at[side])
        fetch(source.at[:, :, rows], src_y.at[side])
        fetch(coil_mask.at[:, rows], mask_y.at[side])
        fetch(labels.at[:, rows], lab_y.at[side])
    for copy in copies:
        copy.wait()
    for side, out in enumerate((x_lo, x_hi)):
        for comp in range(3):
            out[comp * 4 : comp * 4 + 4] = pot_x[side, comp]
            out[12 + comp * 2 : 14 + comp * 2] = (
                2.0 * src_x[side, comp] * mask_x[side].astype(jnp.float32)
            )
        out[18:21] = lab_x[side, side : side + 3].astype(jnp.float32)

    def send(page, low_edge, high_edge, rows=slice(0, 4)):
        first, second = turns(even, low_edge, high_edge)
        y_a[page, rows] = first
        y_b[page, rows] = second

    for x in range(BLOCK):
        mask_lo = 2.0 * mask_y[0, x, 0:2].astype(jnp.float32)
        mask_hi = 2.0 * mask_y[1, x, 6:8].astype(jnp.float32)
        for comp in range(3):
            send(comp * 16 + x, pot_y[0, comp, x, 0:4], pot_y[1, comp, x, 4:8])
            send(
                48 + comp * 8 + x // 2, src_y[0, comp, x, 0:2] * mask_lo,
                src_y[1, comp, x, 6:8] * mask_hi, slice((x % 2) * 2, (x % 2) * 2 + 2),
            )
        send(72 + x, lab_y[0, x, 0:4].astype(jnp.float32), lab_y[1, x, 4:8].astype(jnp.float32))


def pack_first(potential, source, labels, coil_mask):
    depth = potential.shape[-1]
    scratch = [
        pltpu.VMEM((2, 3, 4, BLOCK, depth), jnp.float32),
        pltpu.VMEM((2, 3, 2, BLOCK, depth), jnp.float32),
        pltpu.VMEM((2, 2, BLOCK, depth), jnp.int32),
        pltpu.VMEM((2, 4, BLOCK, depth), jnp.int32),
        pltpu.VMEM((2, 3, BLOCK, 8, depth), jnp.float32),
        pltpu.VMEM((2, 3, BLOCK, 8, depth), jnp.float32),
        pltpu.VMEM((2, BLOCK, 8, depth), jnp.int32),
        pltpu.VMEM((2, BLOCK, 8, depth), jnp.int32),
        pltpu.SemaphoreType.DMA((16,)),
    ]
    return pl.pallas_call(
        pack_first_kernel,
        in_specs=[pl.BlockSpec(memory_space=pl.ANY)] * 4,
        out_specs=[VMEM] * 4,
        out_shape=[f32(X_PAGES, BLOCK, depth)] * 2 + [f32(Y_PAGES, HALO, depth)] * 2,
        scratch_shapes=scratch,
        compiler_params=PARAMS,
        name="pack_first",
    )(potential, source, coil_mask, labels)


def pack_corner_kernel(whole, low, high, out_a, out_b):
    even = lax.axis_index("col") % 2 == 0

    def send(row, count, ref, page):
        rows = slice(row, row + count)
        first, second = turns(even, ref[page, 0:count], ref[page, BLOCK - count : BLOCK])
        out_a[rows, :] = first
        out_b[rows, :] = second

    for comp in range(3):
        for distance, first, count in CORNER_FIELD:
            row = comp * 2 * FIELD_ROWS + first
            send(row, count, low, comp * 4 + 4 - distance)
            send(row + FIELD_ROWS, count, high, comp * 4 + distance - 1)
        if whole:
            send(CORNER_DRIVE + comp * 2, 1, low, 12 + comp * 2 + 1)
            send(CORNER_DRIVE + comp * 2 + 1, 1, high, 12 + comp * 2)
    if whole:
        for distance, first, count in CORNER_LABEL:
            row = CORNER_TABLE + first
            send(row, count, low, 18 + 3 - distance)
            send(row + LABEL_ROWS, count, high, 18 + distance - 1)


def pack_corner(whole, low, high):
    depth = low.shape[-1]
    return pl.pallas_call(
        functools.partial(pack_corner_kernel, whole),
        in_specs=[VMEM] * 2,
        out_specs=[VMEM] * 2,
        out_shape=[f32(CORNER_ALL if whole else CORNER_LATER, depth)] * 2,
        compiler_params=PARAMS,
        name="pack_corner",
    )(low, high)


def coarse_solve(targets, relucts):
    shape = relucts[0].shape
    count = shape[0]
    lane = lax.broadcasted_iota(jnp.int32, shape, 1)
    row = lax.broadcasted_iota(jnp.int32, shape, 0)
    z = lane % 32
    first_y = (lane // 32) % 2 == 0
    first_x = lane // 64 == 0
    up_ok, down_ok = z < 31, z > 0
    far_ok = jnp.logical_not(
        jnp.logical_or(
            jnp.logical_and(first_x, row == 0),
            jnp.logical_and(jnp.logical_not(first_x), row == count - 1),
        )
    )

    def up(v):
        return pltpu.roll(v, LANES - 1, 1)

    def down(v):
        return pltpu.roll(v, 1, 1)

    def side(v):
        return jnp.where(first_y, pltpu.roll(v, LANES - 32, 1), pltpu.roll(v, 32, 1))

    def near(v):
        return pltpu.roll(v, 64, 1)

    def far(swapped):
        return jnp.where(first_x, pltpu.roll(swapped, 1, 0), pltpu.roll(swapped, count - 1, 0))

    sets = []
    for r in relucts:
        swapped = near(r)
        c_up = r + jnp.where(up_ok, up(r), 0.0)
        c_down = r + jnp.where(down_ok, down(r), 0.0)
        c_side = r + side(r)
        c_near = r + swapped
        c_far = r + jnp.where(far_ok, far(swapped), 0.0)
        diag = ((c_up + c_down) + (c_side + r)) + (c_near + c_far)
        c_up = jnp.where(up_ok, c_up, 0.0)
        c_down = jnp.where(down_ok, c_down, 0.0)
        c_far = jnp.where(far_ok, c_far, 0.0)
        sets.append((c_up, c_down, c_side, c_near, c_far, diag, RELAX / diag))

    def neighbours(coeffs, v):
        c_up, c_down, c_side, c_near, c_far = coeffs[:5]
        swapped = near(v)
        return (
            (c_up * up(v) + c_down * down(v)) + (c_side * side(v) + c_near * swapped)
        ) + c_far * far(swapped)

    doubled = [[2.0 * t for t in stripe] for stripe in targets]
    start = [
        [coeffs[6] * t for t in stripe] for coeffs, stripe in zip(sets, doubled)
    ]

    def sweep(step, values):
        return [
            [
                (1.0 - RELAX) * v + coeffs[6] * (t + neighbours(coeffs, v))
                for v, t in zip(stripe, stripe_t)
            ]
            for coeffs, stripe, stripe_t in zip(sets, values, doubled)
        ]

    values = lax.fori_loop(0, COARSE_SWEEPS - 1, sweep, start)
    out = []
    for coeffs, stripe, stripe_t in zip(sets, values, doubled):
        total = jnp.sum(jnp.sum(coeffs[5], axis=1, keepdims=True), axis=0, keepdims=True)
        done = []
        for v, t in zip(stripe, stripe_t):
            left = t - (coeffs[5] * v - neighbours(coeffs, v))
            left = jnp.sum(jnp.sum(left, axis=1, keepdims=True), axis=0, keepdims=True)
            done.append(v + left / total)
        out.append(done)
    return out


def pick_row(values, index):
    row = lax.broadcasted_iota(jnp.int32, values.shape, 0)
    return jnp.sum(jnp.where(row == index, values, 0.0), axis=0, keepdims=True)


def spread_matrix(group):
    lane = lax.broadcasted_iota(jnp.int32, (LANES, 2 * LANES), 0)
    cell = lax.broadcasted_iota(jnp.int32, (LANES, 2 * LANES), 1)
    return jnp.where(lane == group * 32 + cell // COARSEN, 1.0, 0.0)


def gather_matrix(group):
    cell = lax.broadcasted_iota(jnp.int32, (2 * LANES, LANES), 0)
    lane = lax.broadcasted_iota(jnp.int32, (2 * LANES, LANES), 1)
    return jnp.where(lane == group * 32 + cell // COARSEN, 1.0, 0.0)


def load_stripe(table, gathered, count, pick):
    for row in range(count):
        for comp in range(4):
            table[comp, row : row + 1, :] = pick(row)[comp : comp + 1, :]
    scale = 1.0 / float(COARSEN * COARSEN)
    return [table[comp] * scale for comp in range(3)], table[3]


class Place:
    def __init__(self):
        self.row, self.rows = lax.axis_index("row"), lax.axis_size("row")
        self.col, self.cols = lax.axis_index("col"), lax.axis_size("col")
        self.low, self.high = self.row > 0, self.row < self.rows - 1
        self.back, self.front = self.col > 0, self.col < self.cols - 1
        self.even = self.col % 2 == 0

    def sides(self, turn_a, turn_b):
        return jnp.where(self.even, turn_b, turn_a), jnp.where(self.even, turn_a, turn_b)


def put_corner(put, message, place, row, distance, count):
    for side, there in ((0, place.low), (1, place.high)):
        back, front = place.sides(message[0](row[side], count), message[1](row[side], count))
        plane = HALO - distance if side == 0 else HALO + BLOCK - 1 + distance
        put(plane, HALO - count, count, jnp.logical_and(there, place.back), back)
        put(plane, HALO + BLOCK, count, jnp.logical_and(there, place.front), front)


def put_field(field, core, low, high, y_a, y_b, c_a, c_b, place):
    for comp in range(3):
        for half in range(2):
            z = slice(half * LANES, half * LANES + LANES)
            own = slice(CORE, CORE + BLOCK)
            field[comp, half, 4:20, own, :] = core[comp, :, :, z]
            pages = slice(comp * 4, comp * 4 + 4)
            field[comp, half, 0:4, own, :] = jnp.where(place.low, low[pages, :, z], 0.0)
            field[comp, half, 20:24, own, :] = jnp.where(place.high, high[pages, :, z], 0.0)
            pages = slice(comp * 16, comp * 16 + 16)
            back, front = place.sides(y_a[pages, :, z], y_b[pages, :, z])
            field[comp, half, 4:20, TOP : TOP + HALO, :] = jnp.where(place.back, back, 0.0)
            field[comp, half, 4:20, CORE + BLOCK : CORE + BLOCK + HALO, :] = jnp.where(
                place.front, front, 0.0
            )

            def put(plane, row, count, there, value):
                field[comp, half, plane, TOP + row : TOP + row + count, :] = jnp.where(
                    there, value, 0.0
                )

            message = [
                lambda row, count, ref=ref: ref[row : row + count, z] for ref in (c_a, c_b)
            ]
            for distance, first, count in CORNER_FIELD:
                row = comp * 2 * FIELD_ROWS + first
                put_corner(put, message, place, (row, row + FIELD_ROWS), distance, count)


def put_material(
    drive, floor, rise, source, coil_mask, labels, low, high, y_a, y_b, c_a, c_b, floor_table,
    rise_table, place,
):
    for half in range(2):
        z = slice(half * LANES, half * LANES + LANES)
        own = slice(HALO, HALO + BLOCK)
        coil = 2.0 * coil_mask[:, :, z].astype(jnp.float32)
        message = [lambda row, count, ref=ref: ref[row : row + count, z] for ref in (c_a, c_b)]
        for comp in range(3):
            drive[comp, half, 4:20, own, :] = source[comp, :, :, z] * coil
            pages = slice(12 + comp * 2, 14 + comp * 2)
            drive[comp, half, 2:4, own, :] = low[pages, :, z]
            drive[comp, half, 20:22, own, :] = high[pages, :, z]
            for x in range(BLOCK):
                page, part = 48 + comp * 8 + x // 2, slice((x % 2) * 2, (x % 2) * 2 + 2)
                back, front = place.sides(y_a[page, part, z], y_b[page, part, z])
                drive[comp, half, 4 + x, 2:4, :] = back
                drive[comp, half, 4 + x, 20:22, :] = front

            def put_drive(plane, row, count, there, value):
                drive[comp, half, plane, row : row + count, :] = value

            row = CORNER_DRIVE + comp * 2
            put_corner(put_drive, message, place, (row, row + 1), 1, 1)
        floor[half, 4:20, own, :] = labels[:, :, z].astype(jnp.float32)
        floor[half, 1:4, own, :] = jnp.where(place.low, low[18:21, :, z], -1.0)
        floor[half, 20:23, own, :] = jnp.where(place.high, high[18:21, :, z], -1.0)
        back, front = place.sides(y_a[72:88, :, z], y_b[72:88, :, z])
        floor[half, 4:20, 0:HALO, :] = jnp.where(place.back, back, -1.0)
        floor[half, 4:20, HALO + BLOCK : EXT, :] = jnp.where(place.front, front, -1.0)

        def put_label(plane, row, count, there, value):
            floor[half, plane, row : row + count, :] = jnp.where(there, value, -1.0)

        for distance, first, count in CORNER_LABEL:
            row = CORNER_TABLE + first
            put_corner(put_label, message, place, (row, row + LABEL_ROWS), distance, count)

    def look_up(x, carry):
        for half in range(2):
            label = floor[half, x]
            floor_cell = jnp.zeros_like(label)
            rise_cell = jnp.zeros_like(label)
            for number in range(floor_table.shape[0]):
                chosen = label == float(number)
                floor_cell = jnp.where(chosen, floor_table[number], floor_cell)
                rise_cell = jnp.where(chosen, rise_table[number], rise_cell)
            floor[half, x] = floor_cell
            rise[half, x] = rise_cell
        return carry

    lax.fori_loop(1, EXT - 1, look_up, 0)


def right_of(low, high, last):
    a, b = pltpu.roll(low, LANES - 1, 1), pltpu.roll(high, LANES - 1, 1)
    return jnp.where(last, b, a), b


def left_of(low, high, first):
    a, b = pltpu.roll(low, 1, 1), pltpu.roll(high, 1, 1)
    return a, jnp.where(first, a, b)


def in_pairs(begin, end, plane):
    def step(number, carry):
        x = begin + 2 * number
        for ref, value in plane(x) + plane(x + 1):
            ref[...] = value
        return carry

    lax.fori_loop(0, (end - begin) // 2, step, 0)


def fine_iteration(
    field, other, reluct, c_x, c_y, c_up, c_down, weight, diag, sums, drive, floor, rise,
):
    mid = slice(TOP, TOP + EXT)
    plus = slice(TOP + 1, TOP + EXT + 1)
    minus = slice(TOP - 1, TOP + EXT - 1)
    lane = lax.broadcasted_iota(jnp.int32, (EXT, LANES), 1)
    first, last = lane == 0, lane == LANES - 1

    def reluct_plane(x):
        stores = []
        along_z = []
        for comp in range(2):
            low, high = field[comp, 0, x, mid], field[comp, 1, x, mid]
            r0, r1 = right_of(low, high, last)
            l0, l1 = left_of(low, high, first)
            along_z.append((r0 - jnp.where(first, 0.0, l0), jnp.where(last, 0.0, r1) - l1))
        for half in range(2):
            def along_y(comp):
                return field[comp, half, x, plus] - field[comp, half, x, minus]

            def along_x(comp):
                return field[comp, half, x + 1, mid] - field[comp, half, x - 1, mid]

            b0 = along_y(2) - along_z[1][half]
            b1 = along_z[0][half] - along_x(2)
            b2 = along_x(1) - along_y(0)
            square = 0.25 * (b0 * b0 + b1 * b1 + b2 * b2)
            stores.append((
                reluct.at[half, x, mid], floor[half, x] + rise[half, x] * (square / (1.0 + square))
            ))
        return stores

    in_pairs(1, EXT - 1, reluct_plane)

    def apply(src, x, rows, coeffs, first_lane, last_lane):
        rows_plus = slice(rows.start + 1, rows.stop + 1)
        rows_minus = slice(rows.start - 1, rows.stop - 1)
        out = []
        for comp in range(3):
            low, high = src[comp, 0, x, rows], src[comp, 1, x, rows]
            rights = right_of(low, high, last_lane)
            lefts = left_of(low, high, first_lane)
            for half in range(2):
                x_plus, x_minus, y_plus, y_minus, up, down = coeffs[half]
                total = (
                    (x_plus * src[comp, half, x + 1, rows] + x_minus * src[comp, half, x - 1, rows])
                    + (y_plus * src[comp, half, x, rows_plus] + y_minus * src[comp, half, x, rows_minus])
                    + (up * rights[half] + down * lefts[half])
                )
                out.append((comp, half, (low, high)[half], total))
        return out

    def load_coeffs(x, rows):
        rows_minus = slice(rows.start - 1, rows.stop - 1)
        return [
            (
                c_x[half, x, rows], c_x[half, x - 1, rows], c_y[half, x, rows],
                c_y[half, x, rows_minus], c_up[half, x, rows], c_down[half, x, rows],
            )
            for half in range(2)
        ]

    def first_plane(x):
        low, high = reluct[0, x, mid], reluct[1, x, mid]
        r0, r1 = right_of(low, high, last)
        l0, l1 = left_of(low, high, first)
        ups = (low + r0, high + jnp.where(last, 0.0, r1))
        downs = (low + jnp.where(first, 0.0, l0), high + l1)
        stores, coeffs, weights = [], [], []
        for half in range(2):
            here = (low, high)[half]
            x_plus = here + reluct[half, x + 1, mid]
            x_minus = here + reluct[half, x - 1, mid]
            y_plus = here + reluct[half, x, plus]
            y_minus = here + reluct[half, x, minus]
            total = ((x_plus + x_minus) + (y_plus + y_minus)) + (ups[half] + downs[half])
            up = ups[half] if half == 0 else jnp.where(last, 0.0, ups[half])
            down = jnp.where(first, 0.0, downs[half]) if half == 0 else downs[half]
            scale = jnp.where(floor[half, x] > 0.0, RELAX / total, 0.0)
            coeffs.append((x_plus, x_minus, y_plus, y_minus, up, down))
            weights.append(scale)
            for ref, value in (
                (c_x, x_plus), (c_y, y_plus), (c_up, up), (c_down, down), (diag, total), (weight, scale),
            ):
                stores.append((ref.at[half, x, mid], value))
        for comp, half, here, total in apply(field, x, mid, coeffs, first, last):
            stores.append((
                other.at[comp, half, x, mid],
                (1.0 - RELAX) * here + weights[half] * (drive[comp, half, x] + total),
            ))
        return stores

    in_pairs(2, EXT - 2, first_plane)

    def second_plane(x):
        stores = []
        weights = [weight[half, x, mid] for half in range(2)]
        for comp, half, here, total in apply(other, x, mid, load_coeffs(x, mid), first, last):
            stores.append((
                field.at[comp, half, x, mid],
                (1.0 - RELAX) * here + weights[half] * (drive[comp, half, x] + total),
            ))
        return stores

    in_pairs(3, EXT - 3, second_plane)

    own = slice(CORE, CORE + BLOCK)
    lane = lax.broadcasted_iota(jnp.int32, (BLOCK, LANES), 1)
    first_own, last_own = lane == 0, lane == LANES - 1
    zero = jnp.zeros((BLOCK, LANES), jnp.float32)
    result = jnp.zeros((8, LANES), jnp.float32)
    sums[...] = jnp.zeros(sums.shape, jnp.float32)
    for coarse in range(BLOCK // COARSEN):
        def plane(step, totals):
            x = HALO + coarse * COARSEN + step
            out = []
            diags = [diag[half, x, own] for half in range(2)]
            for comp, half, here, off in apply(
                field, x, own, load_coeffs(x, own), first_own, last_own
            ):
                out.append(
                    totals[comp * 2 + half]
                    + (drive[comp, half, x, HALO : HALO + BLOCK] - (diags[half] * here - off))
                )
            for half in range(2):
                out.append(totals[6 + half] + reluct[half, x, own])
            return tuple(out)

        totals = lax.fori_loop(0, COARSEN, plane, (zero,) * 8)
        for part in range(BLOCK // COARSEN):
            group = coarse * 2 + part
            for comp in range(4):
                scale = 0.5 if comp < 3 else 1.0 / float(COARSEN ** 3)
                for half in range(2):
                    block = totals[comp * 2 + half][part * COARSEN : (part + 1) * COARSEN]
                    sums[group, comp : comp + 1, half * LANES : (half + 1) * LANES] = scale * jnp.sum(
                        block, axis=0, keepdims=True
                    )
            result = result + jnp.dot(
                sums[group], gather_matrix(group), precision=HIGH, preferred_element_type=jnp.float32
            )
    return result[0:4]


SCRATCH = (
    [pltpu.VMEM((3, 2, EXT, ROWS, LANES), jnp.float32)] * 2
    + [pltpu.VMEM((2, EXT, ROWS, LANES), jnp.float32)] * 7
    + [pltpu.VMEM((4, 8, 2 * LANES), jnp.float32)]
)


def emit(field, coarse, field_out, edges, coarse_out, place):
    own = slice(CORE, CORE + BLOCK)
    for comp in range(3):
        for half in range(2):
            z = slice(half * LANES, half * LANES + LANES)
            field_out[comp, :, :, z] = field[comp, half, 4:20, own, :]
            if edges:
                x_lo, x_hi, y_a, y_b = edges
                x_lo[comp * 4 : comp * 4 + 4, :, z] = field[comp, half, 4:8, own, :]
                x_hi[comp * 4 : comp * 4 + 4, :, z] = field[comp, half, 16:20, own, :]
                first, second = turns(
                    place.even, field[comp, half, 4:20, CORE : CORE + 4, :],
                    field[comp, half, 4:20, CORE + BLOCK - 4 : CORE + BLOCK, :],
                )
                y_a[comp * 16 : comp * 16 + 16, :, z] = first
                y_b[comp * 16 : comp * 16 + 16, :, z] = second
    coarse_out[...] = jnp.broadcast_to(coarse[None], coarse_out.shape)


def edge_shapes(depth):
    return [f32(3 * HALO, BLOCK, depth)] * 2 + [f32(3 * BLOCK, HALO, depth)] * 2


def first_kernel(
    potential, source, coil_mask, labels, low, high, y_a, y_b, c_a, c_b, floor_table, rise_table,
    field_out, coarse_out, x_lo, x_hi, yo_a, yo_b, drive, floor, rise, *scratch,
):
    place = Place()
    field = scratch[0]
    put_field(field, potential, low, high, y_a, y_b, c_a, c_b, place)
    put_material(
        drive, floor, rise, source, coil_mask, labels, low, high, y_a, y_b, c_a, c_b, floor_table,
        rise_table, place,
    )
    coarse = fine_iteration(*scratch, drive, floor, rise)
    emit(field, coarse, field_out, (x_lo, x_hi, yo_a, yo_b), coarse_out, place)


def first_iteration(potential, source, coil_mask, labels, messages, tables, devices):
    depth = potential.shape[-1]
    return pl.pallas_call(
        first_kernel,
        in_specs=[VMEM] * 10 + [SMEM] * 2,
        out_specs=[VMEM] * 9,
        out_shape=[f32(*potential.shape), f32(devices, 4, LANES)]
        + edge_shapes(depth)
        + [f32(3, 2, EXT, EXT, LANES), f32(2, EXT, EXT, LANES), f32(2, EXT, EXT, LANES)],
        scratch_shapes=SCRATCH,
        compiler_params=PARAMS,
        name="first_iteration",
    )(potential, source, coil_mask, labels, *messages, *tables)


def solve_kernel(gathered, wide_out, table, picked):
    place = Place()
    targets, relucts = [], []
    for stripe in range(3):
        index = jnp.clip(place.col + stripe - 1, 0, place.cols - 1)
        target, reluct = load_stripe(
            table.at[stripe], gathered, gathered.shape[0], lambda r: gathered[r, index]
        )
        targets.append(target)
        relucts.append(reluct)
    corrections = coarse_solve(targets, relucts)
    picked[...] = jnp.zeros(picked.shape, jnp.float32)
    for stripe in range(3):
        there = (place.back, True, place.front)[stripe]
        for comp in range(3):
            for shift in range(3):
                line = pick_row(corrections[stripe][comp], place.row + shift - 1)
                spot = (stripe * 3 + comp) * 3 + shift
                picked[spot : spot + 1, :] = jnp.where(there, line, 0.0)
    for group in range(4):
        wide_out[group] = jnp.dot(
            picked[...], spread_matrix(group), precision=HIGH, preferred_element_type=jnp.float32
        )


def solve(gathered):
    return pl.pallas_call(
        solve_kernel,
        in_specs=[VMEM],
        out_specs=VMEM,
        out_shape=f32(4, 32, 2 * LANES),
        scratch_shapes=[
            pltpu.VMEM((3, 4, gathered.shape[0], LANES), jnp.float32),
            pltpu.VMEM((32, LANES), jnp.float32),
        ],
        compiler_params=PARAMS,
        name="solve",
    )(gathered)


def next_kernel(
    final, wide, core, low, high, y_a, y_b, c_a, c_b, drive, floor, rise, *refs
):
    if final:
        field_out, coarse_out, reluct_out, *scratch = refs
        edges = None
    else:
        field_out, coarse_out, x_lo, x_hi, yo_a, yo_b, *scratch = refs
        edges = (x_lo, x_hi, yo_a, yo_b)
    place = Place()
    field = scratch[0]
    put_field(field, core, low, high, y_a, y_b, c_a, c_b, place)
    mid = slice(TOP, TOP + EXT)
    cell = lax.broadcasted_iota(jnp.int32, (EXT, LANES), 0)
    for begin, end, shift, x in ((0, 4, 0, 1), (4, 12, 1, 0), (12, 20, 1, 1), (20, 24, 2, 0)):
        for comp in range(3):
            for half in range(2):
                def line(stripe, y):
                    spot = (stripe * 3 + comp) * 3 + shift
                    return wide[
                        x * 2 + y, spot : spot + 1, half * LANES : (half + 1) * LANES
                    ]

                tile = jnp.where(
                    cell < 12,
                    jnp.where(cell < 4, line(0, 1), line(1, 0)),
                    jnp.where(cell < 20, line(1, 1), line(2, 0)),
                )
                for plane in range(begin, end):
                    field[comp, half, plane, mid] = field[comp, half, plane, mid] + tile
    coarse = fine_iteration(*scratch, drive, floor, rise)
    emit(field, coarse, field_out, edges, coarse_out, place)
    if final:
        reluct = scratch[2]
        for half in range(2):
            reluct_out[:, :, half * LANES : (half + 1) * LANES] = reluct[
                half, 4:20, CORE : CORE + BLOCK, :
            ]


def next_iteration(final, wide, core, messages, material, devices):
    outs = [f32(*core.shape), f32(devices, 4, LANES)]
    outs += [f32(*core.shape[1:])] if final else edge_shapes(core.shape[-1])
    return pl.pallas_call(
        functools.partial(next_kernel, final),
        in_specs=[VMEM] * 11,
        out_specs=[VMEM] * len(outs),
        out_shape=outs,
        scratch_shapes=SCRATCH,
        compiler_params=PARAMS,
        name="last_iteration" if final else "next_iteration",
    )(wide, core, *messages, *material)


def correct_kernel(gathered, core, field_out, target_out, table, picked):
    row = lax.axis_index("row")
    target, reluct = load_stripe(table, gathered, gathered.shape[0], lambda r: gathered[r])
    correction, = coarse_solve([target], [reluct])
    picked[...] = jnp.zeros(picked.shape, jnp.float32)
    for comp in range(3):
        picked[comp : comp + 1, :] = pick_row(correction[comp], row)
    wide = [
        jnp.dot(picked[...], spread_matrix(group), precision=HIGH, preferred_element_type=jnp.float32)
        for group in range(4)
    ]
    cell = lax.broadcasted_iota(jnp.int32, (BLOCK, 2 * LANES), 0)
    for x in range(2):
        for comp in range(3):
            tile = jnp.where(
                cell < COARSEN, wide[x * 2][comp : comp + 1, :], wide[x * 2 + 1][comp : comp + 1, :]
            )
            for plane in range(x * COARSEN, (x + 1) * COARSEN):
                field_out[comp, plane] = core[comp, plane] + tile
    for comp in range(3):
        for x in range(2):
            for y in range(2):
                group = x * 2 + y
                moved = target[comp] if group == 0 else pltpu.roll(target[comp], LANES - 32 * group, 1)
                for r in range(gathered.shape[0]):
                    target_out[comp, 2 * r + x, y : y + 1, :] = moved[r : r + 1, 0:32]


def correct(gathered, core):
    rows = gathered.shape[0]
    return pl.pallas_call(
        correct_kernel,
        in_specs=[VMEM] * 2,
        out_specs=[VMEM] * 2,
        out_shape=[f32(*core.shape), f32(3, 2 * rows, 2, 32)],
        scratch_shapes=[
            pltpu.VMEM((4, rows, LANES), jnp.float32),
            pltpu.VMEM((8, LANES), jnp.float32),
        ],
        compiler_params=PARAMS,
        name="correct",
    )(gathered, core)


def rings(to_low, to_high):
    count = lax.axis_size("row")
    forward = [(i, (i + 1) % count) for i in range(count)]
    backward = [(target, source) for source, target in forward]
    return lax.ppermute(to_high, "row", forward), lax.ppermute(to_low, "row", backward)


def swaps(turn_a, turn_b):
    count = lax.axis_size("col")
    pairs = []
    for begin in (0, 1):
        partner = list(range(count))
        for i in range(begin, count - 1, 2):
            partner[i], partner[i + 1] = i + 1, i
        pairs.append(list(enumerate(partner)))
    return lax.ppermute(turn_a, "col", pairs[0]), lax.ppermute(turn_b, "col", pairs[1])


def shards(potential, source, labels, coil_mask, floor_table, rise_table):
    rows, cols = lax.axis_size("row"), lax.axis_size("col")
    x_lo, x_hi, y_a, y_b = pack_first(potential, source, labels, coil_mask)
    low, high = rings(x_lo, x_hi)
    y_a, y_b = swaps(y_a, y_b)
    c_a, c_b = swaps(*pack_corner(True, low, high))
    field, coarse, x_lo, x_hi, y_a, y_b, *material = first_iteration(
        potential, source, coil_mask, labels, (low, high, y_a, y_b, c_a, c_b),
        (floor_table, rise_table), rows * cols,
    )
    for iteration in range(1, ITERS):
        final = iteration == ITERS - 1
        low, high = rings(x_lo, x_hi)
        y_a, y_b = swaps(y_a, y_b)
        gathered = lax.all_to_all(coarse, ("row", "col"), 0, 0)
        gathered, low, high = lax.optimization_barrier((gathered, low, high))
        c_a, c_b = swaps(*pack_corner(False, low, high))
        wide = solve(gathered.reshape(rows, cols, 4, LANES))
        outs = next_iteration(
            final, wide, field, (low, high, y_a, y_b, c_a, c_b), material,
            rows if final else rows * cols,
        )
        if final:
            field, coarse, reluct = outs
        else:
            field, coarse, x_lo, x_hi, y_a, y_b = outs
    gathered = lax.all_to_all(coarse, "row", 0, 0)
    field, coarse_target = correct(gathered, field)
    return (field, reluct, coarse_target)


def solution(mesh):
    in_specs = (
        P(None, "row", "col", None),
        P(None, "row", "col", None),
        P("row", "col", None),
        P("row", "col", None),
        P(),
        P(),
    )
    out_specs = (P(None, "row", "col", None), P("row", "col", None), P(None, None, "col", None))
    return jax.shard_map(shards, mesh=mesh, in_specs=in_specs, out_specs=out_specs, check_vma=False)
```

time: 147 us -> 103 us (0.70)
  waiting for transfers between devices: 38.5 us -> 7.56 us
  Pallas kernels: 43.7 us -> 33 us
  blocking collectives: 38.8 us -> 30.6 us
  starting transfers between devices: 20.5 us -> 25.8 us
    ppermute x12 -> x18, waiting for transfers between devices: 38.5 us -> 7.56 us  [the longest x6 3.06 us: swaps(): lax.ppermute(turn_a, 'col', pairs[0])]
    pallas_call x7 -> x9, Pallas kernels: 40.9 us -> 30.2 us  [the longest x2 15.3 us: next_iteration(): pl.pallas_call(functools.partial(next_kernel, final), in_specs=[VMEM] * 1...]
    all_to_all x2, blocking collectives: 31 us -> 23.4 us  [shards(): gathered = lax.all_to_all(coarse, ('row', 'col'), 0, 0)]
    ppermute x12 -> x18, starting transfers between devices: 20.5 us -> 25.8 us  [the longest x6 13 us: swaps(): lax.ppermute(turn_a, 'col', pairs[0])]
    unnamed x12 -> x14, local copies, waits for them, and re-layouts: 4.17 us -> 4.17 us
  transfers between devices with their start and end apart: 12 -> 18, of which waited for: 6 -> 6; matrix products, arithmetic and copies ran while one was open for 0% -> 0% of each run, Pallas kernels for 0% -> 5%
where the time goes in v2:
time: 103 us; the launch traced here: 102 us
  Pallas kernels  33 us (32%)
  blocking collectives  30.6 us (30%)
  starting transfers between devices  25.8 us (25%)
  waiting for transfers between devices  7.56 us (7%)
  local copies, waits for them, and re-layouts  4.17 us (4%)
    all_to_all x2, blocking collectives, shards(): gathered = lax.all_to_all(coarse, ('row', 'col'), 0, 0)  23.4 us
    pallas_call x2, Pallas kernels, next_iteration(): pl.pallas_call(functools.partial(next_kernel, final), in_specs=[VMEM] * 1...  15.3 us
    ppermute x6, starting transfers between devices, swaps(): lax.ppermute(turn_a, 'col', pairs[0])  13 us
    pallas_call x1, Pallas kernels, first_iteration(): pl.pallas_call(first_kernel, in_specs=[VMEM] * 10 + [SMEM] * 2, out_specs...  8.65 us
    ppermute x3, starting transfers between devices, rings(): lax.ppermute(to_low, 'row', backward)  7.31 us
    all_to_all x1, blocking collectives, shards(): gathered = lax.all_to_all(coarse, 'row', 0, 0)  7.11 us
    pallas_call x2, Pallas kernels, solve(): pl.pallas_call(solve_kernel, in_specs=[VMEM], out_specs=VMEM, out_shape=f...  4.97 us
    unnamed x14, local copies, waits for them, and re-layouts  4.17 us
  transfers between devices with their start and end apart: 18, of which 6 were waited for; matrix products, arithmetic and copies ran while one was open for 0% of the time, Pallas kernels for 5%

profile of v2, /device:TPU:0, one launch (start us, length us, event | category | flops | bytes accessed | tf_op | source)
XLA Modules:
  0.0 101.9 jit_solution(5680618104118429642)
XLA Ops:
  0.6 0.0 copy-start
  0.6 1.1 %copy-done = f32[3,16,16,256]{3,2,1,0:T(8,128)S(1)} copy-done((f32[3,16,16,256]{3,2,1,0:T(8,128)S(1)}, f32[3,16,16,256]{3,2,1,0:T(8,128)}, u32[]{:S(2)}) %copy-start) | copy-done | bytes 786456
  1.8 0.0 copy-start.2
  1.8 1.1 %copy-done.2 = f32[3,16,16,256]{3,2,1,0:T(8,128)S(1)} copy-done((f32[3,16,16,256]{3,2,1,0:T(8,128)S(1)}, f32[3,16,16,256]{3,2,1,0:T(8,128)}, u32[]{:S(2)}) %copy-start.2) | copy-done | bytes 786456
  2.9 0.0 copy-start.3
  2.9 0.9 copy-done.3
  3.9 0.0 copy-start.4
  3.9 0.9 copy-done.4
  4.8 0.0 copy-start.1
  4.8 0.0 copy-start.5
  4.8 0.0 copy-start.6
  4.8 1.1 %pack_first.1 = (f32[21,16,256]{2,1,0:T(8,128)S(1)}, f32[21,16,256]{2,1,0:T(8,128)S(1)}, f32[88,4,256]{2,1,0:T(4,128)S(1)}, f32[88,4,256]{2,1,0:T(4,128)S(1)}) custom-call(f32[3,16,16,256]{3,2,1,0:T(8,128)S(1)} %copy-done, f32[3,16,16,256]{3,2,1,0:T(8,128)S(1)} %copy-done.2, s32[16,16,256]{2,1,0:T(8,128)S(1)} %copy-done.3, s32[16,16,256]{2,1,0:T(8,128)S(1)} %copy-done.4), custom_call_target="tpu_custom_call" | custom-call | tf_op jit(solution)/shard_map/pack_first/pallas_call | solution.py:120
  5.9 0.5 collective-permute-start
  6.4 2.9 %collective-permute-start.1 = (f32[21,16,256]{2,1,0:T(8,128)S(1)}, f32[21,16,256]{2,1,0:T(8,128)S(1)}, u32[]{:S(2)}, u32[]{:S(2)}) collective-permute-start(f32[21,16,256]{2,1,0:T(8,128)S(1)} %get-tuple-element.40), channel_id=1, source_target_pairs={{4,0},{8,4},{12,8},{16,12},{20,16},{24,20},{28,24},{0,28},{5,1},{9... | collective-permute-start | bytes 1032200 | tf_op jit(solution)/shard_map/ppermute | solution.py:742
  9.4 2.3 %collective-permute-start.2 = (f32[88,4,256]{2,1,0:T(4,128)S(1)}, f32[88,4,256]{2,1,0:T(4,128)S(1)}, u32[]{:S(2)}, u32[]{:S(2)}) collective-permute-start(f32[88,4,256]{2,1,0:T(4,128)S(1)} %get-tuple-element.41), channel_id=1, source_target_pairs={{0,1},{1,0},{2,3},{3,2},{4,5},{5,4},{6,7},{7,6},{8,9},{9,8},{10,11... | collective-permute-start | bytes 1081352 | tf_op jit(solution)/shard_map/ppermute | solution.py:753
  11.6 0.7 collective-permute-start.3
  12.3 2.9 %collective-permute-done.low = f32[21,16,256]{2,1,0:T(8,128)S(1)} collective-permute-done((f32[21,16,256]{2,1,0:T(8,128)S(1)}, f32[21,16,256]{2,1,0:T(8,128)S(1)}, u32[]{:S(2)}, u32[]{:S(2)}) %collective-permute-start) | collective-permute-done | bytes 344096 | tf_op jit(solution)/shard_map/ppermute | solution.py:742
  15.3 1.5 %collective-permute-done.1.high = f32[21,16,256]{2,1,0:T(8,128)S(1)} collective-permute-done((f32[21,16,256]{2,1,0:T(8,128)S(1)}, f32[21,16,256]{2,1,0:T(8,128)S(1)}, u32[]{:S(2)}, u32[]{:S(2)}) %collective-permute-start.1) | collective-permute-done | bytes 344096 | tf_op jit(solution)/shard_map/ppermute | solution.py:742
  16.8 1.6 %collective-permute-start.4 = (f32[48,256]{1,0:T(8,128)S(1)}, f32[48,256]{1,0:T(8,128)S(1)}, u32[]{:S(2)}, u32[]{:S(2)}) collective-permute-start(f32[48,256]{1,0:T(8,128)S(1)} %get-tuple-element.43), channel_id=1, source_target_pairs={{0,1},{1,0},{2,3},{3,2},{4,5},{5,4},{6,7},{7,6},{8,9},{9,8},{10,11... | collective-permute-start | bytes 147464 | tf_op jit(solution)/shard_map/ppermute | solution.py:753
  18.5 0.7 collective-permute-start.5
  19.2 0.2 collective-permute-done.2.y_a
  19.3 0.0 collective-permute-done.3.y_b
  19.4 1.7 %collective-permute-done.4.c_a = f32[48,256]{1,0:T(8,128)S(1)} collective-permute-done((f32[48,256]{1,0:T(8,128)S(1)}, f32[48,256]{1,0:T(8,128)S(1)}, u32[]{:S(2)}, u32[]{:S(2)}) %collective-permute-start.4) | collective-permute-done | bytes 49184 | tf_op jit(solution)/shard_map/ppermute | solution.py:753
  21.0 0.0 collective-permute-done.5.c_b
  21.0 0.0 copy-done.1
  21.0 0.0 copy-done.5
  21.0 0.0 copy-done.6
  21.0 8.6 %first_iteration.1 = (f32[3,16,16,256]{3,2,1,0:T(8,128)S(1)}, f32[32,4,128]{2,1,0:T(4,128)S(1)}, f32[12,16,256]{2,1,0:T(8,128)S(1)}, f32[12,16,256]{2,1,0:T(8,12...) custom-call(f32[3,16,16,256]{3,2,1,0:T(8,128)S(1)} %copy-done.1, ...), custom_call_target="tpu_custom_call" | custom-call | tf_op jit(solution)/shard_map/first_iteration/pallas_call | solution.py:587
  29.7 1.0 collective-permute-start.6
  30.6 1.7 %collective-permute-start.7 = (f32[12,16,256]{2,1,0:T(8,128)S(1)}, f32[12,16,256]{2,1,0:T(8,128)S(1)}, u32[]{:S(2)}, u32[]{:S(2)}) collective-permute-start(f32[12,16,256]{2,1,0:T(8,128)S(1)} %get-tuple-element.47), channel_id=1, source_target_pairs={{4,0},{8,4},{12,8},{16,12},{20,16},{24,20},{28,24},{0,28},{5,1},{9... | collective-permute-start | bytes 589832 | tf_op jit(solution)/shard_map/ppermute | solution.py:742
  32.4 4.6 %collective-permute-start.8 = (f32[48,4,256]{2,1,0:T(4,128)S(1)}, f32[48,4,256]{2,1,0:T(4,128)S(1)}, u32[]{:S(2)}, u32[]{:S(2)}) collective-permute-start(f32[48,4,256]{2,1,0:T(4,128)S(1)} %get-tuple-element.52), channel_id=1, source_target_pairs={{0,1},{1,0},{2,3},{3,2},{4,5},{5,4},{6,7},{7,6},{8,9},{9,8},{10,11... | collective-permute-start | bytes 589832 | tf_op jit(solution)/shard_map/ppermute | solution.py:753
  37.0 0.7 collective-permute-start.9
  37.6 13.0 %all_to_all.15 = f32[32,4,128]{2,1,0:T(4,128)S(1)} all-to-all(f32[32,4,128]{2,1,0:T(4,128)S(1)} %get-tuple-element.45), channel_id=1, replica_groups=mesh['row'=8,'col'=4] {'row','col'}, dimensions={0} | all-to-all | bytes 131072 | tf_op jit(solution)/shard_map/all_to_all | solution.py:770
  50.6 0.0 collective-permute-done.6.low
  50.6 0.0 collective-permute-done.7.high
  50.7 0.3 collective-permute-start.10
  51.0 0.7 collective-permute-start.11
  51.6 2.5 %solve.2.wide = f32[4,32,256]{2,1,0:T(8,128)S(1)} custom-call(f32[8,4,4,128]{3,2,1,0:T(4,128)S(1)} %bitcast.2), custom_call_target="tpu_custom_call" | custom-call | tf_op jit(solution)/shard_map/solve/pallas_call | solution.py:626
  54.1 0.0 collective-permute-done.8.y_a
  54.1 0.0 collective-permute-done.9.y_b
  54.1 0.6 collective-permute-done.10.c_a
  54.7 0.0 collective-permute-done.11.c_b
  54.7 7.4 %next_iteration.1 = (f32[3,16,16,256]{3,2,1,0:T(8,128)S(1)}, f32[32,4,128]{2,1,0:T(4,128)S(1)}, f32[12,16,256]{2,1,0:T(8,128)S(1)}, f32[12,16,256]{2,1,0:T(8,128...) custom-call(f32[4,32,256]{2,1,0:T(8,128)S(1)} %solve.2.wide, f32[3,16,16,256]{3,2,1,0:T(8,128)S(1)} %get-tuple-element.49.core, ...), custom_call_target="tpu_custom_call" | custom-call | tf_op jit(solution)/shard_map/next_iteration/pallas_call | solution.py:683
  62.1 0.1 collective-permute-start.12
  62.2 2.6 %collective-permute-start.13 = (f32[12,16,256]{2,1,0:T(8,128)S(1)}, f32[12,16,256]{2,1,0:T(8,128)S(1)}, u32[]{:S(2)}, u32[]{:S(2)}) collective-permute-start(f32[12,16,256]{2,1,0:T(8,128)S(1)} %get-tuple-element.61), channel_id=1, source_target_pairs={{4,0},{8,4},{12,8},{16,12},{20,16},{24,20},{28,24},{0,28},{5,1},{9... | collective-permute-start | bytes 589832 | tf_op jit(solution)/shard_map/ppermute | solution.py:742
  64.8 3.9 %collective-permute-start.14 = (f32[48,4,256]{2,1,0:T(4,128)S(1)}, f32[48,4,256]{2,1,0:T(4,128)S(1)}, u32[]{:S(2)}, u32[]{:S(2)}) collective-permute-start(f32[48,4,256]{2,1,0:T(4,128)S(1)} %get-tuple-element.66), channel_id=1, source_target_pairs={{0,1},{1,0},{2,3},{3,2},{4,5},{5,4},{6,7},{7,6},{8,9},{9,8},{10,11... | collective-permute-start | bytes 589832 | tf_op jit(solution)/shard_map/ppermute | solution.py:753
  68.7 0.7 collective-permute-start.15
  69.4 10.5 %all_to_all.16 = f32[32,4,128]{2,1,0:T(4,128)S(1)} all-to-all(f32[32,4,128]{2,1,0:T(4,128)S(1)} %get-tuple-element.59), channel_id=1, replica_groups=mesh['row'=8,'col'=4] {'row','col'}, dimensions={0} | all-to-all | bytes 131072 | tf_op jit(solution)/shard_map/all_to_all | solution.py:770
  79.8 0.0 collective-permute-done.12.low
  79.8 0.0 collective-permute-done.13.high
  79.9 0.3 collective-permute-start.16
  80.2 0.7 collective-permute-start.17
  80.9 2.5 %solve.3.wide = f32[4,32,256]{2,1,0:T(8,128)S(1)} custom-call(f32[8,4,4,128]{3,2,1,0:T(4,128)S(1)} %bitcast.3), custom_call_target="tpu_custom_call" | custom-call | tf_op jit(solution)/shard_map/solve/pallas_call | solution.py:626
  83.3 0.0 collective-permute-done.14.y_a
  83.3 0.0 collective-permute-done.15.y_b
  83.4 0.6 collective-permute-done.16.c_a
  84.0 0.0 collective-permute-done.17.c_b
  84.0 8.0 %last_iteration.1 = (f32[3,16,16,256]{3,2,1,0:T(8,128)S(1)}, f32[8,4,128]{2,1,0:T(4,128)S(1)}, f32[16,16,256]{2,1,0:T(8,128)}) custom-call(f32[4,32,256]{2,1,0:T(8,128)S(1)} %solve.3.wide, f32[3,16,16,256]{3,2,1,0:T(8,128)S(1)} %get-tuple-element.63.core, f32[12,16,256]{2,1,0:T(8,128)S(1)} %collective-permute-done.12.low, ...), custom_call_target="tpu_custom_call" | custom-call | tf_op jit(solution)/shard_map/last_iteration/pallas_call | solution.py:683
  91.9 7.1 %all_to_all.17.gathered = f32[8,4,128]{2,1,0:T(4,128)S(1)} all-to-all(f32[8,4,128]{2,1,0:T(4,128)S(1)} %get-tuple-element.70), channel_id=1, replica_groups=mesh['row'=8,'col'=4] {'row'}, dimensions={0} | all-to-all | bytes 32768 | tf_op jit(solution)/shard_map/all_to_all | solution.py:782
  99.0 2.9 %correct.1 = (f32[3,16,16,256]{3,2,1,0:T(8,128)}, f32[3,16,2,32]{3,2,1,0:T(2,128)}) custom-call(f32[8,4,128]{2,1,0:T(4,128)S(1)} %all_to_all.17.gathered, f32[3,16,16,256]{3,2,1,0:T(8,128)S(1)} %get-tuple-element.71.core), custom_call_target="tpu_custom_call" | custom-call | tf_op jit(solution)/shard_map/correct/pallas_call | solution.py:724
  (3 shorter events, 0.1 us)
Async XLA Ops:
  0.6 1.1 %copy-start = (f32[3,16,16,256]{3,2,1,0:T(8,128)S(1)}, f32[3,16,16,256]{3,2,1,0:T(8,128)}, u32[]{:S(2)}) copy-start(f32[3,16,16,256]{3,2,1,0:T(8,128)} %potential.3) | copy-start | bytes 2359300
  1.8 1.1 %copy-start.2 = (f32[3,16,16,256]{3,2,1,0:T(8,128)S(1)}, f32[3,16,16,256]{3,2,1,0:T(8,128)}, u32[]{:S(2)}) copy-start(f32[3,16,16,256]{3,2,1,0:T(8,128)} %source.3) | copy-start | bytes 2359300
  2.9 0.9 copy-start.3
  3.9 0.9 copy-start.4
  4.8 16.2 %copy-start.1 = (f32[3,16,16,256]{3,2,1,0:T(8,128)S(1)}, f32[3,16,16,256]{3,2,1,0:T(8,128)}, u32[]{:S(2)}) copy-start(f32[3,16,16,256]{3,2,1,0:T(8,128)} %potential.3) | copy-start | bytes 2359300
  4.8 16.2 %copy-start.5 = (f32[8]{0:T(128)S(1)}, f32[8]{0:T(128)}, u32[]{:S(2)}) copy-start(f32[8]{0:T(128)} %floor_table.1) | copy-start | bytes 100
  4.8 16.2 %copy-start.6 = (f32[8]{0:T(128)S(1)}, f32[8]{0:T(128)}, u32[]{:S(2)}) copy-start(f32[8]{0:T(128)} %rise_table.1) | copy-start | bytes 100
  5.9 9.3 %collective-permute-start = (f32[21,16,256]{2,1,0:T(8,128)S(1)}, f32[21,16,256]{2,1,0:T(8,128)S(1)}, u32[]{:S(2)}, u32[]{:S(2)}) collective-permute-start(f32[21,16,256]{2,1,0:T(8,128)S(1)} %get-tuple-element.39), channel_id=1, source_target_pairs={{0,4},{4,8},{8,12},{12,16},{16,20},{20,24},{24,28},{28,0},{1,5},{5... | collective-permute-start | bytes 1032200 | tf_op jit(solution)/shard_map/ppermute | solution.py:742
  6.4 10.4 %collective-permute-start.1 = (f32[21,16,256]{2,1,0:T(8,128)S(1)}, f32[21,16,256]{2,1,0:T(8,128)S(1)}, u32[]{:S(2)}, u32[]{:S(2)}) collective-permute-start(f32[21,16,256]{2,1,0:T(8,128)S(1)} %get-tuple-element.40), channel_id=1, source_target_pairs={{4,0},{8,4},{12,8},{16,12},{20,16},{24,20},{28,24},{0,28},{5,1},{9... | collective-permute-start | bytes 1032200 | tf_op jit(solution)/shard_map/ppermute | solution.py:742
  9.4 10.0 %collective-permute-start.2 = (f32[88,4,256]{2,1,0:T(4,128)S(1)}, f32[88,4,256]{2,1,0:T(4,128)S(1)}, u32[]{:S(2)}, u32[]{:S(2)}) collective-permute-start(f32[88,4,256]{2,1,0:T(4,128)S(1)} %get-tuple-element.41), channel_id=1, source_target_pairs={{0,1},{1,0},{2,3},{3,2},{4,5},{5,4},{6,7},{7,6},{8,9},{9,8},{10,11... | collective-permute-start | bytes 1081352 | tf_op jit(solution)/shard_map/ppermute | solution.py:753
  11.6 7.7 %collective-permute-start.3 = (f32[88,4,256]{2,1,0:T(4,128)S(1)}, f32[88,4,256]{2,1,0:T(4,128)S(1)}, u32[]{:S(2)}, u32[]{:S(2)}) collective-permute-start(f32[88,4,256]{2,1,0:T(4,128)S(1)} %get-tuple-element.42), channel_id=1, source_target_pairs={{0,0},{1,2},{2,1},{3,3},{4,4},{5,6},{6,5},{7,7},{8,8},{9,10},{10,9... | collective-permute-start | bytes 1081352 | tf_op jit(solution)/shard_map/ppermute | solution.py:753
  16.8 4.2 %collective-permute-start.4 = (f32[48,256]{1,0:T(8,128)S(1)}, f32[48,256]{1,0:T(8,128)S(1)}, u32[]{:S(2)}, u32[]{:S(2)}) collective-permute-start(f32[48,256]{1,0:T(8,128)S(1)} %get-tuple-element.43), channel_id=1, source_target_pairs={{0,1},{1,0},{2,3},{3,2},{4,5},{5,4},{6,7},{7,6},{8,9},{9,8},{10,11... | collective-permute-start | bytes 147464 | tf_op jit(solution)/shard_map/ppermute | solution.py:753
  18.5 2.5 %collective-permute-start.5 = (f32[48,256]{1,0:T(8,128)S(1)}, f32[48,256]{1,0:T(8,128)S(1)}, u32[]{:S(2)}, u32[]{:S(2)}) collective-permute-start(f32[48,256]{1,0:T(8,128)S(1)} %get-tuple-element.44), channel_id=1, source_target_pairs={{0,0},{1,2},{2,1},{3,3},{4,4},{5,6},{6,5},{7,7},{8,8},{9,10},{10,9... | collective-permute-start | bytes 147464 | tf_op jit(solution)/shard_map/ppermute | solution.py:753
  29.7 20.9 %collective-permute-start.6 = (f32[12,16,256]{2,1,0:T(8,128)S(1)}, f32[12,16,256]{2,1,0:T(8,128)S(1)}, u32[]{:S(2)}, u32[]{:S(2)}) collective-permute-start(f32[12,16,256]{2,1,0:T(8,128)S(1)} %get-tuple-element.46), channel_id=1, source_target_pairs={{0,4},{4,8},{8,12},{12,16},{16,20},{20,24},{24,28},{28,0},{1,5},{5... | collective-permute-start | bytes 589832 | tf_op jit(solution)/shard_map/ppermute | solution.py:742
  30.6 20.0 %collective-permute-start.7 = (f32[12,16,256]{2,1,0:T(8,128)S(1)}, f32[12,16,256]{2,1,0:T(8,128)S(1)}, u32[]{:S(2)}, u32[]{:S(2)}) collective-permute-start(f32[12,16,256]{2,1,0:T(8,128)S(1)} %get-tuple-element.47), channel_id=1, source_target_pairs={{4,0},{8,4},{12,8},{16,12},{20,16},{24,20},{28,24},{0,28},{5,1},{9... | collective-permute-start | bytes 589832 | tf_op jit(solution)/shard_map/ppermute | solution.py:742
  32.4 21.7 %collective-permute-start.8 = (f32[48,4,256]{2,1,0:T(4,128)S(1)}, f32[48,4,256]{2,1,0:T(4,128)S(1)}, u32[]{:S(2)}, u32[]{:S(2)}) collective-permute-start(f32[48,4,256]{2,1,0:T(4,128)S(1)} %get-tuple-element.52), channel_id=1, source_target_pairs={{0,1},{1,0},{2,3},{3,2},{4,5},{5,4},{6,7},{7,6},{8,9},{9,8},{10,11... | collective-permute-start | bytes 589832 | tf_op jit(solution)/shard_map/ppermute | solution.py:753
  37.0 17.1 %collective-permute-start.9 = (f32[48,4,256]{2,1,0:T(4,128)S(1)}, f32[48,4,256]{2,1,0:T(4,128)S(1)}, u32[]{:S(2)}, u32[]{:S(2)}) collective-permute-start(f32[48,4,256]{2,1,0:T(4,128)S(1)} %get-tuple-element.53), channel_id=1, source_target_pairs={{0,0},{1,2},{2,1},{3,3},{4,4},{5,6},{6,5},{7,7},{8,8},{9,10},{10,9... | collective-permute-start | bytes 589832 | tf_op jit(solution)/shard_map/ppermute | solution.py:753
  50.7 4.1 %collective-permute-start.10 = (f32[40,256]{1,0:T(8,128)S(1)}, f32[40,256]{1,0:T(8,128)S(1)}, u32[]{:S(2)}, u32[]{:S(2)}) collective-permute-start(f32[40,256]{1,0:T(8,128)S(1)} %get-tuple-element.54), channel_id=1, source_target_pairs={{0,1},{1,0},{2,3},{3,2},{4,5},{5,4},{6,7},{7,6},{8,9},{9,8},{10,11... | collective-permute-start | bytes 122888 | tf_op jit(solution)/shard_map/ppermute | solution.py:753
  51.0 3.8 %collective-permute-start.11 = (f32[40,256]{1,0:T(8,128)S(1)}, f32[40,256]{1,0:T(8,128)S(1)}, u32[]{:S(2)}, u32[]{:S(2)}) collective-permute-start(f32[40,256]{1,0:T(8,128)S(1)} %get-tuple-element.55), channel_id=1, source_target_pairs={{0,0},{1,2},{2,1},{3,3},{4,4},{5,6},{6,5},{7,7},{8,8},{9,10},{10,9... | collective-permute-start | bytes 122888 | tf_op jit(solution)/shard_map/ppermute | solution.py:753
  62.1 17.8 %collective-permute-start.12 = (f32[12,16,256]{2,1,0:T(8,128)S(1)}, f32[12,16,256]{2,1,0:T(8,128)S(1)}, u32[]{:S(2)}, u32[]{:S(2)}) collective-permute-start(f32[12,16,256]{2,1,0:T(8,128)S(1)} %get-tuple-element.60), channel_id=1, source_target_pairs={{0,4},{4,8},{8,12},{12,16},{16,20},{20,24},{24,28},{28,0},{1,5},{5... | collective-permute-start | bytes 589832 | tf_op jit(solution)/shard_map/ppermute | solution.py:742
  62.2 17.7 %collective-permute-start.13 = (f32[12,16,256]{2,1,0:T(8,128)S(1)}, f32[12,16,256]{2,1,0:T(8,128)S(1)}, u32[]{:S(2)}, u32[]{:S(2)}) collective-permute-start(f32[12,16,256]{2,1,0:T(8,128)S(1)} %get-tuple-element.61), channel_id=1, source_target_pairs={{4,0},{8,4},{12,8},{16,12},{20,16},{24,20},{28,24},{0,28},{5,1},{9... | collective-permute-start | bytes 589832 | tf_op jit(solution)/shard_map/ppermute | solution.py:742
  64.8 18.6 %collective-permute-start.14 = (f32[48,4,256]{2,1,0:T(4,128)S(1)}, f32[48,4,256]{2,1,0:T(4,128)S(1)}, u32[]{:S(2)}, u32[]{:S(2)}) collective-permute-start(f32[48,4,256]{2,1,0:T(4,128)S(1)} %get-tuple-element.66), channel_id=1, source_target_pairs={{0,1},{1,0},{2,3},{3,2},{4,5},{5,4},{6,7},{7,6},{8,9},{9,8},{10,11... | collective-permute-start | bytes 589832 | tf_op jit(solution)/shard_map/ppermute | solution.py:753
  68.7 14.7 %collective-permute-start.15 = (f32[48,4,256]{2,1,0:T(4,128)S(1)}, f32[48,4,256]{2,1,0:T(4,128)S(1)}, u32[]{:S(2)}, u32[]{:S(2)}) collective-permute-start(f32[48,4,256]{2,1,0:T(4,128)S(1)} %get-tuple-element.67), channel_id=1, source_target_pairs={{0,0},{1,2},{2,1},{3,3},{4,4},{5,6},{6,5},{7,7},{8,8},{9,10},{10,9... | collective-permute-start | bytes 589832 | tf_op jit(solution)/shard_map/ppermute | solution.py:753
  79.9 4.1 %collective-permute-start.16 = (f32[40,256]{1,0:T(8,128)S(1)}, f32[40,256]{1,0:T(8,128)S(1)}, u32[]{:S(2)}, u32[]{:S(2)}) collective-permute-start(f32[40,256]{1,0:T(8,128)S(1)} %get-tuple-element.68), channel_id=1, source_target_pairs={{0,1},{1,0},{2,3},{3,2},{4,5},{5,4},{6,7},{7,6},{8,9},{9,8},{10,11... | collective-permute-start | bytes 122888 | tf_op jit(solution)/shard_map/ppermute | solution.py:753
  80.2 3.8 %collective-permute-start.17 = (f32[40,256]{1,0:T(8,128)S(1)}, f32[40,256]{1,0:T(8,128)S(1)}, u32[]{:S(2)}, u32[]{:S(2)}) collective-permute-start(f32[40,256]{1,0:T(8,128)S(1)} %get-tuple-element.69), channel_id=1, source_target_pairs={{0,0},{1,2},{2,1},{3,3},{4,4},{5,6},{6,5},{7,7},{8,8},{9,10},{10,9... | collective-permute-start | bytes 122888 | tf_op jit(solution)/shard_map/ppermute | solution.py:753

commit v3 on v2

--- a/solution.py
+++ b/solution.py
@@ -50,7 +50,8 @@
 CORNER_DRIVE = 6 * FIELD_ROWS
 CORNER_TABLE = CORNER_DRIVE + 6
 CORNER_ALL = CORNER_TABLE + 2 * LABEL_ROWS
-CORNER_LATER = 40
+CORNER_LATER = 48
+SLABS = ((0, 4, 0, 1), (4, 12, 1, 0), (12, 20, 1, 1), (20, 24, 2, 0))
 
 
 def pack_first_kernel(
@@ -119,7 +120,7 @@
     ]
     return pl.pallas_call(
         pack_first_kernel,
-        in_specs=[pl.BlockSpec(memory_space=pl.ANY)] * 4,
+        in_specs=[pl.BlockSpec(memory_space=pltpu.HBM)] * 4,
         out_specs=[VMEM] * 4,
         out_shape=[f32(X_PAGES, BLOCK, depth)] * 2 + [f32(Y_PAGES, HALO, depth)] * 2,
         scratch_shapes=scratch,
@@ -128,9 +129,7 @@
     )(potential, source, coil_mask, labels)
 
 
-def pack_corner_kernel(whole, low, high, out_a, out_b):
-    even = lax.axis_index("col") % 2 == 0
-
+def corner_sender(low, high, out_a, out_b, even):
     def send(row, count, ref, page):
         rows = slice(row, row + count)
         first, second = turns(even, ref[page, 0:count], ref[page, BLOCK - count : BLOCK])
@@ -142,23 +141,28 @@
             row = comp * 2 * FIELD_ROWS + first
             send(row, count, low, comp * 4 + 4 - distance)
             send(row + FIELD_ROWS, count, high, comp * 4 + distance - 1)
-        if whole:
-            send(CORNER_DRIVE + comp * 2, 1, low, 12 + comp * 2 + 1)
-            send(CORNER_DRIVE + comp * 2 + 1, 1, high, 12 + comp * 2)
-    if whole:
-        for distance, first, count in CORNER_LABEL:
-            row = CORNER_TABLE + first
-            send(row, count, low, 18 + 3 - distance)
-            send(row + LABEL_ROWS, count, high, 18 + distance - 1)
-
-
-def pack_corner(whole, low, high):
+    return send
+
+
+def pack_corner_kernel(low, high, out_a, out_b):
+    even = lax.axis_index("col") % 2 == 0
+    send = corner_sender(low, high, out_a, out_b, even)
+    for comp in range(3):
+        send(CORNER_DRIVE + comp * 2, 1, low, 12 + comp * 2 + 1)
+        send(CORNER_DRIVE + comp * 2 + 1, 1, high, 12 + comp * 2)
+    for distance, first, count in CORNER_LABEL:
+        row = CORNER_TABLE + first
+        send(row, count, low, 18 + 3 - distance)
+        send(row + LABEL_ROWS, count, high, 18 + distance - 1)
+
+
+def pack_corner(low, high):
     depth = low.shape[-1]
     return pl.pallas_call(
-        functools.partial(pack_corner_kernel, whole),
+        pack_corner_kernel,
         in_specs=[VMEM] * 2,
         out_specs=[VMEM] * 2,
-        out_shape=[f32(CORNER_ALL if whole else CORNER_LATER, depth)] * 2,
+        out_shape=[f32(CORNER_ALL, depth)] * 2,
         compiler_params=PARAMS,
         name="pack_corner",
     )(low, high)
@@ -248,24 +252,49 @@
     return jnp.sum(jnp.where(row == index, values, 0.0), axis=0, keepdims=True)
 
 
-def spread_matrix(group):
-    lane = lax.broadcasted_iota(jnp.int32, (LANES, 2 * LANES), 0)
-    cell = lax.broadcasted_iota(jnp.int32, (LANES, 2 * LANES), 1)
-    return jnp.where(lane == group * 32 + cell // COARSEN, 1.0, 0.0)
-
-
-def gather_matrix(group):
+def block_matrix(lanes_first):
+    shape = (LANES, 2 * LANES) if lanes_first else (2 * LANES, LANES)
+    lane = lax.broadcasted_iota(jnp.int32, shape, 0 if lanes_first else 1)
+    cell = lax.broadcasted_iota(jnp.int32, shape, 1 if lanes_first else 0)
+    return jnp.where(lane == cell // COARSEN, 1.0, 0.0)
+
+
+def side_matrix():
+    lane = lax.broadcasted_iota(jnp.int32, (2 * LANES, LANES), 1)
     cell = lax.broadcasted_iota(jnp.int32, (2 * LANES, LANES), 0)
-    lane = lax.broadcasted_iota(jnp.int32, (2 * LANES, LANES), 1)
-    return jnp.where(lane == group * 32 + cell // COARSEN, 1.0, 0.0)
-
-
-def load_stripe(table, gathered, count, pick):
-    for row in range(count):
-        for comp in range(4):
-            table[comp, row : row + 1, :] = pick(row)[comp : comp + 1, :]
+    end = jnp.logical_and(cell % COARSEN == COARSEN - 1, lane < 32)
+    block = cell // COARSEN
+    return jnp.where(
+        end, jnp.where(lane == block, 1.0, jnp.where(lane == block + 1, -1.0, 0.0)), 0.0
+    )
+
+
+def stripe_rows(gathered):
+    rows = gathered.shape[0]
+    spot = lax.broadcasted_iota(jnp.int32, (rows, LANES), 0)
+    out = []
+    for comp in range(4):
+        total = jnp.zeros((rows, LANES), jnp.float32)
+        for row in range(rows):
+            total = jnp.where(spot == row, gathered[row, comp : comp + 1, :], total)
+        out.append(total)
     scale = 1.0 / float(COARSEN * COARSEN)
-    return [table[comp] * scale for comp in range(3)], table[3]
+    return [out[comp] * scale for comp in range(3)], out[3]
+
+
+def widen(correction, row, picked):
+    picked[...] = jnp.zeros(picked.shape, jnp.float32)
+    for comp in range(3):
+        for shift in range(3):
+            spot = comp * 3 + shift
+            picked[spot : spot + 1, :] = pick_row(correction[comp], row + shift - 1)
+    for group in range(1, 4):
+        picked[group * 16 : group * 16 + 16, :] = pltpu.roll(
+            picked[0:16, :], LANES - 32 * group, 1
+        )
+    return jnp.dot(
+        picked[...], block_matrix(True), precision=HIGH, preferred_element_type=jnp.float32
+    )
 
 
 class Place:
@@ -393,7 +422,7 @@
 
 
 def fine_iteration(
-    field, other, reluct, c_x, c_y, c_up, c_down, weight, diag, sums, drive, floor, rise,
+    field, other, reluct, c_x, c_y, c_up, c_down, weight, sums, drive_sums, drive, floor, rise,
 ):
     mid = slice(TOP, TOP + EXT)
     plus = slice(TOP + 1, TOP + EXT + 1)
@@ -475,7 +504,7 @@
             coeffs.append((x_plus, x_minus, y_plus, y_minus, up, down))
             weights.append(scale)
             for ref, value in (
-                (c_x, x_plus), (c_y, y_plus), (c_up, up), (c_down, down), (diag, total), (weight, scale),
+                (c_x, x_plus), (c_y, y_plus), (c_up, up), (c_down, down), (weight, scale),
             ):
                 stores.append((ref.at[half, x, mid], value))
         for comp, half, here, total in apply(field, x, mid, coeffs, first, last):
@@ -500,47 +529,107 @@
     in_pairs(3, EXT - 3, second_plane)
 
     own = slice(CORE, CORE + BLOCK)
+    ends = pl.ds(CORE - 1, 3, stride=COARSEN)
+    beyond = pl.ds(CORE, 3, stride=COARSEN)
     lane = lax.broadcasted_iota(jnp.int32, (BLOCK, LANES), 1)
-    first_own, last_own = lane == 0, lane == LANES - 1
+    last_own = lane == LANES - 1
+    lane = lax.broadcasted_iota(jnp.int32, (1, LANES), 1)
+    rims = (lane == 0, lane == LANES - 1)
     zero = jnp.zeros((BLOCK, LANES), jnp.float32)
-    result = jnp.zeros((8, LANES), jnp.float32)
+    thin = jnp.zeros((3, LANES), jnp.float32)
+
+    def blocks(values):
+        return [
+            jnp.sum(values[part * COARSEN : (part + 1) * COARSEN], axis=0, keepdims=True)
+            for part in range(2)
+        ]
+
+    def side(plane, comp, half):
+        return blocks(
+            c_x[half, plane, own]
+            * (field[comp, half, plane + 1, own] - field[comp, half, plane, own])
+        )
+
     sums[...] = jnp.zeros(sums.shape, jnp.float32)
-    for coarse in range(BLOCK // COARSEN):
+    sides = [
+        [[side(HALO - 1 + COARSEN * k, comp, half) for half in range(2)] for comp in range(3)]
+        for k in range(3)
+    ]
+    for coarse in range(2):
         def plane(step, totals):
             x = HALO + coarse * COARSEN + step
-            out = []
-            diags = [diag[half, x, own] for half in range(2)]
-            for comp, half, here, off in apply(
-                field, x, own, load_coeffs(x, own), first_own, last_own
-            ):
-                out.append(
-                    totals[comp * 2 + half]
-                    + (drive[comp, half, x, HALO : HALO + BLOCK] - (diags[half] * here - off))
-                )
-            for half in range(2):
-                out.append(totals[6 + half] + reluct[half, x, own])
-            return tuple(out)
-
-        totals = lax.fori_loop(0, COARSEN, plane, (zero,) * 8)
-        for part in range(BLOCK // COARSEN):
-            group = coarse * 2 + part
-            for comp in range(4):
-                scale = 0.5 if comp < 3 else 1.0 / float(COARSEN ** 3)
+            across, rim, along, material = totals
+            relucts = [reluct[half, x, own] for half in range(2)]
+            ups = [c_up[half, x, own] for half in range(2)]
+            ys = [c_y[half, x, ends, :] for half in range(2)]
+            across_new, rim_new, along_new = [], [], []
+            for comp in range(3):
+                here = [field[comp, half, x, own] for half in range(2)]
+                rights = right_of(here[0], here[1], last_own)
                 for half in range(2):
-                    block = totals[comp * 2 + half][part * COARSEN : (part + 1) * COARSEN]
-                    sums[group, comp : comp + 1, half * LANES : (half + 1) * LANES] = scale * jnp.sum(
-                        block, axis=0, keepdims=True
+                    number = comp * 2 + half
+                    across_new.append(across[number] + ups[half] * (rights[half] - here[half]))
+                    rim_new.append(rim[number] + relucts[half] * here[half])
+                    along_new.append(
+                        along[number]
+                        + ys[half] * (field[comp, half, x, beyond, :] - field[comp, half, x, ends, :])
                     )
-            result = result + jnp.dot(
-                sums[group], gather_matrix(group), precision=HIGH, preferred_element_type=jnp.float32
+            return (
+                tuple(across_new), tuple(rim_new), tuple(along_new),
+                tuple(material[half] + relucts[half] for half in range(2)),
             )
+
+        across, rim, along, material = lax.fori_loop(
+            0, COARSEN, plane, ((zero,) * 6, (zero,) * 6, (thin,) * 6, (zero,) * 2)
+        )
+        for half in range(2):
+            z = slice(half * LANES, (half + 1) * LANES)
+            means = blocks(material[half])
+            for comp in range(3):
+                number = comp * 2 + half
+                rims_sum, across_sum = blocks(rim[number]), blocks(across[number])
+                for part in range(2):
+                    row = (coarse * 2 + part) * 8
+                    y_side = along[number][part + 1 : part + 2] - along[number][part : part + 1]
+                    x_side = sides[coarse + 1][comp][half][part] - sides[coarse][comp][half][part]
+                    spot = row + comp
+                    sums[0, spot : spot + 1, z] = 0.5 * (
+                        (drive_sums[spot : spot + 1, z] + (x_side + y_side))
+                        - jnp.where(rims[half], rims_sum[part], 0.0)
+                    )
+                    sums[1, spot : spot + 1, z] = 0.5 * across_sum[part]
+            for part in range(2):
+                spot = (coarse * 2 + part) * 8 + 3
+                sums[0, spot : spot + 1, z] = means[part] * (1.0 / float(COARSEN ** 3))
+    totals = jnp.dot(
+        sums[0], block_matrix(False), precision=HIGH, preferred_element_type=jnp.float32
+    ) + jnp.dot(sums[1], side_matrix(), precision=HIGH, preferred_element_type=jnp.float32)
+    result = totals[0:8]
+    for group in range(1, 4):
+        result = result + pltpu.roll(totals[group * 8 : group * 8 + 8], 32 * group, 1)
     return result[0:4]
+
+
+def sum_drive(drive, drive_sums):
+    own = slice(HALO, HALO + BLOCK)
+    drive_sums[...] = jnp.zeros(drive_sums.shape, jnp.float32)
+    for comp in range(3):
+        for half in range(2):
+            for coarse in range(2):
+                total = drive[comp, half, HALO + coarse * COARSEN, own]
+                for x in range(HALO + coarse * COARSEN + 1, HALO + (coarse + 1) * COARSEN):
+                    total = total + drive[comp, half, x, own]
+                for part in range(2):
+                    spot = (coarse * 2 + part) * 8 + comp
+                    drive_sums[spot : spot + 1, half * LANES : (half + 1) * LANES] = jnp.sum(
+                        total[part * COARSEN : (part + 1) * COARSEN], axis=0, keepdims=True
+                    )
 
 
 SCRATCH = (
     [pltpu.VMEM((3, 2, EXT, ROWS, LANES), jnp.float32)] * 2
-    + [pltpu.VMEM((2, EXT, ROWS, LANES), jnp.float32)] * 7
-    + [pltpu.VMEM((4, 8, 2 * LANES), jnp.float32)]
+    + [pltpu.VMEM((2, EXT, ROWS, LANES), jnp.float32)] * 6
+    + [pltpu.VMEM((2, 32, 2 * LANES), jnp.float32)]
 )
 
 
@@ -569,7 +658,7 @@
 
 def first_kernel(
     potential, source, coil_mask, labels, low, high, y_a, y_b, c_a, c_b, floor_table, rise_table,
-    field_out, coarse_out, x_lo, x_hi, yo_a, yo_b, drive, floor, rise, *scratch,
+    field_out, coarse_out, x_lo, x_hi, yo_a, yo_b, drive_sums, drive, floor, rise, *scratch,
 ):
     place = Place()
     field = scratch[0]
@@ -578,67 +667,59 @@
         drive, floor, rise, source, coil_mask, labels, low, high, y_a, y_b, c_a, c_b, floor_table,
         rise_table, place,
     )
-    coarse = fine_iteration(*scratch, drive, floor, rise)
+    sum_drive(drive, drive_sums)
+    coarse = fine_iteration(*scratch, drive_sums, drive, floor, rise)
     emit(field, coarse, field_out, (x_lo, x_hi, yo_a, yo_b), coarse_out, place)
 
 
-def first_iteration(potential, source, coil_mask, labels, messages, tables, devices):
+def first_iteration(potential, source, coil_mask, labels, messages, tables, rows):
     depth = potential.shape[-1]
     return pl.pallas_call(
         first_kernel,
         in_specs=[VMEM] * 10 + [SMEM] * 2,
-        out_specs=[VMEM] * 9,
-        out_shape=[f32(*potential.shape), f32(devices, 4, LANES)]
+        out_specs=[VMEM] * 10,
+        out_shape=[f32(*potential.shape), f32(rows, 4, LANES)]
         + edge_shapes(depth)
-        + [f32(3, 2, EXT, EXT, LANES), f32(2, EXT, EXT, LANES), f32(2, EXT, EXT, LANES)],
+        + [f32(32, 2 * LANES), f32(3, 2, EXT, EXT, LANES), f32(2, EXT, EXT, LANES), f32(2, EXT, EXT, LANES)],
         scratch_shapes=SCRATCH,
         compiler_params=PARAMS,
         name="first_iteration",
     )(potential, source, coil_mask, labels, *messages, *tables)
 
 
-def solve_kernel(gathered, wide_out, table, picked):
+def solve_kernel(gathered, low, high, wide_out, c_a, c_b, picked):
     place = Place()
-    targets, relucts = [], []
-    for stripe in range(3):
-        index = jnp.clip(place.col + stripe - 1, 0, place.cols - 1)
-        target, reluct = load_stripe(
-            table.at[stripe], gathered, gathered.shape[0], lambda r: gathered[r, index]
-        )
-        targets.append(target)
-        relucts.append(reluct)
-    corrections = coarse_solve(targets, relucts)
-    picked[...] = jnp.zeros(picked.shape, jnp.float32)
-    for stripe in range(3):
-        there = (place.back, True, place.front)[stripe]
+    target, reluct = stripe_rows(gathered)
+    correction, = coarse_solve([target], [reluct])
+    wide = widen(correction, place.row, picked)
+    wide_out[...] = wide
+    corner_sender(low, high, c_a, c_b, place.even)
+    for slab, (begin, end, shift, x) in enumerate(SLABS):
         for comp in range(3):
-            for shift in range(3):
-                line = pick_row(corrections[stripe][comp], place.row + shift - 1)
-                spot = (stripe * 3 + comp) * 3 + shift
-                picked[spot : spot + 1, :] = jnp.where(there, line, 0.0)
-    for group in range(4):
-        wide_out[group] = jnp.dot(
-            picked[...], spread_matrix(group), precision=HIGH, preferred_element_type=jnp.float32
-        )
-
-
-def solve(gathered):
+            low_edge, high_edge = (
+                wide[spot : spot + 1] for spot in (x * 32 + 16 * y + comp * 3 + shift for y in range(2))
+            )
+            row = CORNER_DRIVE + slab * 3 + comp
+            first, second = turns(place.even, low_edge, high_edge)
+            c_a[row : row + 1, :] = first
+            c_b[row : row + 1, :] = second
+
+
+def solve(gathered, low, high):
+    depth = low.shape[-1]
     return pl.pallas_call(
         solve_kernel,
-        in_specs=[VMEM],
-        out_specs=VMEM,
-        out_shape=f32(4, 32, 2 * LANES),
-        scratch_shapes=[
-            pltpu.VMEM((3, 4, gathered.shape[0], LANES), jnp.float32),
-            pltpu.VMEM((32, LANES), jnp.float32),
-        ],
+        in_specs=[VMEM] * 3,
+        out_specs=[VMEM] * 3,
+        out_shape=[f32(64, depth)] + [f32(CORNER_LATER, depth)] * 2,
+        scratch_shapes=[pltpu.VMEM((64, LANES), jnp.float32)],
         compiler_params=PARAMS,
         name="solve",
-    )(gathered)
+    )(gathered, low, high)
 
 
 def next_kernel(
-    final, wide, core, low, high, y_a, y_b, c_a, c_b, drive, floor, rise, *refs
+    final, wide, core, low, high, y_a, y_b, c_a, c_b, drive_sums, drive, floor, rise, *refs
 ):
     if final:
         field_out, coarse_out, reluct_out, *scratch = refs
@@ -651,23 +732,24 @@
     put_field(field, core, low, high, y_a, y_b, c_a, c_b, place)
     mid = slice(TOP, TOP + EXT)
     cell = lax.broadcasted_iota(jnp.int32, (EXT, LANES), 0)
-    for begin, end, shift, x in ((0, 4, 0, 1), (4, 12, 1, 0), (12, 20, 1, 1), (20, 24, 2, 0)):
+    for slab, (begin, end, shift, x) in enumerate(SLABS):
         for comp in range(3):
             for half in range(2):
-                def line(stripe, y):
-                    spot = (stripe * 3 + comp) * 3 + shift
-                    return wide[
-                        x * 2 + y, spot : spot + 1, half * LANES : (half + 1) * LANES
-                    ]
-
+                z = slice(half * LANES, (half + 1) * LANES)
+                spot = CORNER_DRIVE + slab * 3 + comp
+                back, front = place.sides(c_a[spot : spot + 1, z], c_b[spot : spot + 1, z])
+                back = jnp.where(place.back, back, 0.0)
+                front = jnp.where(place.front, front, 0.0)
+                spot = x * 32 + comp * 3 + shift
+                own = [wide[spot + 16 * y : spot + 16 * y + 1, z] for y in range(2)]
                 tile = jnp.where(
                     cell < 12,
-                    jnp.where(cell < 4, line(0, 1), line(1, 0)),
-                    jnp.where(cell < 20, line(1, 1), line(2, 0)),
+                    jnp.where(cell < 4, back, own[0]),
+                    jnp.where(cell < 20, own[1], front),
                 )
                 for plane in range(begin, end):
                     field[comp, half, plane, mid] = field[comp, half, plane, mid] + tile
-    coarse = fine_iteration(*scratch, drive, floor, rise)
+    coarse = fine_iteration(*scratch, drive_sums, drive, floor, rise)
     emit(field, coarse, field_out, edges, coarse_out, place)
     if final:
         reluct = scratch[2]
@@ -677,12 +759,12 @@
             ]
 
 
-def next_iteration(final, wide, core, messages, material, devices):
-    outs = [f32(*core.shape), f32(devices, 4, LANES)]
+def next_iteration(final, wide, core, messages, material, rows):
+    outs = [f32(*core.shape), f32(rows, 4, LANES)]
     outs += [f32(*core.shape[1:])] if final else edge_shapes(core.shape[-1])
     return pl.pallas_call(
         functools.partial(next_kernel, final),
-        in_specs=[VMEM] * 11,
+        in_specs=[VMEM] * 12,
         out_specs=[VMEM] * len(outs),
         out_shape=outs,
         scratch_shapes=SCRATCH,
@@ -691,22 +773,18 @@
     )(wide, core, *messages, *material)
 
 
-def correct_kernel(gathered, core, field_out, target_out, table, picked):
+def correct_kernel(gathered, core, field_out, target_out, picked):
     row = lax.axis_index("row")
-    target, reluct = load_stripe(table, gathered, gathered.shape[0], lambda r: gathered[r])
+    rows = gathered.shape[0]
+    target, reluct = stripe_rows(gathered)
     correction, = coarse_solve([target], [reluct])
-    picked[...] = jnp.zeros(picked.shape, jnp.float32)
-    for comp in range(3):
-        picked[comp : comp + 1, :] = pick_row(correction[comp], row)
-    wide = [
-        jnp.dot(picked[...], spread_matrix(group), precision=HIGH, preferred_element_type=jnp.float32)
-        for group in range(4)
-    ]
+    wide = widen(correction, row, picked)
     cell = lax.broadcasted_iota(jnp.int32, (BLOCK, 2 * LANES), 0)
     for x in range(2):
         for comp in range(3):
+            spot = x * 32 + comp * 3 + 1
             tile = jnp.where(
-                cell < COARSEN, wide[x * 2][comp : comp + 1, :], wide[x * 2 + 1][comp : comp + 1, :]
+                cell < COARSEN, wide[spot : spot + 1], wide[spot + 16 : spot + 17]
             )
             for plane in range(x * COARSEN, (x + 1) * COARSEN):
                 field_out[comp, plane] = core[comp, plane] + tile
@@ -715,7 +793,7 @@
             for y in range(2):
                 group = x * 2 + y
                 moved = target[comp] if group == 0 else pltpu.roll(target[comp], LANES - 32 * group, 1)
-                for r in range(gathered.shape[0]):
+                for r in range(rows):
                     target_out[comp, 2 * r + x, y : y + 1, :] = moved[r : r + 1, 0:32]
 
 
@@ -726,10 +804,7 @@
         in_specs=[VMEM] * 2,
         out_specs=[VMEM] * 2,
         out_shape=[f32(*core.shape), f32(3, 2 * rows, 2, 32)],
-        scratch_shapes=[
-            pltpu.VMEM((4, rows, LANES), jnp.float32),
-            pltpu.VMEM((8, LANES), jnp.float32),
-        ],
+        scratch_shapes=[pltpu.VMEM((64, LANES), jnp.float32)],
         compiler_params=PARAMS,
         name="correct",
     )(gathered, core)
@@ -754,27 +829,25 @@
 
 
 def shards(potential, source, labels, coil_mask, floor_table, rise_table):
-    rows, cols = lax.axis_size("row"), lax.axis_size("col")
-    x_lo, x_hi, y_a, y_b = pack_first(potential, source, labels, coil_mask)
+    rows = lax.axis_size("row")
+    x_lo, x_hi, y_a, y_b = pack_first(
+        *(pltpu.with_memory_space_constraint(v, pltpu.HBM) for v in (potential, source, labels, coil_mask))
+    )
     low, high = rings(x_lo, x_hi)
     y_a, y_b = swaps(y_a, y_b)
-    c_a, c_b = swaps(*pack_corner(True, low, high))
+    c_a, c_b = swaps(*pack_corner(low, high))
     field, coarse, x_lo, x_hi, y_a, y_b, *material = first_iteration(
         potential, source, coil_mask, labels, (low, high, y_a, y_b, c_a, c_b),
-        (floor_table, rise_table), rows * cols,
+        (floor_table, rise_table), rows,
     )
     for iteration in range(1, ITERS):
         final = iteration == ITERS - 1
         low, high = rings(x_lo, x_hi)
         y_a, y_b = swaps(y_a, y_b)
-        gathered = lax.all_to_all(coarse, ("row", "col"), 0, 0)
-        gathered, low, high = lax.optimization_barrier((gathered, low, high))
-        c_a, c_b = swaps(*pack_corner(False, low, high))
-        wide = solve(gathered.reshape(rows, cols, 4, LANES))
-        outs = next_iteration(
-            final, wide, field, (low, high, y_a, y_b, c_a, c_b), material,
-            rows if final else rows * cols,
-        )
+        gathered = lax.all_to_all(coarse, "row", 0, 0)
+        wide, c_a, c_b = solve(gathered, low, high)
+        c_a, c_b = swaps(c_a, c_b)
+        outs = next_iteration(final, wide, field, (low, high, y_a, y_b, c_a, c_b), material, rows)
         if final:
             field, coarse, reluct = outs
         else:

time: 103 us -> 97 us (0.942)
  blocking collectives: 30.6 us -> 22.7 us
  starting transfers between devices: 25.8 us -> 30.6 us
  local copies, waits for them, and re-layouts: 4.17 us -> 0.03 us
  waiting for transfers between devices: 7.56 us -> 9.15 us
    all_to_all x2 -> x0, blocking collectives: 23.4 us -> none  [shards(): gathered = lax.all_to_all(coarse, ('row', 'col'), 0, 0)]
    all_to_all x1 -> x3, blocking collectives: 7.11 us -> 22.7 us  [shards(): gathered = lax.all_to_all(coarse, 'row', 0, 0)]
    ppermute x6, starting transfers between devices: 13 us -> 17.8 us  [swaps(): lax.ppermute(turn_a, 'col', pairs[0])]
    unnamed x14 -> x12, local copies, waits for them, and re-layouts: 4.17 us -> 0.03 us
    ppermute x6, waiting for transfers between devices: 3.06 us -> 4.65 us  [swaps(): lax.ppermute(turn_a, 'col', pairs[0])]
    pallas_call x6 -> x4, Pallas kernels: 6.2 us -> 6.17 us  [the longest x2 3.79 us: solve(): pl.pallas_call(solve_kernel, in_specs=[VMEM] * 3, out_specs=[VMEM] * 3, o...]
  transfers between devices with their start and end apart: 18 -> 18, of which waited for: 6 -> 6; matrix products, arithmetic and copies ran while one was open for 0% -> 0% of each run, Pallas kernels for 5% -> 4%
where the time goes in v3:
time: 97 us; the launch traced here: 95.7 us
  Pallas kernels  32.4 us (33%)
  starting transfers between devices  30.6 us (32%)
  blocking collectives  22.7 us (23%)
  waiting for transfers between devices  9.15 us (9%)
    all_to_all x3, blocking collectives, shards(): gathered = lax.all_to_all(coarse, 'row', 0, 0)  22.7 us
    ppermute x6, starting transfers between devices, swaps(): lax.ppermute(turn_a, 'col', pairs[0])  17.8 us
    pallas_call x2, Pallas kernels, next_iteration(): pl.pallas_call(functools.partial(next_kernel, final), in_specs=[VMEM] * 1...  15 us
    pallas_call x1, Pallas kernels, first_iteration(): pl.pallas_call(first_kernel, in_specs=[VMEM] * 10 + [SMEM] * 2, out_specs...  8.47 us
    ppermute x3, starting transfers between devices, rings(): lax.ppermute(to_low, 'row', backward)  7.31 us
    ppermute x6, waiting for transfers between devices, swaps(): lax.ppermute(turn_a, 'col', pairs[0])  4.65 us
    ppermute x6, starting transfers between devices, swaps(): lax.ppermute(turn_b, 'col', pairs[1])  3.95 us
    pallas_call x2, Pallas kernels, solve(): pl.pallas_call(solve_kernel, in_specs=[VMEM] * 3, out_specs=[VMEM] * 3, o...  3.79 us
  transfers between devices with their start and end apart: 18, of which 6 were waited for; matrix products, arithmetic and copies ran while one was open for 0% of the time, Pallas kernels for 4%

profile of v3, /device:TPU:0, one launch (start us, length us, event | category | flops | bytes accessed | tf_op | source)
XLA Modules:
  0.0 95.7 jit_solution(8174436715515377547)
XLA Ops:
  0.6 0.0 copy-start.2
  0.6 0.0 copy-start.3
  0.7 0.0 copy-start.1
  0.7 0.0 copy-start
  0.7 0.0 copy-start.5
  0.7 0.0 copy-start.4
  0.7 2.3 %pack_first.1 = (f32[21,16,256]{2,1,0:T(8,128)S(1)}, f32[21,16,256]{2,1,0:T(8,128)S(1)}, f32[88,4,256]{2,1,0:T(4,128)S(1)}, f32[88,4,256]{2,1,0:T(4,128)S(1)}) custom-call(f32[3,16,16,256]{3,2,1,0:T(8,128)} %potential.3, f32[3,16,16,256]{3,2,1,0:T(8,128)} %source.3, s32[16,16,256]{2,1,0:T(8,128)} %coil_mask.3, s32[16,16,256]{2,1,0:T(8,128)} %labels.3), custom_call_target="tpu_custom_call" | custom-call | tf_op jit(solution)/shard_map/pack_first/pallas_call | solution.py:121
  3.0 0.5 collective-permute-start
  3.5 2.9 %collective-permute-start.1 = (f32[21,16,256]{2,1,0:T(8,128)S(1)}, f32[21,16,256]{2,1,0:T(8,128)S(1)}, u32[]{:S(2)}, u32[]{:S(2)}) collective-permute-start(f32[21,16,256]{2,1,0:T(8,128)S(1)} %get-tuple-element.37), channel_id=1, source_target_pairs={{4,0},{8,4},{12,8},{16,12},{20,16},{24,20},{28,24},{0,28},{5,1},{9... | collective-permute-start | bytes 1032200 | tf_op jit(solution)/shard_map/ppermute | solution.py:817
  6.5 2.3 %collective-permute-start.2 = (f32[88,4,256]{2,1,0:T(4,128)S(1)}, f32[88,4,256]{2,1,0:T(4,128)S(1)}, u32[]{:S(2)}, u32[]{:S(2)}) collective-permute-start(f32[88,4,256]{2,1,0:T(4,128)S(1)} %get-tuple-element.38), channel_id=1, source_target_pairs={{0,1},{1,0},{2,3},{3,2},{4,5},{5,4},{6,7},{7,6},{8,9},{9,8},{10,11... | collective-permute-start | bytes 1081352 | tf_op jit(solution)/shard_map/ppermute | solution.py:828
  8.8 0.7 collective-permute-start.3
  9.4 2.9 %collective-permute-done.low = f32[21,16,256]{2,1,0:T(8,128)S(1)} collective-permute-done((f32[21,16,256]{2,1,0:T(8,128)S(1)}, f32[21,16,256]{2,1,0:T(8,128)S(1)}, u32[]{:S(2)}, u32[]{:S(2)}) %collective-permute-start) | collective-permute-done | bytes 344096 | tf_op jit(solution)/shard_map/ppermute | solution.py:817
  12.4 1.5 %collective-permute-done.1.high = f32[21,16,256]{2,1,0:T(8,128)S(1)} collective-permute-done((f32[21,16,256]{2,1,0:T(8,128)S(1)}, f32[21,16,256]{2,1,0:T(8,128)S(1)}, u32[]{:S(2)}, u32[]{:S(2)}) %collective-permute-start.1) | collective-permute-done | bytes 344096 | tf_op jit(solution)/shard_map/ppermute | solution.py:817
  13.9 0.1 pack_corner.1
  14.0 1.6 %collective-permute-start.4 = (f32[48,256]{1,0:T(8,128)S(1)}, f32[48,256]{1,0:T(8,128)S(1)}, u32[]{:S(2)}, u32[]{:S(2)}) collective-permute-start(f32[48,256]{1,0:T(8,128)S(1)} %get-tuple-element.40), channel_id=1, source_target_pairs={{0,1},{1,0},{2,3},{3,2},{4,5},{5,4},{6,7},{7,6},{8,9},{9,8},{10,11... | collective-permute-start | bytes 147464 | tf_op jit(solution)/shard_map/ppermute | solution.py:828
  15.6 0.7 collective-permute-start.5
  16.3 0.2 collective-permute-done.2.y_a
  16.5 0.0 collective-permute-done.3.y_b
  16.5 1.7 %collective-permute-done.4.c_a = f32[48,256]{1,0:T(8,128)S(1)} collective-permute-done((f32[48,256]{1,0:T(8,128)S(1)}, f32[48,256]{1,0:T(8,128)S(1)}, u32[]{:S(2)}, u32[]{:S(2)}) %collective-permute-start.4) | collective-permute-done | bytes 49184 | tf_op jit(solution)/shard_map/ppermute | solution.py:828
  18.1 0.0 collective-permute-done.5.c_b
  18.1 0.0 copy-done.2
  18.1 0.0 copy-done.3
  18.1 0.0 copy-done.1
  18.1 0.0 copy-done
  18.1 0.0 copy-done.5
  18.2 0.0 copy-done.4
  18.2 8.5 %first_iteration.1 = (f32[3,16,16,256]{3,2,1,0:T(8,128)S(1)}, f32[8,4,128]{2,1,0:T(4,128)S(1)}, f32[12,16,256]{2,1,0:T(8,128)S(1)}, f32[12,16,256]{2,1,0:T(8,128...) custom-call(f32[3,16,16,256]{3,2,1,0:T(8,128)S(1)} %copy-done, ...), custom_call_target="tpu_custom_call" | custom-call | tf_op jit(solution)/shard_map/first_iteration/pallas_call | solution.py:677
  26.6 1.0 %collective-permute-start.6 = (f32[12,16,256]{2,1,0:T(8,128)S(1)}, f32[12,16,256]{2,1,0:T(8,128)S(1)}, u32[]{:S(2)}, u32[]{:S(2)}) collective-permute-start(f32[12,16,256]{2,1,0:T(8,128)S(1)} %get-tuple-element.43), channel_id=1, source_target_pairs={{0,4},{4,8},{8,12},{12,16},{16,20},{20,24},{24,28},{28,0},{1,5},{5... | collective-permute-start | bytes 589832 | tf_op jit(solution)/shard_map/ppermute | solution.py:817
  27.6 1.7 %collective-permute-start.7 = (f32[12,16,256]{2,1,0:T(8,128)S(1)}, f32[12,16,256]{2,1,0:T(8,128)S(1)}, u32[]{:S(2)}, u32[]{:S(2)}) collective-permute-start(f32[12,16,256]{2,1,0:T(8,128)S(1)} %get-tuple-element.44), channel_id=1, source_target_pairs={{4,0},{8,4},{12,8},{16,12},{20,16},{24,20},{28,24},{0,28},{5,1},{9... | collective-permute-start | bytes 589832 | tf_op jit(solution)/shard_map/ppermute | solution.py:817
  29.3 4.6 %collective-permute-start.8 = (f32[48,4,256]{2,1,0:T(4,128)S(1)}, f32[48,4,256]{2,1,0:T(4,128)S(1)}, u32[]{:S(2)}, u32[]{:S(2)}) collective-permute-start(f32[48,4,256]{2,1,0:T(4,128)S(1)} %get-tuple-element.47), channel_id=1, source_target_pairs={{0,1},{1,0},{2,3},{3,2},{4,5},{5,4},{6,7},{7,6},{8,9},{9,8},{10,11... | collective-permute-start | bytes 589832 | tf_op jit(solution)/shard_map/ppermute | solution.py:828
  33.9 0.7 collective-permute-start.9
  34.6 8.4 %all_to_all.15.gathered = f32[8,4,128]{2,1,0:T(4,128)S(1)} all-to-all(f32[8,4,128]{2,1,0:T(4,128)S(1)} %get-tuple-element.42), channel_id=1, replica_groups=mesh['row'=8,'col'=4] {'row'}, dimensions={0} | all-to-all | bytes 32768 | tf_op jit(solution)/shard_map/all_to_all | solution.py:847
  43.0 0.0 collective-permute-done.6.low
  43.0 0.0 collective-permute-done.7.high
  43.0 1.9 %solve.2 = (f32[64,256]{1,0:T(8,128)S(1)}, f32[48,256]{1,0:T(8,128)S(1)}, f32[48,256]{1,0:T(8,128)S(1)}) custom-call(f32[8,4,128]{2,1,0:T(4,128)S(1)} %all_to_all.15.gathered, f32[12,16,256]{2,1,0:T(8,128)S(1)} %collective-permute-done.6.low, f32[12,16,256]{2,1,0:T(8,128)S(1)} %collective-permute-done.7.high), custom_call_target="tpu_custom_call" | custom-call | tf_op jit(solution)/shard_map/solve/pallas_call | solution.py:710
  44.9 3.3 %collective-permute-start.10 = (f32[48,256]{1,0:T(8,128)S(1)}, f32[48,256]{1,0:T(8,128)S(1)}, u32[]{:S(2)}, u32[]{:S(2)}) collective-permute-start(f32[48,256]{1,0:T(8,128)S(1)} %get-tuple-element.49), channel_id=1, source_target_pairs={{0,1},{1,0},{2,3},{3,2},{4,5},{5,4},{6,7},{7,6},{8,9},{9,8},{10,11... | collective-permute-start | bytes 147464 | tf_op jit(solution)/shard_map/ppermute | solution.py:828
  48.3 0.7 collective-permute-start.11
  48.9 0.0 collective-permute-done.8.y_a
  48.9 0.0 collective-permute-done.9.y_b
  48.9 1.4 %collective-permute-done.10.c_a = f32[48,256]{1,0:T(8,128)S(1)} collective-permute-done((f32[48,256]{1,0:T(8,128)S(1)}, f32[48,256]{1,0:T(8,128)S(1)}, u32[]{:S(2)}, u32[]{:S(2)}) %collective-permute-start.10) | collective-permute-done | bytes 49184 | tf_op jit(solution)/shard_map/ppermute | solution.py:828
  50.3 0.0 collective-permute-done.11.c_b
  50.3 7.2 %next_iteration.1 = (f32[3,16,16,256]{3,2,1,0:T(8,128)S(1)}, f32[8,4,128]{2,1,0:T(4,128)S(1)}, f32[12,16,256]{2,1,0:T(8,128)S(1)}, f32[12,16,256]{2,1,0:T(8,128)...) custom-call(f32[64,256]{1,0:T(8,128)S(1)} %get-tuple-element.45.wide, ...), custom_call_target="tpu_custom_call" | custom-call | tf_op jit(solution)/shard_map/next_iteration/pallas_call | solution.py:765
  57.5 0.1 collective-permute-start.12
  57.6 2.6 %collective-permute-start.13 = (f32[12,16,256]{2,1,0:T(8,128)S(1)}, f32[12,16,256]{2,1,0:T(8,128)S(1)}, u32[]{:S(2)}, u32[]{:S(2)}) collective-permute-start(f32[12,16,256]{2,1,0:T(8,128)S(1)} %get-tuple-element.57), channel_id=1, source_target_pairs={{4,0},{8,4},{12,8},{16,12},{20,16},{24,20},{28,24},{0,28},{5,1},{9... | collective-permute-start | bytes 589832 | tf_op jit(solution)/shard_map/ppermute | solution.py:817
  60.2 3.9 %collective-permute-start.14 = (f32[48,4,256]{2,1,0:T(4,128)S(1)}, f32[48,4,256]{2,1,0:T(4,128)S(1)}, u32[]{:S(2)}, u32[]{:S(2)}) collective-permute-start(f32[48,4,256]{2,1,0:T(4,128)S(1)} %get-tuple-element.60), channel_id=1, source_target_pairs={{0,1},{1,0},{2,3},{3,2},{4,5},{5,4},{6,7},{7,6},{8,9},{9,8},{10,11... | collective-permute-start | bytes 589832 | tf_op jit(solution)/shard_map/ppermute | solution.py:828
  64.1 0.7 collective-permute-start.15
  64.8 7.1 %all_to_all.16.gathered = f32[8,4,128]{2,1,0:T(4,128)S(1)} all-to-all(f32[8,4,128]{2,1,0:T(4,128)S(1)} %get-tuple-element.55), channel_id=1, replica_groups=mesh['row'=8,'col'=4] {'row'}, dimensions={0} | all-to-all | bytes 32768 | tf_op jit(solution)/shard_map/all_to_all | solution.py:847
  71.9 0.0 collective-permute-done.12.low
  71.9 0.0 collective-permute-done.13.high
  71.9 1.9 %solve.3 = (f32[64,256]{1,0:T(8,128)S(1)}, f32[48,256]{1,0:T(8,128)S(1)}, f32[48,256]{1,0:T(8,128)S(1)}) custom-call(f32[8,4,128]{2,1,0:T(4,128)S(1)} %all_to_all.16.gathered, f32[12,16,256]{2,1,0:T(8,128)S(1)} %collective-permute-done.12.low, f32[12,16,256]{2,1,0:T(8,128)S(1)} %collective-permute-done.13.high), custom_call_target="tpu_custom_call" | custom-call | tf_op jit(solution)/shard_map/solve/pallas_call | solution.py:710
  73.8 2.1 %collective-permute-start.16 = (f32[48,256]{1,0:T(8,128)S(1)}, f32[48,256]{1,0:T(8,128)S(1)}, u32[]{:S(2)}, u32[]{:S(2)}) collective-permute-start(f32[48,256]{1,0:T(8,128)S(1)} %get-tuple-element.62), channel_id=1, source_target_pairs={{0,1},{1,0},{2,3},{3,2},{4,5},{5,4},{6,7},{7,6},{8,9},{9,8},{10,11... | collective-permute-start | bytes 147464 | tf_op jit(solution)/shard_map/ppermute | solution.py:828
  75.9 0.7 collective-permute-start.17
  76.6 0.0 collective-permute-done.14.y_a
  76.6 0.0 collective-permute-done.15.y_b
  76.6 1.4 %collective-permute-done.16.c_a = f32[48,256]{1,0:T(8,128)S(1)} collective-permute-done((f32[48,256]{1,0:T(8,128)S(1)}, f32[48,256]{1,0:T(8,128)S(1)}, u32[]{:S(2)}, u32[]{:S(2)}) %collective-permute-start.16) | collective-permute-done | bytes 49184 | tf_op jit(solution)/shard_map/ppermute | solution.py:828
  78.0 0.0 collective-permute-done.17.c_b
  78.0 7.8 %last_iteration.1 = (f32[3,16,16,256]{3,2,1,0:T(8,128)S(1)}, f32[8,4,128]{2,1,0:T(4,128)S(1)}, f32[16,16,256]{2,1,0:T(8,128)}) custom-call(f32[64,256]{1,0:T(8,128)S(1)} %get-tuple-element.58.wide, f32[3,16,16,256]{3,2,1,0:T(8,128)S(1)} %get-tuple-element.59.core, f32[12,16,256]{2,1,0:T(8,128)S(1)} %collective-permute-done.12.low, ...), custom_call_target="tpu_custom_call" | custom-call | tf_op jit(solution)/shard_map/last_iteration/pallas_call | solution.py:765
  85.8 7.1 %all_to_all.17.gathered = f32[8,4,128]{2,1,0:T(4,128)S(1)} all-to-all(f32[8,4,128]{2,1,0:T(4,128)S(1)} %get-tuple-element.64), channel_id=1, replica_groups=mesh['row'=8,'col'=4] {'row'}, dimensions={0} | all-to-all | bytes 32768 | tf_op jit(solution)/shard_map/all_to_all | solution.py:855
  92.9 2.8 %correct.1 = (f32[3,16,16,256]{3,2,1,0:T(8,128)}, f32[3,16,2,32]{3,2,1,0:T(2,128)}) custom-call(f32[8,4,128]{2,1,0:T(4,128)S(1)} %all_to_all.17.gathered, f32[3,16,16,256]{3,2,1,0:T(8,128)S(1)} %get-tuple-element.65.core), custom_call_target="tpu_custom_call" | custom-call | tf_op jit(solution)/shard_map/correct/pallas_call | solution.py:802
Async XLA Ops:
  0.6 17.5 %copy-start.2 = (s32[16,16,256]{2,1,0:T(8,128)S(1)}, s32[16,16,256]{2,1,0:T(8,128)}, u32[]{:S(2)}) copy-start(s32[16,16,256]{2,1,0:T(8,128)} %coil_mask.3) | copy-start | bytes 786436
  0.6 17.5 %copy-start.3 = (s32[16,16,256]{2,1,0:T(8,128)S(1)}, s32[16,16,256]{2,1,0:T(8,128)}, u32[]{:S(2)}) copy-start(s32[16,16,256]{2,1,0:T(8,128)} %labels.3) | copy-start | bytes 786436
  0.7 17.5 %copy-start.1 = (f32[3,16,16,256]{3,2,1,0:T(8,128)S(1)}, f32[3,16,16,256]{3,2,1,0:T(8,128)}, u32[]{:S(2)}) copy-start(f32[3,16,16,256]{3,2,1,0:T(8,128)} %source.3) | copy-start | bytes 2359300
  0.7 17.5 %copy-start = (f32[3,16,16,256]{3,2,1,0:T(8,128)S(1)}, f32[3,16,16,256]{3,2,1,0:T(8,128)}, u32[]{:S(2)}) copy-start(f32[3,16,16,256]{3,2,1,0:T(8,128)} %potential.3) | copy-start | bytes 2359300
  0.7 17.5 %copy-start.5 = (f32[8]{0:T(128)S(1)}, f32[8]{0:T(128)}, u32[]{:S(2)}) copy-start(f32[8]{0:T(128)} %rise_table.1) | copy-start | bytes 100
  0.7 17.5 %copy-start.4 = (f32[8]{0:T(128)S(1)}, f32[8]{0:T(128)}, u32[]{:S(2)}) copy-start(f32[8]{0:T(128)} %floor_table.1) | copy-start | bytes 100
  3.0 9.3 %collective-permute-start = (f32[21,16,256]{2,1,0:T(8,128)S(1)}, f32[21,16,256]{2,1,0:T(8,128)S(1)}, u32[]{:S(2)}, u32[]{:S(2)}) collective-permute-start(f32[21,16,256]{2,1,0:T(8,128)S(1)} %get-tuple-element.36), channel_id=1, source_target_pairs={{0,4},{4,8},{8,12},{12,16},{16,20},{20,24},{24,28},{28,0},{1,5},{5... | collective-permute-start | bytes 1032200 | tf_op jit(solution)/shard_map/ppermute | solution.py:817
  3.5 10.4 %collective-permute-start.1 = (f32[21,16,256]{2,1,0:T(8,128)S(1)}, f32[21,16,256]{2,1,0:T(8,128)S(1)}, u32[]{:S(2)}, u32[]{:S(2)}) collective-permute-start(f32[21,16,256]{2,1,0:T(8,128)S(1)} %get-tuple-element.37), channel_id=1, source_target_pairs={{4,0},{8,4},{12,8},{16,12},{20,16},{24,20},{28,24},{0,28},{5,1},{9... | collective-permute-start | bytes 1032200 | tf_op jit(solution)/shard_map/ppermute | solution.py:817
  6.5 10.0 %collective-permute-start.2 = (f32[88,4,256]{2,1,0:T(4,128)S(1)}, f32[88,4,256]{2,1,0:T(4,128)S(1)}, u32[]{:S(2)}, u32[]{:S(2)}) collective-permute-start(f32[88,4,256]{2,1,0:T(4,128)S(1)} %get-tuple-element.38), channel_id=1, source_target_pairs={{0,1},{1,0},{2,3},{3,2},{4,5},{5,4},{6,7},{7,6},{8,9},{9,8},{10,11... | collective-permute-start | bytes 1081352 | tf_op jit(solution)/shard_map/ppermute | solution.py:828
  8.8 7.7 %collective-permute-start.3 = (f32[88,4,256]{2,1,0:T(4,128)S(1)}, f32[88,4,256]{2,1,0:T(4,128)S(1)}, u32[]{:S(2)}, u32[]{:S(2)}) collective-permute-start(f32[88,4,256]{2,1,0:T(4,128)S(1)} %get-tuple-element.39), channel_id=1, source_target_pairs={{0,0},{1,2},{2,1},{3,3},{4,4},{5,6},{6,5},{7,7},{8,8},{9,10},{10,9... | collective-permute-start | bytes 1081352 | tf_op jit(solution)/shard_map/ppermute | solution.py:828
  14.0 4.2 %collective-permute-start.4 = (f32[48,256]{1,0:T(8,128)S(1)}, f32[48,256]{1,0:T(8,128)S(1)}, u32[]{:S(2)}, u32[]{:S(2)}) collective-permute-start(f32[48,256]{1,0:T(8,128)S(1)} %get-tuple-element.40), channel_id=1, source_target_pairs={{0,1},{1,0},{2,3},{3,2},{4,5},{5,4},{6,7},{7,6},{8,9},{9,8},{10,11... | collective-permute-start | bytes 147464 | tf_op jit(solution)/shard_map/ppermute | solution.py:828
  15.6 2.5 %collective-permute-start.5 = (f32[48,256]{1,0:T(8,128)S(1)}, f32[48,256]{1,0:T(8,128)S(1)}, u32[]{:S(2)}, u32[]{:S(2)}) collective-permute-start(f32[48,256]{1,0:T(8,128)S(1)} %get-tuple-element.41), channel_id=1, source_target_pairs={{0,0},{1,2},{2,1},{3,3},{4,4},{5,6},{6,5},{7,7},{8,8},{9,10},{10,9... | collective-permute-start | bytes 147464 | tf_op jit(solution)/shard_map/ppermute | solution.py:828
  26.6 16.4 %collective-permute-start.6 = (f32[12,16,256]{2,1,0:T(8,128)S(1)}, f32[12,16,256]{2,1,0:T(8,128)S(1)}, u32[]{:S(2)}, u32[]{:S(2)}) collective-permute-start(f32[12,16,256]{2,1,0:T(8,128)S(1)} %get-tuple-element.43), channel_id=1, source_target_pairs={{0,4},{4,8},{8,12},{12,16},{16,20},{20,24},{24,28},{28,0},{1,5},{5... | collective-permute-start | bytes 589832 | tf_op jit(solution)/shard_map/ppermute | solution.py:817
  27.6 15.4 %collective-permute-start.7 = (f32[12,16,256]{2,1,0:T(8,128)S(1)}, f32[12,16,256]{2,1,0:T(8,128)S(1)}, u32[]{:S(2)}, u32[]{:S(2)}) collective-permute-start(f32[12,16,256]{2,1,0:T(8,128)S(1)} %get-tuple-element.44), channel_id=1, source_target_pairs={{4,0},{8,4},{12,8},{16,12},{20,16},{24,20},{28,24},{0,28},{5,1},{9... | collective-permute-start | bytes 589832 | tf_op jit(solution)/shard_map/ppermute | solution.py:817
  29.3 19.6 %collective-permute-start.8 = (f32[48,4,256]{2,1,0:T(4,128)S(1)}, f32[48,4,256]{2,1,0:T(4,128)S(1)}, u32[]{:S(2)}, u32[]{:S(2)}) collective-permute-start(f32[48,4,256]{2,1,0:T(4,128)S(1)} %get-tuple-element.47), channel_id=1, source_target_pairs={{0,1},{1,0},{2,3},{3,2},{4,5},{5,4},{6,7},{7,6},{8,9},{9,8},{10,11... | collective-permute-start | bytes 589832 | tf_op jit(solution)/shard_map/ppermute | solution.py:828
  33.9 15.0 %collective-permute-start.9 = (f32[48,4,256]{2,1,0:T(4,128)S(1)}, f32[48,4,256]{2,1,0:T(4,128)S(1)}, u32[]{:S(2)}, u32[]{:S(2)}) collective-permute-start(f32[48,4,256]{2,1,0:T(4,128)S(1)} %get-tuple-element.48), channel_id=1, source_target_pairs={{0,0},{1,2},{2,1},{3,3},{4,4},{5,6},{6,5},{7,7},{8,8},{9,10},{10,9... | collective-permute-start | bytes 589832 | tf_op jit(solution)/shard_map/ppermute | solution.py:828
  44.9 5.4 %collective-permute-start.10 = (f32[48,256]{1,0:T(8,128)S(1)}, f32[48,256]{1,0:T(8,128)S(1)}, u32[]{:S(2)}, u32[]{:S(2)}) collective-permute-start(f32[48,256]{1,0:T(8,128)S(1)} %get-tuple-element.49), channel_id=1, source_target_pairs={{0,1},{1,0},{2,3},{3,2},{4,5},{5,4},{6,7},{7,6},{8,9},{9,8},{10,11... | collective-permute-start | bytes 147464 | tf_op jit(solution)/shard_map/ppermute | solution.py:828
  48.3 2.1 %collective-permute-start.11 = (f32[48,256]{1,0:T(8,128)S(1)}, f32[48,256]{1,0:T(8,128)S(1)}, u32[]{:S(2)}, u32[]{:S(2)}) collective-permute-start(f32[48,256]{1,0:T(8,128)S(1)} %get-tuple-element.50), channel_id=1, source_target_pairs={{0,0},{1,2},{2,1},{3,3},{4,4},{5,6},{6,5},{7,7},{8,8},{9,10},{10,9... | collective-permute-start | bytes 147464 | tf_op jit(solution)/shard_map/ppermute | solution.py:828
  57.5 14.4 %collective-permute-start.12 = (f32[12,16,256]{2,1,0:T(8,128)S(1)}, f32[12,16,256]{2,1,0:T(8,128)S(1)}, u32[]{:S(2)}, u32[]{:S(2)}) collective-permute-start(f32[12,16,256]{2,1,0:T(8,128)S(1)} %get-tuple-element.56), channel_id=1, source_target_pairs={{0,4},{4,8},{8,12},{12,16},{16,20},{20,24},{24,28},{28,0},{1,5},{5... | collective-permute-start | bytes 589832 | tf_op jit(solution)/shard_map/ppermute | solution.py:817
  57.6 14.3 %collective-permute-start.13 = (f32[12,16,256]{2,1,0:T(8,128)S(1)}, f32[12,16,256]{2,1,0:T(8,128)S(1)}, u32[]{:S(2)}, u32[]{:S(2)}) collective-permute-start(f32[12,16,256]{2,1,0:T(8,128)S(1)} %get-tuple-element.57), channel_id=1, source_target_pairs={{4,0},{8,4},{12,8},{16,12},{20,16},{24,20},{28,24},{0,28},{5,1},{9... | collective-permute-start | bytes 589832 | tf_op jit(solution)/shard_map/ppermute | solution.py:817
  60.2 16.3 %collective-permute-start.14 = (f32[48,4,256]{2,1,0:T(4,128)S(1)}, f32[48,4,256]{2,1,0:T(4,128)S(1)}, u32[]{:S(2)}, u32[]{:S(2)}) collective-permute-start(f32[48,4,256]{2,1,0:T(4,128)S(1)} %get-tuple-element.60), channel_id=1, source_target_pairs={{0,1},{1,0},{2,3},{3,2},{4,5},{5,4},{6,7},{7,6},{8,9},{9,8},{10,11... | collective-permute-start | bytes 589832 | tf_op jit(solution)/shard_map/ppermute | solution.py:828
  64.1 12.4 %collective-permute-start.15 = (f32[48,4,256]{2,1,0:T(4,128)S(1)}, f32[48,4,256]{2,1,0:T(4,128)S(1)}, u32[]{:S(2)}, u32[]{:S(2)}) collective-permute-start(f32[48,4,256]{2,1,0:T(4,128)S(1)} %get-tuple-element.61), channel_id=1, source_target_pairs={{0,0},{1,2},{2,1},{3,3},{4,4},{5,6},{6,5},{7,7},{8,8},{9,10},{10,9... | collective-permute-start | bytes 589832 | tf_op jit(solution)/shard_map/ppermute | solution.py:828
  73.8 4.2 %collective-permute-start.16 = (f32[48,256]{1,0:T(8,128)S(1)}, f32[48,256]{1,0:T(8,128)S(1)}, u32[]{:S(2)}, u32[]{:S(2)}) collective-permute-start(f32[48,256]{1,0:T(8,128)S(1)} %get-tuple-element.62), channel_id=1, source_target_pairs={{0,1},{1,0},{2,3},{3,2},{4,5},{5,4},{6,7},{7,6},{8,9},{9,8},{10,11... | collective-permute-start | bytes 147464 | tf_op jit(solution)/shard_map/ppermute | solution.py:828
  75.9 2.1 %collective-permute-start.17 = (f32[48,256]{1,0:T(8,128)S(1)}, f32[48,256]{1,0:T(8,128)S(1)}, u32[]{:S(2)}, u32[]{:S(2)}) collective-permute-start(f32[48,256]{1,0:T(8,128)S(1)} %get-tuple-element.63), channel_id=1, source_target_pairs={{0,0},{1,2},{2,1},{3,3},{4,4},{5,6},{6,5},{7,7},{8,8},{9,10},{10,9... | collective-permute-start | bytes 147464 | tf_op jit(solution)/shard_map/ppermute | solution.py:828

commit v4 on v3

--- a/solution.py
+++ b/solution.py
@@ -196,8 +196,9 @@
     def near(v):
         return pltpu.roll(v, 64, 1)
 
-    def far(swapped):
-        return jnp.where(first_x, pltpu.roll(swapped, 1, 0), pltpu.roll(swapped, count - 1, 0))
+    def far(swapped, turned=False):
+        below, above = pltpu.roll(swapped, 1, 0), pltpu.roll(swapped, count - 1, 0)
+        return jnp.where(first_x, above, below) if turned else jnp.where(first_x, below, above)
 
     sets = []
     for r in relucts:
@@ -213,34 +214,42 @@
         c_far = jnp.where(far_ok, c_far, 0.0)
         sets.append((c_up, c_down, c_side, c_near, c_far, diag, RELAX / diag))
 
-    def neighbours(coeffs, v):
+    def neighbours(coeffs, v, swapped, turned=False):
         c_up, c_down, c_side, c_near, c_far = coeffs[:5]
-        swapped = near(v)
         return (
             (c_up * up(v) + c_down * down(v)) + (c_side * side(v) + c_near * swapped)
-        ) + c_far * far(swapped)
-
-    doubled = [[2.0 * t for t in stripe] for stripe in targets]
-    start = [
-        [coeffs[6] * t for t in stripe] for coeffs, stripe in zip(sets, doubled)
-    ]
-
-    def sweep(step, values):
-        return [
-            [
-                (1.0 - RELAX) * v + coeffs[6] * (t + neighbours(coeffs, v))
-                for v, t in zip(stripe, stripe_t)
-            ]
-            for coeffs, stripe, stripe_t in zip(sets, values, doubled)
-        ]
-
-    values = lax.fori_loop(0, COARSE_SWEEPS - 1, sweep, start)
+        ) + c_far * far(swapped, turned)
+
     out = []
-    for coeffs, stripe, stripe_t in zip(sets, values, doubled):
+    for coeffs, stripe in zip(sets, targets):
+        turned = [near(c) for c in coeffs]
+        doubled = [2.0 * t for t in stripe]
+        swapped_t = [near(t) for t in doubled]
+        start = (
+            tuple(coeffs[6] * t for t in doubled), tuple(turned[6] * t for t in swapped_t),
+        )
+
+        def sweep(values):
+            plain, swapped = values
+            return (
+                tuple(
+                    (1.0 - RELAX) * v + coeffs[6] * (t + neighbours(coeffs, v, s))
+                    for v, s, t in zip(plain, swapped, doubled)
+                ),
+                tuple(
+                    (1.0 - RELAX) * s + turned[6] * (t + neighbours(turned, s, v, True))
+                    for v, s, t in zip(plain, swapped, swapped_t)
+                ),
+            )
+
+        values = start
+        for step in range(COARSE_SWEEPS - 1):
+            values = sweep(values)
+        plain, swapped = values
         total = jnp.sum(jnp.sum(coeffs[5], axis=1, keepdims=True), axis=0, keepdims=True)
         done = []
-        for v, t in zip(stripe, stripe_t):
-            left = t - (coeffs[5] * v - neighbours(coeffs, v))
+        for v, s, t in zip(plain, swapped, doubled):
+            left = t - (coeffs[5] * v - neighbours(coeffs, v, s))
             left = jnp.sum(jnp.sum(left, axis=1, keepdims=True), axis=0, keepdims=True)
             done.append(v + left / total)
         out.append(done)
@@ -385,7 +394,7 @@
             row = CORNER_TABLE + first
             put_corner(put_label, message, place, (row, row + LABEL_ROWS), distance, count)
 
-    def look_up(x, carry):
+    for x in range(1, EXT - 1):
         for half in range(2):
             label = floor[half, x]
             floor_cell = jnp.zeros_like(label)
@@ -396,9 +405,6 @@
                 rise_cell = jnp.where(chosen, rise_table[number], rise_cell)
             floor[half, x] = floor_cell
             rise[half, x] = rise_cell
-        return carry
-
-    lax.fori_loop(1, EXT - 1, look_up, 0)
 
 
 def right_of(low, high, last):
@@ -411,14 +417,10 @@
     return a, jnp.where(first, a, b)
 
 
-def in_pairs(begin, end, plane):
-    def step(number, carry):
-        x = begin + 2 * number
-        for ref, value in plane(x) + plane(x + 1):
+def each(begin, end, plane):
+    for x in range(begin, end):
+        for ref, value in plane(x):
             ref[...] = value
-        return carry
-
-    lax.fori_loop(0, (end - begin) // 2, step, 0)
 
 
 def fine_iteration(
@@ -454,7 +456,7 @@
             ))
         return stores
 
-    in_pairs(1, EXT - 1, reluct_plane)
+    each(1, EXT - 1, reluct_plane)
 
     def apply(src, x, rows, coeffs, first_lane, last_lane):
         rows_plus = slice(rows.start + 1, rows.stop + 1)
@@ -514,7 +516,7 @@
             ))
         return stores
 
-    in_pairs(2, EXT - 2, first_plane)
+    each(2, EXT - 2, first_plane)
 
     def second_plane(x):
         stores = []
@@ -526,7 +528,7 @@
             ))
         return stores
 
-    in_pairs(3, EXT - 3, second_plane)
+    each(3, EXT - 3, second_plane)
 
     own = slice(CORE, CORE + BLOCK)
     ends = pl.ds(CORE - 1, 3, stride=COARSEN)
@@ -556,8 +558,7 @@
         for k in range(3)
     ]
     for coarse in range(2):
-        def plane(step, totals):
-            x = HALO + coarse * COARSEN + step
+        def plane(x, totals):
             across, rim, along, material = totals
             relucts = [reluct[half, x, own] for half in range(2)]
             ups = [c_up[half, x, own] for half in range(2)]
@@ -579,9 +580,10 @@
                 tuple(material[half] + relucts[half] for half in range(2)),
             )
 
-        across, rim, along, material = lax.fori_loop(
-            0, COARSEN, plane, ((zero,) * 6, (zero,) * 6, (thin,) * 6, (zero,) * 2)
-        )
+        totals = ((zero,) * 6, (zero,) * 6, (thin,) * 6, (zero,) * 2)
+        for step in range(COARSEN):
+            totals = plane(HALO + coarse * COARSEN + step, totals)
+        across, rim, along, material = totals
         for half in range(2):
             z = slice(half * LANES, (half + 1) * LANES)
             means = blocks(material[half])

time: 97 us -> 86.8 us (0.89)
  Pallas kernels: 32.4 us -> 22.3 us
    pallas_call x2, Pallas kernels: 15 us -> 8.23 us  [next_iteration(): pl.pallas_call(functools.partial(next_kernel, final), in_specs=[VMEM] * 1...]
    pallas_call x1, Pallas kernels: 8.47 us -> 5.54 us  [first_iteration(): pl.pallas_call(first_kernel, in_specs=[VMEM] * 10 + [SMEM] * 2, out_specs...]
where the time goes in v4:
time: 86.8 us; the launch traced here: 85.5 us
  starting transfers between devices  30.7 us (35%)
  blocking collectives  22.7 us (26%)
  Pallas kernels  22.3 us (26%)
  waiting for transfers between devices  8.97 us (10%)
    all_to_all x3, blocking collectives, shards(): gathered = lax.all_to_all(coarse, 'row', 0, 0)  22.7 us
    ppermute x6, starting transfers between devices, swaps(): lax.ppermute(turn_a, 'col', pairs[0])  17.8 us
    pallas_call x2, Pallas kernels, next_iteration(): pl.pallas_call(functools.partial(next_kernel, final), in_specs=[VMEM] * 1...  8.23 us
    ppermute x3, starting transfers between devices, rings(): lax.ppermute(to_low, 'row', backward)  7.32 us
    pallas_call x1, Pallas kernels, first_iteration(): pl.pallas_call(first_kernel, in_specs=[VMEM] * 10 + [SMEM] * 2, out_specs...  5.54 us
    ppermute x6, waiting for transfers between devices, swaps(): lax.ppermute(turn_a, 'col', pairs[0])  4.47 us
    ppermute x6, starting transfers between devices, swaps(): lax.ppermute(turn_b, 'col', pairs[1])  4.13 us
    pallas_call x2, Pallas kernels, solve(): pl.pallas_call(solve_kernel, in_specs=[VMEM] * 3, out_specs=[VMEM] * 3, o...  3.49 us
  transfers between devices with their start and end apart: 18, of which 6 were waited for; matrix products, arithmetic and copies ran while one was open for 0% of the time, Pallas kernels for 4%

profile of v4, /device:TPU:0, one launch (start us, length us, event | category | flops | bytes accessed | tf_op | source)
XLA Modules:
  0.0 85.5 jit_solution(8039776755520760826)
XLA Ops:
  0.6 0.0 copy-start.2
  0.6 0.0 copy-start.3
  0.7 0.0 copy-start.1
  0.7 0.0 copy-start
  0.7 0.0 copy-start.5
  0.7 0.0 copy-start.4
  0.7 2.3 %pack_first.1 = (f32[21,16,256]{2,1,0:T(8,128)S(1)}, f32[21,16,256]{2,1,0:T(8,128)S(1)}, f32[88,4,256]{2,1,0:T(4,128)S(1)}, f32[88,4,256]{2,1,0:T(4,128)S(1)}) custom-call(f32[3,16,16,256]{3,2,1,0:T(8,128)} %potential.3, f32[3,16,16,256]{3,2,1,0:T(8,128)} %source.3, s32[16,16,256]{2,1,0:T(8,128)} %coil_mask.3, s32[16,16,256]{2,1,0:T(8,128)} %labels.3), custom_call_target="tpu_custom_call" | custom-call | tf_op jit(solution)/shard_map/pack_first/pallas_call | solution.py:121
  3.0 0.5 collective-permute-start
  3.5 2.9 %collective-permute-start.1 = (f32[21,16,256]{2,1,0:T(8,128)S(1)}, f32[21,16,256]{2,1,0:T(8,128)S(1)}, u32[]{:S(2)}, u32[]{:S(2)}) collective-permute-start(f32[21,16,256]{2,1,0:T(8,128)S(1)} %get-tuple-element.37), channel_id=1, source_target_pairs={{4,0},{8,4},{12,8},{16,12},{20,16},{24,20},{28,24},{0,28},{5,1},{9... | collective-permute-start | bytes 1032200 | tf_op jit(solution)/shard_map/ppermute | solution.py:819
  6.5 2.3 %collective-permute-start.2 = (f32[88,4,256]{2,1,0:T(4,128)S(1)}, f32[88,4,256]{2,1,0:T(4,128)S(1)}, u32[]{:S(2)}, u32[]{:S(2)}) collective-permute-start(f32[88,4,256]{2,1,0:T(4,128)S(1)} %get-tuple-element.38), channel_id=1, source_target_pairs={{0,1},{1,0},{2,3},{3,2},{4,5},{5,4},{6,7},{7,6},{8,9},{9,8},{10,11... | collective-permute-start | bytes 1081352 | tf_op jit(solution)/shard_map/ppermute | solution.py:830
  8.8 0.7 collective-permute-start.3
  9.4 2.9 %collective-permute-done.low = f32[21,16,256]{2,1,0:T(8,128)S(1)} collective-permute-done((f32[21,16,256]{2,1,0:T(8,128)S(1)}, f32[21,16,256]{2,1,0:T(8,128)S(1)}, u32[]{:S(2)}, u32[]{:S(2)}) %collective-permute-start) | collective-permute-done | bytes 344096 | tf_op jit(solution)/shard_map/ppermute | solution.py:819
  12.4 1.5 %collective-permute-done.1.high = f32[21,16,256]{2,1,0:T(8,128)S(1)} collective-permute-done((f32[21,16,256]{2,1,0:T(8,128)S(1)}, f32[21,16,256]{2,1,0:T(8,128)S(1)}, u32[]{:S(2)}, u32[]{:S(2)}) %collective-permute-start.1) | collective-permute-done | bytes 344096 | tf_op jit(solution)/shard_map/ppermute | solution.py:819
  13.9 0.1 pack_corner.1
  14.0 1.6 %collective-permute-start.4 = (f32[48,256]{1,0:T(8,128)S(1)}, f32[48,256]{1,0:T(8,128)S(1)}, u32[]{:S(2)}, u32[]{:S(2)}) collective-permute-start(f32[48,256]{1,0:T(8,128)S(1)} %get-tuple-element.40), channel_id=1, source_target_pairs={{0,1},{1,0},{2,3},{3,2},{4,5},{5,4},{6,7},{7,6},{8,9},{9,8},{10,11... | collective-permute-start | bytes 147464 | tf_op jit(solution)/shard_map/ppermute | solution.py:830
  15.6 0.7 collective-permute-start.5
  16.3 0.2 collective-permute-done.2.y_a
  16.5 0.0 collective-permute-done.3.y_b
  16.5 1.7 %collective-permute-done.4.c_a = f32[48,256]{1,0:T(8,128)S(1)} collective-permute-done((f32[48,256]{1,0:T(8,128)S(1)}, f32[48,256]{1,0:T(8,128)S(1)}, u32[]{:S(2)}, u32[]{:S(2)}) %collective-permute-start.4) | collective-permute-done | bytes 49184 | tf_op jit(solution)/shard_map/ppermute | solution.py:830
  18.1 0.0 collective-permute-done.5.c_b
  18.1 0.0 copy-done.2
  18.1 0.0 copy-done.3
  18.1 0.0 copy-done.1
  18.1 0.0 copy-done
  18.1 0.0 copy-done.5
  18.2 0.0 copy-done.4
  18.2 5.5 %first_iteration.1 = (f32[3,16,16,256]{3,2,1,0:T(8,128)S(1)}, f32[8,4,128]{2,1,0:T(4,128)S(1)}, f32[12,16,256]{2,1,0:T(8,128)S(1)}, f32[12,16,256]{2,1,0:T(8,128...) custom-call(f32[3,16,16,256]{3,2,1,0:T(8,128)S(1)} %copy-done, ...), custom_call_target="tpu_custom_call" | custom-call | tf_op jit(solution)/shard_map/first_iteration/pallas_call | solution.py:679
  23.7 0.9 %collective-permute-start.6 = (f32[12,16,256]{2,1,0:T(8,128)S(1)}, f32[12,16,256]{2,1,0:T(8,128)S(1)}, u32[]{:S(2)}, u32[]{:S(2)}) collective-permute-start(f32[12,16,256]{2,1,0:T(8,128)S(1)} %get-tuple-element.43), channel_id=1, source_target_pairs={{0,4},{4,8},{8,12},{12,16},{16,20},{20,24},{24,28},{28,0},{1,5},{5... | collective-permute-start | bytes 589832 | tf_op jit(solution)/shard_map/ppermute | solution.py:819
  24.6 1.7 %collective-permute-start.7 = (f32[12,16,256]{2,1,0:T(8,128)S(1)}, f32[12,16,256]{2,1,0:T(8,128)S(1)}, u32[]{:S(2)}, u32[]{:S(2)}) collective-permute-start(f32[12,16,256]{2,1,0:T(8,128)S(1)} %get-tuple-element.44), channel_id=1, source_target_pairs={{4,0},{8,4},{12,8},{16,12},{20,16},{24,20},{28,24},{0,28},{5,1},{9... | collective-permute-start | bytes 589832 | tf_op jit(solution)/shard_map/ppermute | solution.py:819
  26.4 4.6 %collective-permute-start.8 = (f32[48,4,256]{2,1,0:T(4,128)S(1)}, f32[48,4,256]{2,1,0:T(4,128)S(1)}, u32[]{:S(2)}, u32[]{:S(2)}) collective-permute-start(f32[48,4,256]{2,1,0:T(4,128)S(1)} %get-tuple-element.47), channel_id=1, source_target_pairs={{0,1},{1,0},{2,3},{3,2},{4,5},{5,4},{6,7},{7,6},{8,9},{9,8},{10,11... | collective-permute-start | bytes 589832 | tf_op jit(solution)/shard_map/ppermute | solution.py:830
  30.9 0.7 collective-permute-start.9
  31.6 8.4 %all_to_all.15.gathered = f32[8,4,128]{2,1,0:T(4,128)S(1)} all-to-all(f32[8,4,128]{2,1,0:T(4,128)S(1)} %get-tuple-element.42), channel_id=1, replica_groups=mesh['row'=8,'col'=4] {'row'}, dimensions={0} | all-to-all | bytes 32768 | tf_op jit(solution)/shard_map/all_to_all | solution.py:849
  40.1 0.0 collective-permute-done.6.low
  40.1 0.0 collective-permute-done.7.high
  40.1 1.7 %solve.2 = (f32[64,256]{1,0:T(8,128)S(1)}, f32[48,256]{1,0:T(8,128)S(1)}, f32[48,256]{1,0:T(8,128)S(1)}) custom-call(f32[8,4,128]{2,1,0:T(4,128)S(1)} %all_to_all.15.gathered, f32[12,16,256]{2,1,0:T(8,128)S(1)} %collective-permute-done.6.low, f32[12,16,256]{2,1,0:T(8,128)S(1)} %collective-permute-done.7.high), custom_call_target="tpu_custom_call" | custom-call | tf_op jit(solution)/shard_map/solve/pallas_call | solution.py:712
  41.8 3.3 %collective-permute-start.10 = (f32[48,256]{1,0:T(8,128)S(1)}, f32[48,256]{1,0:T(8,128)S(1)}, u32[]{:S(2)}, u32[]{:S(2)}) collective-permute-start(f32[48,256]{1,0:T(8,128)S(1)} %get-tuple-element.49), channel_id=1, source_target_pairs={{0,1},{1,0},{2,3},{3,2},{4,5},{5,4},{6,7},{7,6},{8,9},{9,8},{10,11... | collective-permute-start | bytes 147464 | tf_op jit(solution)/shard_map/ppermute | solution.py:830
  45.1 0.7 collective-permute-start.11
  45.8 0.0 collective-permute-done.8.y_a
  45.8 0.0 collective-permute-done.9.y_b
  45.8 1.4 %collective-permute-done.10.c_a = f32[48,256]{1,0:T(8,128)S(1)} collective-permute-done((f32[48,256]{1,0:T(8,128)S(1)}, f32[48,256]{1,0:T(8,128)S(1)}, u32[]{:S(2)}, u32[]{:S(2)}) %collective-permute-start.10) | collective-permute-done | bytes 49184 | tf_op jit(solution)/shard_map/ppermute | solution.py:830
  47.2 0.0 collective-permute-done.11.c_b
  47.2 4.0 %next_iteration.1 = (f32[3,16,16,256]{3,2,1,0:T(8,128)S(1)}, f32[8,4,128]{2,1,0:T(4,128)S(1)}, f32[12,16,256]{2,1,0:T(8,128)S(1)}, f32[12,16,256]{2,1,0:T(8,128)...) custom-call(f32[64,256]{1,0:T(8,128)S(1)} %get-tuple-element.45.wide, ...), custom_call_target="tpu_custom_call" | custom-call | tf_op jit(solution)/shard_map/next_iteration/pallas_call | solution.py:767
  51.2 0.0 collective-permute-start.12
  51.2 2.6 %collective-permute-start.13 = (f32[12,16,256]{2,1,0:T(8,128)S(1)}, f32[12,16,256]{2,1,0:T(8,128)S(1)}, u32[]{:S(2)}, u32[]{:S(2)}) collective-permute-start(f32[12,16,256]{2,1,0:T(8,128)S(1)} %get-tuple-element.57), channel_id=1, source_target_pairs={{4,0},{8,4},{12,8},{16,12},{20,16},{24,20},{28,24},{0,28},{5,1},{9... | collective-permute-start | bytes 589832 | tf_op jit(solution)/shard_map/ppermute | solution.py:819
  53.8 3.9 %collective-permute-start.14 = (f32[48,4,256]{2,1,0:T(4,128)S(1)}, f32[48,4,256]{2,1,0:T(4,128)S(1)}, u32[]{:S(2)}, u32[]{:S(2)}) collective-permute-start(f32[48,4,256]{2,1,0:T(4,128)S(1)} %get-tuple-element.60), channel_id=1, source_target_pairs={{0,1},{1,0},{2,3},{3,2},{4,5},{5,4},{6,7},{7,6},{8,9},{9,8},{10,11... | collective-permute-start | bytes 589832 | tf_op jit(solution)/shard_map/ppermute | solution.py:830
  57.7 0.7 collective-permute-start.15
  58.4 7.1 %all_to_all.16.gathered = f32[8,4,128]{2,1,0:T(4,128)S(1)} all-to-all(f32[8,4,128]{2,1,0:T(4,128)S(1)} %get-tuple-element.55), channel_id=1, replica_groups=mesh['row'=8,'col'=4] {'row'}, dimensions={0} | all-to-all | bytes 32768 | tf_op jit(solution)/shard_map/all_to_all | solution.py:849
  65.5 0.0 collective-permute-done.12.low
  65.5 0.0 collective-permute-done.13.high
  65.5 1.7 %solve.3 = (f32[64,256]{1,0:T(8,128)S(1)}, f32[48,256]{1,0:T(8,128)S(1)}, f32[48,256]{1,0:T(8,128)S(1)}) custom-call(f32[8,4,128]{2,1,0:T(4,128)S(1)} %all_to_all.16.gathered, f32[12,16,256]{2,1,0:T(8,128)S(1)} %collective-permute-done.12.low, f32[12,16,256]{2,1,0:T(8,128)S(1)} %collective-permute-done.13.high), custom_call_target="tpu_custom_call" | custom-call | tf_op jit(solution)/shard_map/solve/pallas_call | solution.py:712
  67.3 2.1 %collective-permute-start.16 = (f32[48,256]{1,0:T(8,128)S(1)}, f32[48,256]{1,0:T(8,128)S(1)}, u32[]{:S(2)}, u32[]{:S(2)}) collective-permute-start(f32[48,256]{1,0:T(8,128)S(1)} %get-tuple-element.62), channel_id=1, source_target_pairs={{0,1},{1,0},{2,3},{3,2},{4,5},{5,4},{6,7},{7,6},{8,9},{9,8},{10,11... | collective-permute-start | bytes 147464 | tf_op jit(solution)/shard_map/ppermute | solution.py:830
  69.4 0.8 collective-permute-start.17
  70.2 0.0 collective-permute-done.14.y_a
  70.2 0.0 collective-permute-done.15.y_b
  70.2 1.2 %collective-permute-done.16.c_a = f32[48,256]{1,0:T(8,128)S(1)} collective-permute-done((f32[48,256]{1,0:T(8,128)S(1)}, f32[48,256]{1,0:T(8,128)S(1)}, u32[]{:S(2)}, u32[]{:S(2)}) %collective-permute-start.16) | collective-permute-done | bytes 49184 | tf_op jit(solution)/shard_map/ppermute | solution.py:830
  71.4 0.0 collective-permute-done.17.c_b
  71.4 4.3 %last_iteration.1 = (f32[3,16,16,256]{3,2,1,0:T(8,128)S(1)}, f32[8,4,128]{2,1,0:T(4,128)S(1)}, f32[16,16,256]{2,1,0:T(8,128)}) custom-call(f32[64,256]{1,0:T(8,128)S(1)} %get-tuple-element.58.wide, f32[3,16,16,256]{3,2,1,0:T(8,128)S(1)} %get-tuple-element.59.core, f32[12,16,256]{2,1,0:T(8,128)S(1)} %collective-permute-done.12.low, ...), custom_call_target="tpu_custom_call" | custom-call | tf_op jit(solution)/shard_map/last_iteration/pallas_call | solution.py:767
  75.7 7.1 %all_to_all.17.gathered = f32[8,4,128]{2,1,0:T(4,128)S(1)} all-to-all(f32[8,4,128]{2,1,0:T(4,128)S(1)} %get-tuple-element.64), channel_id=1, replica_groups=mesh['row'=8,'col'=4] {'row'}, dimensions={0} | all-to-all | bytes 32768 | tf_op jit(solution)/shard_map/all_to_all | solution.py:857
  82.8 2.7 %correct.1 = (f32[3,16,16,256]{3,2,1,0:T(8,128)}, f32[3,16,2,32]{3,2,1,0:T(2,128)}) custom-call(f32[8,4,128]{2,1,0:T(4,128)S(1)} %all_to_all.17.gathered, f32[3,16,16,256]{3,2,1,0:T(8,128)S(1)} %get-tuple-element.65.core), custom_call_target="tpu_custom_call" | custom-call | tf_op jit(solution)/shard_map/correct/pallas_call | solution.py:804
Async XLA Ops:
  0.6 17.5 %copy-start.2 = (s32[16,16,256]{2,1,0:T(8,128)S(1)}, s32[16,16,256]{2,1,0:T(8,128)}, u32[]{:S(2)}) copy-start(s32[16,16,256]{2,1,0:T(8,128)} %coil_mask.3) | copy-start | bytes 786436
  0.6 17.5 %copy-start.3 = (s32[16,16,256]{2,1,0:T(8,128)S(1)}, s32[16,16,256]{2,1,0:T(8,128)}, u32[]{:S(2)}) copy-start(s32[16,16,256]{2,1,0:T(8,128)} %labels.3) | copy-start | bytes 786436
  0.7 17.5 %copy-start.1 = (f32[3,16,16,256]{3,2,1,0:T(8,128)S(1)}, f32[3,16,16,256]{3,2,1,0:T(8,128)}, u32[]{:S(2)}) copy-start(f32[3,16,16,256]{3,2,1,0:T(8,128)} %source.3) | copy-start | bytes 2359300
  0.7 17.5 %copy-start = (f32[3,16,16,256]{3,2,1,0:T(8,128)S(1)}, f32[3,16,16,256]{3,2,1,0:T(8,128)}, u32[]{:S(2)}) copy-start(f32[3,16,16,256]{3,2,1,0:T(8,128)} %potential.3) | copy-start | bytes 2359300
  0.7 17.5 %copy-start.5 = (f32[8]{0:T(128)S(1)}, f32[8]{0:T(128)}, u32[]{:S(2)}) copy-start(f32[8]{0:T(128)} %rise_table.1) | copy-start | bytes 100
  0.7 17.5 %copy-start.4 = (f32[8]{0:T(128)S(1)}, f32[8]{0:T(128)}, u32[]{:S(2)}) copy-start(f32[8]{0:T(128)} %floor_table.1) | copy-start | bytes 100
  3.0 9.3 %collective-permute-start = (f32[21,16,256]{2,1,0:T(8,128)S(1)}, f32[21,16,256]{2,1,0:T(8,128)S(1)}, u32[]{:S(2)}, u32[]{:S(2)}) collective-permute-start(f32[21,16,256]{2,1,0:T(8,128)S(1)} %get-tuple-element.36), channel_id=1, source_target_pairs={{0,4},{4,8},{8,12},{12,16},{16,20},{20,24},{24,28},{28,0},{1,5},{5... | collective-permute-start | bytes 1032200 | tf_op jit(solution)/shard_map/ppermute | solution.py:819
  3.5 10.4 %collective-permute-start.1 = (f32[21,16,256]{2,1,0:T(8,128)S(1)}, f32[21,16,256]{2,1,0:T(8,128)S(1)}, u32[]{:S(2)}, u32[]{:S(2)}) collective-permute-start(f32[21,16,256]{2,1,0:T(8,128)S(1)} %get-tuple-element.37), channel_id=1, source_target_pairs={{4,0},{8,4},{12,8},{16,12},{20,16},{24,20},{28,24},{0,28},{5,1},{9... | collective-permute-start | bytes 1032200 | tf_op jit(solution)/shard_map/ppermute | solution.py:819
  6.5 10.0 %collective-permute-start.2 = (f32[88,4,256]{2,1,0:T(4,128)S(1)}, f32[88,4,256]{2,1,0:T(4,128)S(1)}, u32[]{:S(2)}, u32[]{:S(2)}) collective-permute-start(f32[88,4,256]{2,1,0:T(4,128)S(1)} %get-tuple-element.38), channel_id=1, source_target_pairs={{0,1},{1,0},{2,3},{3,2},{4,5},{5,4},{6,7},{7,6},{8,9},{9,8},{10,11... | collective-permute-start | bytes 1081352 | tf_op jit(solution)/shard_map/ppermute | solution.py:830
  8.8 7.7 %collective-permute-start.3 = (f32[88,4,256]{2,1,0:T(4,128)S(1)}, f32[88,4,256]{2,1,0:T(4,128)S(1)}, u32[]{:S(2)}, u32[]{:S(2)}) collective-permute-start(f32[88,4,256]{2,1,0:T(4,128)S(1)} %get-tuple-element.39), channel_id=1, source_target_pairs={{0,0},{1,2},{2,1},{3,3},{4,4},{5,6},{6,5},{7,7},{8,8},{9,10},{10,9... | collective-permute-start | bytes 1081352 | tf_op jit(solution)/shard_map/ppermute | solution.py:830
  14.0 4.2 %collective-permute-start.4 = (f32[48,256]{1,0:T(8,128)S(1)}, f32[48,256]{1,0:T(8,128)S(1)}, u32[]{:S(2)}, u32[]{:S(2)}) collective-permute-start(f32[48,256]{1,0:T(8,128)S(1)} %get-tuple-element.40), channel_id=1, source_target_pairs={{0,1},{1,0},{2,3},{3,2},{4,5},{5,4},{6,7},{7,6},{8,9},{9,8},{10,11... | collective-permute-start | bytes 147464 | tf_op jit(solution)/shard_map/ppermute | solution.py:830
  15.6 2.5 %collective-permute-start.5 = (f32[48,256]{1,0:T(8,128)S(1)}, f32[48,256]{1,0:T(8,128)S(1)}, u32[]{:S(2)}, u32[]{:S(2)}) collective-permute-start(f32[48,256]{1,0:T(8,128)S(1)} %get-tuple-element.41), channel_id=1, source_target_pairs={{0,0},{1,2},{2,1},{3,3},{4,4},{5,6},{6,5},{7,7},{8,8},{9,10},{10,9... | collective-permute-start | bytes 147464 | tf_op jit(solution)/shard_map/ppermute | solution.py:830
  23.7 16.4 %collective-permute-start.6 = (f32[12,16,256]{2,1,0:T(8,128)S(1)}, f32[12,16,256]{2,1,0:T(8,128)S(1)}, u32[]{:S(2)}, u32[]{:S(2)}) collective-permute-start(f32[12,16,256]{2,1,0:T(8,128)S(1)} %get-tuple-element.43), channel_id=1, source_target_pairs={{0,4},{4,8},{8,12},{12,16},{16,20},{20,24},{24,28},{28,0},{1,5},{5... | collective-permute-start | bytes 589832 | tf_op jit(solution)/shard_map/ppermute | solution.py:819
  24.6 15.4 %collective-permute-start.7 = (f32[12,16,256]{2,1,0:T(8,128)S(1)}, f32[12,16,256]{2,1,0:T(8,128)S(1)}, u32[]{:S(2)}, u32[]{:S(2)}) collective-permute-start(f32[12,16,256]{2,1,0:T(8,128)S(1)} %get-tuple-element.44), channel_id=1, source_target_pairs={{4,0},{8,4},{12,8},{16,12},{20,16},{24,20},{28,24},{0,28},{5,1},{9... | collective-permute-start | bytes 589832 | tf_op jit(solution)/shard_map/ppermute | solution.py:819
  26.4 19.4 %collective-permute-start.8 = (f32[48,4,256]{2,1,0:T(4,128)S(1)}, f32[48,4,256]{2,1,0:T(4,128)S(1)}, u32[]{:S(2)}, u32[]{:S(2)}) collective-permute-start(f32[48,4,256]{2,1,0:T(4,128)S(1)} %get-tuple-element.47), channel_id=1, source_target_pairs={{0,1},{1,0},{2,3},{3,2},{4,5},{5,4},{6,7},{7,6},{8,9},{9,8},{10,11... | collective-permute-start | bytes 589832 | tf_op jit(solution)/shard_map/ppermute | solution.py:830
  30.9 14.9 %collective-permute-start.9 = (f32[48,4,256]{2,1,0:T(4,128)S(1)}, f32[48,4,256]{2,1,0:T(4,128)S(1)}, u32[]{:S(2)}, u32[]{:S(2)}) collective-permute-start(f32[48,4,256]{2,1,0:T(4,128)S(1)} %get-tuple-element.48), channel_id=1, source_target_pairs={{0,0},{1,2},{2,1},{3,3},{4,4},{5,6},{6,5},{7,7},{8,8},{9,10},{10,9... | collective-permute-start | bytes 589832 | tf_op jit(solution)/shard_map/ppermute | solution.py:830
  41.8 5.4 %collective-permute-start.10 = (f32[48,256]{1,0:T(8,128)S(1)}, f32[48,256]{1,0:T(8,128)S(1)}, u32[]{:S(2)}, u32[]{:S(2)}) collective-permute-start(f32[48,256]{1,0:T(8,128)S(1)} %get-tuple-element.49), channel_id=1, source_target_pairs={{0,1},{1,0},{2,3},{3,2},{4,5},{5,4},{6,7},{7,6},{8,9},{9,8},{10,11... | collective-permute-start | bytes 147464 | tf_op jit(solution)/shard_map/ppermute | solution.py:830
  45.1 2.1 %collective-permute-start.11 = (f32[48,256]{1,0:T(8,128)S(1)}, f32[48,256]{1,0:T(8,128)S(1)}, u32[]{:S(2)}, u32[]{:S(2)}) collective-permute-start(f32[48,256]{1,0:T(8,128)S(1)} %get-tuple-element.50), channel_id=1, source_target_pairs={{0,0},{1,2},{2,1},{3,3},{4,4},{5,6},{6,5},{7,7},{8,8},{9,10},{10,9... | collective-permute-start | bytes 147464 | tf_op jit(solution)/shard_map/ppermute | solution.py:830
  51.2 14.4 %collective-permute-start.12 = (f32[12,16,256]{2,1,0:T(8,128)S(1)}, f32[12,16,256]{2,1,0:T(8,128)S(1)}, u32[]{:S(2)}, u32[]{:S(2)}) collective-permute-start(f32[12,16,256]{2,1,0:T(8,128)S(1)} %get-tuple-element.56), channel_id=1, source_target_pairs={{0,4},{4,8},{8,12},{12,16},{16,20},{20,24},{24,28},{28,0},{1,5},{5... | collective-permute-start | bytes 589832 | tf_op jit(solution)/shard_map/ppermute | solution.py:819
  51.2 14.4 %collective-permute-start.13 = (f32[12,16,256]{2,1,0:T(8,128)S(1)}, f32[12,16,256]{2,1,0:T(8,128)S(1)}, u32[]{:S(2)}, u32[]{:S(2)}) collective-permute-start(f32[12,16,256]{2,1,0:T(8,128)S(1)} %get-tuple-element.57), channel_id=1, source_target_pairs={{4,0},{8,4},{12,8},{16,12},{20,16},{24,20},{28,24},{0,28},{5,1},{9... | collective-permute-start | bytes 589832 | tf_op jit(solution)/shard_map/ppermute | solution.py:819
  53.8 16.4 %collective-permute-start.14 = (f32[48,4,256]{2,1,0:T(4,128)S(1)}, f32[48,4,256]{2,1,0:T(4,128)S(1)}, u32[]{:S(2)}, u32[]{:S(2)}) collective-permute-start(f32[48,4,256]{2,1,0:T(4,128)S(1)} %get-tuple-element.60), channel_id=1, source_target_pairs={{0,1},{1,0},{2,3},{3,2},{4,5},{5,4},{6,7},{7,6},{8,9},{9,8},{10,11... | collective-permute-start | bytes 589832 | tf_op jit(solution)/shard_map/ppermute | solution.py:830
  57.7 12.5 %collective-permute-start.15 = (f32[48,4,256]{2,1,0:T(4,128)S(1)}, f32[48,4,256]{2,1,0:T(4,128)S(1)}, u32[]{:S(2)}, u32[]{:S(2)}) collective-permute-start(f32[48,4,256]{2,1,0:T(4,128)S(1)} %get-tuple-element.61), channel_id=1, source_target_pairs={{0,0},{1,2},{2,1},{3,3},{4,4},{5,6},{6,5},{7,7},{8,8},{9,10},{10,9... | collective-permute-start | bytes 589832 | tf_op jit(solution)/shard_map/ppermute | solution.py:830
  67.3 4.2 %collective-permute-start.16 = (f32[48,256]{1,0:T(8,128)S(1)}, f32[48,256]{1,0:T(8,128)S(1)}, u32[]{:S(2)}, u32[]{:S(2)}) collective-permute-start(f32[48,256]{1,0:T(8,128)S(1)} %get-tuple-element.62), channel_id=1, source_target_pairs={{0,1},{1,0},{2,3},{3,2},{4,5},{5,4},{6,7},{7,6},{8,9},{9,8},{10,11... | collective-permute-start | bytes 147464 | tf_op jit(solution)/shard_map/ppermute | solution.py:830
  69.4 2.1 %collective-permute-start.17 = (f32[48,256]{1,0:T(8,128)S(1)}, f32[48,256]{1,0:T(8,128)S(1)}, u32[]{:S(2)}, u32[]{:S(2)}) collective-permute-start(f32[48,256]{1,0:T(8,128)S(1)} %get-tuple-element.63), channel_id=1, source_target_pairs={{0,0},{1,2},{2,1},{3,3},{4,4},{5,6},{6,5},{7,7},{8,8},{9,10},{10,9... | collective-permute-start | bytes 147464 | tf_op jit(solution)/shard_map/ppermute | solution.py:830

commit v5 on v4

--- a/solution.py
+++ b/solution.py
@@ -21,7 +21,8 @@
 ROWS = 40
 HIGH = lax.Precision.HIGHEST
 X_PAGES = 21
-Y_PAGES = 88
+Y_PAGES = 91
+DEEP = (1, BLOCK - 2)
 
 VMEM = pl.BlockSpec(memory_space=pltpu.VMEM)
 SMEM = pl.BlockSpec(memory_space=pltpu.SMEM)
@@ -50,7 +51,6 @@
 CORNER_DRIVE = 6 * FIELD_ROWS
 CORNER_TABLE = CORNER_DRIVE + 6
 CORNER_ALL = CORNER_TABLE + 2 * LABEL_ROWS
-CORNER_LATER = 48
 SLABS = ((0, 4, 0, 1), (4, 12, 1, 0), (12, 20, 1, 1), (20, 24, 2, 0))
 
 
@@ -103,6 +103,18 @@
                 src_y[1, comp, x, 6:8] * mask_hi, slice((x % 2) * 2, (x % 2) * 2 + 2),
             )
         send(72 + x, lab_y[0, x, 0:4].astype(jnp.float32), lab_y[1, x, 4:8].astype(jnp.float32))
+    for number, x in enumerate(DEEP):
+        mask_lo = 2.0 * mask_y[0, x, 2:3].astype(jnp.float32)
+        mask_hi = 2.0 * mask_y[1, x, 5:6].astype(jnp.float32)
+        for comp in range(3):
+            send(
+                88 + comp, pot_y[0, comp, x, 4:5], pot_y[1, comp, x, 3:4],
+                slice(number, number + 1),
+            )
+            send(
+                88 + comp, src_y[0, comp, x, 2:3] * mask_lo, src_y[1, comp, x, 5:6] * mask_hi,
+                slice(2 + number, 3 + number),
+            )
 
 
 def pack_first(potential, source, labels, coil_mask):
@@ -129,7 +141,9 @@
     )(potential, source, coil_mask, labels)
 
 
-def corner_sender(low, high, out_a, out_b, even):
+def pack_corner_kernel(low, high, out_a, out_b):
+    even = lax.axis_index("col") % 2 == 0
+
     def send(row, count, ref, page):
         rows = slice(row, row + count)
         first, second = turns(even, ref[page, 0:count], ref[page, BLOCK - count : BLOCK])
@@ -141,12 +155,6 @@
             row = comp * 2 * FIELD_ROWS + first
             send(row, count, low, comp * 4 + 4 - distance)
             send(row + FIELD_ROWS, count, high, comp * 4 + distance - 1)
-    return send
-
-
-def pack_corner_kernel(low, high, out_a, out_b):
-    even = lax.axis_index("col") % 2 == 0
-    send = corner_sender(low, high, out_a, out_b, even)
     for comp in range(3):
         send(CORNER_DRIVE + comp * 2, 1, low, 12 + comp * 2 + 1)
         send(CORNER_DRIVE + comp * 2 + 1, 1, high, 12 + comp * 2)
@@ -220,35 +228,30 @@
             (c_up * up(v) + c_down * down(v)) + (c_side * side(v) + c_near * swapped)
         ) + c_far * far(swapped, turned)
 
+    turned_sets = [[near(c) for c in coeffs] for coeffs in sets]
+    doubled = [[2.0 * t for t in stripe] for stripe in targets]
+    swapped_t = [[near(t) for t in stripe] for stripe in doubled]
+    plain = [[coeffs[6] * t for t in stripe] for coeffs, stripe in zip(sets, doubled)]
+    swapped = [[coeffs[6] * t for t in stripe] for coeffs, stripe in zip(turned_sets, swapped_t)]
+    for step in range(COARSE_SWEEPS - 1):
+        plain, swapped = [
+            [
+                (1.0 - RELAX) * v + coeffs[6] * (t + neighbours(coeffs, v, s))
+                for v, s, t in zip(*stripe)
+            ]
+            for coeffs, stripe in zip(sets, zip(plain, swapped, doubled))
+        ], [
+            [
+                (1.0 - RELAX) * s + coeffs[6] * (t + neighbours(coeffs, s, v, True))
+                for v, s, t in zip(*stripe)
+            ]
+            for coeffs, stripe in zip(turned_sets, zip(plain, swapped, swapped_t))
+        ]
     out = []
-    for coeffs, stripe in zip(sets, targets):
-        turned = [near(c) for c in coeffs]
-        doubled = [2.0 * t for t in stripe]
-        swapped_t = [near(t) for t in doubled]
-        start = (
-            tuple(coeffs[6] * t for t in doubled), tuple(turned[6] * t for t in swapped_t),
-        )
-
-        def sweep(values):
-            plain, swapped = values
-            return (
-                tuple(
-                    (1.0 - RELAX) * v + coeffs[6] * (t + neighbours(coeffs, v, s))
-                    for v, s, t in zip(plain, swapped, doubled)
-                ),
-                tuple(
-                    (1.0 - RELAX) * s + turned[6] * (t + neighbours(turned, s, v, True))
-                    for v, s, t in zip(plain, swapped, swapped_t)
-                ),
-            )
-
-        values = start
-        for step in range(COARSE_SWEEPS - 1):
-            values = sweep(values)
-        plain, swapped = values
+    for coeffs, *stripe in zip(sets, plain, swapped, doubled):
         total = jnp.sum(jnp.sum(coeffs[5], axis=1, keepdims=True), axis=0, keepdims=True)
         done = []
-        for v, s, t in zip(plain, swapped, doubled):
+        for v, s, t in zip(*stripe):
             left = t - (coeffs[5] * v - neighbours(coeffs, v, s))
             left = jnp.sum(jnp.sum(left, axis=1, keepdims=True), axis=0, keepdims=True)
             done.append(v + left / total)
@@ -278,29 +281,34 @@
     )
 
 
-def stripe_rows(gathered):
-    rows = gathered.shape[0]
+def stripe_rows(rows, block):
     spot = lax.broadcasted_iota(jnp.int32, (rows, LANES), 0)
     out = []
     for comp in range(4):
         total = jnp.zeros((rows, LANES), jnp.float32)
         for row in range(rows):
-            total = jnp.where(spot == row, gathered[row, comp : comp + 1, :], total)
+            total = jnp.where(spot == row, block(row, slice(comp, comp + 1)), total)
         out.append(total)
     scale = 1.0 / float(COARSEN * COARSEN)
     return [out[comp] * scale for comp in range(3)], out[3]
 
 
-def widen(correction, row, picked):
-    picked[...] = jnp.zeros(picked.shape, jnp.float32)
-    for comp in range(3):
-        for shift in range(3):
-            spot = comp * 3 + shift
-            picked[spot : spot + 1, :] = pick_row(correction[comp], row + shift - 1)
-    for group in range(1, 4):
-        picked[group * 16 : group * 16 + 16, :] = pltpu.roll(
-            picked[0:16, :], LANES - 32 * group, 1
-        )
+def widen(corrections, slots, row, picked):
+    lines = []
+    for correction in corrections:
+        picked[0:16, :] = jnp.zeros((16, LANES), jnp.float32)
+        for comp in range(3):
+            for shift in range(3):
+                spot = comp * 3 + shift
+                picked[spot : spot + 1, :] = pick_row(correction[comp], row + shift - 1)
+        lines.append(picked[0:16, :])
+    for number, (stripe, y) in enumerate(slots):
+        for x in range(2):
+            group = x * 2 + y
+            spot = (2 * number + x) * 16
+            picked[spot : spot + 16, :] = (
+                lines[stripe] if group == 0 else pltpu.roll(lines[stripe], LANES - 32 * group, 1)
+            )
     return jnp.dot(
         picked[...], block_matrix(True), precision=HIGH, preferred_element_type=jnp.float32
     )
@@ -326,7 +334,7 @@
         put(plane, HALO + BLOCK, count, jnp.logical_and(there, place.front), front)
 
 
-def put_field(field, core, low, high, y_a, y_b, c_a, c_b, place):
+def put_field(field, core, low, high, y_a, y_b, deep, place, corners):
     for comp in range(3):
         for half in range(2):
             z = slice(half * LANES, half * LANES + LANES)
@@ -347,12 +355,50 @@
                     there, value, 0.0
                 )
 
-            message = [
-                lambda row, count, ref=ref: ref[row : row + count, z] for ref in (c_a, c_b)
-            ]
-            for distance, first, count in CORNER_FIELD:
-                row = comp * 2 * FIELD_ROWS + first
-                put_corner(put, message, place, (row, row + FIELD_ROWS), distance, count)
+            for number, x in enumerate(DEEP):
+                rows = slice(number, number + 1)
+                back, front = place.sides(y_a[deep + comp, rows, z], y_b[deep + comp, rows, z])
+                put(HALO + x, -1, 1, place.back, back)
+                put(HALO + x, EXT, 1, place.front, front)
+            corners(put, comp, z)
+
+
+def first_corners(c_a, c_b, place):
+    def corners(put, comp, z):
+        message = [lambda row, count, ref=ref: ref[row : row + count, z] for ref in (c_a, c_b)]
+        for distance, first, count in CORNER_FIELD:
+            row = comp * 2 * FIELD_ROWS + first
+            put_corner(put, message, place, (row, row + FIELD_ROWS), distance, count)
+
+    return corners
+
+
+ROW_CORNERS = ((1, 1), (2, 1), (3, 1), (2, 2))
+X_EDGE = 3 * HALO + 2
+Y_EDGE = 3 * BLOCK + 6
+
+
+def later_corners(low, high, y_a, y_b, place):
+    def corners(put, comp, z):
+        both = jnp.logical_and
+        for ref, there, sign in ((low, place.low, -1), (high, place.high, 1)):
+            for number, (along_x, along_y) in enumerate(ROW_CORNERS):
+                plane = HALO - along_x if sign < 0 else HALO + BLOCK - 1 + along_x
+                for end, side in enumerate((place.back, place.front)):
+                    spot = comp * 8 + end * 4 + number
+                    row = HALO - along_y if end == 0 else HALO + BLOCK - 1 + along_y
+                    value = ref[12 + spot // 16, spot % 16 : spot % 16 + 1, z]
+                    put(plane, row, 1, both(there, side), value)
+        page = 3 * BLOCK + comp
+        for number in range(4):
+            along_y = 2 + number % 2
+            plane, there = ((HALO - 1, place.low), (HALO + BLOCK, place.high))[number // 2]
+            rows = slice(number, number + 1)
+            back, front = place.sides(y_a[page, rows, z], y_b[page, rows, z])
+            put(plane, HALO - along_y, 1, both(there, place.back), back)
+            put(plane, HALO + BLOCK - 1 + along_y, 1, both(there, place.front), front)
+
+    return corners
 
 
 def put_material(
@@ -380,6 +426,11 @@
 
             row = CORNER_DRIVE + comp * 2
             put_corner(put_drive, message, place, (row, row + 1), 1, 1)
+            for number, x in enumerate(DEEP):
+                rows = slice(2 + number, 3 + number)
+                back, front = place.sides(y_a[88 + comp, rows, z], y_b[88 + comp, rows, z])
+                put_drive(HALO + x, 1, 1, None, back)
+                put_drive(HALO + x, HALO + BLOCK + 2, 1, None, front)
         floor[half, 4:20, own, :] = labels[:, :, z].astype(jnp.float32)
         floor[half, 1:4, own, :] = jnp.where(place.low, low[18:21, :, z], -1.0)
         floor[half, 20:23, own, :] = jnp.where(place.high, high[18:21, :, z], -1.0)
@@ -651,11 +702,34 @@
                 )
                 y_a[comp * 16 : comp * 16 + 16, :, z] = first
                 y_b[comp * 16 : comp * 16 + 16, :, z] = second
+
+                def cell(x, y):
+                    return field[comp, half, HALO + x, CORE + y : CORE + y + 1, :]
+
+                def send(page, row, x, low_y, high_y):
+                    first, second = turns(place.even, cell(x, low_y), cell(x, high_y))
+                    y_a[page, row : row + 1, z] = first
+                    y_b[page, row : row + 1, z] = second
+
+                for number, (along_x, along_y) in enumerate(ROW_CORNERS):
+                    for end, y in enumerate((-along_y, BLOCK - 1 + along_y)):
+                        spot = comp * 8 + end * 4 + number
+                        rows = slice(spot % 16, spot % 16 + 1)
+                        x_lo[12 + spot // 16, rows, z] = cell(along_x - 1, y)
+                        x_hi[12 + spot // 16, rows, z] = cell(BLOCK - along_x, y)
+                for number in range(4):
+                    along_y = 2 + number % 2
+                    send(
+                        3 * BLOCK + comp, number, (-1, BLOCK)[number // 2], along_y - 1,
+                        BLOCK - along_y,
+                    )
+                for number, x in enumerate(DEEP):
+                    send(3 * BLOCK + 3 + comp, number, x, HALO, BLOCK - 1 - HALO)
     coarse_out[...] = jnp.broadcast_to(coarse[None], coarse_out.shape)
 
 
 def edge_shapes(depth):
-    return [f32(3 * HALO, BLOCK, depth)] * 2 + [f32(3 * BLOCK, HALO, depth)] * 2
+    return [f32(X_EDGE, BLOCK, depth)] * 2 + [f32(Y_EDGE, HALO, depth)] * 2
 
 
 def first_kernel(
@@ -664,7 +738,9 @@
 ):
     place = Place()
     field = scratch[0]
-    put_field(field, potential, low, high, y_a, y_b, c_a, c_b, place)
+    put_field(
+        field, potential, low, high, y_a, y_b, 88, place, first_corners(c_a, c_b, place)
+    )
     put_material(
         drive, floor, rise, source, coil_mask, labels, low, high, y_a, y_b, c_a, c_b, floor_table,
         rise_table, place,
@@ -674,13 +750,13 @@
     emit(field, coarse, field_out, (x_lo, x_hi, yo_a, yo_b), coarse_out, place)
 
 
-def first_iteration(potential, source, coil_mask, labels, messages, tables, rows):
+def first_iteration(potential, source, coil_mask, labels, messages, tables, devices):
     depth = potential.shape[-1]
     return pl.pallas_call(
         first_kernel,
         in_specs=[VMEM] * 10 + [SMEM] * 2,
         out_specs=[VMEM] * 10,
-        out_shape=[f32(*potential.shape), f32(rows, 4, LANES)]
+        out_shape=[f32(*potential.shape), f32(devices, 4, LANES)]
         + edge_shapes(depth)
         + [f32(32, 2 * LANES), f32(3, 2, EXT, EXT, LANES), f32(2, EXT, EXT, LANES), f32(2, EXT, EXT, LANES)],
         scratch_shapes=SCRATCH,
@@ -689,39 +765,36 @@
     )(potential, source, coil_mask, labels, *messages, *tables)
 
 
-def solve_kernel(gathered, low, high, wide_out, c_a, c_b, picked):
+SLOTS = ((0, 1), (1, 0), (1, 1), (2, 0))
+
+
+def solve_kernel(gathered, wide_out, picked):
     place = Place()
-    target, reluct = stripe_rows(gathered)
-    correction, = coarse_solve([target], [reluct])
-    wide = widen(correction, place.row, picked)
-    wide_out[...] = wide
-    corner_sender(low, high, c_a, c_b, place.even)
-    for slab, (begin, end, shift, x) in enumerate(SLABS):
-        for comp in range(3):
-            low_edge, high_edge = (
-                wide[spot : spot + 1] for spot in (x * 32 + 16 * y + comp * 3 + shift for y in range(2))
-            )
-            row = CORNER_DRIVE + slab * 3 + comp
-            first, second = turns(place.even, low_edge, high_edge)
-            c_a[row : row + 1, :] = first
-            c_b[row : row + 1, :] = second
-
-
-def solve(gathered, low, high):
-    depth = low.shape[-1]
+    targets, relucts = [], []
+    for stripe in range(3):
+        index = jnp.clip(place.col + stripe - 1, 0, place.cols - 1)
+        target, reluct = stripe_rows(
+            gathered.shape[0], lambda row, part, index=index: gathered[row, index, part, :]
+        )
+        targets.append(target)
+        relucts.append(reluct)
+    wide_out[...] = widen(coarse_solve(targets, relucts), SLOTS, place.row, picked)
+
+
+def solve(gathered):
     return pl.pallas_call(
         solve_kernel,
-        in_specs=[VMEM] * 3,
-        out_specs=[VMEM] * 3,
-        out_shape=[f32(64, depth)] + [f32(CORNER_LATER, depth)] * 2,
-        scratch_shapes=[pltpu.VMEM((64, LANES), jnp.float32)],
+        in_specs=[VMEM],
+        out_specs=VMEM,
+        out_shape=f32(128, 2 * LANES),
+        scratch_shapes=[pltpu.VMEM((128, LANES), jnp.float32)],
         compiler_params=PARAMS,
         name="solve",
-    )(gathered, low, high)
+    )(gathered)
 
 
 def next_kernel(
-    final, wide, core, low, high, y_a, y_b, c_a, c_b, drive_sums, drive, floor, rise, *refs
+    final, wide, core, low, high, y_a, y_b, drive_sums, drive, floor, rise, *refs
 ):
     if final:
         field_out, coarse_out, reluct_out, *scratch = refs
@@ -731,26 +804,35 @@
         edges = (x_lo, x_hi, yo_a, yo_b)
     place = Place()
     field = scratch[0]
-    put_field(field, core, low, high, y_a, y_b, c_a, c_b, place)
+    put_field(
+        field, core, low, high, y_a, y_b, 3 * BLOCK + 3, place,
+        later_corners(low, high, y_a, y_b, place),
+    )
     mid = slice(TOP, TOP + EXT)
     cell = lax.broadcasted_iota(jnp.int32, (EXT, LANES), 0)
     for slab, (begin, end, shift, x) in enumerate(SLABS):
         for comp in range(3):
             for half in range(2):
                 z = slice(half * LANES, (half + 1) * LANES)
-                spot = CORNER_DRIVE + slab * 3 + comp
-                back, front = place.sides(c_a[spot : spot + 1, z], c_b[spot : spot + 1, z])
-                back = jnp.where(place.back, back, 0.0)
-                front = jnp.where(place.front, front, 0.0)
-                spot = x * 32 + comp * 3 + shift
-                own = [wide[spot + 16 * y : spot + 16 * y + 1, z] for y in range(2)]
+                lines = [
+                    wide[spot : spot + 1, z]
+                    for spot in ((2 * slot + x) * 16 + comp * 3 + shift for slot in range(4))
+                ]
+                back = jnp.where(place.back, lines[0], 0.0)
+                front = jnp.where(place.front, lines[3], 0.0)
                 tile = jnp.where(
                     cell < 12,
-                    jnp.where(cell < 4, back, own[0]),
-                    jnp.where(cell < 20, own[1], front),
+                    jnp.where(cell < 4, back, lines[1]),
+                    jnp.where(cell < 20, lines[2], front),
                 )
                 for plane in range(begin, end):
                     field[comp, half, plane, mid] = field[comp, half, plane, mid] + tile
+                for plane in (HALO + x for x in DEEP):
+                    if begin <= plane < end:
+                        for row, line in ((TOP - 1, back), (TOP + EXT, front)):
+                            field[comp, half, plane, row : row + 1, :] = (
+                                field[comp, half, plane, row : row + 1, :] + line
+                            )
     coarse = fine_iteration(*scratch, drive_sums, drive, floor, rise)
     emit(field, coarse, field_out, edges, coarse_out, place)
     if final:
@@ -761,12 +843,12 @@
             ]
 
 
-def next_iteration(final, wide, core, messages, material, rows):
-    outs = [f32(*core.shape), f32(rows, 4, LANES)]
+def next_iteration(final, wide, core, messages, material, devices):
+    outs = [f32(*core.shape), f32(devices, 4, LANES)]
     outs += [f32(*core.shape[1:])] if final else edge_shapes(core.shape[-1])
     return pl.pallas_call(
         functools.partial(next_kernel, final),
-        in_specs=[VMEM] * 12,
+        in_specs=[VMEM] * 10,
         out_specs=[VMEM] * len(outs),
         out_shape=outs,
         scratch_shapes=SCRATCH,
@@ -778,15 +860,14 @@
 def correct_kernel(gathered, core, field_out, target_out, picked):
     row = lax.axis_index("row")
     rows = gathered.shape[0]
-    target, reluct = stripe_rows(gathered)
-    correction, = coarse_solve([target], [reluct])
-    wide = widen(correction, row, picked)
+    target, reluct = stripe_rows(rows, lambda row, part: gathered[row, part, :])
+    wide = widen(coarse_solve([target], [reluct]), ((0, 0), (0, 1)), row, picked)
     cell = lax.broadcasted_iota(jnp.int32, (BLOCK, 2 * LANES), 0)
     for x in range(2):
         for comp in range(3):
-            spot = x * 32 + comp * 3 + 1
+            spot = x * 16 + comp * 3 + 1
             tile = jnp.where(
-                cell < COARSEN, wide[spot : spot + 1], wide[spot + 16 : spot + 17]
+                cell < COARSEN, wide[spot : spot + 1], wide[spot + 32 : spot + 33]
             )
             for plane in range(x * COARSEN, (x + 1) * COARSEN):
                 field_out[comp, plane] = core[comp, plane] + tile
@@ -831,7 +912,7 @@
 
 
 def shards(potential, source, labels, coil_mask, floor_table, rise_table):
-    rows = lax.axis_size("row")
+    rows, cols = lax.axis_size("row"), lax.axis_size("col")
     x_lo, x_hi, y_a, y_b = pack_first(
         *(pltpu.with_memory_space_constraint(v, pltpu.HBM) for v in (potential, source, labels, coil_mask))
     )
@@ -840,16 +921,17 @@
     c_a, c_b = swaps(*pack_corner(low, high))
     field, coarse, x_lo, x_hi, y_a, y_b, *material = first_iteration(
         potential, source, coil_mask, labels, (low, high, y_a, y_b, c_a, c_b),
-        (floor_table, rise_table), rows,
+        (floor_table, rise_table), rows * cols,
     )
     for iteration in range(1, ITERS):
         final = iteration == ITERS - 1
         low, high = rings(x_lo, x_hi)
         y_a, y_b = swaps(y_a, y_b)
-        gathered = lax.all_to_all(coarse, "row", 0, 0)
-        wide, c_a, c_b = solve(gathered, low, high)
-        c_a, c_b = swaps(c_a, c_b)
-        outs = next_iteration(final, wide, field, (low, high, y_a, y_b, c_a, c_b), material, rows)
+        gathered = lax.all_to_all(coarse, ("row", "col"), 0, 0)
+        wide = solve(gathered.reshape(rows, cols, 4, LANES))
+        outs = next_iteration(
+            final, wide, field, (low, high, y_a, y_b), material, rows if final else rows * cols
+        )
         if final:
             field, coarse, reluct = outs
         else:

time: 86.8 us -> 82 us (0.945); the launches traced: 85.5 us -> 81.7 us
  starting transfers between devices: 30.7 us -> 20.2 us
  blocking collectives: 22.7 us -> 32.3 us
  waiting for transfers between devices: 8.97 us -> 6.34 us
    all_to_all x0 -> x2, blocking collectives: none -> 25.2 us  [shards(): gathered = lax.all_to_all(coarse, ('row', 'col'), 0, 0)]
    all_to_all x3 -> x1, blocking collectives: 22.7 us -> 7.11 us  [shards(): gathered = lax.all_to_all(coarse, 'row', 0, 0)]
    ppermute x6 -> x4, starting transfers between devices: 17.8 us -> 8.73 us  [swaps(): lax.ppermute(turn_a, 'col', pairs[0])]
    ppermute x6 -> x4, waiting for transfers between devices: 4.47 us -> 1.86 us  [swaps(): lax.ppermute(turn_a, 'col', pairs[0])]
    ppermute x6 -> x4, starting transfers between devices: 4.13 us -> 2.65 us  [swaps(): lax.ppermute(turn_b, 'col', pairs[1])]
  transfers between devices with their start and end apart: 18 -> 14, of which waited for: 6 -> 4; matrix products, arithmetic and copies ran while one was open for 0% -> 0% of each run, Pallas kernels for 4% -> 4%
where the time goes in v5:
time: 82 us; the launch traced here: 81.7 us
  blocking collectives  32.3 us (39%)
  Pallas kernels  21.9 us (27%)
  starting transfers between devices  20.2 us (25%)
  waiting for transfers between devices  6.34 us (8%)
  between operations  0.87 us (1%)
    all_to_all x2, blocking collectives, shards(): gathered = lax.all_to_all(coarse, ('row', 'col'), 0, 0)  25.2 us
    ppermute x4, starting transfers between devices, swaps(): lax.ppermute(turn_a, 'col', pairs[0])  8.73 us
    pallas_call x2, Pallas kernels, next_iteration(): pl.pallas_call(functools.partial(next_kernel, final), in_specs=[VMEM] * 1...  7.89 us
    ppermute x3, starting transfers between devices, rings(): lax.ppermute(to_low, 'row', backward)  7.31 us
    all_to_all x1, blocking collectives, shards(): gathered = lax.all_to_all(coarse, 'row', 0, 0)  7.11 us
    pallas_call x1, Pallas kernels, first_iteration(): pl.pallas_call(first_kernel, in_specs=[VMEM] * 10 + [SMEM] * 2, out_specs...  5.35 us
    pallas_call x2, Pallas kernels, solve(): pl.pallas_call(solve_kernel, in_specs=[VMEM], out_specs=VMEM, out_shape=f...  3.62 us
    ppermute x3, waiting for transfers between devices, rings(): lax.ppermute(to_high, 'row', forward)  2.94 us
  transfers between devices with their start and end apart: 14, of which 4 were waited for; matrix products, arithmetic and copies ran while one was open for 0% of the time, Pallas kernels for 4%

profile of v5, /device:TPU:0, one launch (start us, length us, event | category | flops | bytes accessed | tf_op | source)
XLA Modules:
  0.0 81.7 jit_solution(3290818582296245493)
XLA Ops:
  0.6 0.0 copy-start.2
  0.6 0.0 copy-start.3
  0.7 0.0 copy-start.1
  0.7 0.0 copy-start
  0.7 0.0 copy-start.5
  0.7 0.0 copy-start.4
  0.7 2.3 %pack_first.1 = (f32[21,16,256]{2,1,0:T(8,128)S(1)}, f32[21,16,256]{2,1,0:T(8,128)S(1)}, f32[91,4,256]{2,1,0:T(4,128)S(1)}, f32[91,4,256]{2,1,0:T(4,128)S(1)}) custom-call(f32[3,16,16,256]{3,2,1,0:T(8,128)} %potential.3, f32[3,16,16,256]{3,2,1,0:T(8,128)} %source.3, s32[16,16,256]{2,1,0:T(8,128)} %coil_mask.3, s32[16,16,256]{2,1,0:T(8,128)} %labels.3), custom_call_target="tpu_custom_call" | custom-call | tf_op jit(solution)/shard_map/pack_first/pallas_call | solution.py:133
  3.0 0.5 collective-permute-start
  3.5 2.9 %collective-permute-start.1 = (f32[21,16,256]{2,1,0:T(8,128)S(1)}, f32[21,16,256]{2,1,0:T(8,128)S(1)}, u32[]{:S(2)}, u32[]{:S(2)}) collective-permute-start(f32[21,16,256]{2,1,0:T(8,128)S(1)} %get-tuple-element.31), channel_id=1, source_target_pairs={{4,0},{8,4},{12,8},{16,12},{20,16},{24,20},{28,24},{0,28},{5,1},{9... | collective-permute-start | bytes 1032200 | tf_op jit(solution)/shard_map/ppermute | solution.py:900
  6.5 2.3 %collective-permute-start.2 = (f32[91,4,256]{2,1,0:T(4,128)S(1)}, f32[91,4,256]{2,1,0:T(4,128)S(1)}, u32[]{:S(2)}, u32[]{:S(2)}) collective-permute-start(f32[91,4,256]{2,1,0:T(4,128)S(1)} %get-tuple-element.32), channel_id=1, source_target_pairs={{0,1},{1,0},{2,3},{3,2},{4,5},{5,4},{6,7},{7,6},{8,9},{9,8},{10,11... | collective-permute-start | bytes 1118216 | tf_op jit(solution)/shard_map/ppermute | solution.py:911
  8.8 0.7 collective-permute-start.3
  9.4 2.9 %collective-permute-done.low = f32[21,16,256]{2,1,0:T(8,128)S(1)} collective-permute-done((f32[21,16,256]{2,1,0:T(8,128)S(1)}, f32[21,16,256]{2,1,0:T(8,128)S(1)}, u32[]{:S(2)}, u32[]{:S(2)}) %collective-permute-start) | collective-permute-done | bytes 344096 | tf_op jit(solution)/shard_map/ppermute | solution.py:900
  12.4 1.5 %collective-permute-done.1.high = f32[21,16,256]{2,1,0:T(8,128)S(1)} collective-permute-done((f32[21,16,256]{2,1,0:T(8,128)S(1)}, f32[21,16,256]{2,1,0:T(8,128)S(1)}, u32[]{:S(2)}, u32[]{:S(2)}) %collective-permute-start.1) | collective-permute-done | bytes 344096 | tf_op jit(solution)/shard_map/ppermute | solution.py:900
  13.9 0.1 pack_corner.1
  14.0 1.6 %collective-permute-start.4 = (f32[48,256]{1,0:T(8,128)S(1)}, f32[48,256]{1,0:T(8,128)S(1)}, u32[]{:S(2)}, u32[]{:S(2)}) collective-permute-start(f32[48,256]{1,0:T(8,128)S(1)} %get-tuple-element.34), channel_id=1, source_target_pairs={{0,1},{1,0},{2,3},{3,2},{4,5},{5,4},{6,7},{7,6},{8,9},{9,8},{10,11... | collective-permute-start | bytes 147464 | tf_op jit(solution)/shard_map/ppermute | solution.py:911
  15.6 0.7 collective-permute-start.5
  16.3 0.5 collective-permute-done.2.y_a
  16.7 0.0 collective-permute-done.3.y_b
  16.7 1.4 %collective-permute-done.4.c_a = f32[48,256]{1,0:T(8,128)S(1)} collective-permute-done((f32[48,256]{1,0:T(8,128)S(1)}, f32[48,256]{1,0:T(8,128)S(1)}, u32[]{:S(2)}, u32[]{:S(2)}) %collective-permute-start.4) | collective-permute-done | bytes 49184 | tf_op jit(solution)/shard_map/ppermute | solution.py:911
  18.1 0.0 collective-permute-done.5.c_b
  18.1 0.0 copy-done.2
  18.1 0.0 copy-done.3
  18.1 0.0 copy-done.1
  18.1 0.0 copy-done
  18.2 0.0 copy-done.5
  18.2 0.0 copy-done.4
  18.2 5.3 %first_iteration.1 = (f32[3,16,16,256]{3,2,1,0:T(8,128)S(1)}, f32[32,4,128]{2,1,0:T(4,128)S(1)}, f32[14,16,256]{2,1,0:T(8,128)S(1)}, f32[14,16,256]{2,1,0:T(8,12...) custom-call(f32[3,16,16,256]{3,2,1,0:T(8,128)S(1)} %copy-done, ...), custom_call_target="tpu_custom_call" | custom-call | tf_op jit(solution)/shard_map/first_iteration/pallas_call | solution.py:755
  23.5 1.0 %collective-permute-start.6 = (f32[14,16,256]{2,1,0:T(8,128)S(1)}, f32[14,16,256]{2,1,0:T(8,128)S(1)}, u32[]{:S(2)}, u32[]{:S(2)}) collective-permute-start(f32[14,16,256]{2,1,0:T(8,128)S(1)} %get-tuple-element.38), channel_id=1, source_target_pairs={{0,4},{4,8},{8,12},{12,16},{16,20},{20,24},{24,28},{28,0},{1,5},{5... | collective-permute-start | bytes 688136 | tf_op jit(solution)/shard_map/ppermute | solution.py:900
  24.5 1.7 %collective-permute-start.7 = (f32[14,16,256]{2,1,0:T(8,128)S(1)}, f32[14,16,256]{2,1,0:T(8,128)S(1)}, u32[]{:S(2)}, u32[]{:S(2)}) collective-permute-start(f32[14,16,256]{2,1,0:T(8,128)S(1)} %get-tuple-element.39), channel_id=1, source_target_pairs={{4,0},{8,4},{12,8},{16,12},{20,16},{24,20},{28,24},{0,28},{5,1},{9... | collective-permute-start | bytes 688136 | tf_op jit(solution)/shard_map/ppermute | solution.py:900
  26.2 4.6 %collective-permute-start.8 = (f32[54,4,256]{2,1,0:T(4,128)S(1)}, f32[54,4,256]{2,1,0:T(4,128)S(1)}, u32[]{:S(2)}, u32[]{:S(2)}) collective-permute-start(f32[54,4,256]{2,1,0:T(4,128)S(1)} %get-tuple-element.40), channel_id=1, source_target_pairs={{0,1},{1,0},{2,3},{3,2},{4,5},{5,4},{6,7},{7,6},{8,9},{9,8},{10,11... | collective-permute-start | bytes 663560 | tf_op jit(solution)/shard_map/ppermute | solution.py:911
  30.8 0.7 collective-permute-start.9
  31.5 13.0 %all_to_all.15 = f32[32,4,128]{2,1,0:T(4,128)S(1)} all-to-all(f32[32,4,128]{2,1,0:T(4,128)S(1)} %get-tuple-element.36), channel_id=1, replica_groups=mesh['row'=8,'col'=4] {'row','col'}, dimensions={0} | all-to-all | bytes 131072 | tf_op jit(solution)/shard_map/all_to_all | solution.py:930
  44.5 1.8 %solve.2.wide = f32[128,256]{1,0:T(8,128)S(1)} custom-call(f32[8,4,4,128]{3,2,1,0:T(4,128)S(1)} %bitcast.2), custom_call_target="tpu_custom_call" | custom-call | tf_op jit(solution)/shard_map/solve/pallas_call | solution.py:785
  46.3 0.0 collective-permute-done.8.y_a
  46.3 0.0 collective-permute-done.9.y_b
  46.3 0.0 collective-permute-done.6.low
  46.3 0.0 collective-permute-done.7.high
  46.3 3.8 %next_iteration.1 = (f32[3,16,16,256]{3,2,1,0:T(8,128)S(1)}, f32[32,4,128]{2,1,0:T(4,128)S(1)}, f32[14,16,256]{2,1,0:T(8,128)S(1)}, f32[14,16,256]{2,1,0:T(8,128...) custom-call(f32[128,256]{1,0:T(8,128)S(1)} %solve.2.wide, f32[3,16,16,256]{3,2,1,0:T(8,128)S(1)} %get-tuple-element.37.core, ...), custom_call_target="tpu_custom_call" | custom-call | tf_op jit(solution)/shard_map/next_iteration/pallas_call | solution.py:849
  50.1 0.1 collective-permute-start.10
  50.2 2.6 %collective-permute-start.11 = (f32[14,16,256]{2,1,0:T(8,128)S(1)}, f32[14,16,256]{2,1,0:T(8,128)S(1)}, u32[]{:S(2)}, u32[]{:S(2)}) collective-permute-start(f32[14,16,256]{2,1,0:T(8,128)S(1)} %get-tuple-element.49), channel_id=1, source_target_pairs={{4,0},{8,4},{12,8},{16,12},{20,16},{24,20},{28,24},{0,28},{5,1},{9... | collective-permute-start | bytes 688136 | tf_op jit(solution)/shard_map/ppermute | solution.py:900
  52.8 0.2 collective-permute-start.12
  53.0 0.7 collective-permute-start.13
  53.7 12.3 %all_to_all.16 = f32[32,4,128]{2,1,0:T(4,128)S(1)} all-to-all(f32[32,4,128]{2,1,0:T(4,128)S(1)} %get-tuple-element.46), channel_id=1, replica_groups=mesh['row'=8,'col'=4] {'row','col'}, dimensions={0} | all-to-all | bytes 131072 | tf_op jit(solution)/shard_map/all_to_all | solution.py:930
  66.0 1.8 %solve.3.wide = f32[128,256]{1,0:T(8,128)S(1)} custom-call(f32[8,4,4,128]{3,2,1,0:T(4,128)S(1)} %bitcast.3), custom_call_target="tpu_custom_call" | custom-call | tf_op jit(solution)/shard_map/solve/pallas_call | solution.py:785
  67.8 0.0 collective-permute-done.12.y_a
  67.8 0.0 collective-permute-done.13.y_b
  67.8 0.0 collective-permute-done.10.low
  67.8 0.0 collective-permute-done.11.high
  67.8 4.1 %last_iteration.1 = (f32[3,16,16,256]{3,2,1,0:T(8,128)S(1)}, f32[8,4,128]{2,1,0:T(4,128)S(1)}, f32[16,16,256]{2,1,0:T(8,128)}) custom-call(f32[128,256]{1,0:T(8,128)S(1)} %solve.3.wide, f32[3,16,16,256]{3,2,1,0:T(8,128)S(1)} %get-tuple-element.47.core, f32[14,16,256]{2,1,0:T(8,128)S(1)} %collective-permute-done.10.low, ...), custom_call_target="tpu_custom_call" | custom-call | tf_op jit(solution)/shard_map/last_iteration/pallas_call | solution.py:849
  71.9 7.1 %all_to_all.17.gathered = f32[8,4,128]{2,1,0:T(4,128)S(1)} all-to-all(f32[8,4,128]{2,1,0:T(4,128)S(1)} %get-tuple-element.52), channel_id=1, replica_groups=mesh['row'=8,'col'=4] {'row'}, dimensions={0} | all-to-all | bytes 32768 | tf_op jit(solution)/shard_map/all_to_all | solution.py:939
  79.0 2.7 %correct.1 = (f32[3,16,16,256]{3,2,1,0:T(8,128)}, f32[3,16,2,32]{3,2,1,0:T(2,128)}) custom-call(f32[8,4,128]{2,1,0:T(4,128)S(1)} %all_to_all.17.gathered, f32[3,16,16,256]{3,2,1,0:T(8,128)S(1)} %get-tuple-element.53.core), custom_call_target="tpu_custom_call" | custom-call | tf_op jit(solution)/shard_map/correct/pallas_call | solution.py:885
Async XLA Ops:
  0.6 17.5 %copy-start.2 = (s32[16,16,256]{2,1,0:T(8,128)S(1)}, s32[16,16,256]{2,1,0:T(8,128)}, u32[]{:S(2)}) copy-start(s32[16,16,256]{2,1,0:T(8,128)} %coil_mask.3) | copy-start | bytes 786436
  0.6 17.5 %copy-start.3 = (s32[16,16,256]{2,1,0:T(8,128)S(1)}, s32[16,16,256]{2,1,0:T(8,128)}, u32[]{:S(2)}) copy-start(s32[16,16,256]{2,1,0:T(8,128)} %labels.3) | copy-start | bytes 786436
  0.7 17.5 %copy-start.1 = (f32[3,16,16,256]{3,2,1,0:T(8,128)S(1)}, f32[3,16,16,256]{3,2,1,0:T(8,128)}, u32[]{:S(2)}) copy-start(f32[3,16,16,256]{3,2,1,0:T(8,128)} %source.3) | copy-start | bytes 2359300
  0.7 17.5 %copy-start = (f32[3,16,16,256]{3,2,1,0:T(8,128)S(1)}, f32[3,16,16,256]{3,2,1,0:T(8,128)}, u32[]{:S(2)}) copy-start(f32[3,16,16,256]{3,2,1,0:T(8,128)} %potential.3) | copy-start | bytes 2359300
  0.7 17.5 %copy-start.5 = (f32[8]{0:T(128)S(1)}, f32[8]{0:T(128)}, u32[]{:S(2)}) copy-start(f32[8]{0:T(128)} %rise_table.1) | copy-start | bytes 100
  0.7 17.5 %copy-start.4 = (f32[8]{0:T(128)S(1)}, f32[8]{0:T(128)}, u32[]{:S(2)}) copy-start(f32[8]{0:T(128)} %floor_table.1) | copy-start | bytes 100
  3.0 9.3 %collective-permute-start = (f32[21,16,256]{2,1,0:T(8,128)S(1)}, f32[21,16,256]{2,1,0:T(8,128)S(1)}, u32[]{:S(2)}, u32[]{:S(2)}) collective-permute-start(f32[21,16,256]{2,1,0:T(8,128)S(1)} %get-tuple-element.30), channel_id=1, source_target_pairs={{0,4},{4,8},{8,12},{12,16},{16,20},{20,24},{24,28},{28,0},{1,5},{5... | collective-permute-start | bytes 1032200 | tf_op jit(solution)/shard_map/ppermute | solution.py:900
  3.5 10.4 %collective-permute-start.1 = (f32[21,16,256]{2,1,0:T(8,128)S(1)}, f32[21,16,256]{2,1,0:T(8,128)S(1)}, u32[]{:S(2)}, u32[]{:S(2)}) collective-permute-start(f32[21,16,256]{2,1,0:T(8,128)S(1)} %get-tuple-element.31), channel_id=1, source_target_pairs={{4,0},{8,4},{12,8},{16,12},{20,16},{24,20},{28,24},{0,28},{5,1},{9... | collective-permute-start | bytes 1032200 | tf_op jit(solution)/shard_map/ppermute | solution.py:900
  6.5 10.2 %collective-permute-start.2 = (f32[91,4,256]{2,1,0:T(4,128)S(1)}, f32[91,4,256]{2,1,0:T(4,128)S(1)}, u32[]{:S(2)}, u32[]{:S(2)}) collective-permute-start(f32[91,4,256]{2,1,0:T(4,128)S(1)} %get-tuple-element.32), channel_id=1, source_target_pairs={{0,1},{1,0},{2,3},{3,2},{4,5},{5,4},{6,7},{7,6},{8,9},{9,8},{10,11... | collective-permute-start | bytes 1118216 | tf_op jit(solution)/shard_map/ppermute | solution.py:911
  8.8 8.0 %collective-permute-start.3 = (f32[91,4,256]{2,1,0:T(4,128)S(1)}, f32[91,4,256]{2,1,0:T(4,128)S(1)}, u32[]{:S(2)}, u32[]{:S(2)}) collective-permute-start(f32[91,4,256]{2,1,0:T(4,128)S(1)} %get-tuple-element.33), channel_id=1, source_target_pairs={{0,0},{1,2},{2,1},{3,3},{4,4},{5,6},{6,5},{7,7},{8,8},{9,10},{10,9... | collective-permute-start | bytes 1118216 | tf_op jit(solution)/shard_map/ppermute | solution.py:911
  14.0 4.2 %collective-permute-start.4 = (f32[48,256]{1,0:T(8,128)S(1)}, f32[48,256]{1,0:T(8,128)S(1)}, u32[]{:S(2)}, u32[]{:S(2)}) collective-permute-start(f32[48,256]{1,0:T(8,128)S(1)} %get-tuple-element.34), channel_id=1, source_target_pairs={{0,1},{1,0},{2,3},{3,2},{4,5},{5,4},{6,7},{7,6},{8,9},{9,8},{10,11... | collective-permute-start | bytes 147464 | tf_op jit(solution)/shard_map/ppermute | solution.py:911
  15.6 2.5 %collective-permute-start.5 = (f32[48,256]{1,0:T(8,128)S(1)}, f32[48,256]{1,0:T(8,128)S(1)}, u32[]{:S(2)}, u32[]{:S(2)}) collective-permute-start(f32[48,256]{1,0:T(8,128)S(1)} %get-tuple-element.35), channel_id=1, source_target_pairs={{0,0},{1,2},{2,1},{3,3},{4,4},{5,6},{6,5},{7,7},{8,8},{9,10},{10,9... | collective-permute-start | bytes 147464 | tf_op jit(solution)/shard_map/ppermute | solution.py:911
  23.5 22.8 %collective-permute-start.6 = (f32[14,16,256]{2,1,0:T(8,128)S(1)}, f32[14,16,256]{2,1,0:T(8,128)S(1)}, u32[]{:S(2)}, u32[]{:S(2)}) collective-permute-start(f32[14,16,256]{2,1,0:T(8,128)S(1)} %get-tuple-element.38), channel_id=1, source_target_pairs={{0,4},{4,8},{8,12},{12,16},{16,20},{20,24},{24,28},{28,0},{1,5},{5... | collective-permute-start | bytes 688136 | tf_op jit(solution)/shard_map/ppermute | solution.py:900
  24.5 21.8 %collective-permute-start.7 = (f32[14,16,256]{2,1,0:T(8,128)S(1)}, f32[14,16,256]{2,1,0:T(8,128)S(1)}, u32[]{:S(2)}, u32[]{:S(2)}) collective-permute-start(f32[14,16,256]{2,1,0:T(8,128)S(1)} %get-tuple-element.39), channel_id=1, source_target_pairs={{4,0},{8,4},{12,8},{16,12},{20,16},{24,20},{28,24},{0,28},{5,1},{9... | collective-permute-start | bytes 688136 | tf_op jit(solution)/shard_map/ppermute | solution.py:900
  26.2 20.0 %collective-permute-start.8 = (f32[54,4,256]{2,1,0:T(4,128)S(1)}, f32[54,4,256]{2,1,0:T(4,128)S(1)}, u32[]{:S(2)}, u32[]{:S(2)}) collective-permute-start(f32[54,4,256]{2,1,0:T(4,128)S(1)} %get-tuple-element.40), channel_id=1, source_target_pairs={{0,1},{1,0},{2,3},{3,2},{4,5},{5,4},{6,7},{7,6},{8,9},{9,8},{10,11... | collective-permute-start | bytes 663560 | tf_op jit(solution)/shard_map/ppermute | solution.py:911
  30.8 15.5 %collective-permute-start.9 = (f32[54,4,256]{2,1,0:T(4,128)S(1)}, f32[54,4,256]{2,1,0:T(4,128)S(1)}, u32[]{:S(2)}, u32[]{:S(2)}) collective-permute-start(f32[54,4,256]{2,1,0:T(4,128)S(1)} %get-tuple-element.41), channel_id=1, source_target_pairs={{0,0},{1,2},{2,1},{3,3},{4,4},{5,6},{6,5},{7,7},{8,8},{9,10},{10,9... | collective-permute-start | bytes 663560 | tf_op jit(solution)/shard_map/ppermute | solution.py:911
  50.1 17.7 %collective-permute-start.10 = (f32[14,16,256]{2,1,0:T(8,128)S(1)}, f32[14,16,256]{2,1,0:T(8,128)S(1)}, u32[]{:S(2)}, u32[]{:S(2)}) collective-permute-start(f32[14,16,256]{2,1,0:T(8,128)S(1)} %get-tuple-element.48), channel_id=1, source_target_pairs={{0,4},{4,8},{8,12},{12,16},{16,20},{20,24},{24,28},{28,0},{1,5},{5... | collective-permute-start | bytes 688136 | tf_op jit(solution)/shard_map/ppermute | solution.py:900
  50.2 17.7 %collective-permute-start.11 = (f32[14,16,256]{2,1,0:T(8,128)S(1)}, f32[14,16,256]{2,1,0:T(8,128)S(1)}, u32[]{:S(2)}, u32[]{:S(2)}) collective-permute-start(f32[14,16,256]{2,1,0:T(8,128)S(1)} %get-tuple-element.49), channel_id=1, source_target_pairs={{4,0},{8,4},{12,8},{16,12},{20,16},{24,20},{28,24},{0,28},{5,1},{9... | collective-permute-start | bytes 688136 | tf_op jit(solution)/shard_map/ppermute | solution.py:900
  52.8 15.0 %collective-permute-start.12 = (f32[54,4,256]{2,1,0:T(4,128)S(1)}, f32[54,4,256]{2,1,0:T(4,128)S(1)}, u32[]{:S(2)}, u32[]{:S(2)}) collective-permute-start(f32[54,4,256]{2,1,0:T(4,128)S(1)} %get-tuple-element.50), channel_id=1, source_target_pairs={{0,1},{1,0},{2,3},{3,2},{4,5},{5,4},{6,7},{7,6},{8,9},{9,8},{10,11... | collective-permute-start | bytes 663560 | tf_op jit(solution)/shard_map/ppermute | solution.py:911
  53.0 14.8 %collective-permute-start.13 = (f32[54,4,256]{2,1,0:T(4,128)S(1)}, f32[54,4,256]{2,1,0:T(4,128)S(1)}, u32[]{:S(2)}, u32[]{:S(2)}) collective-permute-start(f32[54,4,256]{2,1,0:T(4,128)S(1)} %get-tuple-element.51), channel_id=1, source_target_pairs={{0,0},{1,2},{2,1},{3,3},{4,4},{5,6},{6,5},{7,7},{8,8},{9,10},{10,9... | collective-permute-start | bytes 663560 | tf_op jit(solution)/shard_map/ppermute | solution.py:911

commit v6 on v5

--- a/solution.py
+++ b/solution.py
@@ -54,39 +54,43 @@
 SLABS = ((0, 4, 0, 1), (4, 12, 1, 0), (12, 20, 1, 1), (20, 24, 2, 0))
 
 
-def pack_first_kernel(
-    potential, source, coil_mask, labels, x_lo, x_hi, y_a, y_b,
-    pot_x, src_x, mask_x, lab_x, pot_y, src_y, mask_y, lab_y, sems,
-):
-    even = lax.axis_index("col") % 2 == 0
-    copies = []
-
-    def fetch(ref, scratch):
-        copy = pltpu.make_async_copy(ref, scratch, sems.at[len(copies)])
+def fetch_all(sems, pairs):
+    copies = [
+        pltpu.make_async_copy(ref, scratch, sems.at[number])
+        for number, (ref, scratch) in enumerate(pairs)
+    ]
+    for copy in copies:
         copy.start()
-        copies.append(copy)
-
-    for side, (cells, pair, rows) in enumerate((
-        (slice(0, 4), slice(0, 2), slice(0, 8)),
-        (slice(BLOCK - 4, BLOCK), slice(BLOCK - 2, BLOCK), slice(BLOCK - 8, BLOCK)),
-    )):
-        fetch(potential.at[:, cells], pot_x.at[side])
-        fetch(source.at[:, pair], src_x.at[side])
-        fetch(coil_mask.at[pair], mask_x.at[side])
-        fetch(labels.at[cells], lab_x.at[side])
-        fetch(potential.at[:, :, rows], pot_y.at[side])
-        fetch(source.at[:, :, rows], src_y.at[side])
-        fetch(coil_mask.at[:, rows], mask_y.at[side])
-        fetch(labels.at[:, rows], lab_y.at[side])
     for copy in copies:
         copy.wait()
+
+
+def pack_x_kernel(potential, source, coil_mask, labels, x_lo, x_hi, pot, src, mask, lab, sems):
+    pairs = []
+    for side, (cells, pair) in enumerate((
+        (slice(0, 4), slice(0, 2)), (slice(BLOCK - 4, BLOCK), slice(BLOCK - 2, BLOCK)),
+    )):
+        pairs += [
+            (potential.at[:, cells], pot.at[side]), (source.at[:, pair], src.at[side]),
+            (coil_mask.at[pair], mask.at[side]), (labels.at[cells], lab.at[side]),
+        ]
+    fetch_all(sems, pairs)
     for side, out in enumerate((x_lo, x_hi)):
         for comp in range(3):
-            out[comp * 4 : comp * 4 + 4] = pot_x[side, comp]
-            out[12 + comp * 2 : 14 + comp * 2] = (
-                2.0 * src_x[side, comp] * mask_x[side].astype(jnp.float32)
-            )
-        out[18:21] = lab_x[side, side : side + 3].astype(jnp.float32)
+            out[comp * 4 : comp * 4 + 4] = pot[side, comp]
+            out[12 + comp * 2 : 14 + comp * 2] = 2.0 * src[side, comp] * mask[side].astype(jnp.float32)
+        out[18:21] = lab[side, side : side + 3].astype(jnp.float32)
+
+
+def pack_y_kernel(potential, source, coil_mask, labels, y_a, y_b, pot, src, mask, lab, sems):
+    even = lax.axis_index("col") % 2 == 0
+    pairs = []
+    for side, rows in enumerate((slice(0, 8), slice(BLOCK - 8, BLOCK))):
+        pairs += [
+            (potential.at[:, :, rows], pot.at[side]), (source.at[:, :, rows], src.at[side]),
+            (coil_mask.at[:, rows], mask.at[side]), (labels.at[:, rows], lab.at[side]),
+        ]
+    fetch_all(sems, pairs)
 
     def send(page, low_edge, high_edge, rows=slice(0, 4)):
         first, second = turns(even, low_edge, high_edge)
@@ -94,51 +98,50 @@
         y_b[page, rows] = second
 
     for x in range(BLOCK):
-        mask_lo = 2.0 * mask_y[0, x, 0:2].astype(jnp.float32)
-        mask_hi = 2.0 * mask_y[1, x, 6:8].astype(jnp.float32)
+        mask_lo = 2.0 * mask[0, x, 0:2].astype(jnp.float32)
+        mask_hi = 2.0 * mask[1, x, 6:8].astype(jnp.float32)
         for comp in range(3):
-            send(comp * 16 + x, pot_y[0, comp, x, 0:4], pot_y[1, comp, x, 4:8])
+            send(comp * 16 + x, pot[0, comp, x, 0:4], pot[1, comp, x, 4:8])
             send(
-                48 + comp * 8 + x // 2, src_y[0, comp, x, 0:2] * mask_lo,
-                src_y[1, comp, x, 6:8] * mask_hi, slice((x % 2) * 2, (x % 2) * 2 + 2),
+                48 + comp * 8 + x // 2, src[0, comp, x, 0:2] * mask_lo,
+                src[1, comp, x, 6:8] * mask_hi, slice((x % 2) * 2, (x % 2) * 2 + 2),
             )
-        send(72 + x, lab_y[0, x, 0:4].astype(jnp.float32), lab_y[1, x, 4:8].astype(jnp.float32))
+        send(72 + x, lab[0, x, 0:4].astype(jnp.float32), lab[1, x, 4:8].astype(jnp.float32))
     for number, x in enumerate(DEEP):
-        mask_lo = 2.0 * mask_y[0, x, 2:3].astype(jnp.float32)
-        mask_hi = 2.0 * mask_y[1, x, 5:6].astype(jnp.float32)
+        mask_lo = 2.0 * mask[0, x, 2:3].astype(jnp.float32)
+        mask_hi = 2.0 * mask[1, x, 5:6].astype(jnp.float32)
         for comp in range(3):
+            send(88 + comp, pot[0, comp, x, 4:5], pot[1, comp, x, 3:4], slice(number, number + 1))
             send(
-                88 + comp, pot_y[0, comp, x, 4:5], pot_y[1, comp, x, 3:4],
-                slice(number, number + 1),
-            )
-            send(
-                88 + comp, src_y[0, comp, x, 2:3] * mask_lo, src_y[1, comp, x, 5:6] * mask_hi,
+                88 + comp, src[0, comp, x, 2:3] * mask_lo, src[1, comp, x, 5:6] * mask_hi,
                 slice(2 + number, 3 + number),
             )
 
 
-def pack_first(potential, source, labels, coil_mask):
-    depth = potential.shape[-1]
-    scratch = [
-        pltpu.VMEM((2, 3, 4, BLOCK, depth), jnp.float32),
-        pltpu.VMEM((2, 3, 2, BLOCK, depth), jnp.float32),
-        pltpu.VMEM((2, 2, BLOCK, depth), jnp.int32),
-        pltpu.VMEM((2, 4, BLOCK, depth), jnp.int32),
-        pltpu.VMEM((2, 3, BLOCK, 8, depth), jnp.float32),
-        pltpu.VMEM((2, 3, BLOCK, 8, depth), jnp.float32),
-        pltpu.VMEM((2, BLOCK, 8, depth), jnp.int32),
-        pltpu.VMEM((2, BLOCK, 8, depth), jnp.int32),
-        pltpu.SemaphoreType.DMA((16,)),
-    ]
+def pack_edges(kernel, name, shapes, out, arrays):
+    types = (jnp.float32, jnp.float32, jnp.int32, jnp.int32)
     return pl.pallas_call(
-        pack_first_kernel,
+        kernel,
         in_specs=[pl.BlockSpec(memory_space=pltpu.HBM)] * 4,
-        out_specs=[VMEM] * 4,
-        out_shape=[f32(X_PAGES, BLOCK, depth)] * 2 + [f32(Y_PAGES, HALO, depth)] * 2,
-        scratch_shapes=scratch,
+        out_specs=[VMEM] * 2,
+        out_shape=[out] * 2,
+        scratch_shapes=[pltpu.VMEM((2,) + shape, kind) for shape, kind in zip(shapes, types)]
+        + [pltpu.SemaphoreType.DMA((8,))],
         compiler_params=PARAMS,
-        name="pack_first",
-    )(potential, source, coil_mask, labels)
+        name=name,
+    )(*(pltpu.with_memory_space_constraint(v, pltpu.HBM) for v in arrays))
+
+
+def pack_x(arrays):
+    depth = arrays[0].shape[-1]
+    shapes = ((3, 4, BLOCK, depth), (3, 2, BLOCK, depth), (2, BLOCK, depth), (4, BLOCK, depth))
+    return pack_edges(pack_x_kernel, "pack_x", shapes, f32(X_PAGES, BLOCK, depth), arrays)
+
+
+def pack_y(arrays):
+    depth = arrays[0].shape[-1]
+    shapes = ((3, BLOCK, 8, depth),) * 2 + ((BLOCK, 8, depth),) * 2
+    return pack_edges(pack_y_kernel, "pack_y", shapes, f32(Y_PAGES, HALO, depth), arrays)
 
 
 def pack_corner_kernel(low, high, out_a, out_b):
@@ -913,14 +916,14 @@
 
 def shards(potential, source, labels, coil_mask, floor_table, rise_table):
     rows, cols = lax.axis_size("row"), lax.axis_size("col")
-    x_lo, x_hi, y_a, y_b = pack_first(
-        *(pltpu.with_memory_space_constraint(v, pltpu.HBM) for v in (potential, source, labels, coil_mask))
-    )
+    arrays = (potential, source, coil_mask, labels)
+    x_lo, x_hi = pack_x(arrays)
     low, high = rings(x_lo, x_hi)
+    y_a, y_b, *arrays = lax.optimization_barrier((*pack_y(arrays), *arrays))
     y_a, y_b = swaps(y_a, y_b)
     c_a, c_b = swaps(*pack_corner(low, high))
     field, coarse, x_lo, x_hi, y_a, y_b, *material = first_iteration(
-        potential, source, coil_mask, labels, (low, high, y_a, y_b, c_a, c_b),
+        *arrays, (low, high, y_a, y_b, c_a, c_b),
         (floor_table, rise_table), rows * cols,
     )
     for iteration in range(1, ITERS):

time: 82 us -> 81.1 us (0.989)
  blocking collectives: 32.3 us -> 31.1 us
    ppermute x3, waiting for transfers between devices: 2.94 us -> 1.09 us  [rings(): lax.ppermute(to_high, 'row', forward)]
    all_to_all x2, blocking collectives: 25.2 us -> 24 us  [shards(): gathered = lax.all_to_all(coarse, ('row', 'col'), 0, 0)]
    ppermute x4, waiting for transfers between devices: 1.86 us -> 2.98 us  [swaps(): lax.ppermute(turn_a, 'col', pairs[0])]
    pallas_call x1 -> x2, Pallas kernels: 2.34 us -> 3.09 us  [pack_edges(): pl.pallas_call(kernel, in_specs=[pl.BlockSpec(memory_space=pltpu.HBM)] *...]
  transfers between devices with their start and end apart: 14 -> 14, of which waited for: 4 -> 4; matrix products, arithmetic and copies ran while one was open for 0% -> 0% of each run, Pallas kernels for 4% -> 7%
where the time goes in v6:
time: 81.1 us; the launch traced here: 80.7 us
  blocking collectives  31.1 us (38%)
  Pallas kernels  22.6 us (28%)
  starting transfers between devices  20.5 us (25%)
  waiting for transfers between devices  5.62 us (7%)
  between operations  0.88 us (1%)
    all_to_all x2, blocking collectives, shards(): gathered = lax.all_to_all(coarse, ('row', 'col'), 0, 0)  24 us
    ppermute x4, starting transfers between devices, swaps(): lax.ppermute(turn_a, 'col', pairs[0])  9.01 us
    ppermute x3, starting transfers between devices, rings(): lax.ppermute(to_low, 'row', backward)  8.11 us
    pallas_call x2, Pallas kernels, next_iteration(): pl.pallas_call(functools.partial(next_kernel, final), in_specs=[VMEM] * 1...  7.86 us
    all_to_all x1, blocking collectives, shards(): gathered = lax.all_to_all(coarse, 'row', 0, 0)  7.11 us
    pallas_call x1, Pallas kernels, first_iteration(): pl.pallas_call(first_kernel, in_specs=[VMEM] * 10 + [SMEM] * 2, out_specs...  5.25 us
    pallas_call x2, Pallas kernels, solve(): pl.pallas_call(solve_kernel, in_specs=[VMEM], out_specs=VMEM, out_shape=f...  3.62 us
    pallas_call x2, Pallas kernels, pack_edges(): pl.pallas_call(kernel, in_specs=[pl.BlockSpec(memory_space=pltpu.HBM)] *...  3.09 us
  transfers between devices with their start and end apart: 14, of which 4 were waited for; matrix products, arithmetic and copies ran while one was open for 0% of the time, Pallas kernels for 7%

profile of v6, /device:TPU:0, one launch (start us, length us, event | category | flops | bytes accessed | tf_op | source)
XLA Modules:
  0.0 80.7 jit_solution(2687631255306759871)
XLA Ops:
  0.6 1.3 %pack_x.1 = (f32[21,16,256]{2,1,0:T(8,128)S(1)}, f32[21,16,256]{2,1,0:T(8,128)S(1)}) custom-call(f32[3,16,16,256]{3,2,1,0:T(8,128)} %potential.4, f32[3,16,16,256]{3,2,1,0:T(8,128)} %source.4, s32[16,16,256]{2,1,0:T(8,128)} %coil_mask.4, s32[16,16,256]{2,1,0:T(8,128)} %labels.4), custom_call_target="tpu_custom_call" | custom-call | tf_op jit(solution)/shard_map/pack_x/pallas_call | solution.py:123
  1.9 0.0 copy-start
  2.0 0.0 copy-start.1
  2.0 0.0 copy-start.2
  2.0 0.0 copy-start.3
  2.0 0.0 copy-start.4
  2.0 0.0 copy-start.5
  2.0 0.5 collective-permute-start
  2.5 2.9 %collective-permute-start.1 = (f32[21,16,256]{2,1,0:T(8,128)S(1)}, f32[21,16,256]{2,1,0:T(8,128)S(1)}, u32[]{:S(2)}, u32[]{:S(2)}) collective-permute-start(f32[21,16,256]{2,1,0:T(8,128)S(1)} %get-tuple-element.43), channel_id=1, source_target_pairs={{4,0},{8,4},{12,8},{16,12},{20,16},{24,20},{28,24},{0,28},{5,1},{9... | collective-permute-start | bytes 1032200 | tf_op jit(solution)/shard_map/ppermute | solution.py:903
  5.5 1.8 %pack_y.1 = (f32[91,4,256]{2,1,0:T(4,128)S(1)}, f32[91,4,256]{2,1,0:T(4,128)S(1)}) custom-call(f32[3,16,16,256]{3,2,1,0:T(8,128)} %potential.4, f32[3,16,16,256]{3,2,1,0:T(8,128)} %source.4, s32[16,16,256]{2,1,0:T(8,128)} %coil_mask.4, s32[16,16,256]{2,1,0:T(8,128)} %labels.4), custom_call_target="tpu_custom_call" | custom-call | tf_op jit(solution)/shard_map/pack_y/pallas_call | solution.py:123
  7.3 2.3 %collective-permute-start.2 = (f32[91,4,256]{2,1,0:T(4,128)S(1)}, f32[91,4,256]{2,1,0:T(4,128)S(1)}, u32[]{:S(2)}, u32[]{:S(2)}) collective-permute-start(f32[91,4,256]{2,1,0:T(4,128)S(1)} %get-tuple-element.44), channel_id=1, source_target_pairs={{0,1},{1,0},{2,3},{3,2},{4,5},{5,4},{6,7},{7,6},{8,9},{9,8},{10,11... | collective-permute-start | bytes 1118216 | tf_op jit(solution)/shard_map/ppermute | solution.py:914
  9.6 0.7 collective-permute-start.3
  10.3 1.1 %collective-permute-done.low = f32[21,16,256]{2,1,0:T(8,128)S(1)} collective-permute-done((f32[21,16,256]{2,1,0:T(8,128)S(1)}, f32[21,16,256]{2,1,0:T(8,128)S(1)}, u32[]{:S(2)}, u32[]{:S(2)}) %collective-permute-start) | collective-permute-done | bytes 344096 | tf_op jit(solution)/shard_map/ppermute | solution.py:903
  11.4 1.5 %collective-permute-done.1.high = f32[21,16,256]{2,1,0:T(8,128)S(1)} collective-permute-done((f32[21,16,256]{2,1,0:T(8,128)S(1)}, f32[21,16,256]{2,1,0:T(8,128)S(1)}, u32[]{:S(2)}, u32[]{:S(2)}) %collective-permute-start.1) | collective-permute-done | bytes 344096 | tf_op jit(solution)/shard_map/ppermute | solution.py:903
  12.9 0.1 pack_corner.1
  12.9 1.9 %collective-permute-start.4 = (f32[48,256]{1,0:T(8,128)S(1)}, f32[48,256]{1,0:T(8,128)S(1)}, u32[]{:S(2)}, u32[]{:S(2)}) collective-permute-start(f32[48,256]{1,0:T(8,128)S(1)} %get-tuple-element.46), channel_id=1, source_target_pairs={{0,1},{1,0},{2,3},{3,2},{4,5},{5,4},{6,7},{7,6},{8,9},{9,8},{10,11... | collective-permute-start | bytes 147464 | tf_op jit(solution)/shard_map/ppermute | solution.py:914
  14.8 0.7 collective-permute-start.5
  15.5 2.1 %collective-permute-done.2.y_a = f32[91,4,256]{2,1,0:T(4,128)S(1)} collective-permute-done((f32[91,4,256]{2,1,0:T(4,128)S(1)}, f32[91,4,256]{2,1,0:T(4,128)S(1)}, u32[]{:S(2)}, u32[]{:S(2)}) %collective-permute-start.2) | collective-permute-done | bytes 372768 | tf_op jit(solution)/shard_map/ppermute | solution.py:914
  17.6 0.0 collective-permute-done.3.y_b
  17.6 0.9 %collective-permute-done.4.c_a = f32[48,256]{1,0:T(8,128)S(1)} collective-permute-done((f32[48,256]{1,0:T(8,128)S(1)}, f32[48,256]{1,0:T(8,128)S(1)}, u32[]{:S(2)}, u32[]{:S(2)}) %collective-permute-start.4) | collective-permute-done | bytes 49184 | tf_op jit(solution)/shard_map/ppermute | solution.py:914
  18.4 0.0 collective-permute-done.5.c_b
  18.4 0.0 copy-done
  18.4 0.0 copy-done.1
  18.5 0.0 copy-done.2
  18.5 0.0 copy-done.3
  18.5 0.0 copy-done.4
  18.5 0.0 copy-done.5
  18.5 5.3 %first_iteration.1 = (f32[3,16,16,256]{3,2,1,0:T(8,128)S(1)}, f32[32,4,128]{2,1,0:T(4,128)S(1)}, f32[14,16,256]{2,1,0:T(8,128)S(1)}, f32[14,16,256]{2,1,0:T(8,12...) custom-call(f32[3,16,16,256]{3,2,1,0:T(8,128)S(1)} %copy-done, ...), custom_call_target="tpu_custom_call" | custom-call | tf_op jit(solution)/shard_map/first_iteration/pallas_call | solution.py:758
  23.8 0.2 collective-permute-start.6
  23.9 2.5 %collective-permute-start.7 = (f32[14,16,256]{2,1,0:T(8,128)S(1)}, f32[14,16,256]{2,1,0:T(8,128)S(1)}, u32[]{:S(2)}, u32[]{:S(2)}) collective-permute-start(f32[14,16,256]{2,1,0:T(8,128)S(1)} %get-tuple-element.51), channel_id=1, source_target_pairs={{4,0},{8,4},{12,8},{16,12},{20,16},{24,20},{28,24},{0,28},{5,1},{9... | collective-permute-start | bytes 688136 | tf_op jit(solution)/shard_map/ppermute | solution.py:903
  26.5 4.6 %collective-permute-start.8 = (f32[54,4,256]{2,1,0:T(4,128)S(1)}, f32[54,4,256]{2,1,0:T(4,128)S(1)}, u32[]{:S(2)}, u32[]{:S(2)}) collective-permute-start(f32[54,4,256]{2,1,0:T(4,128)S(1)} %get-tuple-element.52), channel_id=1, source_target_pairs={{0,1},{1,0},{2,3},{3,2},{4,5},{5,4},{6,7},{7,6},{8,9},{9,8},{10,11... | collective-permute-start | bytes 663560 | tf_op jit(solution)/shard_map/ppermute | solution.py:914
  31.0 0.7 collective-permute-start.9
  31.7 11.8 %all_to_all.15 = f32[32,4,128]{2,1,0:T(4,128)S(1)} all-to-all(f32[32,4,128]{2,1,0:T(4,128)S(1)} %get-tuple-element.48), channel_id=1, replica_groups=mesh['row'=8,'col'=4] {'row','col'}, dimensions={0} | all-to-all | bytes 131072 | tf_op jit(solution)/shard_map/all_to_all | solution.py:933
  43.5 1.8 %solve.2.wide = f32[128,256]{1,0:T(8,128)S(1)} custom-call(f32[8,4,4,128]{3,2,1,0:T(4,128)S(1)} %bitcast.2), custom_call_target="tpu_custom_call" | custom-call | tf_op jit(solution)/shard_map/solve/pallas_call | solution.py:788
  45.3 0.0 collective-permute-done.8.y_a
  45.3 0.0 collective-permute-done.9.y_b
  45.3 0.0 collective-permute-done.6.low
  45.3 0.0 collective-permute-done.7.high
  45.3 3.8 %next_iteration.1 = (f32[3,16,16,256]{3,2,1,0:T(8,128)S(1)}, f32[32,4,128]{2,1,0:T(4,128)S(1)}, f32[14,16,256]{2,1,0:T(8,128)S(1)}, f32[14,16,256]{2,1,0:T(8,128...) custom-call(f32[128,256]{1,0:T(8,128)S(1)} %solve.2.wide, f32[3,16,16,256]{3,2,1,0:T(8,128)S(1)} %get-tuple-element.49.core, ...), custom_call_target="tpu_custom_call" | custom-call | tf_op jit(solution)/shard_map/next_iteration/pallas_call | solution.py:852
  49.1 0.1 collective-permute-start.10
  49.2 2.6 %collective-permute-start.11 = (f32[14,16,256]{2,1,0:T(8,128)S(1)}, f32[14,16,256]{2,1,0:T(8,128)S(1)}, u32[]{:S(2)}, u32[]{:S(2)}) collective-permute-start(f32[14,16,256]{2,1,0:T(8,128)S(1)} %get-tuple-element.61), channel_id=1, source_target_pairs={{4,0},{8,4},{12,8},{16,12},{20,16},{24,20},{28,24},{0,28},{5,1},{9... | collective-permute-start | bytes 688136 | tf_op jit(solution)/shard_map/ppermute | solution.py:903
  51.8 0.2 collective-permute-start.12
  52.0 0.7 collective-permute-start.13
  52.7 12.3 %all_to_all.16 = f32[32,4,128]{2,1,0:T(4,128)S(1)} all-to-all(f32[32,4,128]{2,1,0:T(4,128)S(1)} %get-tuple-element.58), channel_id=1, replica_groups=mesh['row'=8,'col'=4] {'row','col'}, dimensions={0} | all-to-all | bytes 131072 | tf_op jit(solution)/shard_map/all_to_all | solution.py:933
  65.0 1.8 %solve.3.wide = f32[128,256]{1,0:T(8,128)S(1)} custom-call(f32[8,4,4,128]{3,2,1,0:T(4,128)S(1)} %bitcast.3), custom_call_target="tpu_custom_call" | custom-call | tf_op jit(solution)/shard_map/solve/pallas_call | solution.py:788
  66.8 0.0 collective-permute-done.12.y_a
  66.8 0.0 collective-permute-done.13.y_b
  66.8 0.0 collective-permute-done.10.low
  66.8 0.0 collective-permute-done.11.high
  66.8 4.1 %last_iteration.1 = (f32[3,16,16,256]{3,2,1,0:T(8,128)S(1)}, f32[8,4,128]{2,1,0:T(4,128)S(1)}, f32[16,16,256]{2,1,0:T(8,128)}) custom-call(f32[128,256]{1,0:T(8,128)S(1)} %solve.3.wide, f32[3,16,16,256]{3,2,1,0:T(8,128)S(1)} %get-tuple-element.59.core, f32[14,16,256]{2,1,0:T(8,128)S(1)} %collective-permute-done.10.low, ...), custom_call_target="tpu_custom_call" | custom-call | tf_op jit(solution)/shard_map/last_iteration/pallas_call | solution.py:852
  70.9 7.1 %all_to_all.17.gathered = f32[8,4,128]{2,1,0:T(4,128)S(1)} all-to-all(f32[8,4,128]{2,1,0:T(4,128)S(1)} %get-tuple-element.64), channel_id=1, replica_groups=mesh['row'=8,'col'=4] {'row'}, dimensions={0} | all-to-all | bytes 32768 | tf_op jit(solution)/shard_map/all_to_all | solution.py:942
  78.1 2.7 %correct.1 = (f32[3,16,16,256]{3,2,1,0:T(8,128)}, f32[3,16,2,32]{3,2,1,0:T(2,128)}) custom-call(f32[8,4,128]{2,1,0:T(4,128)S(1)} %all_to_all.17.gathered, f32[3,16,16,256]{3,2,1,0:T(8,128)S(1)} %get-tuple-element.65.core), custom_call_target="tpu_custom_call" | custom-call | tf_op jit(solution)/shard_map/correct/pallas_call | solution.py:888
Async XLA Ops:
  1.9 16.5 %copy-start = (f32[3,16,16,256]{3,2,1,0:T(8,128)S(1)}, f32[3,16,16,256]{3,2,1,0:T(8,128)}, u32[]{:S(2)}) copy-start(f32[3,16,16,256]{3,2,1,0:T(8,128)} %potential.4) | copy-start | bytes 2359300
  2.0 16.5 %copy-start.1 = (f32[3,16,16,256]{3,2,1,0:T(8,128)S(1)}, f32[3,16,16,256]{3,2,1,0:T(8,128)}, u32[]{:S(2)}) copy-start(f32[3,16,16,256]{3,2,1,0:T(8,128)} %source.4) | copy-start | bytes 2359300
  2.0 16.5 %copy-start.2 = (s32[16,16,256]{2,1,0:T(8,128)S(1)}, s32[16,16,256]{2,1,0:T(8,128)}, u32[]{:S(2)}) copy-start(s32[16,16,256]{2,1,0:T(8,128)} %coil_mask.4) | copy-start | bytes 786436
  2.0 16.5 %copy-start.3 = (s32[16,16,256]{2,1,0:T(8,128)S(1)}, s32[16,16,256]{2,1,0:T(8,128)}, u32[]{:S(2)}) copy-start(s32[16,16,256]{2,1,0:T(8,128)} %labels.4) | copy-start | bytes 786436
  2.0 16.5 %copy-start.4 = (f32[8]{0:T(128)S(1)}, f32[8]{0:T(128)}, u32[]{:S(2)}) copy-start(f32[8]{0:T(128)} %floor_table.1) | copy-start | bytes 100
  2.0 16.5 %copy-start.5 = (f32[8]{0:T(128)S(1)}, f32[8]{0:T(128)}, u32[]{:S(2)}) copy-start(f32[8]{0:T(128)} %rise_table.1) | copy-start | bytes 100
  2.0 9.3 %collective-permute-start = (f32[21,16,256]{2,1,0:T(8,128)S(1)}, f32[21,16,256]{2,1,0:T(8,128)S(1)}, u32[]{:S(2)}, u32[]{:S(2)}) collective-permute-start(f32[21,16,256]{2,1,0:T(8,128)S(1)} %get-tuple-element.42), channel_id=1, source_target_pairs={{0,4},{4,8},{8,12},{12,16},{16,20},{20,24},{24,28},{28,0},{1,5},{5... | collective-permute-start | bytes 1032200 | tf_op jit(solution)/shard_map/ppermute | solution.py:903
  2.5 10.4 %collective-permute-start.1 = (f32[21,16,256]{2,1,0:T(8,128)S(1)}, f32[21,16,256]{2,1,0:T(8,128)S(1)}, u32[]{:S(2)}, u32[]{:S(2)}) collective-permute-start(f32[21,16,256]{2,1,0:T(8,128)S(1)} %get-tuple-element.43), channel_id=1, source_target_pairs={{4,0},{8,4},{12,8},{16,12},{20,16},{24,20},{28,24},{0,28},{5,1},{9... | collective-permute-start | bytes 1032200 | tf_op jit(solution)/shard_map/ppermute | solution.py:903
  7.3 10.3 %collective-permute-start.2 = (f32[91,4,256]{2,1,0:T(4,128)S(1)}, f32[91,4,256]{2,1,0:T(4,128)S(1)}, u32[]{:S(2)}, u32[]{:S(2)}) collective-permute-start(f32[91,4,256]{2,1,0:T(4,128)S(1)} %get-tuple-element.44), channel_id=1, source_target_pairs={{0,1},{1,0},{2,3},{3,2},{4,5},{5,4},{6,7},{7,6},{8,9},{9,8},{10,11... | collective-permute-start | bytes 1118216 | tf_op jit(solution)/shard_map/ppermute | solution.py:914
  9.6 8.0 %collective-permute-start.3 = (f32[91,4,256]{2,1,0:T(4,128)S(1)}, f32[91,4,256]{2,1,0:T(4,128)S(1)}, u32[]{:S(2)}, u32[]{:S(2)}) collective-permute-start(f32[91,4,256]{2,1,0:T(4,128)S(1)} %get-tuple-element.45), channel_id=1, source_target_pairs={{0,0},{1,2},{2,1},{3,3},{4,4},{5,6},{6,5},{7,7},{8,8},{9,10},{10,9... | collective-permute-start | bytes 1118216 | tf_op jit(solution)/shard_map/ppermute | solution.py:914
  12.9 5.5 %collective-permute-start.4 = (f32[48,256]{1,0:T(8,128)S(1)}, f32[48,256]{1,0:T(8,128)S(1)}, u32[]{:S(2)}, u32[]{:S(2)}) collective-permute-start(f32[48,256]{1,0:T(8,128)S(1)} %get-tuple-element.46), channel_id=1, source_target_pairs={{0,1},{1,0},{2,3},{3,2},{4,5},{5,4},{6,7},{7,6},{8,9},{9,8},{10,11... | collective-permute-start | bytes 147464 | tf_op jit(solution)/shard_map/ppermute | solution.py:914
  14.8 3.6 %collective-permute-start.5 = (f32[48,256]{1,0:T(8,128)S(1)}, f32[48,256]{1,0:T(8,128)S(1)}, u32[]{:S(2)}, u32[]{:S(2)}) collective-permute-start(f32[48,256]{1,0:T(8,128)S(1)} %get-tuple-element.47), channel_id=1, source_target_pairs={{0,0},{1,2},{2,1},{3,3},{4,4},{5,6},{6,5},{7,7},{8,8},{9,10},{10,9... | collective-permute-start | bytes 147464 | tf_op jit(solution)/shard_map/ppermute | solution.py:914
  23.8 21.6 %collective-permute-start.6 = (f32[14,16,256]{2,1,0:T(8,128)S(1)}, f32[14,16,256]{2,1,0:T(8,128)S(1)}, u32[]{:S(2)}, u32[]{:S(2)}) collective-permute-start(f32[14,16,256]{2,1,0:T(8,128)S(1)} %get-tuple-element.50), channel_id=1, source_target_pairs={{0,4},{4,8},{8,12},{12,16},{16,20},{20,24},{24,28},{28,0},{1,5},{5... | collective-permute-start | bytes 688136 | tf_op jit(solution)/shard_map/ppermute | solution.py:903
  23.9 21.4 %collective-permute-start.7 = (f32[14,16,256]{2,1,0:T(8,128)S(1)}, f32[14,16,256]{2,1,0:T(8,128)S(1)}, u32[]{:S(2)}, u32[]{:S(2)}) collective-permute-start(f32[14,16,256]{2,1,0:T(8,128)S(1)} %get-tuple-element.51), channel_id=1, source_target_pairs={{4,0},{8,4},{12,8},{16,12},{20,16},{24,20},{28,24},{0,28},{5,1},{9... | collective-permute-start | bytes 688136 | tf_op jit(solution)/shard_map/ppermute | solution.py:903
  26.5 18.9 %collective-permute-start.8 = (f32[54,4,256]{2,1,0:T(4,128)S(1)}, f32[54,4,256]{2,1,0:T(4,128)S(1)}, u32[]{:S(2)}, u32[]{:S(2)}) collective-permute-start(f32[54,4,256]{2,1,0:T(4,128)S(1)} %get-tuple-element.52), channel_id=1, source_target_pairs={{0,1},{1,0},{2,3},{3,2},{4,5},{5,4},{6,7},{7,6},{8,9},{9,8},{10,11... | collective-permute-start | bytes 663560 | tf_op jit(solution)/shard_map/ppermute | solution.py:914
  31.0 14.3 %collective-permute-start.9 = (f32[54,4,256]{2,1,0:T(4,128)S(1)}, f32[54,4,256]{2,1,0:T(4,128)S(1)}, u32[]{:S(2)}, u32[]{:S(2)}) collective-permute-start(f32[54,4,256]{2,1,0:T(4,128)S(1)} %get-tuple-element.53), channel_id=1, source_target_pairs={{0,0},{1,2},{2,1},{3,3},{4,4},{5,6},{6,5},{7,7},{8,8},{9,10},{10,9... | collective-permute-start | bytes 663560 | tf_op jit(solution)/shard_map/ppermute | solution.py:914
  49.1 17.7 %collective-permute-start.10 = (f32[14,16,256]{2,1,0:T(8,128)S(1)}, f32[14,16,256]{2,1,0:T(8,128)S(1)}, u32[]{:S(2)}, u32[]{:S(2)}) collective-permute-start(f32[14,16,256]{2,1,0:T(8,128)S(1)} %get-tuple-element.60), channel_id=1, source_target_pairs={{0,4},{4,8},{8,12},{12,16},{16,20},{20,24},{24,28},{28,0},{1,5},{5... | collective-permute-start | bytes 688136 | tf_op jit(solution)/shard_map/ppermute | solution.py:903
  49.2 17.7 %collective-permute-start.11 = (f32[14,16,256]{2,1,0:T(8,128)S(1)}, f32[14,16,256]{2,1,0:T(8,128)S(1)}, u32[]{:S(2)}, u32[]{:S(2)}) collective-permute-start(f32[14,16,256]{2,1,0:T(8,128)S(1)} %get-tuple-element.61), channel_id=1, source_target_pairs={{4,0},{8,4},{12,8},{16,12},{20,16},{24,20},{28,24},{0,28},{5,1},{9... | collective-permute-start | bytes 688136 | tf_op jit(solution)/shard_map/ppermute | solution.py:903
  51.8 15.0 %collective-permute-start.12 = (f32[54,4,256]{2,1,0:T(4,128)S(1)}, f32[54,4,256]{2,1,0:T(4,128)S(1)}, u32[]{:S(2)}, u32[]{:S(2)}) collective-permute-start(f32[54,4,256]{2,1,0:T(4,128)S(1)} %get-tuple-element.62), channel_id=1, source_target_pairs={{0,1},{1,0},{2,3},{3,2},{4,5},{5,4},{6,7},{7,6},{8,9},{9,8},{10,11... | collective-permute-start | bytes 663560 | tf_op jit(solution)/shard_map/ppermute | solution.py:914
  52.0 14.8 %collective-permute-start.13 = (f32[54,4,256]{2,1,0:T(4,128)S(1)}, f32[54,4,256]{2,1,0:T(4,128)S(1)}, u32[]{:S(2)}, u32[]{:S(2)}) collective-permute-start(f32[54,4,256]{2,1,0:T(4,128)S(1)} %get-tuple-element.63), channel_id=1, source_target_pairs={{0,0},{1,2},{2,1},{3,3},{4,4},{5,6},{6,5},{7,7},{8,8},{9,10},{10,9... | collective-permute-start | bytes 663560 | tf_op jit(solution)/shard_map/ppermute | solution.py:914

commit v7 on v6

--- a/solution.py
+++ b/solution.py
@@ -404,17 +404,52 @@
     return corners
 
 
-def put_material(
-    drive, floor, rise, source, coil_mask, labels, low, high, y_a, y_b, c_a, c_b, floor_table,
-    rise_table, place,
+def look_up(label, floor_table, rise_table):
+    floor_cell = jnp.zeros(label.shape, jnp.float32)
+    rise_cell = jnp.zeros(label.shape, jnp.float32)
+    for number in range(floor_table.shape[0]):
+        chosen = label == float(number)
+        floor_cell = jnp.where(chosen, floor_table[number], floor_cell)
+        rise_cell = jnp.where(chosen, rise_table[number], rise_cell)
+    return floor_cell, rise_cell
+
+
+def prepare_kernel(
+    source, coil_mask, labels, floor_table, rise_table, drive_sums, drive, floor, rise
 ):
+    own = slice(HALO, HALO + BLOCK)
+    for half in range(2):
+        z = slice(half * LANES, half * LANES + LANES)
+        for x in range(BLOCK):
+            coil = 2.0 * coil_mask[x, :, z].astype(jnp.float32)
+            for comp in range(3):
+                drive[comp, half, HALO + x, own, :] = source[comp, x, :, z] * coil
+            floor[half, HALO + x, own, :], rise[half, HALO + x, own, :] = look_up(
+                labels[x, :, z].astype(jnp.float32), floor_table, rise_table
+            )
+    sum_drive(drive, drive_sums)
+
+
+def prepare(source, coil_mask, labels, tables):
+    return pl.pallas_call(
+        prepare_kernel,
+        in_specs=[VMEM] * 3 + [SMEM] * 2,
+        out_specs=[VMEM] * 4,
+        out_shape=[
+            f32(32, 2 * LANES), f32(3, 2, EXT, EXT, LANES), f32(2, EXT, EXT, LANES),
+            f32(2, EXT, EXT, LANES),
+        ],
+        compiler_params=PARAMS,
+        name="prepare",
+    )(source, coil_mask, labels, *tables)
+
+
+def put_material(drive, floor, rise, low, high, y_a, y_b, c_a, c_b, floor_table, rise_table, place):
     for half in range(2):
         z = slice(half * LANES, half * LANES + LANES)
         own = slice(HALO, HALO + BLOCK)
-        coil = 2.0 * coil_mask[:, :, z].astype(jnp.float32)
         message = [lambda row, count, ref=ref: ref[row : row + count, z] for ref in (c_a, c_b)]
         for comp in range(3):
-            drive[comp, half, 4:20, own, :] = source[comp, :, :, z] * coil
             pages = slice(12 + comp * 2, 14 + comp * 2)
             drive[comp, half, 2:4, own, :] = low[pages, :, z]
             drive[comp, half, 20:22, own, :] = high[pages, :, z]
@@ -434,12 +469,8 @@
                 back, front = place.sides(y_a[88 + comp, rows, z], y_b[88 + comp, rows, z])
                 put_drive(HALO + x, 1, 1, None, back)
                 put_drive(HALO + x, HALO + BLOCK + 2, 1, None, front)
-        floor[half, 4:20, own, :] = labels[:, :, z].astype(jnp.float32)
         floor[half, 1:4, own, :] = jnp.where(place.low, low[18:21, :, z], -1.0)
         floor[half, 20:23, own, :] = jnp.where(place.high, high[18:21, :, z], -1.0)
-        back, front = place.sides(y_a[72:88, :, z], y_b[72:88, :, z])
-        floor[half, 4:20, 0:HALO, :] = jnp.where(place.back, back, -1.0)
-        floor[half, 4:20, HALO + BLOCK : EXT, :] = jnp.where(place.front, front, -1.0)
 
         def put_label(plane, row, count, there, value):
             floor[half, plane, row : row + count, :] = jnp.where(there, value, -1.0)
@@ -447,18 +478,16 @@
         for distance, first, count in CORNER_LABEL:
             row = CORNER_TABLE + first
             put_corner(put_label, message, place, (row, row + LABEL_ROWS), distance, count)
-
-    for x in range(1, EXT - 1):
-        for half in range(2):
-            label = floor[half, x]
-            floor_cell = jnp.zeros_like(label)
-            rise_cell = jnp.zeros_like(label)
-            for number in range(floor_table.shape[0]):
-                chosen = label == float(number)
-                floor_cell = jnp.where(chosen, floor_table[number], floor_cell)
-                rise_cell = jnp.where(chosen, rise_table[number], rise_cell)
-            floor[half, x] = floor_cell
-            rise[half, x] = rise_cell
+        for x in (1, 2, 3, 20, 21, 22):
+            floor[half, x], rise[half, x] = look_up(floor[half, x], floor_table, rise_table)
+        for x in range(BLOCK):
+            back, front = place.sides(y_a[72 + x, :, z], y_b[72 + x, :, z])
+            label = jnp.concatenate(
+                [jnp.where(place.back, back, -1.0), jnp.where(place.front, front, -1.0)], axis=0
+            )
+            for ref, value in zip((floor, rise), look_up(label, floor_table, rise_table)):
+                ref[half, HALO + x, 0:HALO, :] = value[:HALO]
+                ref[half, HALO + x, HALO + BLOCK :, :] = value[HALO:]
 
 
 def right_of(low, high, last):
@@ -736,36 +765,33 @@
 
 
 def first_kernel(
-    potential, source, coil_mask, labels, low, high, y_a, y_b, c_a, c_b, floor_table, rise_table,
-    field_out, coarse_out, x_lo, x_hi, yo_a, yo_b, drive_sums, drive, floor, rise, *scratch,
+    potential, low, high, y_a, y_b, c_a, c_b, floor_table, rise_table, drive_sums, drive_in, floor_in,
+    rise_in, field_out, coarse_out, x_lo, x_hi, yo_a, yo_b, drive, floor, rise, *scratch,
 ):
     place = Place()
     field = scratch[0]
     put_field(
         field, potential, low, high, y_a, y_b, 88, place, first_corners(c_a, c_b, place)
     )
-    put_material(
-        drive, floor, rise, source, coil_mask, labels, low, high, y_a, y_b, c_a, c_b, floor_table,
-        rise_table, place,
-    )
-    sum_drive(drive, drive_sums)
+    put_material(drive, floor, rise, low, high, y_a, y_b, c_a, c_b, floor_table, rise_table, place)
     coarse = fine_iteration(*scratch, drive_sums, drive, floor, rise)
     emit(field, coarse, field_out, (x_lo, x_hi, yo_a, yo_b), coarse_out, place)
 
 
-def first_iteration(potential, source, coil_mask, labels, messages, tables, devices):
+def first_iteration(potential, messages, tables, material, devices):
     depth = potential.shape[-1]
     return pl.pallas_call(
         first_kernel,
-        in_specs=[VMEM] * 10 + [SMEM] * 2,
-        out_specs=[VMEM] * 10,
+        in_specs=[VMEM] * 7 + [SMEM] * 2 + [VMEM] * 4,
+        out_specs=[VMEM] * 9,
         out_shape=[f32(*potential.shape), f32(devices, 4, LANES)]
         + edge_shapes(depth)
-        + [f32(32, 2 * LANES), f32(3, 2, EXT, EXT, LANES), f32(2, EXT, EXT, LANES), f32(2, EXT, EXT, LANES)],
+        + [f32(*part.shape) for part in material[1:]],
         scratch_shapes=SCRATCH,
+        input_output_aliases={10: 6, 11: 7, 12: 8},
         compiler_params=PARAMS,
         name="first_iteration",
-    )(potential, source, coil_mask, labels, *messages, *tables)
+    )(potential, *messages, *tables, *material)
 
 
 SLOTS = ((0, 1), (1, 0), (1, 1), (2, 0))
@@ -921,11 +947,15 @@
     low, high = rings(x_lo, x_hi)
     y_a, y_b, *arrays = lax.optimization_barrier((*pack_y(arrays), *arrays))
     y_a, y_b = swaps(y_a, y_b)
+    tables = (floor_table, rise_table)
+    potential, *rest = arrays
+    drive_sums, *material = prepare(*rest, tables)
+    low, high, drive_sums = lax.optimization_barrier((low, high, drive_sums))
     c_a, c_b = swaps(*pack_corner(low, high))
     field, coarse, x_lo, x_hi, y_a, y_b, *material = first_iteration(
-        *arrays, (low, high, y_a, y_b, c_a, c_b),
-        (floor_table, rise_table), rows * cols,
+        potential, (low, high, y_a, y_b, c_a, c_b), tables, (drive_sums, *material), rows * cols,
     )
+    material = (drive_sums, *material)
     for iteration in range(1, ITERS):
         final = iteration == ITERS - 1
         low, high = rings(x_lo, x_hi)

time: 81.1 us -> 80.8 us (level)
  waiting for transfers between devices: 5.62 us -> 3.93 us
  starting transfers between devices: 20.5 us -> 21.4 us
    ppermute x3, waiting for transfers between devices: 1.09 us -> 0.17 us  [rings(): lax.ppermute(to_high, 'row', forward)]
    ppermute x4, starting transfers between devices: 9.01 us -> 9.92 us  [swaps(): lax.ppermute(turn_a, 'col', pairs[0])]
    pallas_call x1 -> x2, Pallas kernels: 5.25 us -> 5.72 us  [the longest x1 4.86 us: first_iteration(): pl.pallas_call(first_kernel, in_specs=[VMEM] * 7 + [SMEM] * 2 + [VMEM] *...]
  transfers between devices with their start and end apart: 14 -> 14, of which waited for: 4 -> 4; matrix products, arithmetic and copies ran while one was open for 0% -> 0% of each run, Pallas kernels for 7% -> 8%
where the time goes in v7:
time: 80.8 us; the launch traced here: 80.5 us
  blocking collectives  31.1 us (38%)
  Pallas kernels  23.1 us (29%)
  starting transfers between devices  21.4 us (26%)
  waiting for transfers between devices  3.93 us (5%)
  between operations  0.88 us (1%)
    all_to_all x2, blocking collectives, shards(): gathered = lax.all_to_all(coarse, ('row', 'col'), 0, 0)  24 us
    ppermute x4, starting transfers between devices, swaps(): lax.ppermute(turn_a, 'col', pairs[0])  9.92 us
    ppermute x3, starting transfers between devices, rings(): lax.ppermute(to_low, 'row', backward)  8.11 us
    pallas_call x2, Pallas kernels, next_iteration(): pl.pallas_call(functools.partial(next_kernel, final), in_specs=[VMEM] * 1...  7.88 us
    all_to_all x1, blocking collectives, shards(): gathered = lax.all_to_all(coarse, 'row', 0, 0)  7.11 us
    pallas_call x1, Pallas kernels, first_iteration(): pl.pallas_call(first_kernel, in_specs=[VMEM] * 7 + [SMEM] * 2 + [VMEM] *...  4.86 us
    pallas_call x2, Pallas kernels, solve(): pl.pallas_call(solve_kernel, in_specs=[VMEM], out_specs=VMEM, out_shape=f...  3.62 us
    pallas_call x2, Pallas kernels, pack_edges(): pl.pallas_call(kernel, in_specs=[pl.BlockSpec(memory_space=pltpu.HBM)] *...  3.17 us
  transfers between devices with their start and end apart: 14, of which 4 were waited for; matrix products, arithmetic and copies ran while one was open for 0% of the time, Pallas kernels for 8%

profile of v7, /device:TPU:0, one launch (start us, length us, event | category | flops | bytes accessed | tf_op | source)
XLA Modules:
  0.0 80.5 jit_solution(14863371989228168787)
XLA Ops:
  0.6 0.0 copy-start.2
  0.6 0.0 copy-start.3
  0.7 0.0 copy-start
  0.7 0.0 copy-start.5
  0.7 0.0 copy-start.4
  0.7 1.4 %pack_x.1 = (f32[21,16,256]{2,1,0:T(8,128)S(1)}, f32[21,16,256]{2,1,0:T(8,128)S(1)}) custom-call(f32[3,16,16,256]{3,2,1,0:T(8,128)} %potential.4, f32[3,16,16,256]{3,2,1,0:T(8,128)} %source.4, s32[16,16,256]{2,1,0:T(8,128)} %coil_mask.4, s32[16,16,256]{2,1,0:T(8,128)} %labels.4), custom_call_target="tpu_custom_call" | custom-call | tf_op jit(solution)/shard_map/pack_x/pallas_call | solution.py:123
  2.1 0.5 collective-permute-start
  2.6 0.0 copy-start.1
  2.6 3.0 %collective-permute-start.1 = (f32[21,16,256]{2,1,0:T(8,128)S(1)}, f32[21,16,256]{2,1,0:T(8,128)S(1)}, u32[]{:S(2)}, u32[]{:S(2)}) collective-permute-start(f32[21,16,256]{2,1,0:T(8,128)S(1)} %get-tuple-element.46), channel_id=1, source_target_pairs={{4,0},{8,4},{12,8},{16,12},{20,16},{24,20},{28,24},{0,28},{5,1},{9... | collective-permute-start | bytes 1032200 | tf_op jit(solution)/shard_map/ppermute | solution.py:929
  5.6 1.8 %pack_y.1 = (f32[91,4,256]{2,1,0:T(4,128)S(1)}, f32[91,4,256]{2,1,0:T(4,128)S(1)}) custom-call(f32[3,16,16,256]{3,2,1,0:T(8,128)} %potential.4, f32[3,16,16,256]{3,2,1,0:T(8,128)} %source.4, s32[16,16,256]{2,1,0:T(8,128)} %coil_mask.4, s32[16,16,256]{2,1,0:T(8,128)} %labels.4), custom_call_target="tpu_custom_call" | custom-call | tf_op jit(solution)/shard_map/pack_y/pallas_call | solution.py:123
  7.3 2.3 %collective-permute-start.2 = (f32[91,4,256]{2,1,0:T(4,128)S(1)}, f32[91,4,256]{2,1,0:T(4,128)S(1)}, u32[]{:S(2)}, u32[]{:S(2)}) collective-permute-start(f32[91,4,256]{2,1,0:T(4,128)S(1)} %get-tuple-element.53), channel_id=1, source_target_pairs={{0,1},{1,0},{2,3},{3,2},{4,5},{5,4},{6,7},{7,6},{8,9},{9,8},{10,11... | collective-permute-start | bytes 1118216 | tf_op jit(solution)/shard_map/ppermute | solution.py:940
  9.7 0.7 collective-permute-start.3
  10.3 0.0 copy-done.2
  10.4 0.0 copy-done.3
  10.4 0.0 copy-done
  10.4 0.0 copy-done.5
  10.4 0.0 copy-done.4
  10.4 0.9 %prepare.1 = (f32[32,256]{1,0:T(8,128)S(1)}, f32[3,2,24,24,128]{4,3,2,1,0:T(8,128)S(1)}, f32[2,24,24,128]{3,2,1,0:T(8,128)S(1)}, f32[2,24,24,128]{3,2,1,0:T(8,128)S(1)}) custom-call(f32[3,16,16,256]{3,2,1,0:T(8,128)S(1)} %copy-done, s32[16,16,256]{2,1,0:T(8,128)S(1)} %copy-done.2, s32[16,16,256]{2,1,0:T(8,128)S(1)} %copy-done.3, f32[8]{0:T(128)S(1)} %copy-done.4, ...), custom_call_target="tpu_custom_call" | custom-call | tf_op jit(solution)/shard_map/prepare/pallas_call | solution.py:434
  11.3 0.2 collective-permute-done.low
  11.4 1.5 %collective-permute-done.1.high = f32[21,16,256]{2,1,0:T(8,128)S(1)} collective-permute-done((f32[21,16,256]{2,1,0:T(8,128)S(1)}, f32[21,16,256]{2,1,0:T(8,128)S(1)}, u32[]{:S(2)}, u32[]{:S(2)}) %collective-permute-start.1) | collective-permute-done | bytes 344096 | tf_op jit(solution)/shard_map/ppermute | solution.py:929
  13.0 0.1 pack_corner.1
  13.0 2.8 %collective-permute-start.4 = (f32[48,256]{1,0:T(8,128)S(1)}, f32[48,256]{1,0:T(8,128)S(1)}, u32[]{:S(2)}, u32[]{:S(2)}) collective-permute-start(f32[48,256]{1,0:T(8,128)S(1)} %get-tuple-element.55), channel_id=1, source_target_pairs={{0,1},{1,0},{2,3},{3,2},{4,5},{5,4},{6,7},{7,6},{8,9},{9,8},{10,11... | collective-permute-start | bytes 147464 | tf_op jit(solution)/shard_map/ppermute | solution.py:940
  15.8 0.7 collective-permute-start.5
  16.4 1.3 %collective-permute-done.2.y_a = f32[91,4,256]{2,1,0:T(4,128)S(1)} collective-permute-done((f32[91,4,256]{2,1,0:T(4,128)S(1)}, f32[91,4,256]{2,1,0:T(4,128)S(1)}, u32[]{:S(2)}, u32[]{:S(2)}) %collective-permute-start.2) | collective-permute-done | bytes 372768 | tf_op jit(solution)/shard_map/ppermute | solution.py:940
  17.7 0.0 collective-permute-done.3.y_b
  17.7 1.0 %collective-permute-done.4.c_a = f32[48,256]{1,0:T(8,128)S(1)} collective-permute-done((f32[48,256]{1,0:T(8,128)S(1)}, f32[48,256]{1,0:T(8,128)S(1)}, u32[]{:S(2)}, u32[]{:S(2)}) %collective-permute-start.4) | collective-permute-done | bytes 49184 | tf_op jit(solution)/shard_map/ppermute | solution.py:940
  18.7 0.0 collective-permute-done.5.c_b
  18.7 0.0 copy-done.1
  18.7 4.9 %first_iteration.1 = (f32[3,16,16,256]{3,2,1,0:T(8,128)S(1)}, f32[32,4,128]{2,1,0:T(4,128)S(1)}, f32[14,16,256]{2,1,0:T(8,128)S(1)}, f32[14,16,256]{2,1,0:T(8,12...) custom-call(f32[3,16,16,256]{3,2,1,0:T(8,128)S(1)} %copy-done.1, ...), custom_call_target="tpu_custom_call", output_to_operand_aliasing={{6}: (10, {}), {7}: (11, {}), {8}: (12, {})} | custom-call | tf_op jit(solution)/shard_map/first_iteration/pallas_call | solution.py:783
  23.5 0.2 collective-permute-start.6
  23.7 2.5 %collective-permute-start.7 = (f32[14,16,256]{2,1,0:T(8,128)S(1)}, f32[14,16,256]{2,1,0:T(8,128)S(1)}, u32[]{:S(2)}, u32[]{:S(2)}) collective-permute-start(f32[14,16,256]{2,1,0:T(8,128)S(1)} %get-tuple-element.64), channel_id=1, source_target_pairs={{4,0},{8,4},{12,8},{16,12},{20,16},{24,20},{28,24},{0,28},{5,1},{9... | collective-permute-start | bytes 688136 | tf_op jit(solution)/shard_map/ppermute | solution.py:929
  26.2 4.6 %collective-permute-start.8 = (f32[54,4,256]{2,1,0:T(4,128)S(1)}, f32[54,4,256]{2,1,0:T(4,128)S(1)}, u32[]{:S(2)}, u32[]{:S(2)}) collective-permute-start(f32[54,4,256]{2,1,0:T(4,128)S(1)} %get-tuple-element.65), channel_id=1, source_target_pairs={{0,1},{1,0},{2,3},{3,2},{4,5},{5,4},{6,7},{7,6},{8,9},{9,8},{10,11... | collective-permute-start | bytes 663560 | tf_op jit(solution)/shard_map/ppermute | solution.py:940
  30.8 0.7 collective-permute-start.9
  31.5 11.7 %all_to_all.15 = f32[32,4,128]{2,1,0:T(4,128)S(1)} all-to-all(f32[32,4,128]{2,1,0:T(4,128)S(1)} %get-tuple-element.61), channel_id=1, replica_groups=mesh['row'=8,'col'=4] {'row','col'}, dimensions={0} | all-to-all | bytes 131072 | tf_op jit(solution)/shard_map/all_to_all | solution.py:963
  43.2 1.8 %solve.2.wide = f32[128,256]{1,0:T(8,128)S(1)} custom-call(f32[8,4,4,128]{3,2,1,0:T(4,128)S(1)} %bitcast.2), custom_call_target="tpu_custom_call" | custom-call | tf_op jit(solution)/shard_map/solve/pallas_call | solution.py:814
  45.0 0.0 collective-permute-done.8.y_a
  45.0 0.0 collective-permute-done.9.y_b
  45.0 0.0 collective-permute-done.6.low
  45.0 0.0 collective-permute-done.7.high
  45.1 3.8 %next_iteration.1 = (f32[3,16,16,256]{3,2,1,0:T(8,128)S(1)}, f32[32,4,128]{2,1,0:T(4,128)S(1)}, f32[14,16,256]{2,1,0:T(8,128)S(1)}, f32[14,16,256]{2,1,0:T(8,128...) custom-call(f32[128,256]{1,0:T(8,128)S(1)} %solve.2.wide, f32[3,16,16,256]{3,2,1,0:T(8,128)S(1)} %get-tuple-element.62.core, ...), custom_call_target="tpu_custom_call" | custom-call | tf_op jit(solution)/shard_map/next_iteration/pallas_call | solution.py:878
  48.8 0.1 collective-permute-start.10
  48.9 2.6 %collective-permute-start.11 = (f32[14,16,256]{2,1,0:T(8,128)S(1)}, f32[14,16,256]{2,1,0:T(8,128)S(1)}, u32[]{:S(2)}, u32[]{:S(2)}) collective-permute-start(f32[14,16,256]{2,1,0:T(8,128)S(1)} %get-tuple-element.73), channel_id=1, source_target_pairs={{4,0},{8,4},{12,8},{16,12},{20,16},{24,20},{28,24},{0,28},{5,1},{9... | collective-permute-start | bytes 688136 | tf_op jit(solution)/shard_map/ppermute | solution.py:929
  51.5 0.2 collective-permute-start.12
  51.8 0.7 collective-permute-start.13
  52.4 12.3 %all_to_all.16 = f32[32,4,128]{2,1,0:T(4,128)S(1)} all-to-all(f32[32,4,128]{2,1,0:T(4,128)S(1)} %get-tuple-element.70), channel_id=1, replica_groups=mesh['row'=8,'col'=4] {'row','col'}, dimensions={0} | all-to-all | bytes 131072 | tf_op jit(solution)/shard_map/all_to_all | solution.py:963
  64.7 1.8 %solve.3.wide = f32[128,256]{1,0:T(8,128)S(1)} custom-call(f32[8,4,4,128]{3,2,1,0:T(4,128)S(1)} %bitcast.3), custom_call_target="tpu_custom_call" | custom-call | tf_op jit(solution)/shard_map/solve/pallas_call | solution.py:814
  66.5 0.0 collective-permute-done.12.y_a
  66.5 0.0 collective-permute-done.13.y_b
  66.6 0.0 collective-permute-done.10.low
  66.6 0.0 collective-permute-done.11.high
  66.6 4.1 %last_iteration.1 = (f32[3,16,16,256]{3,2,1,0:T(8,128)S(1)}, f32[8,4,128]{2,1,0:T(4,128)S(1)}, f32[16,16,256]{2,1,0:T(8,128)}) custom-call(f32[128,256]{1,0:T(8,128)S(1)} %solve.3.wide, f32[3,16,16,256]{3,2,1,0:T(8,128)S(1)} %get-tuple-element.71.core, f32[14,16,256]{2,1,0:T(8,128)S(1)} %collective-permute-done.10.low, ...), custom_call_target="tpu_custom_call" | custom-call | tf_op jit(solution)/shard_map/last_iteration/pallas_call | solution.py:878
  70.7 7.1 %all_to_all.17.gathered = f32[8,4,128]{2,1,0:T(4,128)S(1)} all-to-all(f32[8,4,128]{2,1,0:T(4,128)S(1)} %get-tuple-element.76), channel_id=1, replica_groups=mesh['row'=8,'col'=4] {'row'}, dimensions={0} | all-to-all | bytes 32768 | tf_op jit(solution)/shard_map/all_to_all | solution.py:972
  77.8 2.7 %correct.1 = (f32[3,16,16,256]{3,2,1,0:T(8,128)}, f32[3,16,2,32]{3,2,1,0:T(2,128)}) custom-call(f32[8,4,128]{2,1,0:T(4,128)S(1)} %all_to_all.17.gathered, f32[3,16,16,256]{3,2,1,0:T(8,128)S(1)} %get-tuple-element.77.core), custom_call_target="tpu_custom_call" | custom-call | tf_op jit(solution)/shard_map/correct/pallas_call | solution.py:914
Async XLA Ops:
  0.6 9.7 %copy-start.2 = (s32[16,16,256]{2,1,0:T(8,128)S(1)}, s32[16,16,256]{2,1,0:T(8,128)}, u32[]{:S(2)}) copy-start(s32[16,16,256]{2,1,0:T(8,128)} %coil_mask.4) | copy-start | bytes 786436
  0.6 9.7 %copy-start.3 = (s32[16,16,256]{2,1,0:T(8,128)S(1)}, s32[16,16,256]{2,1,0:T(8,128)}, u32[]{:S(2)}) copy-start(s32[16,16,256]{2,1,0:T(8,128)} %labels.4) | copy-start | bytes 786436
  0.7 9.7 %copy-start = (f32[3,16,16,256]{3,2,1,0:T(8,128)S(1)}, f32[3,16,16,256]{3,2,1,0:T(8,128)}, u32[]{:S(2)}) copy-start(f32[3,16,16,256]{3,2,1,0:T(8,128)} %source.4) | copy-start | bytes 2359300
  0.7 9.7 %copy-start.5 = (f32[8]{0:T(128)S(1)}, f32[8]{0:T(128)}, u32[]{:S(2)}) copy-start(f32[8]{0:T(128)} %rise_table.3) | copy-start | bytes 100
  0.7 9.7 %copy-start.4 = (f32[8]{0:T(128)S(1)}, f32[8]{0:T(128)}, u32[]{:S(2)}) copy-start(f32[8]{0:T(128)} %floor_table.3) | copy-start | bytes 100
  2.1 9.3 %collective-permute-start = (f32[21,16,256]{2,1,0:T(8,128)S(1)}, f32[21,16,256]{2,1,0:T(8,128)S(1)}, u32[]{:S(2)}, u32[]{:S(2)}) collective-permute-start(f32[21,16,256]{2,1,0:T(8,128)S(1)} %get-tuple-element.45), channel_id=1, source_target_pairs={{0,4},{4,8},{8,12},{12,16},{16,20},{20,24},{24,28},{28,0},{1,5},{5... | collective-permute-start | bytes 1032200 | tf_op jit(solution)/shard_map/ppermute | solution.py:929
  2.6 16.1 %copy-start.1 = (f32[3,16,16,256]{3,2,1,0:T(8,128)S(1)}, f32[3,16,16,256]{3,2,1,0:T(8,128)}, u32[]{:S(2)}) copy-start(f32[3,16,16,256]{3,2,1,0:T(8,128)} %potential.4) | copy-start | bytes 2359300
  2.6 10.4 %collective-permute-start.1 = (f32[21,16,256]{2,1,0:T(8,128)S(1)}, f32[21,16,256]{2,1,0:T(8,128)S(1)}, u32[]{:S(2)}, u32[]{:S(2)}) collective-permute-start(f32[21,16,256]{2,1,0:T(8,128)S(1)} %get-tuple-element.46), channel_id=1, source_target_pairs={{4,0},{8,4},{12,8},{16,12},{20,16},{24,20},{28,24},{0,28},{5,1},{9... | collective-permute-start | bytes 1032200 | tf_op jit(solution)/shard_map/ppermute | solution.py:929
  7.3 10.4 %collective-permute-start.2 = (f32[91,4,256]{2,1,0:T(4,128)S(1)}, f32[91,4,256]{2,1,0:T(4,128)S(1)}, u32[]{:S(2)}, u32[]{:S(2)}) collective-permute-start(f32[91,4,256]{2,1,0:T(4,128)S(1)} %get-tuple-element.53), channel_id=1, source_target_pairs={{0,1},{1,0},{2,3},{3,2},{4,5},{5,4},{6,7},{7,6},{8,9},{9,8},{10,11... | collective-permute-start | bytes 1118216 | tf_op jit(solution)/shard_map/ppermute | solution.py:940
  9.7 8.0 %collective-permute-start.3 = (f32[91,4,256]{2,1,0:T(4,128)S(1)}, f32[91,4,256]{2,1,0:T(4,128)S(1)}, u32[]{:S(2)}, u32[]{:S(2)}) collective-permute-start(f32[91,4,256]{2,1,0:T(4,128)S(1)} %get-tuple-element.54), channel_id=1, source_target_pairs={{0,0},{1,2},{2,1},{3,3},{4,4},{5,6},{6,5},{7,7},{8,8},{9,10},{10,9... | collective-permute-start | bytes 1118216 | tf_op jit(solution)/shard_map/ppermute | solution.py:940
  13.0 5.6 %collective-permute-start.4 = (f32[48,256]{1,0:T(8,128)S(1)}, f32[48,256]{1,0:T(8,128)S(1)}, u32[]{:S(2)}, u32[]{:S(2)}) collective-permute-start(f32[48,256]{1,0:T(8,128)S(1)} %get-tuple-element.55), channel_id=1, source_target_pairs={{0,1},{1,0},{2,3},{3,2},{4,5},{5,4},{6,7},{7,6},{8,9},{9,8},{10,11... | collective-permute-start | bytes 147464 | tf_op jit(solution)/shard_map/ppermute | solution.py:940
  15.8 2.9 %collective-permute-start.5 = (f32[48,256]{1,0:T(8,128)S(1)}, f32[48,256]{1,0:T(8,128)S(1)}, u32[]{:S(2)}, u32[]{:S(2)}) collective-permute-start(f32[48,256]{1,0:T(8,128)S(1)} %get-tuple-element.56), channel_id=1, source_target_pairs={{0,0},{1,2},{2,1},{3,3},{4,4},{5,6},{6,5},{7,7},{8,8},{9,10},{10,9... | collective-permute-start | bytes 147464 | tf_op jit(solution)/shard_map/ppermute | solution.py:940
  23.5 21.5 %collective-permute-start.6 = (f32[14,16,256]{2,1,0:T(8,128)S(1)}, f32[14,16,256]{2,1,0:T(8,128)S(1)}, u32[]{:S(2)}, u32[]{:S(2)}) collective-permute-start(f32[14,16,256]{2,1,0:T(8,128)S(1)} %get-tuple-element.63), channel_id=1, source_target_pairs={{0,4},{4,8},{8,12},{12,16},{16,20},{20,24},{24,28},{28,0},{1,5},{5... | collective-permute-start | bytes 688136 | tf_op jit(solution)/shard_map/ppermute | solution.py:929
  23.7 21.3 %collective-permute-start.7 = (f32[14,16,256]{2,1,0:T(8,128)S(1)}, f32[14,16,256]{2,1,0:T(8,128)S(1)}, u32[]{:S(2)}, u32[]{:S(2)}) collective-permute-start(f32[14,16,256]{2,1,0:T(8,128)S(1)} %get-tuple-element.64), channel_id=1, source_target_pairs={{4,0},{8,4},{12,8},{16,12},{20,16},{24,20},{28,24},{0,28},{5,1},{9... | collective-permute-start | bytes 688136 | tf_op jit(solution)/shard_map/ppermute | solution.py:929
  26.2 18.8 %collective-permute-start.8 = (f32[54,4,256]{2,1,0:T(4,128)S(1)}, f32[54,4,256]{2,1,0:T(4,128)S(1)}, u32[]{:S(2)}, u32[]{:S(2)}) collective-permute-start(f32[54,4,256]{2,1,0:T(4,128)S(1)} %get-tuple-element.65), channel_id=1, source_target_pairs={{0,1},{1,0},{2,3},{3,2},{4,5},{5,4},{6,7},{7,6},{8,9},{9,8},{10,11... | collective-permute-start | bytes 663560 | tf_op jit(solution)/shard_map/ppermute | solution.py:940
  30.8 14.2 %collective-permute-start.9 = (f32[54,4,256]{2,1,0:T(4,128)S(1)}, f32[54,4,256]{2,1,0:T(4,128)S(1)}, u32[]{:S(2)}, u32[]{:S(2)}) collective-permute-start(f32[54,4,256]{2,1,0:T(4,128)S(1)} %get-tuple-element.66), channel_id=1, source_target_pairs={{0,0},{1,2},{2,1},{3,3},{4,4},{5,6},{6,5},{7,7},{8,8},{9,10},{10,9... | collective-permute-start | bytes 663560 | tf_op jit(solution)/shard_map/ppermute | solution.py:940
  48.8 17.7 %collective-permute-start.10 = (f32[14,16,256]{2,1,0:T(8,128)S(1)}, f32[14,16,256]{2,1,0:T(8,128)S(1)}, u32[]{:S(2)}, u32[]{:S(2)}) collective-permute-start(f32[14,16,256]{2,1,0:T(8,128)S(1)} %get-tuple-element.72), channel_id=1, source_target_pairs={{0,4},{4,8},{8,12},{12,16},{16,20},{20,24},{24,28},{28,0},{1,5},{5... | collective-permute-start | bytes 688136 | tf_op jit(solution)/shard_map/ppermute | solution.py:929
  48.9 17.7 %collective-permute-start.11 = (f32[14,16,256]{2,1,0:T(8,128)S(1)}, f32[14,16,256]{2,1,0:T(8,128)S(1)}, u32[]{:S(2)}, u32[]{:S(2)}) collective-permute-start(f32[14,16,256]{2,1,0:T(8,128)S(1)} %get-tuple-element.73), channel_id=1, source_target_pairs={{4,0},{8,4},{12,8},{16,12},{20,16},{24,20},{28,24},{0,28},{5,1},{9... | collective-permute-start | bytes 688136 | tf_op jit(solution)/shard_map/ppermute | solution.py:929
  51.5 15.0 %collective-permute-start.12 = (f32[54,4,256]{2,1,0:T(4,128)S(1)}, f32[54,4,256]{2,1,0:T(4,128)S(1)}, u32[]{:S(2)}, u32[]{:S(2)}) collective-permute-start(f32[54,4,256]{2,1,0:T(4,128)S(1)} %get-tuple-element.74), channel_id=1, source_target_pairs={{0,1},{1,0},{2,3},{3,2},{4,5},{5,4},{6,7},{7,6},{8,9},{9,8},{10,11... | collective-permute-start | bytes 663560 | tf_op jit(solution)/shard_map/ppermute | solution.py:940
  51.8 14.8 %collective-permute-start.13 = (f32[54,4,256]{2,1,0:T(4,128)S(1)}, f32[54,4,256]{2,1,0:T(4,128)S(1)}, u32[]{:S(2)}, u32[]{:S(2)}) collective-permute-start(f32[54,4,256]{2,1,0:T(4,128)S(1)} %get-tuple-element.75), channel_id=1, source_target_pairs={{0,0},{1,2},{2,1},{3,3},{4,4},{5,6},{6,5},{7,7},{8,8},{9,10},{10,9... | collective-permute-start | bytes 663560 | tf_op jit(solution)/shard_map/ppermute | solution.py:940

commit v8 on v7

--- a/solution.py
+++ b/solution.py
@@ -19,7 +19,6 @@
 TOP = 8
 CORE = TOP + HALO
 ROWS = 40
-HIGH = lax.Precision.HIGHEST
 X_PAGES = 21
 Y_PAGES = 91
 DEEP = (1, BLOCK - 2)
@@ -262,6 +261,19 @@
     return out
 
 
+def exact_dot(values, matrix):
+    high = values.astype(jnp.bfloat16)
+    rest = values - high.astype(jnp.float32)
+    middle = rest.astype(jnp.bfloat16)
+    low = (rest - middle.astype(jnp.float32)).astype(jnp.bfloat16)
+    count = values.shape[0]
+    parts = jnp.dot(
+        jnp.concatenate([high, middle, low], axis=0), matrix.astype(jnp.bfloat16),
+        preferred_element_type=jnp.float32,
+    )
+    return (parts[2 * count :] + parts[count : 2 * count]) + parts[:count]
+
+
 def pick_row(values, index):
     row = lax.broadcasted_iota(jnp.int32, values.shape, 0)
     return jnp.sum(jnp.where(row == index, values, 0.0), axis=0, keepdims=True)
@@ -312,9 +324,7 @@
             picked[spot : spot + 16, :] = (
                 lines[stripe] if group == 0 else pltpu.roll(lines[stripe], LANES - 32 * group, 1)
             )
-    return jnp.dot(
-        picked[...], block_matrix(True), precision=HIGH, preferred_element_type=jnp.float32
-    )
+    return exact_dot(picked[...], block_matrix(True))
 
 
 class Place:
@@ -686,9 +696,7 @@
             for part in range(2):
                 spot = (coarse * 2 + part) * 8 + 3
                 sums[0, spot : spot + 1, z] = means[part] * (1.0 / float(COARSEN ** 3))
-    totals = jnp.dot(
-        sums[0], block_matrix(False), precision=HIGH, preferred_element_type=jnp.float32
-    ) + jnp.dot(sums[1], side_matrix(), precision=HIGH, preferred_element_type=jnp.float32)
+    totals = exact_dot(sums[0], block_matrix(False)) + exact_dot(sums[1], side_matrix())
     result = totals[0:8]
     for group in range(1, 4):
         result = result + pltpu.roll(totals[group * 8 : group * 8 + 8], 32 * group, 1)

time: 80.8 us -> 80.5 us (level)
  no operation moved by 1% of the time
where the time goes in v8:
time: 80.5 us; the launch traced here: 80.2 us
  blocking collectives  31.1 us (39%)
  Pallas kernels  22.8 us (28%)
  starting transfers between devices  21.4 us (27%)
  waiting for transfers between devices  3.93 us (5%)
  between operations  0.88 us (1%)
    all_to_all x2, blocking collectives, shards(): gathered = lax.all_to_all(coarse, ('row', 'col'), 0, 0)  24 us
    ppermute x4, starting transfers between devices, swaps(): lax.ppermute(turn_a, 'col', pairs[0])  9.93 us
    ppermute x3, starting transfers between devices, rings(): lax.ppermute(to_low, 'row', backward)  8.11 us
    pallas_call x2, Pallas kernels, next_iteration(): pl.pallas_call(functools.partial(next_kernel, final), in_specs=[VMEM] * 1...  7.74 us
    all_to_all x1, blocking collectives, shards(): gathered = lax.all_to_all(coarse, 'row', 0, 0)  7.11 us
    pallas_call x1, Pallas kernels, first_iteration(): pl.pallas_call(first_kernel, in_specs=[VMEM] * 7 + [SMEM] * 2 + [VMEM] *...  4.82 us
    pallas_call x2, Pallas kernels, solve(): pl.pallas_call(solve_kernel, in_specs=[VMEM], out_specs=VMEM, out_shape=f...  3.53 us
    pallas_call x2, Pallas kernels, pack_edges(): pl.pallas_call(kernel, in_specs=[pl.BlockSpec(memory_space=pltpu.HBM)] *...  3.17 us
  transfers between devices with their start and end apart: 14, of which 4 were waited for; matrix products, arithmetic and copies ran while one was open for 0% of the time, Pallas kernels for 8%

profile of v8, /device:TPU:0, one launch (start us, length us, event | category | flops | bytes accessed | tf_op | source)
XLA Modules:
  0.0 80.2 jit_solution(848610630638165302)
XLA Ops:
  0.6 0.0 copy-start.2
  0.6 0.0 copy-start.3
  0.7 0.0 copy-start
  0.7 0.0 copy-start.5
  0.7 0.0 copy-start.4
  0.7 1.4 %pack_x.1 = (f32[21,16,256]{2,1,0:T(8,128)S(1)}, f32[21,16,256]{2,1,0:T(8,128)S(1)}) custom-call(f32[3,16,16,256]{3,2,1,0:T(8,128)} %potential.4, f32[3,16,16,256]{3,2,1,0:T(8,128)} %source.4, s32[16,16,256]{2,1,0:T(8,128)} %coil_mask.4, s32[16,16,256]{2,1,0:T(8,128)} %labels.4), custom_call_target="tpu_custom_call" | custom-call | tf_op jit(solution)/shard_map/pack_x/pallas_call | solution.py:122
  2.1 0.5 collective-permute-start
  2.6 0.0 copy-start.1
  2.6 3.0 %collective-permute-start.1 = (f32[21,16,256]{2,1,0:T(8,128)S(1)}, f32[21,16,256]{2,1,0:T(8,128)S(1)}, u32[]{:S(2)}, u32[]{:S(2)}) collective-permute-start(f32[21,16,256]{2,1,0:T(8,128)S(1)} %get-tuple-element.46), channel_id=1, source_target_pairs={{4,0},{8,4},{12,8},{16,12},{20,16},{24,20},{28,24},{0,28},{5,1},{9... | collective-permute-start | bytes 1032200 | tf_op jit(solution)/shard_map/ppermute | solution.py:937
  5.6 1.8 %pack_y.1 = (f32[91,4,256]{2,1,0:T(4,128)S(1)}, f32[91,4,256]{2,1,0:T(4,128)S(1)}) custom-call(f32[3,16,16,256]{3,2,1,0:T(8,128)} %potential.4, f32[3,16,16,256]{3,2,1,0:T(8,128)} %source.4, s32[16,16,256]{2,1,0:T(8,128)} %coil_mask.4, s32[16,16,256]{2,1,0:T(8,128)} %labels.4), custom_call_target="tpu_custom_call" | custom-call | tf_op jit(solution)/shard_map/pack_y/pallas_call | solution.py:122
  7.3 2.3 %collective-permute-start.2 = (f32[91,4,256]{2,1,0:T(4,128)S(1)}, f32[91,4,256]{2,1,0:T(4,128)S(1)}, u32[]{:S(2)}, u32[]{:S(2)}) collective-permute-start(f32[91,4,256]{2,1,0:T(4,128)S(1)} %get-tuple-element.53), channel_id=1, source_target_pairs={{0,1},{1,0},{2,3},{3,2},{4,5},{5,4},{6,7},{7,6},{8,9},{9,8},{10,11... | collective-permute-start | bytes 1118216 | tf_op jit(solution)/shard_map/ppermute | solution.py:948
  9.7 0.7 collective-permute-start.3
  10.3 0.0 copy-done.2
  10.4 0.0 copy-done.3
  10.4 0.0 copy-done
  10.4 0.0 copy-done.5
  10.4 0.0 copy-done.4
  10.4 0.9 %prepare.1 = (f32[32,256]{1,0:T(8,128)S(1)}, f32[3,2,24,24,128]{4,3,2,1,0:T(8,128)S(1)}, f32[2,24,24,128]{3,2,1,0:T(8,128)S(1)}, f32[2,24,24,128]{3,2,1,0:T(8,128)S(1)}) custom-call(f32[3,16,16,256]{3,2,1,0:T(8,128)S(1)} %copy-done, s32[16,16,256]{2,1,0:T(8,128)S(1)} %copy-done.2, s32[16,16,256]{2,1,0:T(8,128)S(1)} %copy-done.3, f32[8]{0:T(128)S(1)} %copy-done.4, ...), custom_call_target="tpu_custom_call" | custom-call | tf_op jit(solution)/shard_map/prepare/pallas_call | solution.py:444
  11.3 0.2 collective-permute-done.low
  11.4 1.5 %collective-permute-done.1.high = f32[21,16,256]{2,1,0:T(8,128)S(1)} collective-permute-done((f32[21,16,256]{2,1,0:T(8,128)S(1)}, f32[21,16,256]{2,1,0:T(8,128)S(1)}, u32[]{:S(2)}, u32[]{:S(2)}) %collective-permute-start.1) | collective-permute-done | bytes 344096 | tf_op jit(solution)/shard_map/ppermute | solution.py:937
  13.0 0.1 pack_corner.1
  13.0 2.8 %collective-permute-start.4 = (f32[48,256]{1,0:T(8,128)S(1)}, f32[48,256]{1,0:T(8,128)S(1)}, u32[]{:S(2)}, u32[]{:S(2)}) collective-permute-start(f32[48,256]{1,0:T(8,128)S(1)} %get-tuple-element.55), channel_id=1, source_target_pairs={{0,1},{1,0},{2,3},{3,2},{4,5},{5,4},{6,7},{7,6},{8,9},{9,8},{10,11... | collective-permute-start | bytes 147464 | tf_op jit(solution)/shard_map/ppermute | solution.py:948
  15.8 0.7 collective-permute-start.5
  16.4 1.3 %collective-permute-done.2.y_a = f32[91,4,256]{2,1,0:T(4,128)S(1)} collective-permute-done((f32[91,4,256]{2,1,0:T(4,128)S(1)}, f32[91,4,256]{2,1,0:T(4,128)S(1)}, u32[]{:S(2)}, u32[]{:S(2)}) %collective-permute-start.2) | collective-permute-done | bytes 372768 | tf_op jit(solution)/shard_map/ppermute | solution.py:948
  17.7 0.0 collective-permute-done.3.y_b
  17.7 1.0 %collective-permute-done.4.c_a = f32[48,256]{1,0:T(8,128)S(1)} collective-permute-done((f32[48,256]{1,0:T(8,128)S(1)}, f32[48,256]{1,0:T(8,128)S(1)}, u32[]{:S(2)}, u32[]{:S(2)}) %collective-permute-start.4) | collective-permute-done | bytes 49184 | tf_op jit(solution)/shard_map/ppermute | solution.py:948
  18.7 0.0 collective-permute-done.5.c_b
  18.7 0.0 copy-done.1
  18.7 4.8 %first_iteration.1 = (f32[3,16,16,256]{3,2,1,0:T(8,128)S(1)}, f32[32,4,128]{2,1,0:T(4,128)S(1)}, f32[14,16,256]{2,1,0:T(8,128)S(1)}, f32[14,16,256]{2,1,0:T(8,12...) custom-call(f32[3,16,16,256]{3,2,1,0:T(8,128)S(1)} %copy-done.1, ...), custom_call_target="tpu_custom_call", output_to_operand_aliasing={{6}: (10, {}), {7}: (11, {}), {8}: (12, {})} | custom-call | tf_op jit(solution)/shard_map/first_iteration/pallas_call | solution.py:791
  23.5 0.2 collective-permute-start.6
  23.7 2.5 %collective-permute-start.7 = (f32[14,16,256]{2,1,0:T(8,128)S(1)}, f32[14,16,256]{2,1,0:T(8,128)S(1)}, u32[]{:S(2)}, u32[]{:S(2)}) collective-permute-start(f32[14,16,256]{2,1,0:T(8,128)S(1)} %get-tuple-element.64), channel_id=1, source_target_pairs={{4,0},{8,4},{12,8},{16,12},{20,16},{24,20},{28,24},{0,28},{5,1},{9... | collective-permute-start | bytes 688136 | tf_op jit(solution)/shard_map/ppermute | solution.py:937
  26.2 4.6 %collective-permute-start.8 = (f32[54,4,256]{2,1,0:T(4,128)S(1)}, f32[54,4,256]{2,1,0:T(4,128)S(1)}, u32[]{:S(2)}, u32[]{:S(2)}) collective-permute-start(f32[54,4,256]{2,1,0:T(4,128)S(1)} %get-tuple-element.65), channel_id=1, source_target_pairs={{0,1},{1,0},{2,3},{3,2},{4,5},{5,4},{6,7},{7,6},{8,9},{9,8},{10,11... | collective-permute-start | bytes 663560 | tf_op jit(solution)/shard_map/ppermute | solution.py:948
  30.8 0.7 collective-permute-start.9
  31.5 11.7 %all_to_all.15 = f32[32,4,128]{2,1,0:T(4,128)S(1)} all-to-all(f32[32,4,128]{2,1,0:T(4,128)S(1)} %get-tuple-element.61), channel_id=1, replica_groups=mesh['row'=8,'col'=4] {'row','col'}, dimensions={0} | all-to-all | bytes 131072 | tf_op jit(solution)/shard_map/all_to_all | solution.py:971
  43.2 1.8 %solve.2.wide = f32[128,256]{1,0:T(8,128)S(1)} custom-call(f32[8,4,4,128]{3,2,1,0:T(4,128)S(1)} %bitcast.2), custom_call_target="tpu_custom_call" | custom-call | tf_op jit(solution)/shard_map/solve/pallas_call | solution.py:822
  44.9 0.0 collective-permute-done.8.y_a
  44.9 0.0 collective-permute-done.9.y_b
  45.0 0.0 collective-permute-done.6.low
  45.0 0.0 collective-permute-done.7.high
  45.0 3.8 %next_iteration.1 = (f32[3,16,16,256]{3,2,1,0:T(8,128)S(1)}, f32[32,4,128]{2,1,0:T(4,128)S(1)}, f32[14,16,256]{2,1,0:T(8,128)S(1)}, f32[14,16,256]{2,1,0:T(8,128...) custom-call(f32[128,256]{1,0:T(8,128)S(1)} %solve.2.wide, f32[3,16,16,256]{3,2,1,0:T(8,128)S(1)} %get-tuple-element.62.core, ...), custom_call_target="tpu_custom_call" | custom-call | tf_op jit(solution)/shard_map/next_iteration/pallas_call | solution.py:886
  48.8 0.1 collective-permute-start.10
  48.9 2.6 %collective-permute-start.11 = (f32[14,16,256]{2,1,0:T(8,128)S(1)}, f32[14,16,256]{2,1,0:T(8,128)S(1)}, u32[]{:S(2)}, u32[]{:S(2)}) collective-permute-start(f32[14,16,256]{2,1,0:T(8,128)S(1)} %get-tuple-element.73), channel_id=1, source_target_pairs={{4,0},{8,4},{12,8},{16,12},{20,16},{24,20},{28,24},{0,28},{5,1},{9... | collective-permute-start | bytes 688136 | tf_op jit(solution)/shard_map/ppermute | solution.py:937
  51.5 0.2 collective-permute-start.12
  51.7 0.7 collective-permute-start.13
  52.4 12.3 %all_to_all.16 = f32[32,4,128]{2,1,0:T(4,128)S(1)} all-to-all(f32[32,4,128]{2,1,0:T(4,128)S(1)} %get-tuple-element.70), channel_id=1, replica_groups=mesh['row'=8,'col'=4] {'row','col'}, dimensions={0} | all-to-all | bytes 131072 | tf_op jit(solution)/shard_map/all_to_all | solution.py:971
  64.7 1.8 %solve.3.wide = f32[128,256]{1,0:T(8,128)S(1)} custom-call(f32[8,4,4,128]{3,2,1,0:T(4,128)S(1)} %bitcast.3), custom_call_target="tpu_custom_call" | custom-call | tf_op jit(solution)/shard_map/solve/pallas_call | solution.py:822
  66.5 0.0 collective-permute-done.12.y_a
  66.5 0.0 collective-permute-done.13.y_b
  66.5 0.0 collective-permute-done.10.low
  66.5 0.0 collective-permute-done.11.high
  66.5 3.9 %last_iteration.1 = (f32[3,16,16,256]{3,2,1,0:T(8,128)S(1)}, f32[8,4,128]{2,1,0:T(4,128)S(1)}, f32[16,16,256]{2,1,0:T(8,128)}) custom-call(f32[128,256]{1,0:T(8,128)S(1)} %solve.3.wide, f32[3,16,16,256]{3,2,1,0:T(8,128)S(1)} %get-tuple-element.71.core, f32[14,16,256]{2,1,0:T(8,128)S(1)} %collective-permute-done.10.low, ...), custom_call_target="tpu_custom_call" | custom-call | tf_op jit(solution)/shard_map/last_iteration/pallas_call | solution.py:886
  70.4 7.1 %all_to_all.17.gathered = f32[8,4,128]{2,1,0:T(4,128)S(1)} all-to-all(f32[8,4,128]{2,1,0:T(4,128)S(1)} %get-tuple-element.76), channel_id=1, replica_groups=mesh['row'=8,'col'=4] {'row'}, dimensions={0} | all-to-all | bytes 32768 | tf_op jit(solution)/shard_map/all_to_all | solution.py:980
  77.5 2.7 %correct.1 = (f32[3,16,16,256]{3,2,1,0:T(8,128)}, f32[3,16,2,32]{3,2,1,0:T(2,128)}) custom-call(f32[8,4,128]{2,1,0:T(4,128)S(1)} %all_to_all.17.gathered, f32[3,16,16,256]{3,2,1,0:T(8,128)S(1)} %get-tuple-element.77.core), custom_call_target="tpu_custom_call" | custom-call | tf_op jit(solution)/shard_map/correct/pallas_call | solution.py:922
Async XLA Ops:
  0.6 9.7 %copy-start.2 = (s32[16,16,256]{2,1,0:T(8,128)S(1)}, s32[16,16,256]{2,1,0:T(8,128)}, u32[]{:S(2)}) copy-start(s32[16,16,256]{2,1,0:T(8,128)} %coil_mask.4) | copy-start | bytes 786436
  0.6 9.7 %copy-start.3 = (s32[16,16,256]{2,1,0:T(8,128)S(1)}, s32[16,16,256]{2,1,0:T(8,128)}, u32[]{:S(2)}) copy-start(s32[16,16,256]{2,1,0:T(8,128)} %labels.4) | copy-start | bytes 786436
  0.7 9.7 %copy-start = (f32[3,16,16,256]{3,2,1,0:T(8,128)S(1)}, f32[3,16,16,256]{3,2,1,0:T(8,128)}, u32[]{:S(2)}) copy-start(f32[3,16,16,256]{3,2,1,0:T(8,128)} %source.4) | copy-start | bytes 2359300
  0.7 9.7 %copy-start.5 = (f32[8]{0:T(128)S(1)}, f32[8]{0:T(128)}, u32[]{:S(2)}) copy-start(f32[8]{0:T(128)} %rise_table.3) | copy-start | bytes 100
  0.7 9.7 %copy-start.4 = (f32[8]{0:T(128)S(1)}, f32[8]{0:T(128)}, u32[]{:S(2)}) copy-start(f32[8]{0:T(128)} %floor_table.3) | copy-start | bytes 100
  2.1 9.3 %collective-permute-start = (f32[21,16,256]{2,1,0:T(8,128)S(1)}, f32[21,16,256]{2,1,0:T(8,128)S(1)}, u32[]{:S(2)}, u32[]{:S(2)}) collective-permute-start(f32[21,16,256]{2,1,0:T(8,128)S(1)} %get-tuple-element.45), channel_id=1, source_target_pairs={{0,4},{4,8},{8,12},{12,16},{16,20},{20,24},{24,28},{28,0},{1,5},{5... | collective-permute-start | bytes 1032200 | tf_op jit(solution)/shard_map/ppermute | solution.py:937
  2.6 16.1 %copy-start.1 = (f32[3,16,16,256]{3,2,1,0:T(8,128)S(1)}, f32[3,16,16,256]{3,2,1,0:T(8,128)}, u32[]{:S(2)}) copy-start(f32[3,16,16,256]{3,2,1,0:T(8,128)} %potential.4) | copy-start | bytes 2359300
  2.6 10.4 %collective-permute-start.1 = (f32[21,16,256]{2,1,0:T(8,128)S(1)}, f32[21,16,256]{2,1,0:T(8,128)S(1)}, u32[]{:S(2)}, u32[]{:S(2)}) collective-permute-start(f32[21,16,256]{2,1,0:T(8,128)S(1)} %get-tuple-element.46), channel_id=1, source_target_pairs={{4,0},{8,4},{12,8},{16,12},{20,16},{24,20},{28,24},{0,28},{5,1},{9... | collective-permute-start | bytes 1032200 | tf_op jit(solution)/shard_map/ppermute | solution.py:937
  7.3 10.4 %collective-permute-start.2 = (f32[91,4,256]{2,1,0:T(4,128)S(1)}, f32[91,4,256]{2,1,0:T(4,128)S(1)}, u32[]{:S(2)}, u32[]{:S(2)}) collective-permute-start(f32[91,4,256]{2,1,0:T(4,128)S(1)} %get-tuple-element.53), channel_id=1, source_target_pairs={{0,1},{1,0},{2,3},{3,2},{4,5},{5,4},{6,7},{7,6},{8,9},{9,8},{10,11... | collective-permute-start | bytes 1118216 | tf_op jit(solution)/shard_map/ppermute | solution.py:948
  9.7 8.0 %collective-permute-start.3 = (f32[91,4,256]{2,1,0:T(4,128)S(1)}, f32[91,4,256]{2,1,0:T(4,128)S(1)}, u32[]{:S(2)}, u32[]{:S(2)}) collective-permute-start(f32[91,4,256]{2,1,0:T(4,128)S(1)} %get-tuple-element.54), channel_id=1, source_target_pairs={{0,0},{1,2},{2,1},{3,3},{4,4},{5,6},{6,5},{7,7},{8,8},{9,10},{10,9... | collective-permute-start | bytes 1118216 | tf_op jit(solution)/shard_map/ppermute | solution.py:948
  13.0 5.6 %collective-permute-start.4 = (f32[48,256]{1,0:T(8,128)S(1)}, f32[48,256]{1,0:T(8,128)S(1)}, u32[]{:S(2)}, u32[]{:S(2)}) collective-permute-start(f32[48,256]{1,0:T(8,128)S(1)} %get-tuple-element.55), channel_id=1, source_target_pairs={{0,1},{1,0},{2,3},{3,2},{4,5},{5,4},{6,7},{7,6},{8,9},{9,8},{10,11... | collective-permute-start | bytes 147464 | tf_op jit(solution)/shard_map/ppermute | solution.py:948
  15.8 2.9 %collective-permute-start.5 = (f32[48,256]{1,0:T(8,128)S(1)}, f32[48,256]{1,0:T(8,128)S(1)}, u32[]{:S(2)}, u32[]{:S(2)}) collective-permute-start(f32[48,256]{1,0:T(8,128)S(1)} %get-tuple-element.56), channel_id=1, source_target_pairs={{0,0},{1,2},{2,1},{3,3},{4,4},{5,6},{6,5},{7,7},{8,8},{9,10},{10,9... | collective-permute-start | bytes 147464 | tf_op jit(solution)/shard_map/ppermute | solution.py:948
  23.5 21.5 %collective-permute-start.6 = (f32[14,16,256]{2,1,0:T(8,128)S(1)}, f32[14,16,256]{2,1,0:T(8,128)S(1)}, u32[]{:S(2)}, u32[]{:S(2)}) collective-permute-start(f32[14,16,256]{2,1,0:T(8,128)S(1)} %get-tuple-element.63), channel_id=1, source_target_pairs={{0,4},{4,8},{8,12},{12,16},{16,20},{20,24},{24,28},{28,0},{1,5},{5... | collective-permute-start | bytes 688136 | tf_op jit(solution)/shard_map/ppermute | solution.py:937
  23.7 21.3 %collective-permute-start.7 = (f32[14,16,256]{2,1,0:T(8,128)S(1)}, f32[14,16,256]{2,1,0:T(8,128)S(1)}, u32[]{:S(2)}, u32[]{:S(2)}) collective-permute-start(f32[14,16,256]{2,1,0:T(8,128)S(1)} %get-tuple-element.64), channel_id=1, source_target_pairs={{4,0},{8,4},{12,8},{16,12},{20,16},{24,20},{28,24},{0,28},{5,1},{9... | collective-permute-start | bytes 688136 | tf_op jit(solution)/shard_map/ppermute | solution.py:937
  26.2 18.7 %collective-permute-start.8 = (f32[54,4,256]{2,1,0:T(4,128)S(1)}, f32[54,4,256]{2,1,0:T(4,128)S(1)}, u32[]{:S(2)}, u32[]{:S(2)}) collective-permute-start(f32[54,4,256]{2,1,0:T(4,128)S(1)} %get-tuple-element.65), channel_id=1, source_target_pairs={{0,1},{1,0},{2,3},{3,2},{4,5},{5,4},{6,7},{7,6},{8,9},{9,8},{10,11... | collective-permute-start | bytes 663560 | tf_op jit(solution)/shard_map/ppermute | solution.py:948
  30.8 14.2 %collective-permute-start.9 = (f32[54,4,256]{2,1,0:T(4,128)S(1)}, f32[54,4,256]{2,1,0:T(4,128)S(1)}, u32[]{:S(2)}, u32[]{:S(2)}) collective-permute-start(f32[54,4,256]{2,1,0:T(4,128)S(1)} %get-tuple-element.66), channel_id=1, source_target_pairs={{0,0},{1,2},{2,1},{3,3},{4,4},{5,6},{6,5},{7,7},{8,8},{9,10},{10,9... | collective-permute-start | bytes 663560 | tf_op jit(solution)/shard_map/ppermute | solution.py:948
  48.8 17.7 %collective-permute-start.10 = (f32[14,16,256]{2,1,0:T(8,128)S(1)}, f32[14,16,256]{2,1,0:T(8,128)S(1)}, u32[]{:S(2)}, u32[]{:S(2)}) collective-permute-start(f32[14,16,256]{2,1,0:T(8,128)S(1)} %get-tuple-element.72), channel_id=1, source_target_pairs={{0,4},{4,8},{8,12},{12,16},{16,20},{20,24},{24,28},{28,0},{1,5},{5... | collective-permute-start | bytes 688136 | tf_op jit(solution)/shard_map/ppermute | solution.py:937
  48.9 17.6 %collective-permute-start.11 = (f32[14,16,256]{2,1,0:T(8,128)S(1)}, f32[14,16,256]{2,1,0:T(8,128)S(1)}, u32[]{:S(2)}, u32[]{:S(2)}) collective-permute-start(f32[14,16,256]{2,1,0:T(8,128)S(1)} %get-tuple-element.73), channel_id=1, source_target_pairs={{4,0},{8,4},{12,8},{16,12},{20,16},{24,20},{28,24},{0,28},{5,1},{9... | collective-permute-start | bytes 688136 | tf_op jit(solution)/shard_map/ppermute | solution.py:937
  51.5 15.0 %collective-permute-start.12 = (f32[54,4,256]{2,1,0:T(4,128)S(1)}, f32[54,4,256]{2,1,0:T(4,128)S(1)}, u32[]{:S(2)}, u32[]{:S(2)}) collective-permute-start(f32[54,4,256]{2,1,0:T(4,128)S(1)} %get-tuple-element.74), channel_id=1, source_target_pairs={{0,1},{1,0},{2,3},{3,2},{4,5},{5,4},{6,7},{7,6},{8,9},{9,8},{10,11... | collective-permute-start | bytes 663560 | tf_op jit(solution)/shard_map/ppermute | solution.py:948
  51.7 14.7 %collective-permute-start.13 = (f32[54,4,256]{2,1,0:T(4,128)S(1)}, f32[54,4,256]{2,1,0:T(4,128)S(1)}, u32[]{:S(2)}, u32[]{:S(2)}) collective-permute-start(f32[54,4,256]{2,1,0:T(4,128)S(1)} %get-tuple-element.75), channel_id=1, source_target_pairs={{0,0},{1,2},{2,1},{3,3},{4,4},{5,6},{6,5},{7,7},{8,8},{9,10},{10,9... | collective-permute-start | bytes 663560 | tf_op jit(solution)/shard_map/ppermute | solution.py:948
